TPU v7x, 256 devices: a whole 4x4x8 slice. The times are simulated.
256 devices in a mesh: energy: 16 (over z_lo, y, core), slab: 16 (over z_hi, x).
Axes of the slice: x: 4, y: 4, z: 8 (z_hi: 4, z_lo: 2; z = z_hi * 2 + z_lo), core: 2. Of those that a mesh axis runs over, the one named last changes fastest.
Arguments:
- energies: float32 [32], P('energy'), may hold values from 2 to 3
- hamiltonian: bfloat16 [16, 512, 512], P('slab'), may hold values from -0.125 to 0.125
- coupling: bfloat16 [16, 512, 512], P('slab'), may hold values from -0.09375 to 0.09375
- coulomb: bfloat16 [16, 512, 512], P('slab', 'energy'), may hold values from 0.19921875 to 1
- offsets: int32 [8], replicated, may hold values from -16 to 16
Outputs:
- green: float32 [32, 16, 512, 512], P('energy', 'slab')
- self_part: bfloat16 [32, 16, 512, 512], P('energy', 'slab')
All inputs are finite; a program needn't handle non-finite values.
Results may differ from a plain program's by a relative error of at most 0.0058.
Values may be sent and summed in bfloat16 or wider, within the bound.
No kernel may reach another device: no remote copies, remote signals or barrier semaphores. Data moves between devices by JAX's collectives and lax.ppermute only.
A program may use at most 64 MiB of HBM per device.

v0:
```python
import jax
import jax.numpy as jnp
from jax import lax
from jax.sharding import PartitionSpec as P

ROUNDS = 2
PASSES = 2


BROAD = 0.3


def passed_along(value, axis, steps):
    count = lax.axis_size(axis)
    leading, last = (max(0, -steps), min(count, count - steps))
    return lax.ppermute(value, axis, [(source, source + steps) for source in range(leading, last)])


def unit_tables(matrix_order):
    row_index = lax.broadcasted_iota(jnp.int32, (matrix_order, matrix_order), 0)
    column_index = lax.broadcasted_iota(jnp.int32, (matrix_order, matrix_order), 1)
    half_order = matrix_order // 2
    identity = (row_index == column_index).astype(jnp.float32)
    rotate = jnp.where(
        (row_index < half_order) & (column_index == row_index + half_order), -1.0, 0.0
    ) + jnp.where((row_index >= half_order) & (column_index == row_index - half_order), 1.0, 0.0)
    return (identity, rotate.astype(jnp.float32))


def newton_step(iterate, self_part, base_matrix, identity, link_here):
    green_half = iterate.astype(jnp.bfloat16)
    above_block = passed_along(green_half, "slab", -1)
    inner_term = jnp.einsum(
        "eij,jk->eik", green_half, link_here, preferred_element_type=jnp.float32
    ).astype(jnp.bfloat16)
    own_term = jnp.einsum(
        "ji,ejk->eik", link_here, inner_term, preferred_element_type=jnp.float32
    ).astype(jnp.bfloat16)
    lower_term = passed_along(own_term, "slab", 1)
    right_term = jnp.einsum(
        "eij,kj->eik", above_block, link_here, preferred_element_type=jnp.float32
    ).astype(jnp.bfloat16)
    upper_term = jnp.einsum(
        "ij,ejk->eik", link_here, right_term, preferred_element_type=jnp.float32
    )
    matrix = (
        base_matrix - self_part.astype(jnp.float32) - upper_term - lower_term.astype(jnp.float32)
    )
    product = jnp.einsum(
        "eij,ejk->eik", matrix.astype(jnp.bfloat16), green_half, preferred_element_type=jnp.float32
    )
    residue = (2.0 * identity - product).astype(jnp.bfloat16)
    return jnp.einsum("eij,ejk->eik", green_half, residue, preferred_element_type=jnp.float32)


def self_energy(green_half, coulomb, offsets):
    elements = lax.all_to_all(
        green_half[:, None], "energy", split_axis=2, concat_axis=0, tiled=True
    )
    energy_count = elements.shape[0]
    flat_green = elements.reshape(energy_count, -1)
    flat_wide = flat_green.astype(jnp.float32)
    strength = coulomb.astype(jnp.float32).reshape(-1)
    level_index = lax.broadcasted_iota(jnp.int32, (energy_count, energy_count), 0)
    source_index = lax.broadcasted_iota(jnp.int32, (energy_count, energy_count), 1)
    offset_count = offsets.shape[0]
    running = jnp.zeros(flat_wide.shape, jnp.float32)
    for number in range(offset_count):
        offset_now = offsets[number]
        ahead_table = (source_index == level_index + offset_now).astype(jnp.bfloat16)
        behind_table = (source_index == level_index - offset_now).astype(jnp.bfloat16)
        later_green = jnp.dot(ahead_table, flat_green, preferred_element_type=jnp.float32)
        polarization = 4.0 / energy_count * jnp.sum(flat_wide * later_green, axis=0)
        screened = strength * (1.0 + polarization * strength)
        earlier_green = jnp.dot(behind_table, flat_green, preferred_element_type=jnp.float32)
        running = running + screened[None] * earlier_green
    self_local = (running / offset_count).astype(jnp.bfloat16).reshape(elements.shape)
    returned = lax.all_to_all(self_local, "energy", split_axis=0, concat_axis=2, tiled=True)
    return returned[:, 0]


def local(energies, hamiltonian, coupling, coulomb, offsets):
    matrix_order = hamiltonian.shape[1]
    identity, rotate = unit_tables(matrix_order)
    base_matrix = (
        energies[:, None, None] * identity + BROAD * rotate - hamiltonian[0].astype(jnp.float32)
    )
    iterate = identity[None] / energies[:, None, None]
    self_part = jnp.zeros(iterate.shape, jnp.bfloat16)
    for round_index in range(ROUNDS):
        for pass_index in range(PASSES):
            iterate = newton_step(iterate, self_part, base_matrix, identity, coupling[0])
        self_part = self_energy(iterate.astype(jnp.bfloat16), coulomb, offsets)
    return (iterate[:, None], self_part[:, None])


def solution(mesh):
    placed = (
        P("energy"),
        P("slab", None, None),
        P("slab", None, None),
        P("slab", "energy", None),
        P(),
    )
    return jax.shard_map(
        local,
        mesh=mesh,
        in_specs=placed,
        out_specs=(P("energy", "slab", None, None), P("energy", "slab", None, None)),
        check_vma=False,
    )
```

profile of v0, /device:TPU:70, one launch (start us, length us, event | category | flops | bytes accessed | tf_op | source)
XLA Modules:
  0.0 365.7 jit_solution(2648825465019756250)
XLA Ops:
  0.8 0.9 divide_convert_fusion
  1.7 2.3 fusion.43
  4.0 6.4 %collective-permute-start.1 = (bf16[2,512,512]{2,1,0:T(8,128)(2,1)}, bf16[2,512,512]{2,1,0:T(8,128)(2,1)}, u32[]{:S(2)}, u32[]{:S(2)}) collective-permute-start(bf16[2,512,512]{2,1,0:T(8,128)(2,1)} %fusion.43), channel_id=1, source_target_pairs={{0,1},{1,2},{2,3},{3,4},{4,5},{5,6},{6,7},{7,8},{8,9},{9,10},{10,1... | collective-permute-start | bytes 3145736 | tf_op jit(solution)/shard_map/ppermute | solution.py:16
  10.4 1.9 collective-permute-start
  12.4 1.1 fusion.52
  13.5 1.4 add_multiply_fusion
  14.9 1.2 bitcast_convert_fusion
  16.1 39.5 %collective-permute-done.1 = bf16[2,512,512]{2,1,0:T(8,128)(2,1)} collective-permute-done((bf16[2,512,512]{2,1,0:T(8,128)(2,1)}, bf16[2,512,512]{2,1,0:T(8,128)(2,1)}, u32[]{:S(2)}, u32[]{:S(2)}) %collective-permute-start.1) | collective-permute-done | bytes 1048608 | tf_op jit(solution)/shard_map/ppermute | solution.py:16
  55.6 8.0 %collective-permute-done = bf16[2,512,512]{2,1,0:T(8,128)(2,1)} collective-permute-done((bf16[2,512,512]{2,1,0:T(8,128)(2,1)S(1)}, bf16[2,512,512]{2,1,0:T(8,128)(2,1)}, u32[]{:S(2)}, u32[]{:S(2)}) %collective-permute-start) | collective-permute-done | bytes 1048608 | tf_op jit(solution)/shard_map/ppermute | solution.py:16
  63.6 4.6 %fusion.25 = bf16[2,512,512]{2,1,0:T(8,128)(2,1)} fusion(bf16[2,512,512]{2,1,0:T(8,128)(2,1)} %collective-permute-done.1, f32[512,512]{1,0:T(8,128)} %bitcast_convert_fusion, f32[512,512]{1,0:T(8,128)} %add_multiply_fusion, f32[2]{0:T(128)S(1)} %copy-done.7, f32[512,512]{1,0:T(8,128)S(1)} %fusion.53, bf16[2,512,512]{2,1,0:T(8,128)(2,1)} %collective-permute-done, ...), kind=kOutput, calls=%fused_computation.63 | convolution fusion | flops 1077936128 | bytes 6815752 | tf_op jit(solution)/shard_map/ij,ejk->eik/dot_general | solution.py:43
  68.2 3.8 %convolution_convert_fusion.2 = bf16[2,512,512]{2,1,0:T(8,128)(2,1)} fusion(bf16[2,512,512]{2,1,0:T(8,128)(2,1)S(1)} %divide_convert_fusion, bf16[2,512,512]{2,1,0:T(8,128)(2,1)} %fusion.25, f32[512,512]{1,0:T(8,128)} %fusion.52), kind=kOutput, calls=%fused_computation.74 | convolution fusion | flops 1075314688 | bytes 4194304 | tf_op jit(solution)/shard_map/eij,ejk->eik/dot_general | solution.py:53
  72.0 3.6 fusion.44
  75.6 1.9 collective-permute-start.3
  77.5 3.9 %collective-permute-start.2 = (bf16[2,512,512]{2,1,0:T(8,128)(2,1)}, bf16[2,512,512]{2,1,0:T(8,128)(2,1)}, u32[]{:S(2)}, u32[]{:S(2)}) collective-permute-start(bf16[2,512,512]{2,1,0:T(8,128)(2,1)} %convolution_convert_fusion.2), channel_id=1, source_target_pairs={{1,0},{2,1},{3,2},{4,3},{5,4},{6,5},{7,6},{8,7},{9,8},{10,9},{11,1... | collective-permute-start | bytes 3145736 | tf_op jit(solution)/shard_map/ppermute | solution.py:16
  81.4 40.8 %collective-permute-done.3 = bf16[2,512,512]{2,1,0:T(8,128)(2,1)} collective-permute-done((bf16[2,512,512]{2,1,0:T(8,128)(2,1)}, bf16[2,512,512]{2,1,0:T(8,128)(2,1)}, u32[]{:S(2)}, u32[]{:S(2)}) %collective-permute-start.3) | collective-permute-done | bytes 1048608 | tf_op jit(solution)/shard_map/ppermute | solution.py:16
  122.3 5.8 %collective-permute-done.2 = bf16[2,512,512]{2,1,0:T(8,128)(2,1)} collective-permute-done((bf16[2,512,512]{2,1,0:T(8,128)(2,1)}, bf16[2,512,512]{2,1,0:T(8,128)(2,1)}, u32[]{:S(2)}, u32[]{:S(2)}) %collective-permute-start.2) | collective-permute-done | bytes 1048608 | tf_op jit(solution)/shard_map/ppermute | solution.py:16
  128.1 4.3 %fusion.23 = bf16[2,512,512]{2,1,0:T(8,128)(2,1)} fusion(bf16[2,512,512]{2,1,0:T(8,128)(2,1)} %collective-permute-done.3, f32[512,512]{1,0:T(8,128)} %bitcast_convert_fusion, f32[512,512]{1,0:T(8,128)S(1)} %copy-done.1, f32[2]{0:T(128)S(1)} %copy-done.7, f32[512,512]{1,0:T(8,128)S(1)} %fusion.53, bf16[2,512,512]{2,1,0:T(8,128)(2,1)} %collective-permute-done.2, ...), kind=kOutput, calls=%fused_computation.60 | convolution fusion | flops 1077936128 | bytes 6815752 | tf_op jit(solution)/shard_map/ij,ejk->eik/dot_general | solution.py:43
  132.4 3.5 convolution_convert_fusion.1
  136.0 2.0 copy.12
  138.0 4.6 %all-to-all-start = ((bf16[2,1,512,512]{3,0,1,2:T(2,128)(2,1)}), bf16[2,1,512,512]{3,0,1,2:T(2,128)(2,1)S(1)}, u32[]{:S(2)}, u32[]{:S(2)}) async-start(bf16[2,1,512,512]{3,0,1,2:T(2,128)(2,1)} %copy.12), calls=%async_computation | async-start | bytes 2097152 | tf_op jit(solution)/shard_map/all_to_all | solution.py:57
  142.7 0.7 fusion.104
  143.4 0.7 iota_subtract_fusion.7
  144.0 0.7 iota_subtract_fusion.6
  145.3 0.6 iota_subtract_fusion.4
  145.9 0.7 iota_subtract_fusion.3
  146.6 0.6 iota_subtract_fusion.2
  147.7 0.6 iota_subtract_fusion
  148.3 10.8 %all-to-all-done = bf16[2,1,512,512]{3,0,1,2:T(2,128)(2,1)S(1)} async-done(((bf16[2,1,512,512]{3,0,1,2:T(2,128)(2,1)}), bf16[2,1,512,512]{3,0,1,2:T(2,128)(2,1)S(1)}, u32[]{:S(2)}, u32[]{:S(2)}) %all-to-all-start) | async-done | bytes 1048608 | tf_op jit(solution)/shard_map/all_to_all | solution.py:57
  159.4 0.6 copy.22
  160.5 0.6 fusion.28
  161.6 0.6 fusion.30
  162.2 0.6 fusion.31
  162.8 0.6 fusion.32
  163.3 0.6 fusion.33
  163.9 0.6 fusion.34
  167.5 0.9 fusion.4
  168.3 0.6 fusion.17
  168.9 1.3 copy.23
  170.2 3.7 all-to-all-start.1
  173.9 3.6 fusion.45
  177.5 2.8 collective-permute-start.5
  180.3 3.3 collective-permute-start.4
  183.5 8.6 %all-to-all-done.1 = bf16[32,1,32,512]{3,2,1,0:T(8,128)(2,1)S(1)} async-done(((bf16[32,1,32,512]{3,2,1,0:T(8,128)(2,1)}), bf16[32,1,32,512]{3,2,1,0:T(8,128)(2,1)S(1)}, u32[]{:S(2)}, u32[]{:S(2)}) %all-to-all-start.1) | async-done | bytes 1048608 | tf_op jit(solution)/shard_map/all_to_all | solution.py:78
  192.5 1.5 copy.15
  194.0 37.2 %collective-permute-done.5 = bf16[2,512,512]{2,1,0:T(8,128)(2,1)} collective-permute-done((bf16[2,512,512]{2,1,0:T(8,128)(2,1)}, bf16[2,512,512]{2,1,0:T(8,128)(2,1)}, u32[]{:S(2)}, u32[]{:S(2)}) %collective-permute-start.5) | collective-permute-done | bytes 1048608 | tf_op jit(solution)/shard_map/ppermute | solution.py:16
  231.1 1.5 collective-permute-done.4
  232.6 4.9 %fusion.21 = bf16[2,512,512]{2,1,0:T(8,128)(2,1)} fusion(bf16[2,512,512]{2,1,0:T(8,128)(2,1)} %collective-permute-done.5, f32[2,512,512]{2,1,0:T(8,128)} %bitcast.206, f32[512,512]{1,0:T(8,128)} %bitcast_convert_fusion, f32[512,512]{1,0:T(8,128)S(1)} %copy-done.2, f32[2]{0:T(128)S(1)} %copy-done.7, f32[512,512]{1,0:T(8,128)S(1)} %fusion.53, ...), kind=kOutput, calls=%fused_computation.57 | convolution fusion | flops 1078460416 | bytes 8912904 | tf_op jit(solution)/shard_map/ij,ejk->eik/dot_general | solution.py:43
  237.5 4.4 %convolution_convert_fusion = bf16[2,512,512]{2,1,0:T(8,128)(2,1)} fusion(bf16[2,512,512]{2,1,0:T(8,128)(2,1)} %copy-done.3, bf16[2,512,512]{2,1,0:T(8,128)(2,1)} %fusion.21, f32[512,512]{1,0:T(8,128)} %fusion.52), kind=kOutput, calls=%fused_computation.72 | convolution fusion | flops 1075314688 | bytes 4194304 | tf_op jit(solution)/shard_map/eij,ejk->eik/dot_general | solution.py:53
  242.0 3.5 fusion.46
  245.5 7.1 %collective-permute-start.7 = (bf16[2,512,512]{2,1,0:T(8,128)(2,1)}, bf16[2,512,512]{2,1,0:T(8,128)(2,1)}, u32[]{:S(2)}, u32[]{:S(2)}) collective-permute-start(bf16[2,512,512]{2,1,0:T(8,128)(2,1)} %fusion.46), channel_id=1, source_target_pairs={{0,1},{1,2},{2,3},{3,4},{4,5},{5,6},{6,7},{7,8},{8,9},{9,10},{10,1... | collective-permute-start | bytes 3145736 | tf_op jit(solution)/shard_map/ppermute | solution.py:16
  252.6 1.9 collective-permute-start.6
  254.6 41.7 %collective-permute-done.7 = bf16[2,512,512]{2,1,0:T(8,128)(2,1)} collective-permute-done((bf16[2,512,512]{2,1,0:T(8,128)(2,1)}, bf16[2,512,512]{2,1,0:T(8,128)(2,1)}, u32[]{:S(2)}, u32[]{:S(2)}) %collective-permute-start.7) | collective-permute-done | bytes 1048608 | tf_op jit(solution)/shard_map/ppermute | solution.py:16
  296.2 4.9 %fusion.19 = bf16[2,512,512]{2,1,0:T(8,128)(2,1)} fusion(bf16[2,512,512]{2,1,0:T(8,128)(2,1)} %collective-permute-done.7, f32[2,512,512]{2,1,0:T(8,128)} %bitcast.207, f32[512,512]{1,0:T(8,128)} %bitcast_convert_fusion, f32[512,512]{1,0:T(8,128)S(1)} %copy-done.2, f32[2]{0:T(128)S(1)} %copy-done.7, f32[512,512]{1,0:T(8,128)S(1)} %fusion.53, ...), kind=kOutput, calls=%fused_computation.54 | convolution fusion | flops 1078460416 | bytes 8912904 | tf_op jit(solution)/shard_map/ij,ejk->eik/dot_general | solution.py:43
  301.1 4.7 %fusion.47 = f32[2,512,512]{2,1,0:T(8,128)} fusion(bf16[2,512,512]{2,1,0:T(8,128)(2,1)} %convolution_convert_fusion, bf16[2,512,512]{2,1,0:T(8,128)(2,1)} %fusion.19, f32[512,512]{1,0:T(8,128)} %fusion.52), kind=kOutput, calls=%fused_computation.107 | convolution fusion | flops 1074790400 | bytes 5242880 | tf_op jit(solution)/shard_map/eij,ejk->eik/dot_general | solution.py:53
  305.9 1.7 convert_bitcast_fusion.1
  307.6 1.1 copy.16
  308.7 26.7 %all_to_all.57 = bf16[2,1,512,512]{3,0,1,2:T(2,128)(2,1)S(1)} all-to-all(bf16[2,1,512,512]{3,0,1,2:T(2,128)(2,1)S(1)} %copy.16), channel_id=1, replica_groups=mesh['energy'=16,'slab'=16] {'energy'}, dimensions={2} | all-to-all | bytes 2097152 | tf_op jit(solution)/shard_map/all_to_all | solution.py:57
  335.5 0.6 copy.24
  336.1 0.6 fusion.35
  336.7 0.6 fusion.36
  343.7 0.9 fusion.12
  344.6 0.6 fusion.16
  345.6 19.1 %all_to_all.58 = bf16[32,1,32,512]{3,2,1,0:T(8,128)(2,1)S(1)} all-to-all(bf16[32,1,32,512]{3,2,1,0:T(8,128)(2,1)S(1)} %bitcast.203), channel_id=1, replica_groups=mesh['energy'=16,'slab'=16] {'energy'}, dimensions={0} | all-to-all | bytes 2097152 | tf_op jit(solution)/shard_map/all_to_all | solution.py:78
  364.6 1.0 copy.19
  (50 shorter events, 12.7 us)
Async XLA Ops:
  0.6 1.1 copy-start
  4.0 10.9 %copy-start.4 = (bf16[1,512,512]{2,1,0:T(8,128)(2,1)S(1)}, bf16[1,512,512]{2,1,0:T(8,128)(2,1)}, u32[]{:S(2)}) copy-start(bf16[1,512,512]{2,1,0:T(8,128)(2,1)} %param.6) | copy-start | bytes 1572868
  4.0 59.6 %copy-start.7 = (f32[2]{0:T(128)S(1)}, f32[2]{0:T(128)}, u32[]{:S(2)}) copy-start(f32[2]{0:T(128)} %param.5) | copy-start | bytes 28
  4.0 51.6 %collective-permute-start.1 = (bf16[2,512,512]{2,1,0:T(8,128)(2,1)}, bf16[2,512,512]{2,1,0:T(8,128)(2,1)}, u32[]{:S(2)}, u32[]{:S(2)}) collective-permute-start(bf16[2,512,512]{2,1,0:T(8,128)(2,1)} %fusion.43), channel_id=1, source_target_pairs={{0,1},{1,2},{2,3},{3,4},{4,5},{5,6},{6,7},{7,8},{8,9},{9,10},{10,1... | collective-permute-start | bytes 3145736 | tf_op jit(solution)/shard_map/ppermute | solution.py:16
  10.4 53.2 %collective-permute-start = (bf16[2,512,512]{2,1,0:T(8,128)(2,1)S(1)}, bf16[2,512,512]{2,1,0:T(8,128)(2,1)}, u32[]{:S(2)}, u32[]{:S(2)}) collective-permute-start(bf16[2,512,512]{2,1,0:T(8,128)(2,1)S(1)} %divide_convert_fusion), channel_id=1, source_target_pairs={{1,0},{2,1},{3,2},{4,3},{5,4},{6,5},{7,6},{8,7},{9,8},{10,9},{11,1... | collective-permute-start | bytes 3145736 | tf_op jit(solution)/shard_map/ppermute | solution.py:16
  72.0 56.1 %copy-start.1 = (f32[512,512]{1,0:T(8,128)S(1)}, f32[512,512]{1,0:T(8,128)}, u32[]{:S(2)}) copy-start(f32[512,512]{1,0:T(8,128)} %add_multiply_fusion) | copy-start | bytes 3145732
  75.6 46.7 %collective-permute-start.3 = (bf16[2,512,512]{2,1,0:T(8,128)(2,1)}, bf16[2,512,512]{2,1,0:T(8,128)(2,1)}, u32[]{:S(2)}, u32[]{:S(2)}) collective-permute-start(bf16[2,512,512]{2,1,0:T(8,128)(2,1)} %fusion.44), channel_id=1, source_target_pairs={{0,1},{1,2},{2,3},{3,4},{4,5},{5,6},{6,7},{7,8},{8,9},{9,10},{10,1... | collective-permute-start | bytes 3145736 | tf_op jit(solution)/shard_map/ppermute | solution.py:16
  77.5 50.6 %collective-permute-start.2 = (bf16[2,512,512]{2,1,0:T(8,128)(2,1)}, bf16[2,512,512]{2,1,0:T(8,128)(2,1)}, u32[]{:S(2)}, u32[]{:S(2)}) collective-permute-start(bf16[2,512,512]{2,1,0:T(8,128)(2,1)} %convolution_convert_fusion.2), channel_id=1, source_target_pairs={{1,0},{2,1},{3,2},{4,3},{5,4},{6,5},{7,6},{8,7},{9,8},{10,9},{11,1... | collective-permute-start | bytes 3145736 | tf_op jit(solution)/shard_map/ppermute | solution.py:16
  136.0 2.1 copy-start.3
  136.0 6.6 %copy-start.5 = (bf16[1,32,512]{2,1,0:T(8,128)(2,1)S(1)}, bf16[1,32,512]{2,1,0:T(8,128)(2,1)}, u32[]{:S(2)}) copy-start(bf16[1,32,512]{2,1,0:T(8,128)(2,1)} %param.8) | copy-start | bytes 98308
  136.0 6.7 %copy-start.6 = (s32[8]{0:T(128)S(1)}, s32[8]{0:T(128)}, u32[]{:S(2)}) copy-start(s32[8]{0:T(128)} %param.9) | copy-start | bytes 100
  138.0 21.1 %all-to-all-start = ((bf16[2,1,512,512]{3,0,1,2:T(2,128)(2,1)}), bf16[2,1,512,512]{3,0,1,2:T(2,128)(2,1)S(1)}, u32[]{:S(2)}, u32[]{:S(2)}) async-start(bf16[2,1,512,512]{3,0,1,2:T(2,128)(2,1)} %copy.12), calls=%async_computation | async-start | bytes 2097152 | tf_op jit(solution)/shard_map/all_to_all | solution.py:57
  170.2 21.9 %all-to-all-start.1 = ((bf16[32,1,32,512]{3,2,1,0:T(8,128)(2,1)}), bf16[32,1,32,512]{3,2,1,0:T(8,128)(2,1)S(1)}, u32[]{:S(2)}, u32[]{:S(2)}) async-start(bf16[32,1,32,512]{3,2,1,0:T(8,128)(2,1)} %bitcast.199), calls=%async_computation.1 | async-start | bytes 2097152 | tf_op jit(solution)/shard_map/all_to_all | solution.py:78
  177.5 53.7 %collective-permute-start.5 = (bf16[2,512,512]{2,1,0:T(8,128)(2,1)}, bf16[2,512,512]{2,1,0:T(8,128)(2,1)}, u32[]{:S(2)}, u32[]{:S(2)}) collective-permute-start(bf16[2,512,512]{2,1,0:T(8,128)(2,1)} %fusion.45), channel_id=1, source_target_pairs={{0,1},{1,2},{2,3},{3,4},{4,5},{5,6},{6,7},{7,8},{8,9},{9,10},{10,1... | collective-permute-start | bytes 3145736 | tf_op jit(solution)/shard_map/ppermute | solution.py:16
  180.3 52.3 %collective-permute-start.4 = (bf16[2,512,512]{2,1,0:T(8,128)(2,1)}, bf16[2,512,512]{2,1,0:T(8,128)(2,1)}, u32[]{:S(2)}, u32[]{:S(2)}) collective-permute-start(bf16[2,512,512]{2,1,0:T(8,128)(2,1)} %copy-done.3), channel_id=1, source_target_pairs={{1,0},{2,1},{3,2},{4,3},{5,4},{6,5},{7,6},{8,7},{9,8},{10,9},{11,1... | collective-permute-start | bytes 3145736 | tf_op jit(solution)/shard_map/ppermute | solution.py:16
  192.4 40.2 %copy-start.2 = (f32[512,512]{1,0:T(8,128)S(1)}, f32[512,512]{1,0:T(8,128)}, u32[]{:S(2)}) copy-start(f32[512,512]{1,0:T(8,128)} %add_multiply_fusion) | copy-start | bytes 3145732
  245.5 50.8 %collective-permute-start.7 = (bf16[2,512,512]{2,1,0:T(8,128)(2,1)}, bf16[2,512,512]{2,1,0:T(8,128)(2,1)}, u32[]{:S(2)}, u32[]{:S(2)}) collective-permute-start(bf16[2,512,512]{2,1,0:T(8,128)(2,1)} %fusion.46), channel_id=1, source_target_pairs={{0,1},{1,2},{2,3},{3,4},{4,5},{5,6},{6,7},{7,8},{8,9},{9,10},{10,1... | collective-permute-start | bytes 3145736 | tf_op jit(solution)/shard_map/ppermute | solution.py:16
  252.6 43.6 %collective-permute-start.6 = (bf16[2,512,512]{2,1,0:T(8,128)(2,1)}, bf16[2,512,512]{2,1,0:T(8,128)(2,1)}, u32[]{:S(2)}, u32[]{:S(2)}) collective-permute-start(bf16[2,512,512]{2,1,0:T(8,128)(2,1)} %convolution_convert_fusion), channel_id=1, source_target_pairs={{1,0},{2,1},{3,2},{4,3},{5,4},{6,5},{7,6},{8,7},{9,8},{10,9},{11,1... | collective-permute-start | bytes 3145736 | tf_op jit(solution)/shard_map/ppermute | solution.py:16
where the time goes:
time: 367 us; the launch traced here: 366 us
  waiting for transfers between devices  194 us (53%)
  matrix products  65.8 us (18%)
  blocking collectives  45.7 us (12%)
  starting transfers between devices  37.5 us (10%)
  other arithmetic  11.8 us (3%)
  local copies, waits for them, and re-layouts  9.66 us (3%)
    ppermute x8, waiting for transfers between devices, passed_along(): lax.ppermute(value, axis, [(source, source + steps) for source in range(l...  175 us
    ppermute x8, starting transfers between devices, passed_along(): lax.ppermute(value, axis, [(source, source + steps) for source in range(l...  29.3 us
    all_to_all x1, blocking collectives, self_energy(): lax.all_to_all(green_half[:, None], 'energy', split_axis=2, concat_axis=0...  26.7 us
    all_to_all x1, blocking collectives, self_energy(): lax.all_to_all(self_local, 'energy', split_axis=0, concat_axis=2, tiled=T...  19.1 us
    dot_general x4, matrix products, newton_step(): jnp.einsum('ij,ejk->eik', link_here, right_term, preferred_element_type=j...  18.7 us
    dot_general x4, matrix products, newton_step(): jnp.einsum('eij,ejk->eik', green_half, residue, preferred_element_type=jn...  16.5 us
    dot_general x4, matrix products, newton_step(): jnp.einsum('ji,ejk->eik', link_here, inner_term, preferred_element_type=j...  13 us
    all_to_all x1, waiting for transfers between devices, self_energy(): lax.all_to_all(green_half[:, None], 'energy', split_axis=2, concat_axis=0...  10.8 us
  transfers between devices with their start and end apart: 10, of which 9 were waited for; matrix products, arithmetic and copies ran while one was open for 4% of the time, Pallas kernels for 0%

commit v1 on v0

v1 whole, which is shorter than its diff:
```python
import functools

import jax
import jax.numpy as jnp
from jax import lax
from jax.experimental import pallas as pl
from jax.experimental.pallas import tpu as pltpu
from jax.sharding import PartitionSpec as P

BROAD = 0.3
REACH = 16

VM = pl.BlockSpec(memory_space=pltpu.VMEM)
SM = pl.BlockSpec(memory_space=pltpu.SMEM)


def passed_along(value, axis, steps):
    count = lax.axis_size(axis)
    leading, last = (max(0, -steps), min(count, count - steps))
    return lax.ppermute(value, axis, [(source, source + steps) for source in range(leading, last)])


def call(body, out_shape, in_specs, scratch=()):
    return pl.pallas_call(
        body,
        out_shape=out_shape,
        in_specs=in_specs,
        out_specs=jax.tree.map(lambda _: VM, out_shape),
        scratch_shapes=list(scratch),
        compiler_params=pltpu.CompilerParams(vmem_limit_bytes=56 * 1024 * 1024),
    )


def dot(a, b):
    return jnp.dot(a, b, preferred_element_type=jnp.float32)


def dot_t(a, b):
    return lax.dot_general(a, b, (((1,), (1,)), ((), ())), preferred_element_type=jnp.float32)


def tables(n):
    row = lax.broadcasted_iota(jnp.int32, (n, n), 0)
    col = lax.broadcasted_iota(jnp.int32, (n, n), 1)
    half = n // 2
    eye = jnp.where(row == col, 1.0, 0.0)
    rotate = jnp.where(col == row + half, -1.0, 0.0) + jnp.where(col == row - half, 1.0, 0.0)
    return eye, rotate


def own_body(keep_ref, c_ref, own_ref):
    own_ref[...] = dot_t(c_ref[...], c_ref[...]) * keep_ref[0]


def pair_body(own_ref, below_ref, pair_ref, half_ref, turned_ref):
    turned = below_ref[...].T
    turned_ref[...] = turned
    pair = own_ref[...] + dot(turned, below_ref[...])
    pair_ref[...] = pair
    half_ref[...] = pair.astype(jnp.bfloat16)


def first_step(energy, inverse, ham, pair, eye, rotate):
    base = energy * eye + BROAD * rotate - ham.astype(jnp.float32)
    matrix = (base - inverse * pair.astype(jnp.float32)).astype(jnp.bfloat16).astype(jnp.float32)
    residue = (2.0 * eye - inverse * matrix).astype(jnp.bfloat16).astype(jnp.float32)
    return (inverse * residue).astype(jnp.bfloat16)


def neighbour_terms(above, below, c, lower_c, lower_turned):
    right = dot_t(above, c).astype(jnp.bfloat16)
    inner = dot(below, lower_c).astype(jnp.bfloat16)
    return dot(c, right) + dot(lower_turned, inner).astype(jnp.bfloat16).astype(jnp.float32)


def finish(matrix, green, eye):
    product = dot(matrix, green)
    residue = (2.0 * eye - product).astype(jnp.bfloat16)
    return dot(green, residue)


def second_body(
    energy_ref, inverse_ref, edge_ref, ham_ref, ham_up_ref, ham_down_ref, pair_ref, pair_up_ref, pair_down_ref,
    c_ref, lower_c_ref, lower_turned_ref, out_ref,
):
    n = c_ref.shape[0]
    eye, rotate = tables(n)
    chunks = out_ref.shape[0]
    for e in range(2):
        energy, inverse = energy_ref[e], inverse_ref[e]
        above = first_step(energy, inverse * edge_ref[0], ham_up_ref[...], pair_up_ref[...], eye, rotate)
        below = first_step(energy, inverse * edge_ref[1], ham_down_ref[...], pair_down_ref[...], eye, rotate)
        green = first_step(energy, inverse, ham_ref[...], pair_ref[...], eye, rotate)
        terms = neighbour_terms(above, below, c_ref[...], lower_c_ref[...], lower_turned_ref[...])
        base = energy * eye + BROAD * rotate - ham_ref[...].astype(jnp.float32)
        matrix = (base - terms).astype(jnp.bfloat16)
        result = finish(matrix, green, eye).astype(jnp.bfloat16)
        out_ref[:, e] = result.reshape(chunks, n // chunks, n)


def terms_body(energy_ref, ham_ref, up_ref, down_ref, c_ref, lower_c_ref, lower_turned_ref, out_ref):
    n = c_ref.shape[0]
    eye, rotate = tables(n)
    for e in range(2):
        terms = neighbour_terms(
            up_ref[:, e].reshape(n, n), down_ref[:, e].reshape(n, n), c_ref[...], lower_c_ref[...],
            lower_turned_ref[...],
        )
        base = energy_ref[e] * eye + BROAD * rotate - ham_ref[...].astype(jnp.float32)
        out_ref[e] = base - terms


def third_body(open_ref, self_ref, green_ref, out_ref):
    n = open_ref.shape[1]
    eye, _ = tables(n)
    for e in range(2):
        self_part = self_ref[:, e].reshape(n, n).astype(jnp.float32)
        matrix = (open_ref[e] - self_part).astype(jnp.bfloat16)
        out_ref[e] = finish(matrix, green_ref[:, e].reshape(n, n), eye).astype(jnp.bfloat16)


def fourth_body(
    energy_ref, ham_ref, up_ref, down_ref, c_ref, lower_c_ref, lower_turned_ref, self_ref, green_ref,
    wide_ref, out_ref,
):
    n = c_ref.shape[0]
    eye, rotate = tables(n)
    chunks = out_ref.shape[0]
    for e in range(2):
        terms = neighbour_terms(up_ref[e], down_ref[e], c_ref[...], lower_c_ref[...], lower_turned_ref[...])
        base = energy_ref[e] * eye + BROAD * rotate - ham_ref[...].astype(jnp.float32)
        self_part = self_ref[:, e].reshape(n, n).astype(jnp.float32)
        matrix = (base - self_part - terms).astype(jnp.bfloat16)
        result = finish(matrix, green_ref[e], eye)
        wide_ref[e] = result
        out_ref[:, e] = result.astype(jnp.bfloat16).reshape(chunks, n // chunks, n)


def energy_body(offset_ref, green_ref, coulomb_ref, out_ref, padded, wide):
    count, rows, columns = green_ref.shape
    offset_count = offset_ref.shape[0]
    none = jnp.zeros((REACH, rows, columns), jnp.float32)
    padded[:REACH] = none
    padded[REACH + count :] = none
    padded[REACH : REACH + count] = green_ref[...].astype(jnp.float32)
    wide[...] = coulomb_ref[...].astype(jnp.float32)
    column_tiles = columns // 128

    def tile(t, carry):
        place = (pl.ds(pl.multiple_of(8 * (t // column_tiles), 8), 8), pl.ds(pl.multiple_of(128 * (t % column_tiles), 128), 128))
        strength = wide[place]
        own = [padded[(REACH + e,) + place] for e in range(count)]
        screened = []
        for k in range(offset_count):
            shift = REACH + offset_ref[k]
            sums = [None] * 4
            for e in range(count):
                term = own[e] * padded[(shift + e,) + place]
                sums[e % 4] = term if sums[e % 4] is None else sums[e % 4] + term
            polarization = (4.0 / count) * ((sums[0] + sums[1]) + (sums[2] + sums[3]))
            screened.append(strength * (1.0 + polarization * strength) * (1.0 / offset_count))
        shifts = [REACH - offset_ref[k] for k in range(offset_count)]
        for e in range(count):
            total = screened[0] * padded[(shifts[0] + e,) + place]
            for k in range(1, offset_count):
                total = total + screened[k] * padded[(shifts[k] + e,) + place]
            out_ref[(e,) + place] = total.astype(jnp.bfloat16)
        return carry

    lax.fori_loop(0, (rows // 8) * column_tiles, tile, 0)


def self_energy(chunks, coulomb, offsets):
    parts, per, rows, columns = chunks.shape
    received = lax.all_to_all(chunks, "energy", split_axis=0, concat_axis=0, tiled=True)
    count = parts * per
    result = call(
        energy_body,
        jax.ShapeDtypeStruct((count, rows, columns), jnp.bfloat16),
        [SM, VM, VM],
        [pltpu.VMEM((count + 2 * REACH, rows, columns), jnp.float32), pltpu.VMEM((rows, columns), jnp.float32)],
    )(offsets, received.reshape(count, rows, columns), coulomb)
    return lax.all_to_all(
        result.reshape(parts, per, rows, columns), "energy", split_axis=0, concat_axis=0, tiled=True
    )


def local(energies, hamiltonian, coupling, coulomb, offsets):
    c, ham = coupling[0], hamiltonian[0]
    n = c.shape[0]
    parts = lax.axis_size("energy")
    place = lax.axis_index("slab")
    has_above = (place < lax.axis_size("slab") - 1).astype(jnp.float32)
    has_below = (place > 0).astype(jnp.float32)
    edge = jnp.stack([has_above, has_below])
    inverse = (1.0 / energies).astype(jnp.bfloat16).astype(jnp.float32)
    square = lambda kind: jax.ShapeDtypeStruct((n, n), kind)

    lower_c = passed_along(c, "slab", 1)
    ham_up = passed_along(ham, "slab", -1)
    ham_down = passed_along(ham, "slab", 1)
    own = call(own_body, square(jnp.float32), [SM, VM])(edge[:1], c)
    pair, pair_half, lower_turned = call(
        pair_body, (square(jnp.float32), square(jnp.bfloat16), square(jnp.bfloat16)), [VM, VM]
    )(own, lower_c)
    pair_up = passed_along(pair_half, "slab", -1)
    pair_down = passed_along(pair_half, "slab", 1)
    packed = jax.ShapeDtypeStruct((parts, 2, n // parts, n), jnp.bfloat16)
    green = call(second_body, packed, [SM] * 3 + [VM] * 9)(
        energies, inverse, edge, ham, ham_up, ham_down, pair, pair_up, pair_down, c, lower_c, lower_turned
    )
    up = passed_along(green, "slab", -1)
    down = passed_along(green, "slab", 1)
    open_part = call(terms_body, jax.ShapeDtypeStruct((2, n, n), jnp.float32), [SM] + [VM] * 6)(
        energies, ham, up, down, c, lower_c, lower_turned
    )
    self_part = self_energy(green, coulomb[0], offsets)
    green = call(third_body, jax.ShapeDtypeStruct((2, n, n), jnp.bfloat16), [VM] * 3)(open_part, self_part, green)
    up = passed_along(green, "slab", -1)
    down = passed_along(green, "slab", 1)
    wide, green = call(fourth_body, (jax.ShapeDtypeStruct((2, n, n), jnp.float32), packed), [SM] + [VM] * 8)(
        energies, ham, up, down, c, lower_c, lower_turned, self_part, green
    )
    self_part = self_energy(green, coulomb[0], offsets)
    self_part = jnp.swapaxes(self_part, 0, 1).reshape(2, n, n)
    return (wide[:, None], self_part[:, None])


def solution(mesh):
    placed = (
        P("energy"),
        P("slab", None, None),
        P("slab", None, None),
        P("slab", "energy", None),
        P(),
    )
    return jax.shard_map(
        local,
        mesh=mesh,
        in_specs=placed,
        out_specs=(P("energy", "slab", None, None), P("energy", "slab", None, None)),
        check_vma=False,
    )
```

time: 367 us -> 318 us (0.87)
  matrix products: 65.8 us -> 0 us
  Pallas kernels: 0 us -> 53.6 us
  waiting for transfers between devices: 194 us -> 144 us
  blocking collectives: 45.7 us -> 68.7 us
  other arithmetic: 11.8 us -> 0.61 us
  starting transfers between devices: 37.5 us -> 42.8 us
    dot_general x44 -> x0, matrix products: 65.8 us -> none  [the longest x4 18.7 us: newton_step(): jnp.einsum('ij,ejk->eik', link_here, right_term, preferred_element_type=j...]
    pallas_call x0 -> x8, Pallas kernels: none -> 53.6 us  [the longest x2 20.5 us: self_energy(): call(energy_body, jax.ShapeDtypeStruct((count, rows, columns), jnp.bfloat...]
    ppermute x8 -> x9, waiting for transfers between devices: 175 us -> 144 us  [passed_along(): lax.ppermute(value, axis, [(source, source + steps) for source in range(l...]
    all_to_all x2 -> x3, blocking collectives: 45.7 us -> 68.7 us  [the longest x2 48.6 us: self_energy(): lax.all_to_all(chunks, 'energy', split_axis=0, concat_axis=0, tiled=True)]
    all_to_all x2 -> x1, waiting for transfers between devices: 19.5 us -> 0.01 us  [self_energy(): lax.all_to_all(result.reshape(parts, per, rows, columns), 'energy', split...]
    ppermute x8 -> x9, starting transfers between devices: 29.3 us -> 39.2 us  [passed_along(): lax.ppermute(value, axis, [(source, source + steps) for source in range(l...]
    sub x10 -> x0, other arithmetic: 6.06 us -> none  [the longest x8 4.89 us: self_energy(): level_index - offset_now]
    all_to_all x2 -> x1, starting transfers between devices: 8.21 us -> 3.65 us  [self_energy(): lax.all_to_all(result.reshape(parts, per, rows, columns), 'energy', split...]
  transfers between devices with their start and end apart: 10 -> 10, of which waited for: 9 -> 6; matrix products, arithmetic and copies ran while one was open for 4% -> 0% of each run, Pallas kernels for 0% -> 4%
where the time goes in v1:
time: 318 us; the launch traced here: 317 us
  waiting for transfers between devices  144 us (45%)
  blocking collectives  68.7 us (22%)
  Pallas kernels  53.6 us (17%)
  starting transfers between devices  42.8 us (13%)
  local copies, waits for them, and re-layouts  6.69 us (2%)
    ppermute x9, waiting for transfers between devices, passed_along(): lax.ppermute(value, axis, [(source, source + steps) for source in range(l...  144 us
    all_to_all x2, blocking collectives, self_energy(): lax.all_to_all(chunks, 'energy', split_axis=0, concat_axis=0, tiled=True)  48.6 us
    ppermute x9, starting transfers between devices, passed_along(): lax.ppermute(value, axis, [(source, source + steps) for source in range(l...  39.2 us
    pallas_call x2, Pallas kernels, self_energy(): call(energy_body, jax.ShapeDtypeStruct((count, rows, columns), jnp.bfloat...  20.5 us
    all_to_all x1, blocking collectives, self_energy(): lax.all_to_all(result.reshape(parts, per, rows, columns), 'energy', split...  20.1 us
    pallas_call x1, Pallas kernels, local(): call(fourth_body, (jax.ShapeDtypeStruct((2, n, n), jnp.float32), packed),...  8.45 us
    pallas_call x1, Pallas kernels, local(): call(second_body, packed, [SM] * 3 + [VM] * 9)  8.31 us
  transfers between devices with their start and end apart: 10, of which 6 were waited for; matrix products, arithmetic and copies ran while one was open for 0% of the time, Pallas kernels for 4%

profile of v1, /device:TPU:70, one launch (start us, length us, event | category | flops | bytes accessed | tf_op | source)
XLA Modules:
  0.0 316.8 jit_solution(7710493804982648952)
XLA Ops:
  0.6 0.0 copy-start.11
  0.6 6.3 %collective-permute-start.2 = (bf16[512,512]{1,0:T(8,128)(2,1)}, bf16[512,512]{1,0:T(8,128)(2,1)S(1)}, u32[]{:S(2)}, u32[]{:S(2)}) collective-permute-start(bf16[512,512]{1,0:T(8,128)(2,1)} %bitcast.14), channel_id=1, source_target_pairs={{0,1},{1,2},{2,3},{3,4},{4,5},{5,6},{6,7},{7,8},{8,9},{9,10},{10,1... | collective-permute-start | bytes 1572872 | tf_op jit(solution)/shard_map/ppermute | solution.py:20
  7.0 3.4 %collective-permute-start.1 = (bf16[512,512]{1,0:T(8,128)(2,1)}, bf16[512,512]{1,0:T(8,128)(2,1)S(1)}, u32[]{:S(2)}, u32[]{:S(2)}) collective-permute-start(bf16[512,512]{1,0:T(8,128)(2,1)} %bitcast.19), channel_id=1, source_target_pairs={{0,1},{1,2},{2,3},{3,4},{4,5},{5,6},{6,7},{7,8},{8,9},{9,10},{10,1... | collective-permute-start | bytes 1572872 | tf_op jit(solution)/shard_map/ppermute | solution.py:20
  10.4 2.4 collective-permute-start
  12.8 2.5 shard_map.68.own_ref
  15.3 4.3 %collective-permute-done.2.below_ref.lower_c_ref = bf16[512,512]{1,0:T(8,128)(2,1)S(1)} collective-permute-done((bf16[512,512]{1,0:T(8,128)(2,1)}, bf16[512,512]{1,0:T(8,128)(2,1)S(1)}, u32[]{:S(2)}, u32[]{:S(2)}) %collective-permute-start.2) | collective-permute-done | bytes 524320 | tf_op jit(solution)/shard_map/ppermute | solution.py:20
  19.6 0.0 copy-start.2
  19.6 0.8 copy-done.2
  20.4 3.1 shard_map.69
  23.5 8.5 %collective-permute-start.4 = (bf16[512,512]{1,0:T(8,128)(2,1)}, bf16[512,512]{1,0:T(8,128)(2,1)S(1)}, u32[]{:S(2)}, u32[]{:S(2)}) collective-permute-start(bf16[512,512]{1,0:T(8,128)(2,1)} %get-tuple-element.8), channel_id=1, source_target_pairs={{0,1},{1,2},{2,3},{3,4},{4,5},{5,6},{6,7},{7,8},{8,9},{9,10},{10,1... | collective-permute-start | bytes 1572872 | tf_op jit(solution)/shard_map/ppermute | solution.py:20
  32.1 1.9 collective-permute-start.3
  34.0 0.0 copy-done.11
  34.0 0.6 pad_maximum_fusion
  34.6 0.0 collective-permute-done.1.ham_down_ref
  34.6 0.0 copy-start.7
  34.6 6.8 %collective-permute-done.ham_up_ref = bf16[512,512]{1,0:T(8,128)(2,1)S(1)} collective-permute-done((bf16[512,512]{1,0:T(8,128)(2,1)}, bf16[512,512]{1,0:T(8,128)(2,1)S(1)}, u32[]{:S(2)}, u32[]{:S(2)}) %collective-permute-start) | collective-permute-done | bytes 524320 | tf_op jit(solution)/shard_map/ppermute | solution.py:20
  41.4 0.0 copy-start.8
  41.4 33.8 %collective-permute-done.4.pair_down_ref = bf16[512,512]{1,0:T(8,128)(2,1)S(1)} collective-permute-done((bf16[512,512]{1,0:T(8,128)(2,1)}, bf16[512,512]{1,0:T(8,128)(2,1)S(1)}, u32[]{:S(2)}, u32[]{:S(2)}) %collective-permute-start.4) | collective-permute-done | bytes 524320 | tf_op jit(solution)/shard_map/ppermute | solution.py:20
  75.2 0.0 copy-start.9
  75.2 0.0 collective-permute-done.3.pair_up_ref
  75.2 0.0 copy-start.10
  75.2 0.0 copy-done.7
  75.2 0.0 copy-done.8
  75.2 0.8 copy-done.9
  76.0 0.2 copy-done.10
  76.2 8.3 %shard_map.70.green_ref = bf16[16,2,32,512]{3,2,1,0:T(8,128)(2,1)} custom-call(f32[2]{0:T(128)} %energy_ref.5, f32[2]{0:T(128)} %get-tuple-element.15.inverse_ref, f32[2]{0:T(128)} %get-tuple-element.14.edge_ref, bf16[512,512]{1,0:T(8,128)(2,1)} %bitcast.21, bf16[512,512]{1,0:T(8,128)(2,1)} %copy-done.8, bf16[512,512]{1,0:T(8,128)(2,1)} %copy-done.7, ...), custom_call_target="tpu_custom_call" | custom-call | tf_op jit(solution)/shard_map/pallas_call | solution.py:209
  84.5 27.7 %all_to_all.20 = bf16[16,2,32,512]{3,2,1,0:T(8,128)(2,1)} all-to-all(bf16[16,2,32,512]{3,2,1,0:T(8,128)(2,1)} %shard_map.70.green_ref), channel_id=1, replica_groups=mesh['energy'=16,'slab'=16] {'energy'}, dimensions={0} | all-to-all | bytes 2097152 | tf_op jit(solution)/shard_map/all_to_all | solution.py:175
  112.1 0.0 copy-start.1
  112.1 10.3 %shard_map.72 = bf16[32,32,512]{2,1,0:T(8,128)(2,1)} custom-call(s32[8]{0:T(128)} %offset_ref.3, bf16[32,32,512]{2,1,0:T(8,128)(2,1)} %bitcast.27, bf16[32,512]{1,0:T(8,128)(2,1)} %bitcast.30), custom_call_target="tpu_custom_call" | custom-call | tf_op jit(solution)/shard_map/pallas_call | solution.py:177
  122.4 3.7 %all-to-all-start.1 = ((bf16[16,2,32,512]{3,2,1,0:T(8,128)(2,1)}), bf16[16,2,32,512]{3,2,1,0:T(8,128)(2,1)S(1)}, u32[]{:S(2)}, u32[]{:S(2)}) async-start(bf16[16,2,32,512]{3,2,1,0:T(8,128)(2,1)} %bitcast.24), calls=%async_computation.1 | async-start | bytes 2097152 | tf_op jit(solution)/shard_map/all_to_all | solution.py:183
  126.1 0.0 copy-done.1
  126.1 1.9 collective-permute-start.6
  128.1 3.9 %collective-permute-start.5 = (bf16[16,2,32,512]{3,2,1,0:T(8,128)(2,1)S(1)}, bf16[16,2,32,512]{3,2,1,0:T(8,128)(2,1)S(1)}, u32[]{:S(2)}, u32[]{:S(2)}) collective-permute-start(bf16[16,2,32,512]{3,2,1,0:T(8,128)(2,1)S(1)} %copy-done.1), channel_id=1, source_target_pairs={{1,0},{2,1},{3,2},{4,3},{5,4},{6,5},{7,6},{8,7},{9,8},{10,9},{11,1... | collective-permute-start | bytes 3145736 | tf_op jit(solution)/shard_map/ppermute | solution.py:20
  132.0 51.2 %collective-permute-done.6.down_ref = bf16[16,2,32,512]{3,2,1,0:T(8,128)(2,1)S(1)} collective-permute-done((bf16[16,2,32,512]{3,2,1,0:T(8,128)(2,1)S(1)}, bf16[16,2,32,512]{3,2,1,0:T(8,128)(2,1)S(1)}, u32[]{:S(2)}, u32[]{:S(2)}) %collective-permute-start.6) | collective-permute-done | bytes 1048608 | tf_op jit(solution)/shard_map/ppermute | solution.py:20
  183.2 0.0 copy-start.5
  183.2 0.0 collective-permute-done.5.up_ref
  183.2 1.0 copy-done.5
  184.2 0.0 copy-start.6
  184.2 1.0 copy-done.6
  185.2 6.1 %shard_map.71.open_ref = f32[2,512,512]{2,1,0:T(8,128)} custom-call(f32[2]{0:T(128)} %energy_ref.5, bf16[512,512]{1,0:T(8,128)(2,1)} %bitcast.22, bf16[16,2,32,512]{3,2,1,0:T(8,128)(2,1)} %copy-done.6, bf16[16,2,32,512]{3,2,1,0:T(8,128)(2,1)} %copy-done.5, bf16[512,512]{1,0:T(8,128)(2,1)} %bitcast.17, bf16[512,512]{1,0:T(8,128)(2,1)} %copy-done.2, ...), custom_call_target="tpu_custom_call" | custom-call | tf_op jit(solution)/shard_map/pallas_call | solution.py:214
  191.3 0.0 all-to-all-done.1.self_ref
  191.3 0.0 copy-start
  191.3 1.0 copy-done
  192.3 4.6 %shard_map.73.green_ref = bf16[2,512,512]{2,1,0:T(8,128)(2,1)} custom-call(f32[2,512,512]{2,1,0:T(8,128)} %shard_map.71.open_ref, bf16[16,2,32,512]{3,2,1,0:T(8,128)(2,1)} %copy-done, bf16[16,2,32,512]{3,2,1,0:T(8,128)(2,1)} %shard_map.70.green_ref), custom_call_target="tpu_custom_call" | custom-call | tf_op jit(solution)/shard_map/pallas_call | solution.py:218
  196.8 8.6 %collective-permute-start.8 = (bf16[2,512,512]{2,1,0:T(8,128)(2,1)}, bf16[2,512,512]{2,1,0:T(8,128)(2,1)S(1)}, u32[]{:S(2)}, u32[]{:S(2)}) collective-permute-start(bf16[2,512,512]{2,1,0:T(8,128)(2,1)} %shard_map.73.green_ref), channel_id=1, source_target_pairs={{0,1},{1,2},{2,3},{3,4},{4,5},{5,6},{6,7},{7,8},{8,9},{9,10},{10,1... | collective-permute-start | bytes 3145736 | tf_op jit(solution)/shard_map/ppermute | solution.py:20
  205.4 2.1 collective-permute-start.7
  207.5 43.0 %collective-permute-done.8.down_ref = bf16[2,512,512]{2,1,0:T(8,128)(2,1)S(1)} collective-permute-done((bf16[2,512,512]{2,1,0:T(8,128)(2,1)}, bf16[2,512,512]{2,1,0:T(8,128)(2,1)S(1)}, u32[]{:S(2)}, u32[]{:S(2)}) %collective-permute-start.8) | collective-permute-done | bytes 1048608 | tf_op jit(solution)/shard_map/ppermute | solution.py:20
  250.5 0.0 copy-start.3
  250.5 4.6 %collective-permute-done.7.up_ref = bf16[2,512,512]{2,1,0:T(8,128)(2,1)S(1)} collective-permute-done((bf16[2,512,512]{2,1,0:T(8,128)(2,1)}, bf16[2,512,512]{2,1,0:T(8,128)(2,1)S(1)}, u32[]{:S(2)}, u32[]{:S(2)}) %collective-permute-start.7) | collective-permute-done | bytes 1048608 | tf_op jit(solution)/shard_map/ppermute | solution.py:20
  255.1 0.0 copy-done.3
  255.1 0.0 copy-start.4
  255.1 1.0 copy-done.4
  256.1 8.4 %shard_map.74 = (f32[2,512,512]{2,1,0:T(8,128)}, bf16[16,2,32,512]{3,2,1,0:T(8,128)(2,1)}) custom-call(f32[2]{0:T(128)} %energy_ref.5, bf16[512,512]{1,0:T(8,128)(2,1)} %bitcast.23, bf16[2,512,512]{2,1,0:T(8,128)(2,1)} %copy-done.4, bf16[2,512,512]{2,1,0:T(8,128)(2,1)} %copy-done.3, bf16[512,512]{1,0:T(8,128)(2,1)} %bitcast.18, bf16[512,512]{1,0:T(8,128)(2,1)} %copy-done.2, ...), custom_call_target="tpu_custom_call" | custom-call | tf_op jit(solution)/shard_map/pallas_call | solution.py:221
  264.6 21.0 %all_to_all.21 = bf16[16,2,32,512]{3,2,1,0:T(8,128)(2,1)} all-to-all(bf16[16,2,32,512]{3,2,1,0:T(8,128)(2,1)} %get-tuple-element.11), channel_id=1, replica_groups=mesh['energy'=16,'slab'=16] {'energy'}, dimensions={0} | all-to-all | bytes 2097152 | tf_op jit(solution)/shard_map/all_to_all | solution.py:175
  285.5 10.2 %shard_map.75 = bf16[32,32,512]{2,1,0:T(8,128)(2,1)} custom-call(s32[8]{0:T(128)} %offset_ref.3, bf16[32,32,512]{2,1,0:T(8,128)(2,1)} %bitcast.25, bf16[32,512]{1,0:T(8,128)(2,1)} %bitcast.31), custom_call_target="tpu_custom_call" | custom-call | tf_op jit(solution)/shard_map/pallas_call | solution.py:177
  295.7 20.1 %all_to_all.22 = bf16[16,2,32,512]{3,2,1,0:T(8,128)(2,1)S(1)} all-to-all(bf16[16,2,32,512]{3,2,1,0:T(8,128)(2,1)} %bitcast.26), channel_id=1, replica_groups=mesh['energy'=16,'slab'=16] {'energy'}, dimensions={0} | all-to-all | bytes 2097152 | tf_op jit(solution)/shard_map/all_to_all | solution.py:183
  315.8 1.0 copy.7
Async XLA Ops:
  0.6 33.4 %copy-start.11 = (f32[2]{0:T(128)S(1)}, f32[2]{0:T(128)}, u32[]{:S(2)}) copy-start(f32[2]{0:T(128)} %energy_ref.5) | copy-start | bytes 28
  0.6 18.9 %collective-permute-start.2 = (bf16[512,512]{1,0:T(8,128)(2,1)}, bf16[512,512]{1,0:T(8,128)(2,1)S(1)}, u32[]{:S(2)}, u32[]{:S(2)}) collective-permute-start(bf16[512,512]{1,0:T(8,128)(2,1)} %bitcast.14), channel_id=1, source_target_pairs={{0,1},{1,2},{2,3},{3,4},{4,5},{5,6},{6,7},{7,8},{8,9},{9,10},{10,1... | collective-permute-start | bytes 1572872 | tf_op jit(solution)/shard_map/ppermute | solution.py:20
  7.0 27.7 %collective-permute-start.1 = (bf16[512,512]{1,0:T(8,128)(2,1)}, bf16[512,512]{1,0:T(8,128)(2,1)S(1)}, u32[]{:S(2)}, u32[]{:S(2)}) collective-permute-start(bf16[512,512]{1,0:T(8,128)(2,1)} %bitcast.19), channel_id=1, source_target_pairs={{0,1},{1,2},{2,3},{3,4},{4,5},{5,6},{6,7},{7,8},{8,9},{9,10},{10,1... | collective-permute-start | bytes 1572872 | tf_op jit(solution)/shard_map/ppermute | solution.py:20
  10.4 31.1 %collective-permute-start = (bf16[512,512]{1,0:T(8,128)(2,1)}, bf16[512,512]{1,0:T(8,128)(2,1)S(1)}, u32[]{:S(2)}, u32[]{:S(2)}) collective-permute-start(bf16[512,512]{1,0:T(8,128)(2,1)} %bitcast.20), channel_id=1, source_target_pairs={{1,0},{2,1},{3,2},{4,3},{5,4},{6,5},{7,6},{8,7},{9,8},{10,9},{11,1... | collective-permute-start | bytes 1572872 | tf_op jit(solution)/shard_map/ppermute | solution.py:20
  19.6 0.8 copy-start.2
  23.5 51.7 %collective-permute-start.4 = (bf16[512,512]{1,0:T(8,128)(2,1)}, bf16[512,512]{1,0:T(8,128)(2,1)S(1)}, u32[]{:S(2)}, u32[]{:S(2)}) collective-permute-start(bf16[512,512]{1,0:T(8,128)(2,1)} %get-tuple-element.8), channel_id=1, source_target_pairs={{0,1},{1,2},{2,3},{3,4},{4,5},{5,6},{6,7},{7,8},{8,9},{9,10},{10,1... | collective-permute-start | bytes 1572872 | tf_op jit(solution)/shard_map/ppermute | solution.py:20
  32.1 43.1 %collective-permute-start.3 = (bf16[512,512]{1,0:T(8,128)(2,1)}, bf16[512,512]{1,0:T(8,128)(2,1)S(1)}, u32[]{:S(2)}, u32[]{:S(2)}) collective-permute-start(bf16[512,512]{1,0:T(8,128)(2,1)} %get-tuple-element.8), channel_id=1, source_target_pairs={{1,0},{2,1},{3,2},{4,3},{5,4},{6,5},{7,6},{8,7},{9,8},{10,9},{11,1... | collective-permute-start | bytes 1572872 | tf_op jit(solution)/shard_map/ppermute | solution.py:20
  34.6 40.6 %copy-start.7 = (bf16[512,512]{1,0:T(8,128)(2,1)}, bf16[512,512]{1,0:T(8,128)(2,1)S(1)}, u32[]{:S(2)}) copy-start(bf16[512,512]{1,0:T(8,128)(2,1)S(1)} %collective-permute-done.1.ham_down_ref) | copy-start | bytes 1572868
  41.4 33.8 %copy-start.8 = (bf16[512,512]{1,0:T(8,128)(2,1)}, bf16[512,512]{1,0:T(8,128)(2,1)S(1)}, u32[]{:S(2)}) copy-start(bf16[512,512]{1,0:T(8,128)(2,1)S(1)} %collective-permute-done.ham_up_ref) | copy-start | bytes 1572868
  75.2 0.8 copy-start.9
  75.2 1.0 copy-start.10
  112.1 14.0 %copy-start.1 = (bf16[16,2,32,512]{3,2,1,0:T(8,128)(2,1)S(1)}, bf16[16,2,32,512]{3,2,1,0:T(8,128)(2,1)}, u32[]{:S(2)}) copy-start(bf16[16,2,32,512]{3,2,1,0:T(8,128)(2,1)} %shard_map.70.green_ref) | copy-start | bytes 3145732
  122.4 68.9 %all-to-all-start.1 = ((bf16[16,2,32,512]{3,2,1,0:T(8,128)(2,1)}), bf16[16,2,32,512]{3,2,1,0:T(8,128)(2,1)S(1)}, u32[]{:S(2)}, u32[]{:S(2)}) async-start(bf16[16,2,32,512]{3,2,1,0:T(8,128)(2,1)} %bitcast.24), calls=%async_computation.1 | async-start | bytes 2097152 | tf_op jit(solution)/shard_map/all_to_all | solution.py:183
  126.1 57.1 %collective-permute-start.6 = (bf16[16,2,32,512]{3,2,1,0:T(8,128)(2,1)S(1)}, bf16[16,2,32,512]{3,2,1,0:T(8,128)(2,1)S(1)}, u32[]{:S(2)}, u32[]{:S(2)}) collective-permute-start(bf16[16,2,32,512]{3,2,1,0:T(8,128)(2,1)S(1)} %copy-done.1), channel_id=1, source_target_pairs={{0,1},{1,2},{2,3},{3,4},{4,5},{5,6},{6,7},{7,8},{8,9},{9,10},{10,1... | collective-permute-start | bytes 3145736 | tf_op jit(solution)/shard_map/ppermute | solution.py:20
  128.1 55.1 %collective-permute-start.5 = (bf16[16,2,32,512]{3,2,1,0:T(8,128)(2,1)S(1)}, bf16[16,2,32,512]{3,2,1,0:T(8,128)(2,1)S(1)}, u32[]{:S(2)}, u32[]{:S(2)}) collective-permute-start(bf16[16,2,32,512]{3,2,1,0:T(8,128)(2,1)S(1)} %copy-done.1), channel_id=1, source_target_pairs={{1,0},{2,1},{3,2},{4,3},{5,4},{6,5},{7,6},{8,7},{9,8},{10,9},{11,1... | collective-permute-start | bytes 3145736 | tf_op jit(solution)/shard_map/ppermute | solution.py:20
  183.2 1.0 copy-start.5
  184.2 1.0 copy-start.6
  191.3 1.0 copy-start
  196.8 53.7 %collective-permute-start.8 = (bf16[2,512,512]{2,1,0:T(8,128)(2,1)}, bf16[2,512,512]{2,1,0:T(8,128)(2,1)S(1)}, u32[]{:S(2)}, u32[]{:S(2)}) collective-permute-start(bf16[2,512,512]{2,1,0:T(8,128)(2,1)} %shard_map.73.green_ref), channel_id=1, source_target_pairs={{0,1},{1,2},{2,3},{3,4},{4,5},{5,6},{6,7},{7,8},{8,9},{9,10},{10,1... | collective-permute-start | bytes 3145736 | tf_op jit(solution)/shard_map/ppermute | solution.py:20
  205.4 49.7 %collective-permute-start.7 = (bf16[2,512,512]{2,1,0:T(8,128)(2,1)}, bf16[2,512,512]{2,1,0:T(8,128)(2,1)S(1)}, u32[]{:S(2)}, u32[]{:S(2)}) collective-permute-start(bf16[2,512,512]{2,1,0:T(8,128)(2,1)} %shard_map.73.green_ref), channel_id=1, source_target_pairs={{1,0},{2,1},{3,2},{4,3},{5,4},{6,5},{7,6},{8,7},{9,8},{10,9},{11,1... | collective-permute-start | bytes 3145736 | tf_op jit(solution)/shard_map/ppermute | solution.py:20
  250.5 4.6 %copy-start.3 = (bf16[2,512,512]{2,1,0:T(8,128)(2,1)}, bf16[2,512,512]{2,1,0:T(8,128)(2,1)S(1)}, u32[]{:S(2)}) copy-start(bf16[2,512,512]{2,1,0:T(8,128)(2,1)S(1)} %collective-permute-done.8.down_ref) | copy-start | bytes 3145732
  255.1 1.0 copy-start.4

commit v2 on v1

v2 whole, which is shorter than its diff:
```python
import functools

import jax
import jax.numpy as jnp
from jax import lax
from jax.experimental import pallas as pl
from jax.experimental.pallas import tpu as pltpu
from jax.sharding import PartitionSpec as P


BROAD = 0.3
REACH = 16

VM = pl.BlockSpec(memory_space=pltpu.VMEM)
SM = pl.BlockSpec(memory_space=pltpu.SMEM)


def passed_along(value, axis, steps):
    count = lax.axis_size(axis)
    leading, last = (max(0, -steps), min(count, count - steps))
    return lax.ppermute(value, axis, [(source, source + steps) for source in range(leading, last)])


def call(body, out_shape, in_specs, scratch=()):
    return pl.pallas_call(
        body,
        out_shape=out_shape,
        in_specs=in_specs,
        out_specs=jax.tree.map(lambda _: VM, out_shape),
        scratch_shapes=list(scratch),
        compiler_params=pltpu.CompilerParams(vmem_limit_bytes=56 * 1024 * 1024),
    )


def dot(a, b):
    return jnp.dot(a, b, preferred_element_type=jnp.float32)


def dot_t(a, b):
    return lax.dot_general(a, b, (((1,), (1,)), ((), ())), preferred_element_type=jnp.float32)


def tables(n):
    row = lax.broadcasted_iota(jnp.int32, (n, n), 0)
    col = lax.broadcasted_iota(jnp.int32, (n, n), 1)
    half = n // 2
    eye = jnp.where(row == col, 1.0, 0.0)
    rotate = jnp.where(col == row + half, -1.0, 0.0) + jnp.where(col == row - half, 1.0, 0.0)
    return eye, rotate


def own_body(keep_ref, c_ref, own_ref):
    own_ref[...] = dot_t(c_ref[...], c_ref[...]) * keep_ref[0]


def place_halves(core, whole, mine, theirs):
    half = mine.shape[0]
    whole[pl.ds(pl.multiple_of(core * half, half), half)] = mine
    whole[pl.ds(pl.multiple_of((1 - core) * half, half), half)] = theirs


def pair_body(core_ref, own_ref, mine_ref, theirs_ref, pair_ref, half_ref, below_ref, turned_ref):
    core = core_ref[0]
    half = half_ref.shape[0]
    place_halves(core, below_ref, mine_ref[...], theirs_ref[...])
    below = below_ref[...]
    turned = below.T
    turned_ref[...] = turned
    pair_ref[...] = own_ref[...] + dot(turned, below)
    half_ref[...] = pair_ref[pl.ds(pl.multiple_of(core * half, half), half)].astype(jnp.bfloat16)


def first_step(energy, inverse, ham, pair, eye, rotate):
    base = energy * eye + BROAD * rotate - ham.astype(jnp.float32)
    matrix = (base - inverse * pair.astype(jnp.float32)).astype(jnp.bfloat16).astype(jnp.float32)
    residue = (2.0 * eye - inverse * matrix).astype(jnp.bfloat16).astype(jnp.float32)
    return (inverse * residue).astype(jnp.bfloat16)


def neighbour_terms(above, below, c, lower_c, lower_turned):
    right = dot_t(above, c).astype(jnp.bfloat16)
    inner = dot(below, lower_c).astype(jnp.bfloat16)
    return dot(c, right) + dot(lower_turned, inner)


def finish(matrix, green, eye):
    product = dot(matrix, green)
    residue = (2.0 * eye - product).astype(jnp.bfloat16)
    return dot(green, residue)


def second_body(
    energy_ref, inverse_ref, edge_ref, core_ref, ham_ref, pair_ref, mine_ref, theirs_ref, c_ref, lower_c_ref,
    lower_turned_ref, out_ref, first_ref, second_ref, whole,
):
    n = c_ref.shape[0]
    eye, rotate = tables(n)
    chunks = out_ref.shape[0]
    for i in range(4):
        place_halves(core_ref[0], whole.at[i], mine_ref[i], theirs_ref[i])
    for e in range(2):
        energy, inverse = energy_ref[e], inverse_ref[e]
        above = first_step(energy, inverse * edge_ref[0], whole[0], whole[2], eye, rotate)
        below = first_step(energy, inverse * edge_ref[1], whole[1], whole[3], eye, rotate)
        green = first_step(energy, inverse, ham_ref[...], pair_ref[...], eye, rotate)
        terms = neighbour_terms(above, below, c_ref[...], lower_c_ref[...], lower_turned_ref[...])
        base = energy * eye + BROAD * rotate - ham_ref[...].astype(jnp.float32)
        matrix = (base - terms).astype(jnp.bfloat16)
        result = finish(matrix, green, eye).astype(jnp.bfloat16)
        out_ref[:, e] = result.reshape(chunks, n // chunks, n)
        (first_ref, second_ref)[e][...] = result


def terms_body(e, energy_ref, ham_ref, up_ref, down_ref, c_ref, lower_c_ref, lower_turned_ref, out_ref):
    eye, rotate = tables(c_ref.shape[0])
    terms = neighbour_terms(up_ref[...], down_ref[...], c_ref[...], lower_c_ref[...], lower_turned_ref[...])
    base = energy_ref[e] * eye + BROAD * rotate - ham_ref[...].astype(jnp.float32)
    out_ref[...] = base - terms


def third_body(e, open_ref, self_ref, green_ref, out_ref):
    n = open_ref.shape[0]
    eye, _ = tables(n)
    self_part = self_ref[:, e].reshape(n, n).astype(jnp.float32)
    matrix = (open_ref[...] - self_part).astype(jnp.bfloat16)
    out_ref[...] = finish(matrix, green_ref[...], eye).astype(jnp.bfloat16)


def fourth_body(
    e, energy_ref, ham_ref, up_ref, down_ref, c_ref, lower_c_ref, lower_turned_ref, self_ref, green_ref,
    wide_ref, out_ref,
):
    n = c_ref.shape[0]
    eye, rotate = tables(n)
    terms = neighbour_terms(up_ref[...], down_ref[...], c_ref[...], lower_c_ref[...], lower_turned_ref[...])
    base = energy_ref[e] * eye + BROAD * rotate - ham_ref[...].astype(jnp.float32)
    self_part = self_ref[:, e].reshape(n, n).astype(jnp.float32)
    matrix = (base - self_part - terms).astype(jnp.bfloat16)
    result = finish(matrix, green_ref[...], eye)
    wide_ref[...] = result
    out_ref[...] = result.astype(jnp.bfloat16)


def energy_body(offset_ref, green_ref, coulomb_ref, out_ref, padded, wide):
    count, rows, columns = green_ref.shape
    offset_count = offset_ref.shape[0]
    none = jnp.zeros((REACH, rows, columns), jnp.float32)
    padded[:REACH] = none
    padded[REACH + count :] = none
    padded[REACH : REACH + count] = green_ref[...].astype(jnp.float32)
    wide[...] = coulomb_ref[...].astype(jnp.float32)
    column_tiles = columns // 128

    def tile(t, carry):
        row = pl.ds(pl.multiple_of(8 * (t // column_tiles), 8), 8)
        column = pl.ds(pl.multiple_of(128 * (t % column_tiles), 128), 128)
        strength = wide[row, column]
        own = padded[REACH : REACH + count, row, column]
        total = jnp.zeros(own.shape, jnp.float32)
        screened = []
        for k in range(offset_count):
            later = padded[pl.ds(REACH + offset_ref[k], count), row, column]
            polarization = (4.0 / count) * jnp.sum(own * later, axis=0)
            screened.append(strength * (1.0 + polarization * strength) * (1.0 / offset_count))
        for k in range(offset_count):
            total = total + screened[k][None] * padded[pl.ds(REACH - offset_ref[k], count), row, column]
        out_ref[:, row, column] = total.astype(jnp.bfloat16)
        return carry

    lax.fori_loop(0, (rows // 8) * column_tiles, tile, 0)


def self_energy(chunks, coulomb, offsets):
    parts, per, rows, columns = chunks.shape
    received = lax.all_to_all(chunks, "energy", split_axis=0, concat_axis=0, tiled=True)
    count = parts * per
    result = call(
        energy_body,
        jax.ShapeDtypeStruct((count, rows, columns), jnp.bfloat16),
        [SM, VM, VM],
        [pltpu.VMEM((count + 2 * REACH, rows, columns), jnp.float32), pltpu.VMEM((rows, columns), jnp.float32)],
    )(offsets, received.reshape(count, rows, columns), coulomb)
    return lax.all_to_all(result.reshape(parts, per, rows, columns), "energy", split_axis=0, concat_axis=0, tiled=True)


WIDTH = 4


def row_hop(value, step):
    count = lax.axis_size("slab")
    start = WIDTH - 1 if step > 0 else WIDTH
    pairs = [(s, s + step * WIDTH) for s in range(start, count, WIDTH) if 0 <= s + step * WIDTH < count]
    return lax.ppermute(value, "slab", pairs)


def row_ring(value, hopped, step):
    count = lax.axis_size("slab")
    pairs = [(s, s // WIDTH * WIDTH + (s + step) % WIDTH) for s in range(count)]
    end = lax.axis_index("slab") % WIDTH == (WIDTH - 1 if step > 0 else 0)
    return lax.ppermute(jnp.where(end, hopped, value), "slab", pairs)


def swapped(value):
    count = lax.axis_size("energy")
    return lax.ppermute(value, "energy", [(s, s ^ 1) for s in range(count)])


def exchange(first, second):
    up_hop, down_hop = row_hop(first, -1), row_hop(first, 1)
    up_second, down_second = passed_along(second, "slab", -1), passed_along(second, "slab", 1)
    up_first, down_first = row_ring(first, up_hop, -1), row_ring(first, down_hop, 1)
    return (up_first, down_first), (up_second, down_second)


def whole_run(energies, hamiltonian, coupling, coulomb, offsets):
    c, ham = coupling[0], hamiltonian[0]
    n = c.shape[0]
    parts = lax.axis_size("energy")
    place = lax.axis_index("slab")
    has_above = (place < lax.axis_size("slab") - 1).astype(jnp.float32)
    has_below = (place > 0).astype(jnp.float32)
    edge = jnp.stack([has_above, has_below])
    core = lax.rem(lax.axis_index("energy"), 2)
    inverse = (1.0 / energies).astype(jnp.bfloat16).astype(jnp.float32)
    shape = lambda kind, *dims: jax.ShapeDtypeStruct(dims, kind)
    half = lambda value: lax.dynamic_slice_in_dim(value, core * (n // 2), n // 2, 0)
    wide, narrow = jnp.float32, jnp.bfloat16
    cores = core[None]

    lower_mine = passed_along(half(c), "slab", 1)
    ham_half = half(ham)
    ham_hop = row_hop(ham_half, 1)
    ham_up = passed_along(ham_half, "slab", -1)
    own = call(own_body, shape(wide, n, n), [SM, VM])(edge[:1], c)
    lower_theirs = swapped(lower_mine)
    pair, pair_half, lower_c, lower_turned = call(
        pair_body,
        (shape(wide, n, n), shape(narrow, n // 2, n), shape(narrow, n, n), shape(narrow, n, n)),
        [SM, VM, VM, VM],
    )(cores, own, lower_mine, lower_theirs)
    ham_down = row_ring(ham_half, ham_hop, 1)
    pair_up = passed_along(pair_half, "slab", -1)
    pair_down = passed_along(pair_half, "slab", 1)
    mine = jnp.stack([ham_up, ham_down, pair_up, pair_down])
    theirs = swapped(mine)
    packed = shape(narrow, parts, 2, n // parts, n)
    greens = call(
        second_body,
        (packed, shape(narrow, n, n), shape(narrow, n, n)),
        [SM] * 4 + [VM] * 7,
        [pltpu.VMEM((4, n, n), narrow)],
    )(energies, inverse, edge, cores, ham, pair, mine, theirs, c, lower_c, lower_turned)
    chunks, greens = greens[0], greens[1:]
    near = exchange(*greens)
    opened = [
        call(functools.partial(terms_body, e), shape(wide, n, n), [SM] + [VM] * 6)(
            energies, ham, *near[e], c, lower_c, lower_turned
        )
        for e in range(2)
    ]
    self_part = self_energy(chunks, coulomb[0], offsets)
    greens = [
        call(functools.partial(third_body, e), shape(narrow, n, n), [VM] * 3)(opened[e], self_part, greens[e])
        for e in range(2)
    ]
    near = exchange(*greens)
    last = [
        call(functools.partial(fourth_body, e), (shape(wide, n, n), shape(narrow, n, n)), [SM] + [VM] * 8)(
            energies, ham, *near[e], c, lower_c, lower_turned, self_part, greens[e]
        )
        for e in range(2)
    ]
    chunks = jnp.stack([last[e][1].reshape(parts, n // parts, n) for e in range(2)], 1)
    self_part = self_energy(chunks, coulomb[0], offsets)
    self_part = jnp.swapaxes(self_part, 0, 1).reshape(2, n, n)
    return (jnp.stack([last[0][0], last[1][0]])[:, None], self_part[:, None])


def solution(mesh):
    placed = (
        P("energy"),
        P("slab", None, None),
        P("slab", None, None),
        P("slab", "energy", None),
        P(),
    )
    return jax.shard_map(
        whole_run,
        mesh=mesh,
        in_specs=placed,
        out_specs=(P("energy", "slab", None, None), P("energy", "slab", None, None)),
        check_vma=False,
    )
```

time: 318 us -> 292 us (0.918)
  waiting for transfers between devices: 144 us -> 97.3 us
  starting transfers between devices: 42.8 us -> 70.7 us
  blocking collectives: 68.7 us -> 49.1 us
  local copies, waits for them, and re-layouts: 6.69 us -> 10.5 us
  Pallas kernels: 53.6 us -> 57.1 us
    ppermute x9 -> x8, waiting for transfers between devices: 144 us -> 23.4 us  [passed_along(): lax.ppermute(value, axis, [(source, source + steps) for source in range(l...]
    ppermute x0 -> x12, waiting for transfers between devices: none -> 58.8 us  [the longest x5 40.2 us: row_hop(): return lax.ppermute(value, 'slab', pairs)]
    ppermute x0 -> x12, starting transfers between devices: none -> 31.4 us  [the longest x5 18.6 us: row_ring(): return lax.ppermute(jnp.where(end, hopped, value), 'slab', pairs)]
    all_to_all x1 -> x0, blocking collectives: 20.1 us -> none  [self_energy(): lax.all_to_all(result.reshape(parts, per, rows, columns), 'energy', split...]
    all_to_all x1 -> x2, waiting for transfers between devices: 0.01 us -> 15 us  [self_energy(): lax.all_to_all(result.reshape(parts, per, rows, columns), 'energy', split...]
    ppermute x9 -> x8, starting transfers between devices: 39.2 us -> 31.9 us  [passed_along(): lax.ppermute(value, axis, [(source, source + steps) for source in range(l...]
    pallas_call x6 -> x9, Pallas kernels: 33.1 us -> 40.1 us  [the longest x2 11.1 us: whole_run(): call(functools.partial(fourth_body, e), (shape(wide, n, n), shape(narrow,...]
    all_to_all x1 -> x2, starting transfers between devices: 3.65 us -> 7.44 us  [self_energy(): lax.all_to_all(result.reshape(parts, per, rows, columns), 'energy', split...]
  transfers between devices with their start and end apart: 10 -> 22, of which waited for: 6 -> 12; matrix products, arithmetic and copies ran while one was open for 0% -> 1% of each run, Pallas kernels for 4% -> 9%
where the time goes in v2:
time: 292 us; the launch traced here: 289 us
  waiting for transfers between devices  97.3 us (33%)
  starting transfers between devices  70.7 us (24%)
  Pallas kernels  57.1 us (20%)
  blocking collectives  49.1 us (17%)
  local copies, waits for them, and re-layouts  10.5 us (4%)
  other arithmetic  3.72 us (1%)
    all_to_all x2, blocking collectives, self_energy(): lax.all_to_all(chunks, 'energy', split_axis=0, concat_axis=0, tiled=True)  49.1 us
    ppermute x5, waiting for transfers between devices, row_hop(): return lax.ppermute(value, 'slab', pairs)  40.2 us
    ppermute x8, starting transfers between devices, passed_along(): lax.ppermute(value, axis, [(source, source + steps) for source in range(l...  31.9 us
    ppermute x8, waiting for transfers between devices, passed_along(): lax.ppermute(value, axis, [(source, source + steps) for source in range(l...  23.4 us
    ppermute x5, starting transfers between devices, row_ring(): return lax.ppermute(jnp.where(end, hopped, value), 'slab', pairs)  18.6 us
    pallas_call x2, Pallas kernels, self_energy(): call(energy_body, jax.ShapeDtypeStruct((count, rows, columns), jnp.bfloat...  16.9 us
    ppermute x5, waiting for transfers between devices, row_ring(): return lax.ppermute(jnp.where(end, hopped, value), 'slab', pairs)  16.7 us
    all_to_all x2, waiting for transfers between devices, self_energy(): lax.all_to_all(result.reshape(parts, per, rows, columns), 'energy', split...  15 us
  transfers between devices with their start and end apart: 22, of which 12 were waited for; matrix products, arithmetic and copies ran while one was open for 1% of the time, Pallas kernels for 9%

profile of v2, /device:TPU:70, one launch (start us, length us, event | category | flops | bytes accessed | tf_op | source)
XLA Modules:
  0.0 289.5 jit_solution(16897027291373053773)
XLA Ops:
  0.7 1.0 dynamic-slice_bitcast_fusion.1
  1.7 6.3 %collective-permute-start = (bf16[256,512]{1,0:T(8,128)(2,1)S(1)}, bf16[256,512]{1,0:T(8,128)(2,1)S(1)}, u32[]{:S(2)}, u32[]{:S(2)}) collective-permute-start(bf16[256,512]{1,0:T(8,128)(2,1)S(1)} %dynamic-slice_bitcast_fusion.1), channel_id=1, source_target_pairs={{0,1},{1,2},{2,3},{3,4},{4,5},{5,6},{6,7},{7,8},{8,9},{9,10},{10,1... | collective-permute-start | bytes 786440 | tf_op jit(solution)/shard_map/ppermute | solution.py:21
  8.0 1.0 dynamic-slice_bitcast_fusion
  9.0 3.4 %collective-permute-start.3 = (bf16[256,512]{1,0:T(8,128)(2,1)S(1)}, bf16[256,512]{1,0:T(8,128)(2,1)S(1)}, u32[]{:S(2)}, u32[]{:S(2)}) collective-permute-start(bf16[256,512]{1,0:T(8,128)(2,1)S(1)} %dynamic-slice_bitcast_fusion), channel_id=1, source_target_pairs={{3,7},{7,11},{11,15},{19,23},{23,27},{27,31},{35,39},{39,43},{43,4... | collective-permute-start | bytes 786440 | tf_op jit(solution)/shard_map/ppermute | solution.py:193
  12.4 3.8 %collective-permute-done.mine_ref = bf16[256,512]{1,0:T(8,128)(2,1)S(1)} collective-permute-done((bf16[256,512]{1,0:T(8,128)(2,1)S(1)}, bf16[256,512]{1,0:T(8,128)(2,1)S(1)}, u32[]{:S(2)}, u32[]{:S(2)}) %collective-permute-start) | collective-permute-done | bytes 262176 | tf_op jit(solution)/shard_map/ppermute | solution.py:21
  16.2 1.9 collective-permute-start.2
  18.1 2.5 shard_map.68.own_ref
  20.6 9.8 %collective-permute-done.3 = bf16[256,512]{1,0:T(8,128)(2,1)S(1)} collective-permute-done((bf16[256,512]{1,0:T(8,128)(2,1)S(1)}, bf16[256,512]{1,0:T(8,128)(2,1)S(1)}, u32[]{:S(2)}, u32[]{:S(2)}) %collective-permute-start.3) | collective-permute-done | bytes 262176 | tf_op jit(solution)/shard_map/ppermute | solution.py:193
  30.4 0.1 broadcast_select_fusion.4
  30.5 0.1 collective-permute-start.4
  30.6 0.7 copy-done.19
  31.3 3.1 %shard_map.69 = (f32[512,512]{1,0:T(8,128)}, bf16[256,512]{1,0:T(8,128)(2,1)}, bf16[512,512]{1,0:T(8,128)(2,1)}, bf16[512,512]{1,0:T(8,128)(2,1)}) custom-call(s32[1]{0:T(128)} %bitcast.3.core_ref, f32[512,512]{1,0:T(8,128)} %shard_map.68.own_ref, bf16[256,512]{1,0:T(8,128)(2,1)} %copy-done.18, bf16[256,512]{1,0:T(8,128)(2,1)} %copy-done.19), custom_call_target="tpu_custom_call" | custom-call | tf_op jit(solution)/shard_map/pallas_call | solution.py:236
  34.3 1.9 collective-permute-start.6
  36.3 3.9 %collective-permute-start.5 = (bf16[256,512]{1,0:T(8,128)(2,1)}, bf16[256,512]{1,0:T(8,128)(2,1)S(1)}, u32[]{:S(2)}, u32[]{:S(2)}) collective-permute-start(bf16[256,512]{1,0:T(8,128)(2,1)} %get-tuple-element.14), channel_id=1, source_target_pairs={{1,0},{2,1},{3,2},{4,3},{5,4},{6,5},{7,6},{8,7},{9,8},{10,9},{11,1... | collective-permute-start | bytes 786440 | tf_op jit(solution)/shard_map/ppermute | solution.py:21
  40.2 0.6 collective-permute-done.4
  40.8 6.4 %collective-permute-done.6 = bf16[256,512]{1,0:T(8,128)(2,1)S(1)} collective-permute-done((bf16[256,512]{1,0:T(8,128)(2,1)}, bf16[256,512]{1,0:T(8,128)(2,1)S(1)}, u32[]{:S(2)}, u32[]{:S(2)}) %collective-permute-start.6) | collective-permute-done | bytes 262176 | tf_op jit(solution)/shard_map/ppermute | solution.py:21
  47.2 2.7 collective-permute-done.5
  49.9 0.1 pad_maximum_fusion.mine_ref
  50.1 0.1 collective-permute-start.7
  50.2 0.7 pad_maximum_fusion.2
  50.9 1.9 collective-permute-done.7.theirs_ref
  52.8 1.0 copy-done.5
  53.8 8.5 %shard_map.70 = (bf16[16,2,32,512]{3,2,1,0:T(8,128)(2,1)}, bf16[512,512]{1,0:T(8,128)(2,1)}, bf16[512,512]{1,0:T(8,128)(2,1)}) custom-call(f32[2]{0:T(128)} %energy_ref.9, f32[2]{0:T(128)} %get-tuple-element.31.inverse_ref, f32[2]{0:T(128)} %get-tuple-element.30.edge_ref, s32[1]{0:T(128)} %bitcast.3.core_ref, bf16[512,512]{1,0:T(8,128)(2,1)} %bitcast.40, ...), custom_call_target="tpu_custom_call" | custom-call | tf_op jit(solution)/shard_map/pallas_call | solution.py:247
  62.3 28.4 %all_to_all.20 = bf16[16,2,32,512]{3,2,1,0:T(8,128)(2,1)} all-to-all(bf16[16,2,32,512]{3,2,1,0:T(8,128)(2,1)} %get-tuple-element.18), channel_id=1, replica_groups=mesh['energy'=16,'slab'=16] {'energy'}, dimensions={0} | all-to-all | bytes 2097152 | tf_op jit(solution)/shard_map/all_to_all | solution.py:175
  90.7 8.4 %shard_map.72 = bf16[32,32,512]{2,1,0:T(8,128)(2,1)} custom-call(s32[8]{0:T(128)} %offset_ref.3, bf16[32,32,512]{2,1,0:T(8,128)(2,1)} %bitcast.47, bf16[32,512]{1,0:T(8,128)(2,1)} %bitcast.59), custom_call_target="tpu_custom_call" | custom-call | tf_op jit(solution)/shard_map/pallas_call | solution.py:177
  99.2 3.8 %all-to-all-start.1 = ((bf16[16,2,32,512]{3,2,1,0:T(8,128)(2,1)}), bf16[16,2,32,512]{3,2,1,0:T(8,128)(2,1)S(1)}, u32[]{:S(2)}, u32[]{:S(2)}) async-start(bf16[16,2,32,512]{3,2,1,0:T(8,128)(2,1)} %bitcast.45), calls=%async_computation.1 | async-start | bytes 2097152 | tf_op jit(solution)/shard_map/all_to_all | solution.py:183
  103.0 3.5 %collective-permute-start.10 = (bf16[512,512]{1,0:T(8,128)(2,1)S(1)}, bf16[512,512]{1,0:T(8,128)(2,1)S(1)}, u32[]{:S(2)}, u32[]{:S(2)}) collective-permute-start(bf16[512,512]{1,0:T(8,128)(2,1)S(1)} %copy-done.4), channel_id=1, source_target_pairs={{3,7},{7,11},{11,15},{19,23},{23,27},{27,31},{35,39},{39,43},{43,4... | collective-permute-start | bytes 1572872 | tf_op jit(solution)/shard_map/ppermute | solution.py:193
  106.5 0.7 collective-permute-start.8
  107.2 30.4 %collective-permute-done.10 = bf16[512,512]{1,0:T(8,128)(2,1)S(1)} collective-permute-done((bf16[512,512]{1,0:T(8,128)(2,1)S(1)}, bf16[512,512]{1,0:T(8,128)(2,1)S(1)}, u32[]{:S(2)}, u32[]{:S(2)}) %collective-permute-start.10) | collective-permute-done | bytes 524320 | tf_op jit(solution)/shard_map/ppermute | solution.py:193
  137.6 0.1 broadcast_select_fusion.1
  137.7 0.1 collective-permute-start.11
  137.8 2.0 collective-permute-start.9
  139.8 7.2 %collective-permute-start.17 = (bf16[512,512]{1,0:T(8,128)(2,1)S(1)}, bf16[512,512]{1,0:T(8,128)(2,1)S(1)}, u32[]{:S(2)}, u32[]{:S(2)}) collective-permute-start(bf16[512,512]{1,0:T(8,128)(2,1)S(1)} %copy-done.16), channel_id=1, source_target_pairs={{0,1},{1,2},{2,3},{3,4},{4,5},{5,6},{6,7},{7,8},{8,9},{9,10},{10,1... | collective-permute-start | bytes 1572872 | tf_op jit(solution)/shard_map/ppermute | solution.py:21
  147.0 2.1 collective-permute-start.16
  149.1 11.3 %collective-permute-done.11.down_ref = bf16[512,512]{1,0:T(8,128)(2,1)S(1)} collective-permute-done((bf16[512,512]{1,0:T(8,128)(2,1)S(1)}, bf16[512,512]{1,0:T(8,128)(2,1)S(1)}, u32[]{:S(2)}, u32[]{:S(2)}) %collective-permute-start.11) | collective-permute-done | bytes 524320 | tf_op jit(solution)/shard_map/ppermute | solution.py:200
  160.5 0.8 copy-done.14
  161.3 0.8 copy-done.15
  162.1 4.2 %shard_map.71.open_ref = f32[512,512]{1,0:T(8,128)} custom-call(f32[2]{0:T(128)} %energy_ref.9, bf16[512,512]{1,0:T(8,128)(2,1)} %bitcast.41, bf16[512,512]{1,0:T(8,128)(2,1)} %copy-done.15, bf16[512,512]{1,0:T(8,128)(2,1)} %copy-done.14, bf16[512,512]{1,0:T(8,128)(2,1)} %bitcast.36, bf16[512,512]{1,0:T(8,128)(2,1)} %get-tuple-element.15.lower_c_ref, ...), custom_call_target="tpu_custom_call" | custom-call | tf_op jit(solution)/shard_map/pallas_call | solution.py:256
  166.3 1.0 copy-done
  167.2 3.3 %shard_map.73.green_ref = bf16[512,512]{1,0:T(8,128)(2,1)} custom-call(f32[512,512]{1,0:T(8,128)} %shard_map.71.open_ref, bf16[16,2,32,512]{3,2,1,0:T(8,128)(2,1)} %copy-done, bf16[512,512]{1,0:T(8,128)(2,1)} %get-tuple-element.17.green_ref), custom_call_target="tpu_custom_call" | custom-call | tf_op jit(solution)/shard_map/pallas_call | solution.py:263
  170.5 4.4 %collective-permute-start.14 = (bf16[512,512]{1,0:T(8,128)(2,1)}, bf16[512,512]{1,0:T(8,128)(2,1)S(1)}, u32[]{:S(2)}, u32[]{:S(2)}) collective-permute-start(bf16[512,512]{1,0:T(8,128)(2,1)} %shard_map.73.green_ref), channel_id=1, source_target_pairs={{3,7},{7,11},{11,15},{19,23},{23,27},{27,31},{35,39},{39,43},{43,4... | collective-permute-start | bytes 1572872 | tf_op jit(solution)/shard_map/ppermute | solution.py:193
  175.0 0.7 collective-permute-start.12
  175.7 0.8 copy-done.8
  176.5 0.8 copy-done.10
  177.3 4.2 %shard_map.75.open_ref = f32[512,512]{1,0:T(8,128)} custom-call(f32[2]{0:T(128)} %energy_ref.9, bf16[512,512]{1,0:T(8,128)(2,1)} %bitcast.42, bf16[512,512]{1,0:T(8,128)(2,1)} %copy-done.10, bf16[512,512]{1,0:T(8,128)(2,1)} %copy-done.8, bf16[512,512]{1,0:T(8,128)(2,1)} %bitcast.37, bf16[512,512]{1,0:T(8,128)(2,1)} %get-tuple-element.15.lower_c_ref, ...), custom_call_target="tpu_custom_call" | custom-call | tf_op jit(solution)/shard_map/pallas_call | solution.py:256
  181.5 3.3 %shard_map.76.green_ref = bf16[512,512]{1,0:T(8,128)(2,1)} custom-call(f32[512,512]{1,0:T(8,128)} %shard_map.75.open_ref, bf16[16,2,32,512]{3,2,1,0:T(8,128)(2,1)} %copy-done, bf16[512,512]{1,0:T(8,128)(2,1)} %get-tuple-element.20.green_ref), custom_call_target="tpu_custom_call" | custom-call | tf_op jit(solution)/shard_map/pallas_call | solution.py:263
  184.8 6.6 %collective-permute-start.19 = (bf16[512,512]{1,0:T(8,128)(2,1)}, bf16[512,512]{1,0:T(8,128)(2,1)S(1)}, u32[]{:S(2)}, u32[]{:S(2)}) collective-permute-start(bf16[512,512]{1,0:T(8,128)(2,1)} %shard_map.76.green_ref), channel_id=1, source_target_pairs={{0,1},{1,2},{2,3},{3,4},{4,5},{5,6},{6,7},{7,8},{8,9},{9,10},{10,1... | collective-permute-start | bytes 1572872 | tf_op jit(solution)/shard_map/ppermute | solution.py:21
  191.4 1.9 collective-permute-start.18
  193.4 0.1 broadcast_select_fusion
  193.5 16.4 %collective-permute-start.15 = (bf16[512,512]{1,0:T(8,128)(2,1)S(1)}, bf16[512,512]{1,0:T(8,128)(2,1)S(1)}, u32[]{:S(2)}, u32[]{:S(2)}) collective-permute-start(bf16[512,512]{1,0:T(8,128)(2,1)S(1)} %get-tuple-element.26), channel_id=1, source_target_pairs={{0,1},{1,2},{2,3},{3,0},{4,5},{5,6},{6,7},{7,4},{8,9},{9,10},{10,1... | collective-permute-start | bytes 1572872 | tf_op jit(solution)/shard_map/ppermute | solution.py:200
  209.9 9.3 %collective-permute-done.19.down_ref = bf16[512,512]{1,0:T(8,128)(2,1)S(1)} collective-permute-done((bf16[512,512]{1,0:T(8,128)(2,1)}, bf16[512,512]{1,0:T(8,128)(2,1)S(1)}, u32[]{:S(2)}, u32[]{:S(2)}) %collective-permute-start.19) | collective-permute-done | bytes 524320 | tf_op jit(solution)/shard_map/ppermute | solution.py:21
  219.2 1.2 collective-permute-done.18.up_ref
  220.4 0.8 copy-done.11
  221.2 5.5 %shard_map.77 = (f32[512,512]{1,0:T(8,128)}, bf16[512,512]{1,0:T(8,128)(2,1)}) custom-call(f32[2]{0:T(128)} %energy_ref.9, bf16[512,512]{1,0:T(8,128)(2,1)} %bitcast.43, bf16[512,512]{1,0:T(8,128)(2,1)} %copy-done.11, bf16[512,512]{1,0:T(8,128)(2,1)} %copy-done.9, bf16[512,512]{1,0:T(8,128)(2,1)} %bitcast.38, ...), custom_call_target="tpu_custom_call" | custom-call | tf_op jit(solution)/shard_map/pallas_call | solution.py:268
  226.8 4.8 %collective-permute-done.13.up_ref = bf16[512,512]{1,0:T(8,128)(2,1)S(1)} collective-permute-done((bf16[512,512]{1,0:T(8,128)(2,1)S(1)}, bf16[512,512]{1,0:T(8,128)(2,1)S(1)}, u32[]{:S(2)}, u32[]{:S(2)}) %collective-permute-start.13) | collective-permute-done | bytes 524320 | tf_op jit(solution)/shard_map/ppermute | solution.py:200
  231.6 0.8 copy-done.13
  232.3 5.5 %shard_map.74 = (f32[512,512]{1,0:T(8,128)}, bf16[512,512]{1,0:T(8,128)(2,1)}) custom-call(f32[2]{0:T(128)} %energy_ref.9, bf16[512,512]{1,0:T(8,128)(2,1)} %bitcast.44, bf16[512,512]{1,0:T(8,128)(2,1)} %copy-done.13, bf16[512,512]{1,0:T(8,128)(2,1)} %copy-done.12, bf16[512,512]{1,0:T(8,128)(2,1)} %bitcast.39, ...), custom_call_target="tpu_custom_call" | custom-call | tf_op jit(solution)/shard_map/pallas_call | solution.py:268
  237.9 1.1 pad_maximum_fusion.1
  239.0 20.7 %all_to_all.21 = bf16[16,2,32,512]{3,2,1,0:T(8,128)(2,1)} all-to-all(bf16[16,2,32,512]{3,2,1,0:T(8,128)(2,1)S(1)} %pad_maximum_fusion.1), channel_id=1, replica_groups=mesh['energy'=16,'slab'=16] {'energy'}, dimensions={0} | all-to-all | bytes 2097152 | tf_op jit(solution)/shard_map/all_to_all | solution.py:175
  259.7 8.5 %shard_map.78 = bf16[32,32,512]{2,1,0:T(8,128)(2,1)} custom-call(s32[8]{0:T(128)} %offset_ref.3, bf16[32,32,512]{2,1,0:T(8,128)(2,1)} %bitcast.48, bf16[32,512]{1,0:T(8,128)(2,1)} %bitcast.60), custom_call_target="tpu_custom_call" | custom-call | tf_op jit(solution)/shard_map/pallas_call | solution.py:177
  268.2 3.7 %all-to-all-start.3 = ((bf16[16,2,32,512]{3,2,1,0:T(8,128)(2,1)}), bf16[16,2,32,512]{3,2,1,0:T(8,128)(2,1)S(1)}, u32[]{:S(2)}, u32[]{:S(2)}) async-start(bf16[16,2,32,512]{3,2,1,0:T(8,128)(2,1)} %bitcast.46), calls=%async_computation.3 | async-start | bytes 2097152 | tf_op jit(solution)/shard_map/all_to_all | solution.py:183
  271.9 1.5 maximum_bitcast_fusion
  273.4 15.0 %all-to-all-done.3 = bf16[16,2,32,512]{3,2,1,0:T(8,128)(2,1)S(1)} async-done(((bf16[16,2,32,512]{3,2,1,0:T(8,128)(2,1)}), bf16[16,2,32,512]{3,2,1,0:T(8,128)(2,1)S(1)}, u32[]{:S(2)}, u32[]{:S(2)}) %all-to-all-start.3) | async-done | bytes 1048608 | tf_op jit(solution)/shard_map/all_to_all | solution.py:183
  288.4 1.0 copy.9
  (45 shorter events, 0.1 us)
Async XLA Ops:
  0.6 29.8 %copy-start.1 = (bf16[1,512,512]{2,1,0:T(8,128)(2,1)S(1)}, bf16[1,512,512]{2,1,0:T(8,128)(2,1)}, u32[]{:S(2)}) copy-start(bf16[1,512,512]{2,1,0:T(8,128)(2,1)} %param.6) | copy-start | bytes 1572868
  1.7 14.5 %collective-permute-start = (bf16[256,512]{1,0:T(8,128)(2,1)S(1)}, bf16[256,512]{1,0:T(8,128)(2,1)S(1)}, u32[]{:S(2)}, u32[]{:S(2)}) collective-permute-start(bf16[256,512]{1,0:T(8,128)(2,1)S(1)} %dynamic-slice_bitcast_fusion.1), channel_id=1, source_target_pairs={{0,1},{1,2},{2,3},{3,4},{4,5},{5,6},{6,7},{7,8},{8,9},{9,10},{10,1... | collective-permute-start | bytes 786440 | tf_op jit(solution)/shard_map/ppermute | solution.py:21
  9.0 21.4 %collective-permute-start.3 = (bf16[256,512]{1,0:T(8,128)(2,1)S(1)}, bf16[256,512]{1,0:T(8,128)(2,1)S(1)}, u32[]{:S(2)}, u32[]{:S(2)}) collective-permute-start(bf16[256,512]{1,0:T(8,128)(2,1)S(1)} %dynamic-slice_bitcast_fusion), channel_id=1, source_target_pairs={{3,7},{7,11},{11,15},{19,23},{23,27},{27,31},{35,39},{39,43},{43,4... | collective-permute-start | bytes 786440 | tf_op jit(solution)/shard_map/ppermute | solution.py:193
  16.2 14.4 %copy-start.18 = (bf16[256,512]{1,0:T(8,128)(2,1)}, bf16[256,512]{1,0:T(8,128)(2,1)S(1)}, u32[]{:S(2)}) copy-start(bf16[256,512]{1,0:T(8,128)(2,1)S(1)} %collective-permute-done.mine_ref) | copy-start | bytes 786436
  16.2 14.4 %collective-permute-start.1 = (bf16[256,512]{1,0:T(8,128)(2,1)S(1)}, bf16[256,512]{1,0:T(8,128)(2,1)S(1)}, u32[]{:S(2)}, u32[]{:S(2)}) collective-permute-start(bf16[256,512]{1,0:T(8,128)(2,1)S(1)} %collective-permute-done.mine_ref), channel_id=1, source_target_pairs={{0,16},{16,0},{32,48},{48,32},{64,80},{80,64},{96,112},{112,96},{1... | collective-permute-start | bytes 786440 | tf_op jit(solution)/shard_map/ppermute | solution.py:205
  16.2 24.0 %collective-permute-start.2 = (bf16[256,512]{1,0:T(8,128)(2,1)S(1)}, bf16[256,512]{1,0:T(8,128)(2,1)S(1)}, u32[]{:S(2)}, u32[]{:S(2)}) collective-permute-start(bf16[256,512]{1,0:T(8,128)(2,1)S(1)} %dynamic-slice_bitcast_fusion), channel_id=1, source_target_pairs={{1,0},{2,1},{3,2},{4,3},{5,4},{6,5},{7,6},{8,7},{9,8},{10,9},{11,1... | collective-permute-start | bytes 786440 | tf_op jit(solution)/shard_map/ppermute | solution.py:21
  20.6 29.6 %copy-start.20 = (f32[2]{0:T(128)S(1)}, f32[2]{0:T(128)}, u32[]{:S(2)}) copy-start(f32[2]{0:T(128)} %energy_ref.9) | copy-start | bytes 28
  30.5 10.3 %collective-permute-start.4 = (bf16[256,512]{1,0:T(8,128)(2,1)S(1)}, bf16[256,512]{1,0:T(8,128)(2,1)S(1)}, u32[]{:S(2)}, u32[]{:S(2)}) collective-permute-start(bf16[256,512]{1,0:T(8,128)(2,1)S(1)} %broadcast_select_fusion.4), channel_id=1, source_target_pairs={{0,1},{1,2},{2,3},{3,0},{4,5},{5,6},{6,7},{7,4},{8,9},{9,10},{10,1... | collective-permute-start | bytes 786440 | tf_op jit(solution)/shard_map/ppermute | solution.py:200
  30.6 0.7 copy-start.19
  34.3 12.9 %collective-permute-start.6 = (bf16[256,512]{1,0:T(8,128)(2,1)}, bf16[256,512]{1,0:T(8,128)(2,1)S(1)}, u32[]{:S(2)}, u32[]{:S(2)}) collective-permute-start(bf16[256,512]{1,0:T(8,128)(2,1)} %get-tuple-element.14), channel_id=1, source_target_pairs={{0,1},{1,2},{2,3},{3,4},{4,5},{5,6},{6,7},{7,8},{8,9},{9,10},{10,1... | collective-permute-start | bytes 786440 | tf_op jit(solution)/shard_map/ppermute | solution.py:21
  36.3 13.7 %collective-permute-start.5 = (bf16[256,512]{1,0:T(8,128)(2,1)}, bf16[256,512]{1,0:T(8,128)(2,1)S(1)}, u32[]{:S(2)}, u32[]{:S(2)}) collective-permute-start(bf16[256,512]{1,0:T(8,128)(2,1)} %get-tuple-element.14), channel_id=1, source_target_pairs={{1,0},{2,1},{3,2},{4,3},{5,4},{6,5},{7,6},{8,7},{9,8},{10,9},{11,1... | collective-permute-start | bytes 786440 | tf_op jit(solution)/shard_map/ppermute | solution.py:21
  50.0 2.8 copy-start.3
  50.1 2.7 collective-permute-start.7
  52.8 1.0 copy-start.5
  90.7 12.2 %copy-start.4 = (bf16[512,512]{1,0:T(8,128)(2,1)S(1)}, bf16[512,512]{1,0:T(8,128)(2,1)}, u32[]{:S(2)}) copy-start(bf16[512,512]{1,0:T(8,128)(2,1)} %get-tuple-element.17.green_ref) | copy-start | bytes 1572868
  99.2 40.6 %copy-start.16 = (bf16[512,512]{1,0:T(8,128)(2,1)S(1)}, bf16[512,512]{1,0:T(8,128)(2,1)}, u32[]{:S(2)}) copy-start(bf16[512,512]{1,0:T(8,128)(2,1)} %get-tuple-element.20.green_ref) | copy-start | bytes 1572868
  99.2 67.1 %all-to-all-start.1 = ((bf16[16,2,32,512]{3,2,1,0:T(8,128)(2,1)}), bf16[16,2,32,512]{3,2,1,0:T(8,128)(2,1)S(1)}, u32[]{:S(2)}, u32[]{:S(2)}) async-start(bf16[16,2,32,512]{3,2,1,0:T(8,128)(2,1)} %bitcast.45), calls=%async_computation.1 | async-start | bytes 2097152 | tf_op jit(solution)/shard_map/all_to_all | solution.py:183
  103.0 34.6 %collective-permute-start.10 = (bf16[512,512]{1,0:T(8,128)(2,1)S(1)}, bf16[512,512]{1,0:T(8,128)(2,1)S(1)}, u32[]{:S(2)}, u32[]{:S(2)}) collective-permute-start(bf16[512,512]{1,0:T(8,128)(2,1)S(1)} %copy-done.4), channel_id=1, source_target_pairs={{3,7},{7,11},{11,15},{19,23},{23,27},{27,31},{35,39},{39,43},{43,4... | collective-permute-start | bytes 1572872 | tf_op jit(solution)/shard_map/ppermute | solution.py:193
  106.5 31.1 %collective-permute-start.8 = (bf16[512,512]{1,0:T(8,128)(2,1)S(1)}, bf16[512,512]{1,0:T(8,128)(2,1)S(1)}, u32[]{:S(2)}, u32[]{:S(2)}) collective-permute-start(bf16[512,512]{1,0:T(8,128)(2,1)S(1)} %copy-done.4), channel_id=1, source_target_pairs={{4,0},{8,4},{12,8},{20,16},{24,20},{28,24},{36,32},{40,36},{44,40}... | collective-permute-start | bytes 1572872 | tf_op jit(solution)/shard_map/ppermute | solution.py:193
  137.7 22.8 %collective-permute-start.11 = (bf16[512,512]{1,0:T(8,128)(2,1)S(1)}, bf16[512,512]{1,0:T(8,128)(2,1)S(1)}, u32[]{:S(2)}, u32[]{:S(2)}) collective-permute-start(bf16[512,512]{1,0:T(8,128)(2,1)S(1)} %get-tuple-element.28), channel_id=1, source_target_pairs={{0,1},{1,2},{2,3},{3,0},{4,5},{5,6},{6,7},{7,4},{8,9},{9,10},{10,1... | collective-permute-start | bytes 1572872 | tf_op jit(solution)/shard_map/ppermute | solution.py:200
  137.8 22.7 %collective-permute-start.9 = (bf16[512,512]{1,0:T(8,128)(2,1)S(1)}, bf16[512,512]{1,0:T(8,128)(2,1)S(1)}, u32[]{:S(2)}, u32[]{:S(2)}) collective-permute-start(bf16[512,512]{1,0:T(8,128)(2,1)S(1)} %get-tuple-element.29), channel_id=1, source_target_pairs={{0,3},{1,0},{2,1},{3,2},{4,7},{5,4},{6,5},{7,6},{8,11},{9,8},{10,9... | collective-permute-start | bytes 1572872 | tf_op jit(solution)/shard_map/ppermute | solution.py:200
  139.8 35.9 %collective-permute-start.17 = (bf16[512,512]{1,0:T(8,128)(2,1)S(1)}, bf16[512,512]{1,0:T(8,128)(2,1)S(1)}, u32[]{:S(2)}, u32[]{:S(2)}) collective-permute-start(bf16[512,512]{1,0:T(8,128)(2,1)S(1)} %copy-done.16), channel_id=1, source_target_pairs={{0,1},{1,2},{2,3},{3,4},{4,5},{5,6},{6,7},{7,8},{8,9},{9,10},{10,1... | collective-permute-start | bytes 1572872 | tf_op jit(solution)/shard_map/ppermute | solution.py:21
  147.0 28.7 %collective-permute-start.16 = (bf16[512,512]{1,0:T(8,128)(2,1)S(1)}, bf16[512,512]{1,0:T(8,128)(2,1)S(1)}, u32[]{:S(2)}, u32[]{:S(2)}) collective-permute-start(bf16[512,512]{1,0:T(8,128)(2,1)S(1)} %copy-done.16), channel_id=1, source_target_pairs={{1,0},{2,1},{3,2},{4,3},{5,4},{6,5},{7,6},{8,7},{9,8},{10,9},{11,1... | collective-permute-start | bytes 1572872 | tf_op jit(solution)/shard_map/ppermute | solution.py:21
  160.4 0.8 copy-start.14
  161.3 0.8 copy-start.15
  166.3 1.0 copy-start
  170.5 22.8 %collective-permute-start.14 = (bf16[512,512]{1,0:T(8,128)(2,1)}, bf16[512,512]{1,0:T(8,128)(2,1)S(1)}, u32[]{:S(2)}, u32[]{:S(2)}) collective-permute-start(bf16[512,512]{1,0:T(8,128)(2,1)} %shard_map.73.green_ref), channel_id=1, source_target_pairs={{3,7},{7,11},{11,15},{19,23},{23,27},{27,31},{35,39},{39,43},{43,4... | collective-permute-start | bytes 1572872 | tf_op jit(solution)/shard_map/ppermute | solution.py:193
  175.0 18.4 %collective-permute-start.12 = (bf16[512,512]{1,0:T(8,128)(2,1)}, bf16[512,512]{1,0:T(8,128)(2,1)S(1)}, u32[]{:S(2)}, u32[]{:S(2)}) collective-permute-start(bf16[512,512]{1,0:T(8,128)(2,1)} %shard_map.73.green_ref), channel_id=1, source_target_pairs={{4,0},{8,4},{12,8},{20,16},{24,20},{28,24},{36,32},{40,36},{44,40}... | collective-permute-start | bytes 1572872 | tf_op jit(solution)/shard_map/ppermute | solution.py:193
  175.7 0.8 copy-start.8
  176.5 0.8 copy-start.10
  181.5 11.9 %copy-start.2 = (bf16[512,512]{1,0:T(8,128)(2,1)S(1)}, bf16[512,512]{1,0:T(8,128)(2,1)}, u32[]{:S(2)}) copy-start(bf16[512,512]{1,0:T(8,128)(2,1)} %shard_map.73.green_ref) | copy-start | bytes 1572868
  184.8 34.4 %collective-permute-start.19 = (bf16[512,512]{1,0:T(8,128)(2,1)}, bf16[512,512]{1,0:T(8,128)(2,1)S(1)}, u32[]{:S(2)}, u32[]{:S(2)}) collective-permute-start(bf16[512,512]{1,0:T(8,128)(2,1)} %shard_map.76.green_ref), channel_id=1, source_target_pairs={{0,1},{1,2},{2,3},{3,4},{4,5},{5,6},{6,7},{7,8},{8,9},{9,10},{10,1... | collective-permute-start | bytes 1572872 | tf_op jit(solution)/shard_map/ppermute | solution.py:21
  191.4 29.0 %collective-permute-start.18 = (bf16[512,512]{1,0:T(8,128)(2,1)}, bf16[512,512]{1,0:T(8,128)(2,1)S(1)}, u32[]{:S(2)}, u32[]{:S(2)}) collective-permute-start(bf16[512,512]{1,0:T(8,128)(2,1)} %shard_map.76.green_ref), channel_id=1, source_target_pairs={{1,0},{2,1},{3,2},{4,3},{5,4},{6,5},{7,6},{8,7},{9,8},{10,9},{11,1... | collective-permute-start | bytes 1572872 | tf_op jit(solution)/shard_map/ppermute | solution.py:21
  193.5 33.3 %collective-permute-start.15 = (bf16[512,512]{1,0:T(8,128)(2,1)S(1)}, bf16[512,512]{1,0:T(8,128)(2,1)S(1)}, u32[]{:S(2)}, u32[]{:S(2)}) collective-permute-start(bf16[512,512]{1,0:T(8,128)(2,1)S(1)} %get-tuple-element.26), channel_id=1, source_target_pairs={{0,1},{1,2},{2,3},{3,0},{4,5},{5,6},{6,7},{7,4},{8,9},{9,10},{10,1... | collective-permute-start | bytes 1572872 | tf_op jit(solution)/shard_map/ppermute | solution.py:200
  209.9 21.6 %collective-permute-start.13 = (bf16[512,512]{1,0:T(8,128)(2,1)S(1)}, bf16[512,512]{1,0:T(8,128)(2,1)S(1)}, u32[]{:S(2)}, u32[]{:S(2)}) collective-permute-start(bf16[512,512]{1,0:T(8,128)(2,1)S(1)} %get-tuple-element.27), channel_id=1, source_target_pairs={{0,3},{1,0},{2,1},{3,2},{4,7},{5,4},{6,5},{7,6},{8,11},{9,8},{10,9... | collective-permute-start | bytes 1572872 | tf_op jit(solution)/shard_map/ppermute | solution.py:200
  219.2 1.2 copy-start.9
  220.4 0.8 copy-start.11
  226.7 11.2 %copy-start.17 = (bf16[512,512]{1,0:T(8,128)(2,1)S(1)}, bf16[512,512]{1,0:T(8,128)(2,1)}, u32[]{:S(2)}) copy-start(bf16[512,512]{1,0:T(8,128)(2,1)} %get-tuple-element.23) | copy-start | bytes 1572868
  226.8 4.8 %copy-start.12 = (bf16[512,512]{1,0:T(8,128)(2,1)}, bf16[512,512]{1,0:T(8,128)(2,1)S(1)}, u32[]{:S(2)}) copy-start(bf16[512,512]{1,0:T(8,128)(2,1)S(1)} %collective-permute-done.15.down_ref) | copy-start | bytes 1572868
  231.6 0.8 copy-start.13
  259.7 12.2 %copy-start.6 = (f32[512,512]{1,0:T(8,128)S(1)}, f32[512,512]{1,0:T(8,128)}, u32[]{:S(2)}) copy-start(f32[512,512]{1,0:T(8,128)} %get-tuple-element.21) | copy-start | bytes 3145732
  259.7 12.2 %copy-start.7 = (f32[512,512]{1,0:T(8,128)S(1)}, f32[512,512]{1,0:T(8,128)}, u32[]{:S(2)}) copy-start(f32[512,512]{1,0:T(8,128)} %get-tuple-element.19) | copy-start | bytes 3145732
  268.2 20.2 %all-to-all-start.3 = ((bf16[16,2,32,512]{3,2,1,0:T(8,128)(2,1)}), bf16[16,2,32,512]{3,2,1,0:T(8,128)(2,1)S(1)}, u32[]{:S(2)}, u32[]{:S(2)}) async-start(bf16[16,2,32,512]{3,2,1,0:T(8,128)(2,1)} %bitcast.46), calls=%async_computation.3 | async-start | bytes 2097152 | tf_op jit(solution)/shard_map/all_to_all | solution.py:183

commit v3 on v2

v3 whole, which is shorter than its diff:
```python
import functools

import jax
import jax.numpy as jnp
from jax import lax
from jax.experimental import pallas as pl
from jax.experimental.pallas import tpu as pltpu
from jax.sharding import PartitionSpec as P


BROAD = 0.3
REACH = 16

VM = pl.BlockSpec(memory_space=pltpu.VMEM)
SM = pl.BlockSpec(memory_space=pltpu.SMEM)


SLAB = ("row", "x")
ENERGY = ("zlo", "y", "core")
WIDTH = 4


def passed_along(value, steps):
    count = lax.axis_size(SLAB)
    leading, last = (max(0, -steps), min(count, count - steps))
    return lax.ppermute(value, SLAB, [(source, source + steps) for source in range(leading, last)])


def row_ring(value, steps):
    return lax.ppermute(value, "x", [(s, (s + steps) % WIDTH) for s in range(WIDTH)])


def row_climb(value):
    count = lax.axis_size(SLAB)
    return lax.ppermute(value, SLAB, [(s, s + WIDTH) for s in range(0, count - WIDTH, WIDTH)])


def swapped(value):
    return lax.ppermute(value, "core", [(0, 1), (1, 0)])


def row_above(value, both):
    rows = lax.axis_size("row")
    pairs = [(rows + r, r + 1) for r in range(rows - 1)]
    if both:
        pairs += [(r, rows + r - 1) for r in range(1, rows)]
    return lax.ppermute(value, ("core", "row"), pairs)


def flipped(value, side):
    pairs = [(c * WIDTH + i, (i // 2) * WIDTH + 2 * c + (i % 2 + side) % 2) for c in range(2) for i in range(WIDTH)]
    return lax.ppermute(value, ("core", "x"), pairs)


def call(body, out_shape, in_specs, scratch=()):
    return pl.pallas_call(
        body,
        out_shape=out_shape,
        in_specs=in_specs,
        out_specs=jax.tree.map(lambda _: VM, out_shape),
        scratch_shapes=list(scratch),
        compiler_params=pltpu.CompilerParams(vmem_limit_bytes=56 * 1024 * 1024),
    )


def dot(a, b):
    return jnp.dot(a, b, preferred_element_type=jnp.float32)


def dot_t(a, b):
    return lax.dot_general(a, b, (((1,), (1,)), ((), ())), preferred_element_type=jnp.float32)


def tables(n):
    row = lax.broadcasted_iota(jnp.int32, (n, n), 0)
    col = lax.broadcasted_iota(jnp.int32, (n, n), 1)
    half = n // 2
    eye = jnp.where(row == col, 1.0, 0.0)
    rotate = jnp.where(col == row + half, -1.0, 0.0) + jnp.where(col == row - half, 1.0, 0.0)
    return eye, rotate


def own_body(keep_ref, at_ref, c_ref, ham_ref, own_ref, load_ref):
    own_ref[...] = dot_t(c_ref[...], c_ref[...]) * keep_ref[0]
    load_ref[...] = jnp.where(at_ref[0] == 0, ham_ref[...], c_ref[...])


def place_halves(core, whole, mine, theirs):
    half = mine.shape[0]
    whole[pl.ds(pl.multiple_of(core * half, half), half)] = mine
    whole[pl.ds(pl.multiple_of((1 - core) * half, half), half)] = theirs


def pair_body(at_ref, own_ref, mine_ref, theirs_ref, pair_ref, half_ref, below_ref, turned_ref):
    core = at_ref[0]
    half = half_ref.shape[0]
    place_halves(core, below_ref, mine_ref[...], theirs_ref[...])
    below = below_ref[...]
    turned = below.T
    turned_ref[...] = turned
    pair_ref[...] = own_ref[...] + dot(turned, below)
    half_ref[...] = pair_ref[pl.ds(pl.multiple_of(core * half, half), half)].astype(jnp.bfloat16)


def first_step(energy, inverse, ham, pair, eye, rotate):
    base = energy * eye + BROAD * rotate - ham.astype(jnp.float32)
    matrix = (base - inverse * pair.astype(jnp.float32)).astype(jnp.bfloat16).astype(jnp.float32)
    residue = (2.0 * eye - inverse * matrix).astype(jnp.bfloat16).astype(jnp.float32)
    return (inverse * residue).astype(jnp.bfloat16)


def linked(green, link):
    return dot(link, dot_t(green, link).astype(jnp.bfloat16))


def finish(matrix, green, eye):
    product = dot(matrix, green)
    residue = (2.0 * eye - product).astype(jnp.bfloat16)
    return dot(green, residue)


def second_body(
    energy_ref, inverse_ref, edge_ref, at_ref, ham_ref, pair_ref, mine_ref, theirs_ref, c_ref, lower_turned_ref,
    out_ref, first_ref, second_ref, whole,
):
    n = c_ref.shape[0]
    eye, rotate = tables(n)
    chunks = out_ref.shape[0]
    for i in range(4):
        place_halves(at_ref[0], whole.at[i], mine_ref[i], theirs_ref[i])
    odd = lax.rem(at_ref[1], 2)
    for e, same_ref in ((odd, first_ref), (1 - odd, second_ref)):
        energy, inverse = energy_ref[e], inverse_ref[e]
        above = first_step(energy, inverse * edge_ref[0], whole[0], whole[2], eye, rotate)
        below = first_step(energy, inverse * edge_ref[1], whole[1], whole[3], eye, rotate)
        green = first_step(energy, inverse, ham_ref[...], pair_ref[...], eye, rotate)
        base = energy * eye + BROAD * rotate - ham_ref[...].astype(jnp.float32)
        matrix = (base - linked(above, c_ref[...]) - linked(below, lower_turned_ref[...])).astype(jnp.bfloat16)
        result = finish(matrix, green, eye).astype(jnp.bfloat16)
        out_ref[:, e] = result.reshape(chunks, n // chunks, n)
        same_ref[...] = result


def gather_body(at_ref, here_ref, one_ref, two_ref, three_ref, all_ref, give_ref, last_ref):
    core, x = at_ref[0], at_ref[1]
    for k, ref in enumerate((here_ref, one_ref, two_ref, three_ref)):
        all_ref[lax.rem(x + WIDTH - k, WIDTH)] = ref[...]
    give_ref[...] = all_ref[pl.ds(2 * (1 - core), 2)]
    last_ref[...] = all_ref[WIDTH - 1]


def link_body(at_ref, all_ref, got_ref, below_ref, outer_ham, inner_ham, far, mid, mid_turned, near):
    @pl.when(at_ref[0] == 0)
    def _():
        outer_ham[...] = all_ref[0]
        inner_ham[...] = all_ref[1]
        far[...] = below_ref[...].T
        mid[...] = got_ref[0]
        mid_turned[...] = got_ref[0].T
        near[...] = got_ref[1]

    @pl.when(at_ref[0] == 1)
    def _():
        outer_ham[...] = got_ref[1]
        inner_ham[...] = got_ref[0]
        far[...] = all_ref[3]
        mid[...] = all_ref[2].T
        mid_turned[...] = all_ref[2]
        near[...] = all_ref[1].T


def role_body(at_ref, first_ref, second_ref, outer_ref, inner_ref):
    match = lax.rem(at_ref[1], 2) == at_ref[0]
    outer_ref[...] = jnp.where(match, first_ref[...], second_ref[...])
    inner_ref[...] = jnp.where(match, second_ref[...], first_ref[...])


def open_body(
    energy_ref, outer_ham, inner_ham, far, mid, mid_turned, near, outer, inner, beyond, beside, open_outer, open_inner,
):
    eye, rotate = tables(outer.shape[0])
    base = energy_ref[0] * eye + BROAD * rotate
    open_outer[...] = (
        base - outer_ham[...].astype(jnp.float32) - linked(inner[...], mid[...]) - linked(beyond[...], far[...])
    )
    open_inner[...] = (
        base - inner_ham[...].astype(jnp.float32) - linked(outer[...], mid_turned[...]) - linked(beside[...], near[...])
    )


def joined_rows(core, slot, mine_ref, theirs_ref, scratch):
    scratch[:, core] = mine_ref[2 * core + slot]
    scratch[:, 1 - core] = theirs_ref[slot]
    n = scratch.shape[-1]
    return scratch[...].reshape(n, n).astype(jnp.float32)


def third_body(inner, at_ref, open_ref, mine_ref, theirs_ref, green_ref, out_ref, scratch):
    core = at_ref[0]
    eye, _ = tables(open_ref.shape[0])
    self_part = joined_rows(core, 1 - core if inner else core, mine_ref, theirs_ref, scratch)
    matrix = (open_ref[...] - self_part).astype(jnp.bfloat16)
    out_ref[...] = finish(matrix, green_ref[...], eye).astype(jnp.bfloat16)


def split_rows(core, result, keep_ref, give_ref, scratch):
    scratch[...] = result.reshape(scratch.shape)
    keep_ref[...] = scratch[:, core]
    give_ref[...] = scratch[:, 1 - core]


def inner_body(
    energy_ref, at_ref, outer_ham, inner_ham, mid, mid_turned, near, mine_ref, theirs_ref, outer, inner, beside,
    open_outer, whole_ref, keep_ref, give_ref, scratch,
):
    core = at_ref[0]
    eye, rotate = tables(outer.shape[0])
    base = energy_ref[0] * eye + BROAD * rotate
    self_part = joined_rows(core, 1 - core, mine_ref, theirs_ref, scratch)
    matrix = (
        base - inner_ham[...].astype(jnp.float32) - self_part - linked(outer[...], mid_turned[...])
        - linked(beside[...], near[...])
    ).astype(jnp.bfloat16)
    result = finish(matrix, inner[...], eye).astype(jnp.bfloat16)
    whole_ref[...] = result
    split_rows(core, result, keep_ref, give_ref, scratch)
    self_part = joined_rows(core, core, mine_ref, theirs_ref, scratch)
    open_outer[...] = base - outer_ham[...].astype(jnp.float32) - self_part - linked(inner[...], mid[...])


def outer_body(at_ref, far, open_ref, outer, beyond, whole_ref, keep_ref, give_ref, scratch):
    eye, _ = tables(outer.shape[0])
    matrix = (open_ref[...] - linked(beyond[...], far[...])).astype(jnp.bfloat16)
    result = finish(matrix, outer[...], eye).astype(jnp.bfloat16)
    whole_ref[...] = result
    split_rows(at_ref[0], result, keep_ref, give_ref, scratch)


def join_body(at_ref, keep_outer, keep_inner, got_outer, got_inner, out_ref):
    first = at_ref[0] == 0
    out_ref[0] = jnp.where(first, keep_outer[...], got_outer[...])
    out_ref[1] = jnp.where(first, keep_inner[...], got_inner[...])
    out_ref[2] = jnp.where(first, got_inner[...], keep_inner[...])
    out_ref[3] = jnp.where(first, got_outer[...], keep_outer[...])


def spread_body(at_ref, first_ref, second_ref, out_ref):
    odd = lax.rem(at_ref[1], 2)
    out_ref[odd] = first_ref[...].astype(jnp.float32)
    out_ref[1 - odd] = second_ref[...].astype(jnp.float32)


def energy_body(place_in, place_out, offset_ref, green_ref, coulomb_ref, out_ref, padded, wide):
    count, rows, columns = green_ref.shape
    offset_count = offset_ref.shape[0]
    none = jnp.zeros((REACH, rows, columns), jnp.float32)
    padded[:REACH] = none
    padded[REACH + count :] = none
    for e in range(count):
        padded[REACH + e] = green_ref[place_in[e]].astype(jnp.float32)
    wide[...] = coulomb_ref[...].astype(jnp.float32)
    column_tiles = columns // 128

    def tile(t, carry):
        row = pl.ds(pl.multiple_of(8 * (t // column_tiles), 8), 8)
        column = pl.ds(pl.multiple_of(128 * (t % column_tiles), 128), 128)
        strength = wide[row, column]
        own = padded[REACH : REACH + count, row, column]
        total = jnp.zeros(own.shape, jnp.float32)
        screened = []
        for k in range(offset_count):
            later = padded[pl.ds(REACH + offset_ref[k], count), row, column]
            polarization = (4.0 / count) * jnp.sum(own * later, axis=0)
            screened.append(strength * (1.0 + polarization * strength) * (1.0 / offset_count))
        for k in range(offset_count):
            total = total + screened[k][None] * padded[pl.ds(REACH - offset_ref[k], count), row, column]
        total = total.astype(jnp.bfloat16)
        for e in range(count):
            out_ref[place_out[e], row, column] = total[e]
        return carry

    lax.fori_loop(0, (rows // 8) * column_tiles, tile, 0)


def convolved(received, coulomb, offsets, place_in, place_out):
    count, rows, columns = received.shape
    return call(
        functools.partial(energy_body, place_in, place_out),
        jax.ShapeDtypeStruct((count, rows, columns), jnp.bfloat16),
        [SM, VM, VM],
        [pltpu.VMEM((count + 2 * REACH, rows, columns), jnp.float32), pltpu.VMEM((rows, columns), jnp.float32)],
    )(offsets, received, coulomb)


def all_to_all(value, axes):
    return lax.all_to_all(value, axes, split_axis=0, concat_axis=0, tiled=True)


def whole_run(energies, hamiltonian, coupling, coulomb, offsets):
    c, ham, strength = coupling[0], hamiltonian[0], coulomb[0]
    n = c.shape[0]
    parts = lax.axis_size(ENERGY)
    rows, pairs = n // parts, parts // 2
    count = 2 * parts
    place, x, core = lax.axis_index(SLAB), lax.axis_index("x"), lax.axis_index("core")
    edge = jnp.stack([place < lax.axis_size(SLAB) - 1, place > 0]).astype(jnp.float32)
    at = jnp.stack([core, x]).astype(jnp.int32)
    inverse = (1.0 / energies).astype(jnp.bfloat16).astype(jnp.float32)
    half = lambda value: lax.dynamic_slice_in_dim(value, core * (n // 2), n // 2, 0)
    wide = lambda *dims: jax.ShapeDtypeStruct(dims, jnp.float32)
    thin = lambda *dims: jax.ShapeDtypeStruct(dims, jnp.bfloat16)
    natural = list(range(count))
    by_chip = [(e % WIDTH) * (count // WIDTH) + e // WIDTH for e in range(count)]

    lower_mine = passed_along(half(c), 1)
    ham_half = half(ham)
    ham_ring = row_ring(ham_half, 1)
    ham_up = passed_along(ham_half, -1)
    energy_pair = swapped(energies)
    own, load = call(own_body, (wide(n, n), thin(n, n)), [SM, SM, VM, VM])(edge[:1], at, c, ham)
    lower_theirs = swapped(lower_mine)
    ham_climb = row_climb(ham_ring)
    pair, pair_half, _, lower_turned = call(
        pair_body, (wide(n, n), thin(n // 2, n), thin(n, n), thin(n, n)), [SM, VM, VM, VM]
    )(at, own, lower_mine, lower_theirs)
    pair_up = passed_along(pair_half, -1)
    pair_down = passed_along(pair_half, 1)
    mine = jnp.stack([ham_up, jnp.where(x == 0, ham_climb, ham_ring), pair_up, pair_down])
    theirs = swapped(mine)
    one, three = row_ring(load, 1), row_ring(load, -1)
    chunks, first, second = call(
        second_body,
        (thin(parts, 2, rows, n), thin(n, n), thin(n, n)),
        [SM] * 4 + [VM] * 6,
        [pltpu.VMEM((4, n, n), jnp.bfloat16)],
    )(energies, inverse, edge, at, ham, pair, mine, theirs, c, lower_turned)
    first, second = flipped(first, 0), flipped(second, 1)
    two = row_ring(one, 1)
    received = all_to_all(chunks, ENERGY)

    everything, give, last = call(gather_body, (thin(WIDTH, n, n), thin(2, n, n), thin(n, n)), [SM] + [VM] * 4)(
        at, load, one, two, three
    )
    got = swapped(give)
    below_c = row_above(last, False)
    outer_ham, inner_ham, far, mid, mid_turned, near = call(link_body, (thin(n, n),) * 6, [SM] + [VM] * 3)(
        at, everything, got, below_c
    )
    fours = jnp.where(core == 0, jnp.concatenate([energies, energy_pair]), jnp.concatenate([energy_pair, energies]))
    energy = lax.dynamic_slice_in_dim(fours, x, 1)
    outer, inner = call(role_body, (thin(n, n),) * 2, [SM, VM, VM])(at, first, second)
    beyond = row_above(outer, True)
    beside = swapped(inner)
    open_outer, open_inner = call(open_body, (wide(n, n),) * 2, [SM] + [VM] * 10)(
        energy, outer_ham, inner_ham, far, mid, mid_turned, near, outer, inner, beyond, beside
    )
    result = convolved(received.reshape(count, rows, n), strength, offsets, natural, by_chip)
    self_mine = all_to_all(result, ("x", "zlo", "y")).reshape(WIDTH, pairs, rows, n)
    self_theirs = swapped(lax.dynamic_slice_in_dim(self_mine, 2 * (1 - core), 2, 0))
    mix = [pltpu.VMEM((pairs, 2, rows, n), jnp.bfloat16)]
    third = lambda role, opened, green: call(
        functools.partial(third_body, role), thin(n, n), [SM] + [VM] * 4, mix
    )(at, opened, self_mine, self_theirs, green)
    outer = third(False, open_outer, outer)
    beyond = row_above(outer, True)
    inner = third(True, open_inner, inner)
    beside = swapped(inner)
    open_outer, whole_inner, keep_inner, give_inner = call(
        inner_body, (wide(n, n), thin(n, n), thin(pairs, rows, n), thin(pairs, rows, n)), [SM] * 2 + [VM] * 10, mix
    )(energy, at, outer_ham, inner_ham, mid, mid_turned, near, self_mine, self_theirs, outer, inner, beside)
    got_inner = swapped(give_inner)
    whole_outer, keep_outer, give_outer = call(
        outer_body, (thin(n, n), thin(pairs, rows, n), thin(pairs, rows, n)), [SM] + [VM] * 4, mix
    )(at, far, open_outer, outer, beyond)
    got_outer = swapped(give_outer)
    chunks = call(join_body, thin(WIDTH, pairs, rows, n), [SM] + [VM] * 4)(
        at, keep_outer, keep_inner, got_outer, got_inner
    )
    received = all_to_all(chunks.reshape(count, rows, n), ("x", "zlo", "y"))
    first, second = call(role_body, (thin(n, n),) * 2, [SM, VM, VM])(at, whole_outer, whole_inner)
    first, second = flipped(first, 0), flipped(second, 1)
    result = convolved(received, strength, offsets, by_chip, natural)
    self_part = all_to_all(result.reshape(parts, 2, rows, n), ENERGY)
    green = call(spread_body, wide(2, n, n), [SM, VM, VM])(at, first, second)
    self_part = jnp.swapaxes(self_part, 0, 1).reshape(2, n, n)
    return (green[:, None], self_part[:, None])


def fine_mesh(mesh):
    energy, slab = mesh.shape["energy"], mesh.shape["slab"]
    zlo, y = (2, energy // 4) if energy > 2 else (1, 1)
    devices = mesh.devices.reshape(zlo, y, 2, slab // WIDTH, WIDTH)
    return jax.sharding.Mesh(devices, ("zlo", "y", "core", "row", "x"))


def solution(mesh):
    mesh = fine_mesh(mesh)
    return jax.shard_map(
        whole_run,
        mesh=mesh,
        in_specs=(P(ENERGY), P(SLAB), P(SLAB), P(SLAB, ENERGY), P()),
        out_specs=(P(ENERGY, SLAB), P(ENERGY, SLAB)),
        check_vma=False,
    )
```

time: 292 us -> 287 us (0.983)
  waiting for transfers between devices: 97.3 us -> 79.9 us
  Pallas kernels: 57.1 us -> 73.5 us
  starting transfers between devices: 70.7 us -> 55.7 us
  blocking collectives: 49.1 us -> 60.3 us
    ppermute x20 -> x25, starting transfers between devices: 63.3 us -> 46.4 us  [the longest x4 20.4 us: passed_along(): lax.ppermute(value, SLAB, [(source, source + steps) for source in range(l...]
    pallas_call x11 -> x16, Pallas kernels: 57.1 us -> 73.5 us  [the longest x2 16.8 us: convolved(): call(functools.partial(energy_body, place_in, place_out), jax.ShapeDtypeS...]
    all_to_all x2, waiting for transfers between devices: 15 us -> 0.01 us  [all_to_all(): return lax.all_to_all(value, axes, split_axis=0, concat_axis=0, tiled=True)]
    all_to_all x2, blocking collectives: 49.1 us -> 60.3 us  [all_to_all(): return lax.all_to_all(value, axes, split_axis=0, concat_axis=0, tiled=True)]
    ppermute x20 -> x25, waiting for transfers between devices: 82.3 us -> 79.9 us  [the longest x4 29.9 us: row_ring(): lax.ppermute(value, 'x', [(s, (s + steps) % WIDTH) for s in range(WIDTH)])]
  transfers between devices with their start and end apart: 22 -> 27, of which waited for: 12 -> 13; matrix products, arithmetic and copies ran while one was open for 1% -> 1% of each run, Pallas kernels for 9% -> 14%
where the time goes in v3:
time: 287 us; the launch traced here: 284 us
  waiting for transfers between devices  79.9 us (28%)
  Pallas kernels  73.5 us (26%)
  blocking collectives  60.3 us (21%)
  starting transfers between devices  55.7 us (19%)
  local copies, waits for them, and re-layouts  11.2 us (4%)
    all_to_all x2, blocking collectives, all_to_all(): return lax.all_to_all(value, axes, split_axis=0, concat_axis=0, tiled=True)  60.3 us
    ppermute x4, waiting for transfers between devices, row_ring(): lax.ppermute(value, 'x', [(s, (s + steps) % WIDTH) for s in range(WIDTH)])  29.9 us
    ppermute x4, waiting for transfers between devices, passed_along(): lax.ppermute(value, SLAB, [(source, source + steps) for source in range(l...  26.2 us
    ppermute x4, starting transfers between devices, passed_along(): lax.ppermute(value, SLAB, [(source, source + steps) for source in range(l...  20.4 us
    ppermute x4, waiting for transfers between devices, flipped(): return lax.ppermute(value, ('core', 'x'), pairs)  17.1 us
    pallas_call x2, Pallas kernels, convolved(): call(functools.partial(energy_body, place_in, place_out), jax.ShapeDtypeS...  16.8 us
    all_to_all x2, starting transfers between devices, all_to_all(): return lax.all_to_all(value, axes, split_axis=0, concat_axis=0, tiled=True)  9.34 us
    ppermute x4, starting transfers between devices, flipped(): return lax.ppermute(value, ('core', 'x'), pairs)  8.99 us
  transfers between devices with their start and end apart: 27, of which 13 were waited for; matrix products, arithmetic and copies ran while one was open for 1% of the time, Pallas kernels for 14%

profile of v3, /device:TPU:70, one launch (start us, length us, event | category | flops | bytes accessed | tf_op | source)
XLA Modules:
  0.0 283.9 jit_solution(7081885069481256745)
XLA Ops:
  0.6 1.0 dynamic-slice_bitcast_fusion.1
  1.6 6.3 %collective-permute-start.6 = (bf16[256,512]{1,0:T(8,128)(2,1)S(1)}, bf16[256,512]{1,0:T(8,128)(2,1)S(1)}, u32[]{:S(2)}, u32[]{:S(2)}) collective-permute-start(bf16[256,512]{1,0:T(8,128)(2,1)S(1)} %dynamic-slice_bitcast_fusion.1), channel_id=1, source_target_pairs={{0,1},{1,2},{2,3},{3,4},{4,5},{5,6},{6,7},{7,8},{8,9},{9,10},{10,1... | collective-permute-start | bytes 786440 | tf_op jit(solution)/shard_map/ppermute | solution.py:26
  7.9 1.0 dynamic-slice_bitcast_fusion
  9.0 10.0 %collective-permute-done.6.mine_ref = bf16[256,512]{1,0:T(8,128)(2,1)S(1)} collective-permute-done((bf16[256,512]{1,0:T(8,128)(2,1)S(1)}, bf16[256,512]{1,0:T(8,128)(2,1)S(1)}, u32[]{:S(2)}, u32[]{:S(2)}) %collective-permute-start.6) | collective-permute-done | bytes 262176 | tf_op jit(solution)/shard_map/ppermute | solution.py:26
  19.0 0.7 collective-permute-start.10
  19.7 1.9 collective-permute-start.8
  21.7 0.7 pad_add_fusion.at_ref
  22.3 0.6 add_convert_fusion.edge_ref
  22.9 3.5 %shard_map.68 = (f32[512,512]{1,0:T(8,128)}, bf16[512,512]{1,0:T(8,128)(2,1)}) custom-call(f32[1]{0:T(128)} %bitcast.45, s32[2]{0:T(128)} %pad_add_fusion.at_ref, bf16[512,512]{1,0:T(8,128)(2,1)} %bitcast.34, bf16[512,512]{1,0:T(8,128)(2,1)} %bitcast.36), custom_call_target="tpu_custom_call" | custom-call | tf_op jit(solution)/shard_map/pallas_call | solution.py:320
  26.4 0.7 copy-done.17
  27.1 3.1 %shard_map.71 = (f32[512,512]{1,0:T(8,128)}, bf16[256,512]{1,0:T(8,128)(2,1)}, bf16[512,512]{1,0:T(8,128)(2,1)}, bf16[512,512]{1,0:T(8,128)(2,1)}) custom-call(s32[2]{0:T(128)} %pad_add_fusion.at_ref, f32[512,512]{1,0:T(8,128)} %get-tuple-element.42.own_ref, bf16[256,512]{1,0:T(8,128)(2,1)} %copy-done.16, bf16[256,512]{1,0:T(8,128)(2,1)} %copy-done.17), custom_call_target="tpu_custom_call" | custom-call | tf_op jit(solution)/shard_map/pallas_call | solution.py:323
  30.2 10.3 %collective-permute-start.12 = (bf16[256,512]{1,0:T(8,128)(2,1)}, bf16[256,512]{1,0:T(8,128)(2,1)S(1)}, u32[]{:S(2)}, u32[]{:S(2)}) collective-permute-start(bf16[256,512]{1,0:T(8,128)(2,1)} %get-tuple-element.44), channel_id=1, source_target_pairs={{0,1},{1,2},{2,3},{3,4},{4,5},{5,6},{6,7},{7,8},{8,9},{9,10},{10,1... | collective-permute-start | bytes 786440 | tf_op jit(solution)/shard_map/ppermute | solution.py:26
  40.5 1.9 collective-permute-start.11
  42.5 6.3 %collective-permute-done.12 = bf16[256,512]{1,0:T(8,128)(2,1)S(1)} collective-permute-done((bf16[256,512]{1,0:T(8,128)(2,1)}, bf16[256,512]{1,0:T(8,128)(2,1)S(1)}, u32[]{:S(2)}, u32[]{:S(2)}) %collective-permute-start.12) | collective-permute-done | bytes 262176 | tf_op jit(solution)/shard_map/ppermute | solution.py:26
  48.8 9.9 %collective-permute-done.11 = bf16[256,512]{1,0:T(8,128)(2,1)S(1)} collective-permute-done((bf16[256,512]{1,0:T(8,128)(2,1)}, bf16[256,512]{1,0:T(8,128)(2,1)S(1)}, u32[]{:S(2)}, u32[]{:S(2)}) %collective-permute-start.11) | collective-permute-done | bytes 262176 | tf_op jit(solution)/shard_map/ppermute | solution.py:26
  58.9 0.8 convert_convert_fusion.inverse_ref
  59.7 1.9 collective-permute-done.13.theirs_ref
  61.5 1.0 copy-done.4
  62.5 8.4 %shard_map.72 = (bf16[16,2,32,512]{3,2,1,0:T(8,128)(2,1)}, bf16[512,512]{1,0:T(8,128)(2,1)}, bf16[512,512]{1,0:T(8,128)(2,1)}) custom-call(f32[2]{0:T(128)} %energy_ref.1, f32[2]{0:T(128)} %convert_convert_fusion.inverse_ref, f32[2]{0:T(128)} %add_convert_fusion.edge_ref, s32[2]{0:T(128)} %pad_add_fusion.at_ref, bf16[512,512]{1,0:T(8,128)(2,1)} %bitcast.37, ...), custom_call_target="tpu_custom_call" | custom-call | tf_op jit(solution)/shard_map/pallas_call | solution.py:331
  70.9 23.0 %all_to_all.20 = bf16[16,2,32,512]{3,2,1,0:T(8,128)(2,1)} all-to-all(bf16[16,2,32,512]{3,2,1,0:T(8,128)(2,1)} %get-tuple-element.46), channel_id=1, replica_groups=mesh['zlo'=2,'y'=4,'core'=2,'row'=4,'x'=4] {'zlo','y','core'}, dimensions={0} | all-to-all | bytes 2097152 | tf_op jit(solution)/shard_map/all_to_all | solution.py:296
  94.0 8.5 %shard_map.73 = bf16[32,32,512]{2,1,0:T(8,128)(2,1)} custom-call(s32[8]{0:T(128)} %offset_ref.3, bf16[32,32,512]{2,1,0:T(8,128)(2,1)} %bitcast.32, bf16[32,512]{1,0:T(8,128)(2,1)} %bitcast.43), custom_call_target="tpu_custom_call" | custom-call | tf_op jit(solution)/shard_map/pallas_call | solution.py:287
  102.4 5.7 %all-to-all-start.1 = ((bf16[32,32,512]{2,1,0:T(8,128)(2,1)}), bf16[32,32,512]{2,1,0:T(8,128)(2,1)S(1)}, u32[]{:S(2)}, u32[]{:S(2)}) async-start(bf16[32,32,512]{2,1,0:T(8,128)(2,1)} %shard_map.73), calls=%async_computation.1 | async-start | bytes 2097152 | tf_op jit(solution)/shard_map/all_to_all | solution.py:296
  108.4 1.8 collective-permute-start.2
  110.2 21.7 %collective-permute-done.one_ref = bf16[512,512]{1,0:T(8,128)(2,1)S(1)} collective-permute-done((bf16[512,512]{1,0:T(8,128)(2,1)S(1)}, bf16[512,512]{1,0:T(8,128)(2,1)S(1)}, u32[]{:S(2)}, u32[]{:S(2)}) %collective-permute-start) | collective-permute-done | bytes 524320 | tf_op jit(solution)/shard_map/ppermute | solution.py:30
  131.9 2.4 collective-permute-start.1
  134.3 1.9 collective-permute-start.15
  136.3 2.3 collective-permute-start.16
  138.5 8.2 %collective-permute-done.1.two_ref = bf16[512,512]{1,0:T(8,128)(2,1)S(1)} collective-permute-done((bf16[512,512]{1,0:T(8,128)(2,1)S(1)}, bf16[512,512]{1,0:T(8,128)(2,1)S(1)}, u32[]{:S(2)}, u32[]{:S(2)}) %collective-permute-start.1) | collective-permute-done | bytes 524320 | tf_op jit(solution)/shard_map/ppermute | solution.py:30
  146.7 0.8 copy-done.9
  147.5 3.5 %shard_map.69 = (bf16[4,512,512]{2,1,0:T(8,128)(2,1)}, bf16[2,512,512]{2,1,0:T(8,128)(2,1)}, bf16[512,512]{1,0:T(8,128)(2,1)}) custom-call(s32[2]{0:T(128)} %pad_add_fusion.at_ref, bf16[512,512]{1,0:T(8,128)(2,1)} %get-tuple-element.32.here_ref, bf16[512,512]{1,0:T(8,128)(2,1)} %copy-done.6, bf16[512,512]{1,0:T(8,128)(2,1)} %copy-done.9, ...), custom_call_target="tpu_custom_call" | custom-call | tf_op jit(solution)/shard_map/pallas_call | solution.py:341
  151.0 0.5 collective-permute-start.5
  151.5 1.3 collective-permute-start.4
  152.8 3.6 %collective-permute-done.16.second_ref = bf16[512,512]{1,0:T(8,128)(2,1)} collective-permute-done((bf16[512,512]{1,0:T(8,128)(2,1)}, bf16[512,512]{1,0:T(8,128)(2,1)}, u32[]{:S(2)}, u32[]{:S(2)}) %collective-permute-start.16) | collective-permute-done | bytes 524320 | tf_op jit(solution)/shard_map/ppermute | solution.py:52
  156.4 2.3 shard_map.74
  158.7 3.2 %collective-permute-start.17 = (bf16[512,512]{1,0:T(8,128)(2,1)}, bf16[512,512]{1,0:T(8,128)(2,1)}, u32[]{:S(2)}, u32[]{:S(2)}) collective-permute-start(bf16[512,512]{1,0:T(8,128)(2,1)} %get-tuple-element.49.outer.green_ref), channel_id=1, source_target_pairs={{16,4},{20,8},{24,12},{4,16},{8,20},{12,24},{17,5},{21,9},{25,13},... | collective-permute-start | bytes 1572872 | tf_op jit(solution)/shard_map/ppermute | solution.py:47
  162.0 0.6 collective-permute-start.14
  162.7 0.6 dynamic_slice.16.energy_ref
  163.3 1.0 copy-done.3
  164.3 4.0 %shard_map.70 = (bf16[512,512]{1,0:T(8,128)(2,1)}, bf16[512,512]{1,0:T(8,128)(2,1)}, bf16[512,512]{1,0:T(8,128)(2,1)}, bf16[512,512]{1,0:T(8,128)(2,1)}, bf16[51...) custom-call(s32[2]{0:T(128)} %pad_add_fusion.at_ref, bf16[4,512,512]{2,1,0:T(8,128)(2,1)} %get-tuple-element.33.all_ref, ...), custom_call_target="tpu_custom_call" | custom-call | tf_op jit(solution)/shard_map/pallas_call | solution.py:346
  168.3 3.1 %collective-permute-done.17.beyond = bf16[512,512]{1,0:T(8,128)(2,1)} collective-permute-done((bf16[512,512]{1,0:T(8,128)(2,1)}, bf16[512,512]{1,0:T(8,128)(2,1)}, u32[]{:S(2)}, u32[]{:S(2)}) %collective-permute-start.17) | collective-permute-done | bytes 524320 | tf_op jit(solution)/shard_map/ppermute | solution.py:47
  171.4 6.7 %shard_map.75 = (f32[512,512]{1,0:T(8,128)}, f32[512,512]{1,0:T(8,128)}) custom-call(f32[1]{0:T(128)} %dynamic_slice.16.energy_ref, bf16[512,512]{1,0:T(8,128)(2,1)} %get-tuple-element.37.outer_ham, bf16[512,512]{1,0:T(8,128)(2,1)} %get-tuple-element.38.inner_ham, bf16[512,512]{1,0:T(8,128)(2,1)} %get-tuple-element.36.far, ...), custom_call_target="tpu_custom_call" | custom-call | tf_op jit(solution)/shard_map/pallas_call | solution.py:354
  178.2 0.8 copy-done.1
  179.0 3.5 %shard_map.77.inner = bf16[512,512]{1,0:T(8,128)(2,1)} custom-call(s32[2]{0:T(128)} %pad_add_fusion.at_ref, f32[512,512]{1,0:T(8,128)} %get-tuple-element.52.open_ref, bf16[4,8,32,512]{3,2,1,0:T(8,128)(2,1)} %bitcast.27, bf16[2,8,32,512]{3,2,1,0:T(8,128)(2,1)} %copy-done.1, bf16[512,512]{1,0:T(8,128)(2,1)} %get-tuple-element.50.inner.green_ref), custom_call_target="tpu_custom_call" | custom-call | tf_op jit(solution)/shard_map/pallas_call | solution.py:361
  182.4 0.9 collective-permute-start.19
  183.3 3.4 %shard_map.76.outer = bf16[512,512]{1,0:T(8,128)(2,1)} custom-call(s32[2]{0:T(128)} %pad_add_fusion.at_ref, f32[512,512]{1,0:T(8,128)} %get-tuple-element.51.open_ref, bf16[4,8,32,512]{3,2,1,0:T(8,128)(2,1)} %bitcast.28, bf16[2,8,32,512]{3,2,1,0:T(8,128)(2,1)} %copy-done.1, bf16[512,512]{1,0:T(8,128)(2,1)} %get-tuple-element.49.outer.green_ref), custom_call_target="tpu_custom_call" | custom-call | tf_op jit(solution)/shard_map/pallas_call | solution.py:361
  186.8 3.8 %collective-permute-start.20 = (bf16[512,512]{1,0:T(8,128)(2,1)}, bf16[512,512]{1,0:T(8,128)(2,1)S(1)}, u32[]{:S(2)}, u32[]{:S(2)}) collective-permute-start(bf16[512,512]{1,0:T(8,128)(2,1)} %shard_map.76.outer), channel_id=1, source_target_pairs={{16,4},{20,8},{24,12},{4,16},{8,20},{12,24},{17,5},{21,9},{25,13},... | collective-permute-start | bytes 1572872 | tf_op jit(solution)/shard_map/ppermute | solution.py:47
  190.6 0.8 copy-done.8
  191.4 7.0 %shard_map.78 = (f32[512,512]{1,0:T(8,128)}, bf16[512,512]{1,0:T(8,128)(2,1)}, bf16[8,32,512]{2,1,0:T(8,128)(2,1)}, bf16[8,32,512]{2,1,0:T(8,128)(2,1)}) custom-call(f32[1]{0:T(128)} %dynamic_slice.16.energy_ref, s32[2]{0:T(128)} %pad_add_fusion.at_ref, bf16[512,512]{1,0:T(8,128)(2,1)} %get-tuple-element.37.outer_ham, ...), custom_call_target="tpu_custom_call" | custom-call | tf_op jit(solution)/shard_map/pallas_call | solution.py:368
  198.4 0.8 copy-done.11
  199.2 4.1 %shard_map.79 = (bf16[512,512]{1,0:T(8,128)(2,1)}, bf16[8,32,512]{2,1,0:T(8,128)(2,1)}, bf16[8,32,512]{2,1,0:T(8,128)(2,1)}) custom-call(s32[2]{0:T(128)} %pad_add_fusion.at_ref, bf16[512,512]{1,0:T(8,128)(2,1)} %get-tuple-element.36.far, f32[512,512]{1,0:T(8,128)} %get-tuple-element.53.open_ref, bf16[512,512]{1,0:T(8,128)(2,1)} %shard_map.76.outer, ...), custom_call_target="tpu_custom_call" | custom-call | tf_op jit(solution)/shard_map/pallas_call | solution.py:372
  203.3 1.2 collective-permute-start.23
  204.6 1.3 collective-permute-done.23.got_outer
  206.9 2.3 shard_map.82
  209.2 37.3 %all_to_all.21.green_ref = bf16[32,32,512]{2,1,0:T(8,128)(2,1)} all-to-all(bf16[32,32,512]{2,1,0:T(8,128)(2,1)} %bitcast.31), channel_id=1, replica_groups=mesh['zlo'=2,'y'=4,'core'=2,'row'=4,'x'=4] {'x','zlo','y'}, dimensions={0} | all-to-all | bytes 2097152 | tf_op jit(solution)/shard_map/all_to_all | solution.py:296
  246.5 8.4 %shard_map.83 = bf16[32,32,512]{2,1,0:T(8,128)(2,1)} custom-call(s32[8]{0:T(128)} %offset_ref.3, bf16[32,32,512]{2,1,0:T(8,128)(2,1)} %all_to_all.21.green_ref, bf16[32,512]{1,0:T(8,128)(2,1)} %bitcast.44), custom_call_target="tpu_custom_call" | custom-call | tf_op jit(solution)/shard_map/pallas_call | solution.py:287
  254.8 3.7 %all-to-all-start.3 = ((bf16[16,2,32,512]{3,2,1,0:T(8,128)(2,1)}), bf16[16,2,32,512]{3,2,1,0:T(8,128)(2,1)S(1)}, u32[]{:S(2)}, u32[]{:S(2)}) async-start(bf16[16,2,32,512]{3,2,1,0:T(8,128)(2,1)} %bitcast.30), calls=%async_computation.3 | async-start | bytes 2097152 | tf_op jit(solution)/shard_map/all_to_all | solution.py:296
  258.5 2.3 shard_map.80
  260.7 3.2 %collective-permute-start.21 = (bf16[512,512]{1,0:T(8,128)(2,1)}, bf16[512,512]{1,0:T(8,128)(2,1)S(1)}, u32[]{:S(2)}, u32[]{:S(2)}) collective-permute-start(bf16[512,512]{1,0:T(8,128)(2,1)} %get-tuple-element.56), channel_id=1, source_target_pairs={{0,0},{1,1},{2,16},{3,17},{16,2},{17,3},{18,18},{19,19},{4,4},{5,5... | collective-permute-start | bytes 1572872 | tf_op jit(solution)/shard_map/ppermute | solution.py:52
  264.0 1.6 collective-permute-start.22
  265.6 13.0 %collective-permute-done.21.first_ref = bf16[512,512]{1,0:T(8,128)(2,1)S(1)} collective-permute-done((bf16[512,512]{1,0:T(8,128)(2,1)}, bf16[512,512]{1,0:T(8,128)(2,1)S(1)}, u32[]{:S(2)}, u32[]{:S(2)}) %collective-permute-start.21) | collective-permute-done | bytes 524320 | tf_op jit(solution)/shard_map/ppermute | solution.py:52
  278.5 0.6 collective-permute-done.22.second_ref
  279.3 0.8 copy-done.13
  280.1 2.7 shard_map.81
  282.8 1.0 copy.7
  (61 shorter events, 2.4 us)
Async XLA Ops:
  1.6 17.4 %collective-permute-start.6 = (bf16[256,512]{1,0:T(8,128)(2,1)S(1)}, bf16[256,512]{1,0:T(8,128)(2,1)S(1)}, u32[]{:S(2)}, u32[]{:S(2)}) collective-permute-start(bf16[256,512]{1,0:T(8,128)(2,1)S(1)} %dynamic-slice_bitcast_fusion.1), channel_id=1, source_target_pairs={{0,1},{1,2},{2,3},{3,4},{4,5},{5,6},{6,7},{7,8},{8,9},{9,10},{10,1... | collective-permute-start | bytes 786440 | tf_op jit(solution)/shard_map/ppermute | solution.py:26
  8.9 10.1 %collective-permute-start.9 = (bf16[256,512]{1,0:T(8,128)(2,1)S(1)}, bf16[256,512]{1,0:T(8,128)(2,1)S(1)}, u32[]{:S(2)}, u32[]{:S(2)}) collective-permute-start(bf16[256,512]{1,0:T(8,128)(2,1)S(1)} %dynamic-slice_bitcast_fusion), channel_id=1, source_target_pairs={{0,1},{1,2},{2,3},{3,0},{4,5},{5,6},{6,7},{7,4},{8,9},{9,10},{10,1... | collective-permute-start | bytes 786440 | tf_op jit(solution)/shard_map/ppermute | solution.py:30
  19.0 7.4 %copy-start.16 = (bf16[256,512]{1,0:T(8,128)(2,1)}, bf16[256,512]{1,0:T(8,128)(2,1)S(1)}, u32[]{:S(2)}) copy-start(bf16[256,512]{1,0:T(8,128)(2,1)S(1)} %collective-permute-done.6.mine_ref) | copy-start | bytes 786436
  19.0 7.4 %collective-permute-start.7 = (bf16[256,512]{1,0:T(8,128)(2,1)S(1)}, bf16[256,512]{1,0:T(8,128)(2,1)S(1)}, u32[]{:S(2)}, u32[]{:S(2)}) collective-permute-start(bf16[256,512]{1,0:T(8,128)(2,1)S(1)} %collective-permute-done.6.mine_ref), channel_id=1, source_target_pairs={{0,16},{16,0},{1,17},{17,1},{2,18},{18,2},{3,19},{19,3},{4,20},{20... | collective-permute-start | bytes 786440 | tf_op jit(solution)/shard_map/ppermute | solution.py:39
  19.0 23.4 %collective-permute-start.10 = (bf16[256,512]{1,0:T(8,128)(2,1)S(1)}, bf16[256,512]{1,0:T(8,128)(2,1)S(1)}, u32[]{:S(2)}, u32[]{:S(2)}) collective-permute-start(bf16[256,512]{1,0:T(8,128)(2,1)S(1)} %collective-permute-done.9), channel_id=1, source_target_pairs={{0,4},{4,8},{8,12},{16,20},{20,24},{24,28},{32,36},{36,40},{40,44}... | collective-permute-start | bytes 786440 | tf_op jit(solution)/shard_map/ppermute | solution.py:35
  19.7 22.7 %collective-permute-start.8 = (bf16[256,512]{1,0:T(8,128)(2,1)S(1)}, bf16[256,512]{1,0:T(8,128)(2,1)S(1)}, u32[]{:S(2)}, u32[]{:S(2)}) collective-permute-start(bf16[256,512]{1,0:T(8,128)(2,1)S(1)} %dynamic-slice_bitcast_fusion), channel_id=1, source_target_pairs={{1,0},{2,1},{3,2},{4,3},{5,4},{6,5},{7,6},{8,7},{9,8},{10,9},{11,1... | collective-permute-start | bytes 786440 | tf_op jit(solution)/shard_map/ppermute | solution.py:26
  26.4 0.7 copy-start.17
  27.1 31.8 %copy-start.18 = (f32[2]{0:T(128)S(1)}, f32[2]{0:T(128)}, u32[]{:S(2)}) copy-start(f32[2]{0:T(128)} %energy_ref.1) | copy-start | bytes 28
  30.2 18.6 %collective-permute-start.12 = (bf16[256,512]{1,0:T(8,128)(2,1)}, bf16[256,512]{1,0:T(8,128)(2,1)S(1)}, u32[]{:S(2)}, u32[]{:S(2)}) collective-permute-start(bf16[256,512]{1,0:T(8,128)(2,1)} %get-tuple-element.44), channel_id=1, source_target_pairs={{0,1},{1,2},{2,3},{3,4},{4,5},{5,6},{6,7},{7,8},{8,9},{9,10},{10,1... | collective-permute-start | bytes 786440 | tf_op jit(solution)/shard_map/ppermute | solution.py:26
  40.5 18.2 %collective-permute-start.11 = (bf16[256,512]{1,0:T(8,128)(2,1)}, bf16[256,512]{1,0:T(8,128)(2,1)S(1)}, u32[]{:S(2)}, u32[]{:S(2)}) collective-permute-start(bf16[256,512]{1,0:T(8,128)(2,1)} %get-tuple-element.44), channel_id=1, source_target_pairs={{1,0},{2,1},{3,2},{4,3},{5,4},{6,5},{7,6},{8,7},{9,8},{10,9},{11,1... | collective-permute-start | bytes 786440 | tf_op jit(solution)/shard_map/ppermute | solution.py:26
  58.8 2.8 copy-start.2
  58.8 2.7 collective-permute-start.13
  61.5 1.0 copy-start.4
  94.0 14.2 %copy-start.5 = (bf16[512,512]{1,0:T(8,128)(2,1)S(1)}, bf16[512,512]{1,0:T(8,128)(2,1)}, u32[]{:S(2)}) copy-start(bf16[512,512]{1,0:T(8,128)(2,1)} %get-tuple-element.32.here_ref) | copy-start | bytes 1572868
  102.4 48.6 %copy-start.19 = (f32[2]{0:T(128)S(1)}, f32[2]{0:T(128)}, u32[]{:S(2)}) copy-start(f32[2]{0:T(128)} %energy_ref.1) | copy-start | bytes 28
  102.4 59.5 %all-to-all-start.1 = ((bf16[32,32,512]{2,1,0:T(8,128)(2,1)}), bf16[32,32,512]{2,1,0:T(8,128)(2,1)S(1)}, u32[]{:S(2)}, u32[]{:S(2)}) async-start(bf16[32,32,512]{2,1,0:T(8,128)(2,1)} %shard_map.73), calls=%async_computation.1 | async-start | bytes 2097152 | tf_op jit(solution)/shard_map/all_to_all | solution.py:296
  108.1 23.8 %collective-permute-start = (bf16[512,512]{1,0:T(8,128)(2,1)S(1)}, bf16[512,512]{1,0:T(8,128)(2,1)S(1)}, u32[]{:S(2)}, u32[]{:S(2)}) collective-permute-start(bf16[512,512]{1,0:T(8,128)(2,1)S(1)} %copy-done.5), channel_id=1, source_target_pairs={{0,1},{1,2},{2,3},{3,0},{4,5},{5,6},{6,7},{7,4},{8,9},{9,10},{10,1... | collective-permute-start | bytes 1572872 | tf_op jit(solution)/shard_map/ppermute | solution.py:30
  108.4 30.1 %collective-permute-start.2 = (bf16[512,512]{1,0:T(8,128)(2,1)S(1)}, bf16[512,512]{1,0:T(8,128)(2,1)S(1)}, u32[]{:S(2)}, u32[]{:S(2)}) collective-permute-start(bf16[512,512]{1,0:T(8,128)(2,1)S(1)} %copy-done.5), channel_id=1, source_target_pairs={{0,3},{1,0},{2,1},{3,2},{4,7},{5,4},{6,5},{7,6},{8,11},{9,8},{10,9... | collective-permute-start | bytes 1572872 | tf_op jit(solution)/shard_map/ppermute | solution.py:30
  131.9 14.8 %copy-start.6 = (bf16[512,512]{1,0:T(8,128)(2,1)}, bf16[512,512]{1,0:T(8,128)(2,1)S(1)}, u32[]{:S(2)}) copy-start(bf16[512,512]{1,0:T(8,128)(2,1)S(1)} %collective-permute-done.one_ref) | copy-start | bytes 1572868
  131.9 14.8 %collective-permute-start.1 = (bf16[512,512]{1,0:T(8,128)(2,1)S(1)}, bf16[512,512]{1,0:T(8,128)(2,1)S(1)}, u32[]{:S(2)}, u32[]{:S(2)}) collective-permute-start(bf16[512,512]{1,0:T(8,128)(2,1)S(1)} %collective-permute-done.one_ref), channel_id=1, source_target_pairs={{0,1},{1,2},{2,3},{3,0},{4,5},{5,6},{6,7},{7,4},{8,9},{9,10},{10,1... | collective-permute-start | bytes 1572872 | tf_op jit(solution)/shard_map/ppermute | solution.py:30
  134.3 18.5 %collective-permute-start.15 = (bf16[512,512]{1,0:T(8,128)(2,1)}, bf16[512,512]{1,0:T(8,128)(2,1)S(1)}, u32[]{:S(2)}, u32[]{:S(2)}) collective-permute-start(bf16[512,512]{1,0:T(8,128)(2,1)} %get-tuple-element.47), channel_id=1, source_target_pairs={{0,0},{1,1},{2,16},{3,17},{16,2},{17,3},{18,18},{19,19},{4,4},{5,5... | collective-permute-start | bytes 1572872 | tf_op jit(solution)/shard_map/ppermute | solution.py:52
  136.3 20.1 %collective-permute-start.16 = (bf16[512,512]{1,0:T(8,128)(2,1)}, bf16[512,512]{1,0:T(8,128)(2,1)}, u32[]{:S(2)}, u32[]{:S(2)}) collective-permute-start(bf16[512,512]{1,0:T(8,128)(2,1)} %get-tuple-element.48), channel_id=1, source_target_pairs={{0,1},{1,0},{2,17},{3,16},{16,3},{17,2},{18,19},{19,18},{4,5},{5,4... | collective-permute-start | bytes 1572872 | tf_op jit(solution)/shard_map/ppermute | solution.py:52
  138.5 8.2 %copy-start.7 = (bf16[512,512]{1,0:T(8,128)(2,1)}, bf16[512,512]{1,0:T(8,128)(2,1)S(1)}, u32[]{:S(2)}) copy-start(bf16[512,512]{1,0:T(8,128)(2,1)S(1)} %collective-permute-done.2.three_ref) | copy-start | bytes 1572868
  146.7 0.8 copy-start.9
  151.0 12.3 %collective-permute-start.3 = (bf16[2,512,512]{2,1,0:T(8,128)(2,1)}, bf16[2,512,512]{2,1,0:T(8,128)(2,1)S(1)}, u32[]{:S(2)}, u32[]{:S(2)}) collective-permute-start(bf16[2,512,512]{2,1,0:T(8,128)(2,1)} %get-tuple-element.34), channel_id=1, source_target_pairs={{0,16},{16,0},{1,17},{17,1},{2,18},{18,2},{3,19},{19,3},{4,20},{20... | collective-permute-start | bytes 3145736 | tf_op jit(solution)/shard_map/ppermute | solution.py:39
  151.0 11.0 %collective-permute-start.5 = (f32[2]{0:T(128)S(1)}, f32[2]{0:T(128)S(1)}, u32[]{:S(2)}, u32[]{:S(2)}) collective-permute-start(f32[2]{0:T(128)S(1)} %copy-done.19), channel_id=1, source_target_pairs={{0,16},{16,0},{1,17},{17,1},{2,18},{18,2},{3,19},{19,3},{4,20},{20... | collective-permute-start | bytes 32 | tf_op jit(solution)/shard_map/ppermute | solution.py:39
  151.5 11.8 %collective-permute-start.4 = (bf16[512,512]{1,0:T(8,128)(2,1)}, bf16[512,512]{1,0:T(8,128)(2,1)}, u32[]{:S(2)}, u32[]{:S(2)}) collective-permute-start(bf16[512,512]{1,0:T(8,128)(2,1)} %get-tuple-element.35), channel_id=1, source_target_pairs={{16,4},{20,8},{24,12},{17,5},{21,9},{25,13},{18,6},{22,10},{26,14}... | collective-permute-start | bytes 1572872 | tf_op jit(solution)/shard_map/ppermute | solution.py:47
  152.8 3.6 %copy-start.10 = (bf16[512,512]{1,0:T(8,128)(2,1)}, bf16[512,512]{1,0:T(8,128)(2,1)S(1)}, u32[]{:S(2)}) copy-start(bf16[512,512]{1,0:T(8,128)(2,1)S(1)} %collective-permute-done.15.first_ref) | copy-start | bytes 1572868
  158.7 12.8 %collective-permute-start.17 = (bf16[512,512]{1,0:T(8,128)(2,1)}, bf16[512,512]{1,0:T(8,128)(2,1)}, u32[]{:S(2)}, u32[]{:S(2)}) collective-permute-start(bf16[512,512]{1,0:T(8,128)(2,1)} %get-tuple-element.49.outer.green_ref), channel_id=1, source_target_pairs={{16,4},{20,8},{24,12},{4,16},{8,20},{12,24},{17,5},{21,9},{25,13},... | collective-permute-start | bytes 1572872 | tf_op jit(solution)/shard_map/ppermute | solution.py:47
  161.8 9.6 %collective-permute-start.18 = (bf16[512,512]{1,0:T(8,128)(2,1)}, bf16[512,512]{1,0:T(8,128)(2,1)}, u32[]{:S(2)}, u32[]{:S(2)}) collective-permute-start(bf16[512,512]{1,0:T(8,128)(2,1)} %get-tuple-element.50.inner.green_ref), channel_id=1, source_target_pairs={{0,16},{16,0},{1,17},{17,1},{2,18},{18,2},{3,19},{19,3},{4,20},{20... | collective-permute-start | bytes 1572872 | tf_op jit(solution)/shard_map/ppermute | solution.py:39
  162.0 6.4 %copy-start = (bf16[32,32,512]{2,1,0:T(8,128)(2,1)}, bf16[32,32,512]{2,1,0:T(8,128)(2,1)S(1)}, u32[]{:S(2)}) copy-start(bf16[32,32,512]{2,1,0:T(8,128)(2,1)S(1)} %all-to-all-done.1) | copy-start | bytes 3145732
  162.0 16.1 %collective-permute-start.14 = (bf16[2,8,32,512]{3,2,1,0:T(8,128)(2,1)S(1)}, bf16[2,8,32,512]{3,2,1,0:T(8,128)(2,1)S(1)}, u32[]{:S(2)}, u32[]{:S(2)}) collective-permute-start(bf16[2,8,32,512]{3,2,1,0:T(8,128)(2,1)S(1)} %constant_dynamic-slice_fusion), channel_id=1, source_target_pairs={{0,16},{16,0},{1,17},{17,1},{2,18},{18,2},{3,19},{19,3},{4,20},{20... | collective-permute-start | bytes 1572872 | tf_op jit(solution)/shard_map/ppermute | solution.py:39
  163.3 1.0 copy-start.3
  178.2 0.8 copy-start.1
  182.4 8.2 %collective-permute-start.19 = (bf16[512,512]{1,0:T(8,128)(2,1)}, bf16[512,512]{1,0:T(8,128)(2,1)S(1)}, u32[]{:S(2)}, u32[]{:S(2)}) collective-permute-start(bf16[512,512]{1,0:T(8,128)(2,1)} %shard_map.77.inner), channel_id=1, source_target_pairs={{0,16},{16,0},{1,17},{17,1},{2,18},{18,2},{3,19},{19,3},{4,20},{20... | collective-permute-start | bytes 1572872 | tf_op jit(solution)/shard_map/ppermute | solution.py:39
  186.8 11.6 %collective-permute-start.20 = (bf16[512,512]{1,0:T(8,128)(2,1)}, bf16[512,512]{1,0:T(8,128)(2,1)S(1)}, u32[]{:S(2)}, u32[]{:S(2)}) collective-permute-start(bf16[512,512]{1,0:T(8,128)(2,1)} %shard_map.76.outer), channel_id=1, source_target_pairs={{16,4},{20,8},{24,12},{4,16},{8,20},{12,24},{17,5},{21,9},{25,13},... | collective-permute-start | bytes 1572872 | tf_op jit(solution)/shard_map/ppermute | solution.py:47
  190.6 0.8 copy-start.8
  198.4 6.1 %copy-start.20 = (bf16[8,32,512]{2,1,0:T(8,128)(2,1)S(1)}, bf16[8,32,512]{2,1,0:T(8,128)(2,1)}, u32[]{:S(2)}) copy-start(bf16[8,32,512]{2,1,0:T(8,128)(2,1)} %get-tuple-element.61) | copy-start | bytes 786436
  198.4 0.8 copy-start.11
  203.3 2.6 collective-permute-start.23
  204.5 1.7 collective-permute-start.24
  205.9 0.7 copy-start.14
  206.2 0.7 copy-start.15
  254.8 28.0 %all-to-all-start.3 = ((bf16[16,2,32,512]{3,2,1,0:T(8,128)(2,1)}), bf16[16,2,32,512]{3,2,1,0:T(8,128)(2,1)S(1)}, u32[]{:S(2)}, u32[]{:S(2)}) async-start(bf16[16,2,32,512]{3,2,1,0:T(8,128)(2,1)} %bitcast.30), calls=%async_computation.3 | async-start | bytes 2097152 | tf_op jit(solution)/shard_map/all_to_all | solution.py:296
  260.7 17.8 %collective-permute-start.21 = (bf16[512,512]{1,0:T(8,128)(2,1)}, bf16[512,512]{1,0:T(8,128)(2,1)S(1)}, u32[]{:S(2)}, u32[]{:S(2)}) collective-permute-start(bf16[512,512]{1,0:T(8,128)(2,1)} %get-tuple-element.56), channel_id=1, source_target_pairs={{0,0},{1,1},{2,16},{3,17},{16,2},{17,3},{18,18},{19,19},{4,4},{5,5... | collective-permute-start | bytes 1572872 | tf_op jit(solution)/shard_map/ppermute | solution.py:52
  264.0 15.1 %collective-permute-start.22 = (bf16[512,512]{1,0:T(8,128)(2,1)}, bf16[512,512]{1,0:T(8,128)(2,1)S(1)}, u32[]{:S(2)}, u32[]{:S(2)}) collective-permute-start(bf16[512,512]{1,0:T(8,128)(2,1)} %get-tuple-element.57), channel_id=1, source_target_pairs={{0,1},{1,0},{2,17},{3,16},{16,3},{17,2},{18,19},{19,18},{4,5},{5,4... | collective-permute-start | bytes 1572872 | tf_op jit(solution)/shard_map/ppermute | solution.py:52
  278.5 0.8 copy-start.12
  279.3 0.8 copy-start.13

commit v4 on v3

--- a/solution.py
+++ b/solution.py
@@ -28,11 +28,6 @@
 
 def row_ring(value, steps):
     return lax.ppermute(value, "x", [(s, (s + steps) % WIDTH) for s in range(WIDTH)])
-
-
-def row_climb(value):
-    count = lax.axis_size(SLAB)
-    return lax.ppermute(value, SLAB, [(s, s + WIDTH) for s in range(0, count - WIDTH, WIDTH)])
 
 
 def swapped(value):
@@ -120,14 +115,15 @@
 
 
 def second_body(
-    energy_ref, inverse_ref, edge_ref, at_ref, ham_ref, pair_ref, mine_ref, theirs_ref, c_ref, lower_turned_ref,
-    out_ref, first_ref, second_ref, whole,
+    energy_ref, inverse_ref, edge_ref, at_ref, ham_ref, pair_ref, c_ref, lower_turned_ref, *refs
 ):
+    mine_refs, theirs_refs = refs[:4], refs[4:8]
+    out_ref, first_ref, second_ref, whole = refs[8:]
     n = c_ref.shape[0]
     eye, rotate = tables(n)
     chunks = out_ref.shape[0]
     for i in range(4):
-        place_halves(at_ref[0], whole.at[i], mine_ref[i], theirs_ref[i])
+        place_halves(at_ref[0], whole.at[i], mine_refs[i][...], theirs_refs[i][...])
     odd = lax.rem(at_ref[1], 2)
     for e, same_ref in ((odd, first_ref), (1 - odd, second_ref)):
         energy, inverse = energy_ref[e], inverse_ref[e]
@@ -169,6 +165,11 @@
         near[...] = all_ref[1].T
 
 
+def row_energy(at_ref, energy_ref, pair_ref):
+    core, x = at_ref[0], at_ref[1]
+    return jnp.where(x // 2 == core, energy_ref[lax.rem(x, 2)], pair_ref[lax.rem(x, 2)])
+
+
 def role_body(at_ref, first_ref, second_ref, outer_ref, inner_ref):
     match = lax.rem(at_ref[1], 2) == at_ref[0]
     outer_ref[...] = jnp.where(match, first_ref[...], second_ref[...])
@@ -176,10 +177,10 @@
 
 
 def open_body(
-    energy_ref, outer_ham, inner_ham, far, mid, mid_turned, near, outer, inner, beyond, beside, open_outer, open_inner,
+    at_ref, energy_ref, energy_pair_ref, outer_ham, inner_ham, far, mid, mid_turned, near, outer, inner, beyond, beside, open_outer, open_inner,
 ):
     eye, rotate = tables(outer.shape[0])
-    base = energy_ref[0] * eye + BROAD * rotate
+    base = row_energy(at_ref, energy_ref, energy_pair_ref) * eye + BROAD * rotate
     open_outer[...] = (
         base - outer_ham[...].astype(jnp.float32) - linked(inner[...], mid[...]) - linked(beyond[...], far[...])
     )
@@ -210,12 +211,12 @@
 
 
 def inner_body(
-    energy_ref, at_ref, outer_ham, inner_ham, mid, mid_turned, near, mine_ref, theirs_ref, outer, inner, beside,
+    at_ref, energy_ref, energy_pair_ref, outer_ham, inner_ham, mid, mid_turned, near, mine_ref, theirs_ref, outer, inner, beside,
     open_outer, whole_ref, keep_ref, give_ref, scratch,
 ):
     core = at_ref[0]
     eye, rotate = tables(outer.shape[0])
-    base = energy_ref[0] * eye + BROAD * rotate
+    base = row_energy(at_ref, energy_ref, energy_pair_ref) * eye + BROAD * rotate
     self_part = joined_rows(core, 1 - core, mine_ref, theirs_ref, scratch)
     matrix = (
         base - inner_ham[...].astype(jnp.float32) - self_part - linked(outer[...], mid_turned[...])
@@ -228,20 +229,20 @@
     open_outer[...] = base - outer_ham[...].astype(jnp.float32) - self_part - linked(inner[...], mid[...])
 
 
-def outer_body(at_ref, far, open_ref, outer, beyond, whole_ref, keep_ref, give_ref, scratch):
+def outer_body(
+    at_ref, far, open_ref, outer, beyond, keep_inner, got_inner, whole_ref, out_ref, give_ref, scratch
+):
+    core = at_ref[0]
     eye, _ = tables(outer.shape[0])
     matrix = (open_ref[...] - linked(beyond[...], far[...])).astype(jnp.bfloat16)
     result = finish(matrix, outer[...], eye).astype(jnp.bfloat16)
     whole_ref[...] = result
-    split_rows(at_ref[0], result, keep_ref, give_ref, scratch)
-
-
-def join_body(at_ref, keep_outer, keep_inner, got_outer, got_inner, out_ref):
-    first = at_ref[0] == 0
-    out_ref[0] = jnp.where(first, keep_outer[...], got_outer[...])
-    out_ref[1] = jnp.where(first, keep_inner[...], got_inner[...])
-    out_ref[2] = jnp.where(first, got_inner[...], keep_inner[...])
-    out_ref[3] = jnp.where(first, got_outer[...], keep_outer[...])
+    scratch[...] = result.reshape(scratch.shape)
+    give_ref[...] = scratch[:, 1 - core]
+    out_ref[3 * core] = scratch[:, core]
+    out_ref[1 + core] = keep_inner[...]
+    out_ref[2 - core] = got_inner[...]
+    out_ref[3 - 3 * core] = got_inner[...]
 
 
 def spread_body(at_ref, first_ref, second_ref, out_ref):
@@ -312,76 +313,79 @@
     natural = list(range(count))
     by_chip = [(e % WIDTH) * (count // WIDTH) + e // WIDTH for e in range(count)]
 
+    def run(body, out_shape, in_specs, *operands, scratch=()):
+        return call(body, out_shape, in_specs, scratch)(*operands)
+
     lower_mine = passed_along(half(c), 1)
     ham_half = half(ham)
-    ham_ring = row_ring(ham_half, 1)
     ham_up = passed_along(ham_half, -1)
+    ham_down = passed_along(ham_half, 1)
     energy_pair = swapped(energies)
-    own, load = call(own_body, (wide(n, n), thin(n, n)), [SM, SM, VM, VM])(edge[:1], at, c, ham)
+    own, load = run(own_body, (wide(n, n), thin(n, n)), [SM, SM, VM, VM], edge[:1], at, c, ham)
     lower_theirs = swapped(lower_mine)
-    ham_climb = row_climb(ham_ring)
-    pair, pair_half, _, lower_turned = call(
-        pair_body, (wide(n, n), thin(n // 2, n), thin(n, n), thin(n, n)), [SM, VM, VM, VM]
-    )(at, own, lower_mine, lower_theirs)
-    pair_up = passed_along(pair_half, -1)
-    pair_down = passed_along(pair_half, 1)
-    mine = jnp.stack([ham_up, jnp.where(x == 0, ham_climb, ham_ring), pair_up, pair_down])
-    theirs = swapped(mine)
     one, three = row_ring(load, 1), row_ring(load, -1)
-    chunks, first, second = call(
-        second_body,
-        (thin(parts, 2, rows, n), thin(n, n), thin(n, n)),
-        [SM] * 4 + [VM] * 6,
-        [pltpu.VMEM((4, n, n), jnp.bfloat16)],
-    )(energies, inverse, edge, at, ham, pair, mine, theirs, c, lower_turned)
+    pair, pair_half, _, lower_turned = run(
+        pair_body, (wide(n, n), thin(n // 2, n), thin(n, n), thin(n, n)), [SM, VM, VM, VM],
+        at, own, lower_mine, lower_theirs,
+    )
+    pair_up, pair_down = passed_along(pair_half, -1), passed_along(pair_half, 1)
+    two = row_ring(one, 1)
+    mine = [ham_up, ham_down, pair_up, pair_down]
+    theirs = [swapped(v) for v in mine[:2]] + [swapped(v) for v in mine[2:]]
+    chunks, first, second = run(
+        second_body, (thin(parts, 2, rows, n), thin(n, n), thin(n, n)), [SM] * 4 + [VM] * 12,
+        energies, inverse, edge, at, ham, pair, c, lower_turned, *mine, *theirs,
+        scratch=[pltpu.VMEM((4, n, n), jnp.bfloat16)],
+    )
     first, second = flipped(first, 0), flipped(second, 1)
-    two = row_ring(one, 1)
     received = all_to_all(chunks, ENERGY)
 
-    everything, give, last = call(gather_body, (thin(WIDTH, n, n), thin(2, n, n), thin(n, n)), [SM] + [VM] * 4)(
-        at, load, one, two, three
-    )
+    everything, give, last = run(
+        gather_body, (thin(WIDTH, n, n), thin(2, n, n), thin(n, n)), [SM] + [VM] * 4,
+        at, load, one, two, three,
+    )
+    below_c = row_above(last, False)
     got = swapped(give)
-    below_c = row_above(last, False)
-    outer_ham, inner_ham, far, mid, mid_turned, near = call(link_body, (thin(n, n),) * 6, [SM] + [VM] * 3)(
-        at, everything, got, below_c
-    )
-    fours = jnp.where(core == 0, jnp.concatenate([energies, energy_pair]), jnp.concatenate([energy_pair, energies]))
-    energy = lax.dynamic_slice_in_dim(fours, x, 1)
-    outer, inner = call(role_body, (thin(n, n),) * 2, [SM, VM, VM])(at, first, second)
+    outer_ham, inner_ham, far, mid, mid_turned, near = run(
+        link_body, (thin(n, n),) * 6, [SM] + [VM] * 3, at, everything, got, below_c
+    )
+    outer, inner = run(role_body, (thin(n, n),) * 2, [SM, VM, VM], at, first, second)
     beyond = row_above(outer, True)
     beside = swapped(inner)
-    open_outer, open_inner = call(open_body, (wide(n, n),) * 2, [SM] + [VM] * 10)(
-        energy, outer_ham, inner_ham, far, mid, mid_turned, near, outer, inner, beyond, beside
+    open_outer, open_inner = run(
+        open_body, (wide(n, n),) * 2, [SM] * 3 + [VM] * 10,
+        at, energies, energy_pair, outer_ham, inner_ham, far, mid, mid_turned, near, outer, inner, beyond, beside,
     )
     result = convolved(received.reshape(count, rows, n), strength, offsets, natural, by_chip)
     self_mine = all_to_all(result, ("x", "zlo", "y")).reshape(WIDTH, pairs, rows, n)
     self_theirs = swapped(lax.dynamic_slice_in_dim(self_mine, 2 * (1 - core), 2, 0))
     mix = [pltpu.VMEM((pairs, 2, rows, n), jnp.bfloat16)]
-    third = lambda role, opened, green: call(
-        functools.partial(third_body, role), thin(n, n), [SM] + [VM] * 4, mix
-    )(at, opened, self_mine, self_theirs, green)
+    third = lambda role, opened, green: run(
+        functools.partial(third_body, role), thin(n, n), [SM] + [VM] * 4,
+        at, opened, self_mine, self_theirs, green, scratch=mix,
+    )
     outer = third(False, open_outer, outer)
     beyond = row_above(outer, True)
     inner = third(True, open_inner, inner)
     beside = swapped(inner)
-    open_outer, whole_inner, keep_inner, give_inner = call(
-        inner_body, (wide(n, n), thin(n, n), thin(pairs, rows, n), thin(pairs, rows, n)), [SM] * 2 + [VM] * 10, mix
-    )(energy, at, outer_ham, inner_ham, mid, mid_turned, near, self_mine, self_theirs, outer, inner, beside)
+    open_outer, whole_inner, keep_inner, give_inner = run(
+        inner_body, (wide(n, n), thin(n, n), thin(pairs, rows, n), thin(pairs, rows, n)),
+        [SM] * 3 + [VM] * 10, at, energies, energy_pair, outer_ham, inner_ham, mid, mid_turned, near, self_mine,
+        self_theirs, outer, inner, beside, scratch=mix,
+    )
     got_inner = swapped(give_inner)
-    whole_outer, keep_outer, give_outer = call(
-        outer_body, (thin(n, n), thin(pairs, rows, n), thin(pairs, rows, n)), [SM] + [VM] * 4, mix
-    )(at, far, open_outer, outer, beyond)
+    whole_outer, chunks, give_outer = run(
+        outer_body, (thin(n, n), thin(WIDTH, pairs, rows, n), thin(pairs, rows, n)), [SM] + [VM] * 6,
+        at, far, open_outer, outer, beyond, keep_inner, got_inner, scratch=mix,
+    )
     got_outer = swapped(give_outer)
-    chunks = call(join_body, thin(WIDTH, pairs, rows, n), [SM] + [VM] * 4)(
-        at, keep_outer, keep_inner, got_outer, got_inner
-    )
+    chunks = lax.dynamic_update_slice_in_dim(chunks, got_outer[None], 3 - 3 * core, 0)
     received = all_to_all(chunks.reshape(count, rows, n), ("x", "zlo", "y"))
-    first, second = call(role_body, (thin(n, n),) * 2, [SM, VM, VM])(at, whole_outer, whole_inner)
+    first, second = run(role_body, (thin(n, n),) * 2, [SM, VM, VM], at, whole_outer, whole_inner)
     first, second = flipped(first, 0), flipped(second, 1)
     result = convolved(received, strength, offsets, by_chip, natural)
     self_part = all_to_all(result.reshape(parts, 2, rows, n), ENERGY)
-    green = call(spread_body, wide(2, n, n), [SM, VM, VM])(at, first, second)
+    green = run(spread_body, wide(2, n, n), [SM, VM, VM], at, first, second)
     self_part = jnp.swapaxes(self_part, 0, 1).reshape(2, n, n)
     return (green[:, None], self_part[:, None])
 

time: 287 us -> 284 us (0.990)
  starting transfers between devices: 55.7 us -> 75.7 us
  blocking collectives: 60.3 us -> 47 us
  waiting for transfers between devices: 79.9 us -> 73.3 us
  Pallas kernels: 73.5 us -> 70.3 us
    ppermute x9 -> x12, starting transfers between devices: 3.45 us -> 20.4 us  [swapped(): return lax.ppermute(value, 'core', [(0, 1), (1, 0)])]
    all_to_all x2, blocking collectives: 60.3 us -> 47 us  [all_to_all(): return lax.all_to_all(value, axes, split_axis=0, concat_axis=0, tiled=True)]
    ppermute x4 -> x5, waiting for transfers between devices: 26.2 us -> 19.5 us  [passed_along(): lax.ppermute(value, SLAB, [(source, source + steps) for source in range(l...]
    ppermute x4 -> x5, starting transfers between devices: 20.4 us -> 26.9 us  [passed_along(): lax.ppermute(value, SLAB, [(source, source + steps) for source in range(l...]
    pallas_call x14 -> x13, Pallas kernels: 56.6 us -> 53.5 us  [run(): return call(body, out_shape, in_specs, scratch)(*operands)]
    unnamed x42 -> x58, local copies, waits for them, and re-layouts: 7.58 us -> 8.27 us
    ppermute x4 -> x3, waiting for transfers between devices: 29.9 us -> 30 us  [row_ring(): lax.ppermute(value, 'x', [(s, (s + steps) % WIDTH) for s in range(WIDTH)])]
  transfers between devices with their start and end apart: 27 -> 29, of which waited for: 13 -> 13; matrix products, arithmetic and copies ran while one was open for 1% -> 1% of each run, Pallas kernels for 14% -> 13%
where the time goes in v4:
time: 284 us; the launch traced here: 281 us
  starting transfers between devices  75.7 us (27%)
  waiting for transfers between devices  73.3 us (26%)
  Pallas kernels  70.3 us (25%)
  blocking collectives  47 us (17%)
  local copies, waits for them, and re-layouts  12.1 us (4%)
    pallas_call x13, Pallas kernels, run(): return call(body, out_shape, in_specs, scratch)(*operands)  53.5 us
    all_to_all x2, blocking collectives, all_to_all(): return lax.all_to_all(value, axes, split_axis=0, concat_axis=0, tiled=True)  47 us
    ppermute x3, waiting for transfers between devices, row_ring(): lax.ppermute(value, 'x', [(s, (s + steps) % WIDTH) for s in range(WIDTH)])  30 us
    ppermute x5, starting transfers between devices, passed_along(): lax.ppermute(value, SLAB, [(source, source + steps) for source in range(l...  26.9 us
    ppermute x12, starting transfers between devices, swapped(): return lax.ppermute(value, 'core', [(0, 1), (1, 0)])  20.4 us
    ppermute x5, waiting for transfers between devices, passed_along(): lax.ppermute(value, SLAB, [(source, source + steps) for source in range(l...  19.5 us
    ppermute x4, waiting for transfers between devices, flipped(): return lax.ppermute(value, ('core', 'x'), pairs)  17.6 us
    pallas_call x2, Pallas kernels, convolved(): call(functools.partial(energy_body, place_in, place_out), jax.ShapeDtypeS...  16.8 us
  transfers between devices with their start and end apart: 29, of which 13 were waited for; matrix products, arithmetic and copies ran while one was open for 1% of the time, Pallas kernels for 13%

profile of v4, /device:TPU:70, one launch (start us, length us, event | category | flops | bytes accessed | tf_op | source)
XLA Modules:
  0.0 281.2 jit_solution(743284808985444473)
XLA Ops:
  0.6 1.0 dynamic-slice_bitcast_fusion.1
  1.6 6.3 %collective-permute-start.6 = (bf16[256,512]{1,0:T(8,128)(2,1)S(1)}, bf16[256,512]{1,0:T(8,128)(2,1)S(1)}, u32[]{:S(2)}, u32[]{:S(2)}) collective-permute-start(bf16[256,512]{1,0:T(8,128)(2,1)S(1)} %dynamic-slice_bitcast_fusion.1), channel_id=1, source_target_pairs={{0,1},{1,2},{2,3},{3,4},{4,5},{5,6},{6,7},{7,8},{8,9},{9,10},{10,1... | collective-permute-start | bytes 786440 | tf_op jit(solution)/shard_map/ppermute | solution.py:26
  7.9 11.1 %collective-permute-done.6.mine_ref = bf16[256,512]{1,0:T(8,128)(2,1)S(1)} collective-permute-done((bf16[256,512]{1,0:T(8,128)(2,1)S(1)}, bf16[256,512]{1,0:T(8,128)(2,1)S(1)}, u32[]{:S(2)}, u32[]{:S(2)}) %collective-permute-start.6) | collective-permute-done | bytes 262176 | tf_op jit(solution)/shard_map/ppermute | solution.py:26
  19.0 1.1 dynamic-slice_bitcast_fusion
  20.1 1.9 collective-permute-start.8
  22.0 8.6 %collective-permute-start.9 = (bf16[256,512]{1,0:T(8,128)(2,1)S(1)}, bf16[256,512]{1,0:T(8,128)(2,1)S(1)}, u32[]{:S(2)}, u32[]{:S(2)}) collective-permute-start(bf16[256,512]{1,0:T(8,128)(2,1)S(1)} %dynamic-slice_bitcast_fusion), channel_id=1, source_target_pairs={{0,1},{1,2},{2,3},{3,4},{4,5},{5,6},{6,7},{7,8},{8,9},{9,10},{10,1... | collective-permute-start | bytes 786440 | tf_op jit(solution)/shard_map/ppermute | solution.py:26
  30.7 0.7 pad_add_fusion.at_ref
  31.3 0.6 add_convert_fusion.edge_ref
  31.9 3.4 %shard_map.68 = (f32[512,512]{1,0:T(8,128)}, bf16[512,512]{1,0:T(8,128)(2,1)}) custom-call(f32[1]{0:T(128)} %bitcast.39, s32[2]{0:T(128)} %pad_add_fusion.at_ref, bf16[512,512]{1,0:T(8,128)(2,1)} %bitcast.30, bf16[512,512]{1,0:T(8,128)(2,1)} %bitcast.32), custom_call_target="tpu_custom_call" | custom-call | tf_op jit(solution)/shard_map/pallas_call | solution.py:317
  35.3 0.7 copy-done.24
  36.0 3.1 %shard_map.71 = (f32[512,512]{1,0:T(8,128)}, bf16[256,512]{1,0:T(8,128)(2,1)}, bf16[512,512]{1,0:T(8,128)(2,1)}, bf16[512,512]{1,0:T(8,128)(2,1)}) custom-call(s32[2]{0:T(128)} %pad_add_fusion.at_ref, f32[512,512]{1,0:T(8,128)} %get-tuple-element.42.own_ref, bf16[256,512]{1,0:T(8,128)(2,1)} %copy-done.23, bf16[256,512]{1,0:T(8,128)(2,1)} %copy-done.24), custom_call_target="tpu_custom_call" | custom-call | tf_op jit(solution)/shard_map/pallas_call | solution.py:317
  39.1 1.9 collective-permute-start.10
  41.0 8.1 %collective-permute-start.11 = (bf16[256,512]{1,0:T(8,128)(2,1)}, bf16[256,512]{1,0:T(8,128)(2,1)S(1)}, u32[]{:S(2)}, u32[]{:S(2)}) collective-permute-start(bf16[256,512]{1,0:T(8,128)(2,1)} %get-tuple-element.45), channel_id=1, source_target_pairs={{0,1},{1,2},{2,3},{3,4},{4,5},{5,6},{6,7},{7,8},{8,9},{9,10},{10,1... | collective-permute-start | bytes 786440 | tf_op jit(solution)/shard_map/ppermute | solution.py:26
  49.8 8.4 %collective-permute-done.10.refs_2_ = bf16[256,512]{1,0:T(8,128)(2,1)S(1)} collective-permute-done((bf16[256,512]{1,0:T(8,128)(2,1)}, bf16[256,512]{1,0:T(8,128)(2,1)S(1)}, u32[]{:S(2)}, u32[]{:S(2)}) %collective-permute-start.10) | collective-permute-done | bytes 262176 | tf_op jit(solution)/shard_map/ppermute | solution.py:26
  58.7 0.6 convert_convert_fusion.inverse_ref
  60.8 8.4 %shard_map.72 = (bf16[16,2,32,512]{3,2,1,0:T(8,128)(2,1)}, bf16[512,512]{1,0:T(8,128)(2,1)}, bf16[512,512]{1,0:T(8,128)(2,1)}) custom-call(f32[2]{0:T(128)} %energy_ref.5, f32[2]{0:T(128)} %convert_convert_fusion.inverse_ref, f32[2]{0:T(128)} %add_convert_fusion.edge_ref, s32[2]{0:T(128)} %pad_add_fusion.at_ref, bf16[512,512]{1,0:T(8,128)(2,1)} %bitcast.33, ...), custom_call_target="tpu_custom_call" | custom-call | tf_op jit(solution)/shard_map/pallas_call | solution.py:317
  69.2 21.9 %all_to_all.20 = bf16[16,2,32,512]{3,2,1,0:T(8,128)(2,1)} all-to-all(bf16[16,2,32,512]{3,2,1,0:T(8,128)(2,1)} %get-tuple-element.46), channel_id=1, replica_groups=mesh['zlo'=2,'y'=4,'core'=2,'row'=4,'x'=4] {'zlo','y','core'}, dimensions={0} | all-to-all | bytes 2097152 | tf_op jit(solution)/shard_map/all_to_all | solution.py:297
  91.1 8.5 %shard_map.73 = bf16[32,32,512]{2,1,0:T(8,128)(2,1)} custom-call(s32[8]{0:T(128)} %offset_ref.3, bf16[32,32,512]{2,1,0:T(8,128)(2,1)} %bitcast.28, bf16[32,512]{1,0:T(8,128)(2,1)} %bitcast.37), custom_call_target="tpu_custom_call" | custom-call | tf_op jit(solution)/shard_map/pallas_call | solution.py:288
  99.5 5.6 %all-to-all-start.1 = ((bf16[32,32,512]{2,1,0:T(8,128)(2,1)}), bf16[32,32,512]{2,1,0:T(8,128)(2,1)S(1)}, u32[]{:S(2)}, u32[]{:S(2)}) async-start(bf16[32,32,512]{2,1,0:T(8,128)(2,1)} %shard_map.73), calls=%async_computation.1 | async-start | bytes 2097152 | tf_op jit(solution)/shard_map/all_to_all | solution.py:297
  105.4 1.8 collective-permute-start.2
  107.2 21.7 %collective-permute-done.one_ref = bf16[512,512]{1,0:T(8,128)(2,1)S(1)} collective-permute-done((bf16[512,512]{1,0:T(8,128)(2,1)S(1)}, bf16[512,512]{1,0:T(8,128)(2,1)S(1)}, u32[]{:S(2)}, u32[]{:S(2)}) %collective-permute-start) | collective-permute-done | bytes 524320 | tf_op jit(solution)/shard_map/ppermute | solution.py:30
  128.9 2.4 collective-permute-start.1
  131.3 1.9 collective-permute-start.17
  133.2 2.1 collective-permute-start.18
  135.3 8.4 %collective-permute-done.1.two_ref = bf16[512,512]{1,0:T(8,128)(2,1)S(1)} collective-permute-done((bf16[512,512]{1,0:T(8,128)(2,1)S(1)}, bf16[512,512]{1,0:T(8,128)(2,1)S(1)}, u32[]{:S(2)}, u32[]{:S(2)}) %collective-permute-start.1) | collective-permute-done | bytes 524320 | tf_op jit(solution)/shard_map/ppermute | solution.py:30
  143.7 0.8 copy-done.9
  144.5 3.5 %shard_map.69 = (bf16[4,512,512]{2,1,0:T(8,128)(2,1)}, bf16[2,512,512]{2,1,0:T(8,128)(2,1)}, bf16[512,512]{1,0:T(8,128)(2,1)}) custom-call(s32[2]{0:T(128)} %pad_add_fusion.at_ref, bf16[512,512]{1,0:T(8,128)(2,1)} %get-tuple-element.32.here_ref, bf16[512,512]{1,0:T(8,128)(2,1)} %copy-done.6, bf16[512,512]{1,0:T(8,128)(2,1)} %copy-done.9, ...), custom_call_target="tpu_custom_call" | custom-call | tf_op jit(solution)/shard_map/pallas_call | solution.py:317
  148.0 1.3 collective-permute-start.4
  149.3 4.1 %collective-permute-done.18.second_ref = bf16[512,512]{1,0:T(8,128)(2,1)S(1)} collective-permute-done((bf16[512,512]{1,0:T(8,128)(2,1)}, bf16[512,512]{1,0:T(8,128)(2,1)S(1)}, u32[]{:S(2)}, u32[]{:S(2)}) %collective-permute-start.18) | collective-permute-done | bytes 524320 | tf_op jit(solution)/shard_map/ppermute | solution.py:47
  153.4 0.8 copy-done.11
  154.2 2.3 shard_map.74
  156.4 2.7 collective-permute-start.19
  159.1 4.0 %collective-permute-start.20 = (bf16[512,512]{1,0:T(8,128)(2,1)}, bf16[512,512]{1,0:T(8,128)(2,1)S(1)}, u32[]{:S(2)}, u32[]{:S(2)}) collective-permute-start(bf16[512,512]{1,0:T(8,128)(2,1)} %get-tuple-element.50.inner.green_ref), channel_id=1, source_target_pairs={{0,16},{16,0},{1,17},{17,1},{2,18},{18,2},{3,19},{19,3},{4,20},{20... | collective-permute-start | bytes 1572872 | tf_op jit(solution)/shard_map/ppermute | solution.py:34
  163.3 0.7 collective-permute-start.5
  164.1 1.0 copy-done.2
  165.0 4.1 %shard_map.70 = (bf16[512,512]{1,0:T(8,128)(2,1)}, bf16[512,512]{1,0:T(8,128)(2,1)}, bf16[512,512]{1,0:T(8,128)(2,1)}, bf16[512,512]{1,0:T(8,128)(2,1)}, bf16[51...) custom-call(s32[2]{0:T(128)} %pad_add_fusion.at_ref, bf16[4,512,512]{2,1,0:T(8,128)(2,1)} %get-tuple-element.33.all_ref, ...), custom_call_target="tpu_custom_call" | custom-call | tf_op jit(solution)/shard_map/pallas_call | solution.py:317
  169.2 2.6 collective-permute-done.19.beyond
  171.7 0.8 copy-done.4
  172.7 6.2 %shard_map.75 = (f32[512,512]{1,0:T(8,128)}, f32[512,512]{1,0:T(8,128)}) custom-call(s32[2]{0:T(128)} %pad_add_fusion.at_ref, f32[2]{0:T(128)} %energy_ref.5, f32[2]{0:T(128)} %copy-done.28, bf16[512,512]{1,0:T(8,128)(2,1)} %get-tuple-element.37.outer_ham, bf16[512,512]{1,0:T(8,128)(2,1)} %get-tuple-element.38.inner_ham, ...), custom_call_target="tpu_custom_call" | custom-call | tf_op jit(solution)/shard_map/pallas_call | solution.py:317
  178.9 0.8 copy-done.1
  179.7 3.4 %shard_map.77.inner = bf16[512,512]{1,0:T(8,128)(2,1)} custom-call(s32[2]{0:T(128)} %pad_add_fusion.at_ref, f32[512,512]{1,0:T(8,128)} %get-tuple-element.52.open_ref, bf16[4,8,32,512]{3,2,1,0:T(8,128)(2,1)} %bitcast.24, bf16[2,8,32,512]{3,2,1,0:T(8,128)(2,1)} %copy-done.1, bf16[512,512]{1,0:T(8,128)(2,1)} %get-tuple-element.50.inner.green_ref), custom_call_target="tpu_custom_call" | custom-call | tf_op jit(solution)/shard_map/pallas_call | solution.py:317
  183.1 6.3 %collective-permute-start.21 = (bf16[512,512]{1,0:T(8,128)(2,1)}, bf16[512,512]{1,0:T(8,128)(2,1)S(1)}, u32[]{:S(2)}, u32[]{:S(2)}) collective-permute-start(bf16[512,512]{1,0:T(8,128)(2,1)} %shard_map.77.inner), channel_id=1, source_target_pairs={{0,16},{16,0},{1,17},{17,1},{2,18},{18,2},{3,19},{19,3},{4,20},{20... | collective-permute-start | bytes 1572872 | tf_op jit(solution)/shard_map/ppermute | solution.py:34
  189.4 3.4 %shard_map.76.outer = bf16[512,512]{1,0:T(8,128)(2,1)} custom-call(s32[2]{0:T(128)} %pad_add_fusion.at_ref, f32[512,512]{1,0:T(8,128)} %get-tuple-element.51.open_ref, bf16[4,8,32,512]{3,2,1,0:T(8,128)(2,1)} %bitcast.25, bf16[2,8,32,512]{3,2,1,0:T(8,128)(2,1)} %copy-done.1, bf16[512,512]{1,0:T(8,128)(2,1)} %get-tuple-element.49.outer.green_ref), custom_call_target="tpu_custom_call" | custom-call | tf_op jit(solution)/shard_map/pallas_call | solution.py:317
  192.9 1.9 collective-permute-start.22
  194.8 0.8 copy-done.8
  195.6 6.4 %shard_map.78 = (f32[512,512]{1,0:T(8,128)}, bf16[512,512]{1,0:T(8,128)(2,1)}, bf16[8,32,512]{2,1,0:T(8,128)(2,1)}, bf16[8,32,512]{2,1,0:T(8,128)(2,1)}) custom-call(s32[2]{0:T(128)} %pad_add_fusion.at_ref, f32[2]{0:T(128)} %energy_ref.5, f32[2]{0:T(128)} %copy-done.28, bf16[512,512]{1,0:T(8,128)(2,1)} %get-tuple-element.37.outer_ham, ...), custom_call_target="tpu_custom_call" | custom-call | tf_op jit(solution)/shard_map/pallas_call | solution.py:317
  202.0 4.5 %collective-permute-start.23 = (bf16[8,32,512]{2,1,0:T(8,128)(2,1)}, bf16[8,32,512]{2,1,0:T(8,128)(2,1)S(1)}, u32[]{:S(2)}, u32[]{:S(2)}) collective-permute-start(bf16[8,32,512]{2,1,0:T(8,128)(2,1)} %get-tuple-element.55), channel_id=1, source_target_pairs={{0,16},{16,0},{1,17},{17,1},{2,18},{18,2},{3,19},{19,3},{4,20},{20... | collective-permute-start | bytes 786440 | tf_op jit(solution)/shard_map/ppermute | solution.py:34
  206.5 0.7 collective-permute-done.22.beyond
  207.2 0.6 collective-permute-done.23.got_inner
  208.5 4.5 %shard_map.79 = (bf16[512,512]{1,0:T(8,128)(2,1)}, bf16[4,8,32,512]{3,2,1,0:T(8,128)(2,1)}, bf16[8,32,512]{2,1,0:T(8,128)(2,1)}) custom-call(s32[2]{0:T(128)} %pad_add_fusion.at_ref, bf16[512,512]{1,0:T(8,128)(2,1)} %get-tuple-element.36.far, f32[512,512]{1,0:T(8,128)} %get-tuple-element.53.open_ref, bf16[512,512]{1,0:T(8,128)(2,1)} %shard_map.76.outer, ...), custom_call_target="tpu_custom_call" | custom-call | tf_op jit(solution)/shard_map/pallas_call | solution.py:317
  213.0 3.6 %collective-permute-start.26 = (bf16[8,32,512]{2,1,0:T(8,128)(2,1)}, bf16[8,32,512]{2,1,0:T(8,128)(2,1)S(1)}, u32[]{:S(2)}, u32[]{:S(2)}) collective-permute-start(bf16[8,32,512]{2,1,0:T(8,128)(2,1)} %get-tuple-element.61), channel_id=1, source_target_pairs={{0,16},{16,0},{1,17},{17,1},{2,18},{18,2},{3,19},{19,3},{4,20},{20... | collective-permute-start | bytes 786440 | tf_op jit(solution)/shard_map/ppermute | solution.py:34
  216.6 1.4 collective-permute-done.26
  218.0 0.7 bitcast_dynamic-update-slice_fusion
  218.7 25.1 %all_to_all.21.green_ref = bf16[32,32,512]{2,1,0:T(8,128)(2,1)} all-to-all(bf16[32,32,512]{2,1,0:T(8,128)(2,1)} %bitcast.35), channel_id=1, replica_groups=mesh['zlo'=2,'y'=4,'core'=2,'row'=4,'x'=4] {'x','zlo','y'}, dimensions={0} | all-to-all | bytes 2097152 | tf_op jit(solution)/shard_map/all_to_all | solution.py:297
  243.8 8.4 %shard_map.82 = bf16[32,32,512]{2,1,0:T(8,128)(2,1)} custom-call(s32[8]{0:T(128)} %offset_ref.3, bf16[32,32,512]{2,1,0:T(8,128)(2,1)} %all_to_all.21.green_ref, bf16[32,512]{1,0:T(8,128)(2,1)} %bitcast.38), custom_call_target="tpu_custom_call" | custom-call | tf_op jit(solution)/shard_map/pallas_call | solution.py:288
  252.2 3.7 %all-to-all-start.3 = ((bf16[16,2,32,512]{3,2,1,0:T(8,128)(2,1)}), bf16[16,2,32,512]{3,2,1,0:T(8,128)(2,1)S(1)}, u32[]{:S(2)}, u32[]{:S(2)}) async-start(bf16[16,2,32,512]{3,2,1,0:T(8,128)(2,1)} %bitcast.27), calls=%async_computation.3 | async-start | bytes 2097152 | tf_op jit(solution)/shard_map/all_to_all | solution.py:297
  255.9 2.2 shard_map.80
  258.1 3.2 %collective-permute-start.24 = (bf16[512,512]{1,0:T(8,128)(2,1)}, bf16[512,512]{1,0:T(8,128)(2,1)S(1)}, u32[]{:S(2)}, u32[]{:S(2)}) collective-permute-start(bf16[512,512]{1,0:T(8,128)(2,1)} %get-tuple-element.58), channel_id=1, source_target_pairs={{0,0},{1,1},{2,16},{3,17},{16,2},{17,3},{18,18},{19,19},{4,4},{5,5... | collective-permute-start | bytes 1572872 | tf_op jit(solution)/shard_map/ppermute | solution.py:47
  261.4 1.6 collective-permute-start.25
  262.9 13.0 %collective-permute-done.24.first_ref = bf16[512,512]{1,0:T(8,128)(2,1)S(1)} collective-permute-done((bf16[512,512]{1,0:T(8,128)(2,1)}, bf16[512,512]{1,0:T(8,128)(2,1)S(1)}, u32[]{:S(2)}, u32[]{:S(2)}) %collective-permute-start.24) | collective-permute-done | bytes 524320 | tf_op jit(solution)/shard_map/ppermute | solution.py:47
  275.9 0.6 collective-permute-done.25.second_ref
  276.7 0.8 copy-done.14
  277.5 2.7 shard_map.81
  280.2 1.0 copy.7
  (77 shorter events, 4.2 us)
Async XLA Ops:
  0.6 58.1 %copy-start.26 = (f32[2]{0:T(128)S(1)}, f32[2]{0:T(128)}, u32[]{:S(2)}) copy-start(f32[2]{0:T(128)} %energy_ref.5) | copy-start | bytes 28
  1.6 17.4 %collective-permute-start.6 = (bf16[256,512]{1,0:T(8,128)(2,1)S(1)}, bf16[256,512]{1,0:T(8,128)(2,1)S(1)}, u32[]{:S(2)}, u32[]{:S(2)}) collective-permute-start(bf16[256,512]{1,0:T(8,128)(2,1)S(1)} %dynamic-slice_bitcast_fusion.1), channel_id=1, source_target_pairs={{0,1},{1,2},{2,3},{3,4},{4,5},{5,6},{6,7},{7,8},{8,9},{9,10},{10,1... | collective-permute-start | bytes 786440 | tf_op jit(solution)/shard_map/ppermute | solution.py:26
  19.0 16.3 %copy-start.23 = (bf16[256,512]{1,0:T(8,128)(2,1)}, bf16[256,512]{1,0:T(8,128)(2,1)S(1)}, u32[]{:S(2)}) copy-start(bf16[256,512]{1,0:T(8,128)(2,1)S(1)} %collective-permute-done.6.mine_ref) | copy-start | bytes 786436
  19.0 16.3 %collective-permute-start.7 = (bf16[256,512]{1,0:T(8,128)(2,1)S(1)}, bf16[256,512]{1,0:T(8,128)(2,1)S(1)}, u32[]{:S(2)}, u32[]{:S(2)}) collective-permute-start(bf16[256,512]{1,0:T(8,128)(2,1)S(1)} %collective-permute-done.6.mine_ref), channel_id=1, source_target_pairs={{0,16},{16,0},{1,17},{17,1},{2,18},{18,2},{3,19},{19,3},{4,20},{20... | collective-permute-start | bytes 786440 | tf_op jit(solution)/shard_map/ppermute | solution.py:34
  20.1 29.1 %collective-permute-start.8 = (bf16[256,512]{1,0:T(8,128)(2,1)S(1)}, bf16[256,512]{1,0:T(8,128)(2,1)S(1)}, u32[]{:S(2)}, u32[]{:S(2)}) collective-permute-start(bf16[256,512]{1,0:T(8,128)(2,1)S(1)} %dynamic-slice_bitcast_fusion), channel_id=1, source_target_pairs={{1,0},{2,1},{3,2},{4,3},{5,4},{6,5},{7,6},{8,7},{9,8},{10,9},{11,1... | collective-permute-start | bytes 786440 | tf_op jit(solution)/shard_map/ppermute | solution.py:26
  22.0 27.3 %collective-permute-start.9 = (bf16[256,512]{1,0:T(8,128)(2,1)S(1)}, bf16[256,512]{1,0:T(8,128)(2,1)S(1)}, u32[]{:S(2)}, u32[]{:S(2)}) collective-permute-start(bf16[256,512]{1,0:T(8,128)(2,1)S(1)} %dynamic-slice_bitcast_fusion), channel_id=1, source_target_pairs={{0,1},{1,2},{2,3},{3,4},{4,5},{5,6},{6,7},{7,8},{8,9},{9,10},{10,1... | collective-permute-start | bytes 786440 | tf_op jit(solution)/shard_map/ppermute | solution.py:26
  35.3 0.7 copy-start.24
  39.1 19.1 %collective-permute-start.10 = (bf16[256,512]{1,0:T(8,128)(2,1)}, bf16[256,512]{1,0:T(8,128)(2,1)S(1)}, u32[]{:S(2)}, u32[]{:S(2)}) collective-permute-start(bf16[256,512]{1,0:T(8,128)(2,1)} %get-tuple-element.45), channel_id=1, source_target_pairs={{1,0},{2,1},{3,2},{4,3},{5,4},{6,5},{7,6},{8,7},{9,8},{10,9},{11,1... | collective-permute-start | bytes 786440 | tf_op jit(solution)/shard_map/ppermute | solution.py:26
  41.0 17.2 %collective-permute-start.11 = (bf16[256,512]{1,0:T(8,128)(2,1)}, bf16[256,512]{1,0:T(8,128)(2,1)S(1)}, u32[]{:S(2)}, u32[]{:S(2)}) collective-permute-start(bf16[256,512]{1,0:T(8,128)(2,1)} %get-tuple-element.45), channel_id=1, source_target_pairs={{0,1},{1,2},{2,3},{3,4},{4,5},{5,6},{6,7},{7,8},{8,9},{9,10},{10,1... | collective-permute-start | bytes 786440 | tf_op jit(solution)/shard_map/ppermute | solution.py:26
  49.2 10.9 %copy-start.15 = (bf16[256,512]{1,0:T(8,128)(2,1)}, bf16[256,512]{1,0:T(8,128)(2,1)S(1)}, u32[]{:S(2)}) copy-start(bf16[256,512]{1,0:T(8,128)(2,1)S(1)} %collective-permute-done.8.refs_0_) | copy-start | bytes 786436
  49.2 10.1 %collective-permute-start.12 = (bf16[256,512]{1,0:T(8,128)(2,1)S(1)}, bf16[256,512]{1,0:T(8,128)(2,1)S(1)}, u32[]{:S(2)}, u32[]{:S(2)}) collective-permute-start(bf16[256,512]{1,0:T(8,128)(2,1)S(1)} %collective-permute-done.8.refs_0_), channel_id=1, source_target_pairs={{0,16},{16,0},{1,17},{17,1},{2,18},{18,2},{3,19},{19,3},{4,20},{20... | collective-permute-start | bytes 786440 | tf_op jit(solution)/shard_map/ppermute | solution.py:34
  49.3 10.8 %copy-start.16 = (bf16[256,512]{1,0:T(8,128)(2,1)}, bf16[256,512]{1,0:T(8,128)(2,1)S(1)}, u32[]{:S(2)}) copy-start(bf16[256,512]{1,0:T(8,128)(2,1)S(1)} %collective-permute-done.9.refs_1_) | copy-start | bytes 786436
  49.3 10.0 %collective-permute-start.13 = (bf16[256,512]{1,0:T(8,128)(2,1)S(1)}, bf16[256,512]{1,0:T(8,128)(2,1)S(1)}, u32[]{:S(2)}, u32[]{:S(2)}) collective-permute-start(bf16[256,512]{1,0:T(8,128)(2,1)S(1)} %collective-permute-done.9.refs_1_), channel_id=1, source_target_pairs={{0,16},{16,0},{1,17},{17,1},{2,18},{18,2},{3,19},{19,3},{4,20},{20... | collective-permute-start | bytes 786440 | tf_op jit(solution)/shard_map/ppermute | solution.py:34
  58.2 1.9 copy-start.17
  58.2 1.5 collective-permute-start.14
  58.2 1.9 copy-start.18
  58.2 1.9 collective-permute-start.15
  59.3 0.8 copy-start.19
  59.3 0.8 copy-start.20
  59.7 0.7 copy-start.21
  60.1 0.7 copy-start.22
  91.1 14.0 %copy-start.3 = (bf16[512,512]{1,0:T(8,128)(2,1)S(1)}, bf16[512,512]{1,0:T(8,128)(2,1)}, u32[]{:S(2)}) copy-start(bf16[512,512]{1,0:T(8,128)(2,1)} %get-tuple-element.32.here_ref) | copy-start | bytes 1572868
  99.5 63.6 %all-to-all-start.1 = ((bf16[32,32,512]{2,1,0:T(8,128)(2,1)}), bf16[32,32,512]{2,1,0:T(8,128)(2,1)S(1)}, u32[]{:S(2)}, u32[]{:S(2)}) async-start(bf16[32,32,512]{2,1,0:T(8,128)(2,1)} %shard_map.73), calls=%async_computation.1 | async-start | bytes 2097152 | tf_op jit(solution)/shard_map/all_to_all | solution.py:297
  105.1 23.8 %collective-permute-start = (bf16[512,512]{1,0:T(8,128)(2,1)S(1)}, bf16[512,512]{1,0:T(8,128)(2,1)S(1)}, u32[]{:S(2)}, u32[]{:S(2)}) collective-permute-start(bf16[512,512]{1,0:T(8,128)(2,1)S(1)} %copy-done.3), channel_id=1, source_target_pairs={{0,1},{1,2},{2,3},{3,0},{4,5},{5,6},{6,7},{7,4},{8,9},{9,10},{10,1... | collective-permute-start | bytes 1572872 | tf_op jit(solution)/shard_map/ppermute | solution.py:30
  105.4 29.9 %collective-permute-start.2 = (bf16[512,512]{1,0:T(8,128)(2,1)S(1)}, bf16[512,512]{1,0:T(8,128)(2,1)S(1)}, u32[]{:S(2)}, u32[]{:S(2)}) collective-permute-start(bf16[512,512]{1,0:T(8,128)(2,1)S(1)} %copy-done.3), channel_id=1, source_target_pairs={{0,3},{1,0},{2,1},{3,2},{4,7},{5,4},{6,5},{7,6},{8,11},{9,8},{10,9... | collective-permute-start | bytes 1572872 | tf_op jit(solution)/shard_map/ppermute | solution.py:30
  128.9 14.8 %copy-start.6 = (bf16[512,512]{1,0:T(8,128)(2,1)}, bf16[512,512]{1,0:T(8,128)(2,1)S(1)}, u32[]{:S(2)}) copy-start(bf16[512,512]{1,0:T(8,128)(2,1)S(1)} %collective-permute-done.one_ref) | copy-start | bytes 1572868
  128.9 14.8 %collective-permute-start.1 = (bf16[512,512]{1,0:T(8,128)(2,1)S(1)}, bf16[512,512]{1,0:T(8,128)(2,1)S(1)}, u32[]{:S(2)}, u32[]{:S(2)}) collective-permute-start(bf16[512,512]{1,0:T(8,128)(2,1)S(1)} %collective-permute-done.one_ref), channel_id=1, source_target_pairs={{0,1},{1,2},{2,3},{3,0},{4,5},{5,6},{6,7},{7,4},{8,9},{9,10},{10,1... | collective-permute-start | bytes 1572872 | tf_op jit(solution)/shard_map/ppermute | solution.py:30
  131.3 18.0 %collective-permute-start.17 = (bf16[512,512]{1,0:T(8,128)(2,1)}, bf16[512,512]{1,0:T(8,128)(2,1)S(1)}, u32[]{:S(2)}, u32[]{:S(2)}) collective-permute-start(bf16[512,512]{1,0:T(8,128)(2,1)} %get-tuple-element.47), channel_id=1, source_target_pairs={{0,0},{1,1},{2,16},{3,17},{16,2},{17,3},{18,18},{19,19},{4,4},{5,5... | collective-permute-start | bytes 1572872 | tf_op jit(solution)/shard_map/ppermute | solution.py:47
  133.2 30.1 %copy-start.27 = (f32[2]{0:T(128)S(1)}, f32[2]{0:T(128)}, u32[]{:S(2)}) copy-start(f32[2]{0:T(128)} %energy_ref.5) | copy-start | bytes 28
  133.2 20.1 %collective-permute-start.18 = (bf16[512,512]{1,0:T(8,128)(2,1)}, bf16[512,512]{1,0:T(8,128)(2,1)S(1)}, u32[]{:S(2)}, u32[]{:S(2)}) collective-permute-start(bf16[512,512]{1,0:T(8,128)(2,1)} %get-tuple-element.48), channel_id=1, source_target_pairs={{0,1},{1,0},{2,17},{3,16},{16,3},{17,2},{18,19},{19,18},{4,5},{5,4... | collective-permute-start | bytes 1572872 | tf_op jit(solution)/shard_map/ppermute | solution.py:47
  135.3 8.4 %copy-start.7 = (bf16[512,512]{1,0:T(8,128)(2,1)}, bf16[512,512]{1,0:T(8,128)(2,1)S(1)}, u32[]{:S(2)}) copy-start(bf16[512,512]{1,0:T(8,128)(2,1)S(1)} %collective-permute-done.2.three_ref) | copy-start | bytes 1572868
  143.7 0.8 copy-start.9
  148.0 16.1 %collective-permute-start.3 = (bf16[2,512,512]{2,1,0:T(8,128)(2,1)}, bf16[2,512,512]{2,1,0:T(8,128)(2,1)S(1)}, u32[]{:S(2)}, u32[]{:S(2)}) collective-permute-start(bf16[2,512,512]{2,1,0:T(8,128)(2,1)} %get-tuple-element.34), channel_id=1, source_target_pairs={{0,16},{16,0},{1,17},{17,1},{2,18},{18,2},{3,19},{19,3},{4,20},{20... | collective-permute-start | bytes 3145736 | tf_op jit(solution)/shard_map/ppermute | solution.py:34
  148.0 15.3 %collective-permute-start.4 = (bf16[512,512]{1,0:T(8,128)(2,1)}, bf16[512,512]{1,0:T(8,128)(2,1)}, u32[]{:S(2)}, u32[]{:S(2)}) collective-permute-start(bf16[512,512]{1,0:T(8,128)(2,1)} %get-tuple-element.35), channel_id=1, source_target_pairs={{16,4},{20,8},{24,12},{17,5},{21,9},{25,13},{18,6},{22,10},{26,14}... | collective-permute-start | bytes 1572872 | tf_op jit(solution)/shard_map/ppermute | solution.py:42
  149.3 4.1 %copy-start.10 = (bf16[512,512]{1,0:T(8,128)(2,1)}, bf16[512,512]{1,0:T(8,128)(2,1)S(1)}, u32[]{:S(2)}) copy-start(bf16[512,512]{1,0:T(8,128)(2,1)S(1)} %collective-permute-done.17.first_ref) | copy-start | bytes 1572868
  153.4 0.8 copy-start.11
  156.4 15.3 %collective-permute-start.19 = (bf16[512,512]{1,0:T(8,128)(2,1)}, bf16[512,512]{1,0:T(8,128)(2,1)S(1)}, u32[]{:S(2)}, u32[]{:S(2)}) collective-permute-start(bf16[512,512]{1,0:T(8,128)(2,1)} %get-tuple-element.49.outer.green_ref), channel_id=1, source_target_pairs={{16,4},{20,8},{24,12},{4,16},{8,20},{12,24},{17,5},{21,9},{25,13},... | collective-permute-start | bytes 1572872 | tf_op jit(solution)/shard_map/ppermute | solution.py:42
  159.1 12.6 %collective-permute-start.20 = (bf16[512,512]{1,0:T(8,128)(2,1)}, bf16[512,512]{1,0:T(8,128)(2,1)S(1)}, u32[]{:S(2)}, u32[]{:S(2)}) collective-permute-start(bf16[512,512]{1,0:T(8,128)(2,1)} %get-tuple-element.50.inner.green_ref), channel_id=1, source_target_pairs={{0,16},{16,0},{1,17},{17,1},{2,18},{18,2},{3,19},{19,3},{4,20},{20... | collective-permute-start | bytes 1572872 | tf_op jit(solution)/shard_map/ppermute | solution.py:34
  163.1 6.0 %copy-start = (bf16[32,32,512]{2,1,0:T(8,128)(2,1)}, bf16[32,32,512]{2,1,0:T(8,128)(2,1)S(1)}, u32[]{:S(2)}) copy-start(bf16[32,32,512]{2,1,0:T(8,128)(2,1)S(1)} %all-to-all-done.1) | copy-start | bytes 3145732
  163.2 15.7 %collective-permute-start.16 = (bf16[2,8,32,512]{3,2,1,0:T(8,128)(2,1)S(1)}, bf16[2,8,32,512]{3,2,1,0:T(8,128)(2,1)S(1)}, u32[]{:S(2)}, u32[]{:S(2)}) collective-permute-start(bf16[2,8,32,512]{3,2,1,0:T(8,128)(2,1)S(1)} %constant_dynamic-slice_fusion), channel_id=1, source_target_pairs={{0,16},{16,0},{1,17},{17,1},{2,18},{18,2},{3,19},{19,3},{4,20},{20... | collective-permute-start | bytes 1572872 | tf_op jit(solution)/shard_map/ppermute | solution.py:34
  163.3 5.8 %collective-permute-start.5 = (f32[2]{0:T(128)S(1)}, f32[2]{0:T(128)S(1)}, u32[]{:S(2)}, u32[]{:S(2)}) collective-permute-start(f32[2]{0:T(128)S(1)} %copy-done.27), channel_id=1, source_target_pairs={{0,16},{16,0},{1,17},{17,1},{2,18},{18,2},{3,19},{19,3},{4,20},{20... | collective-permute-start | bytes 32 | tf_op jit(solution)/shard_map/ppermute | solution.py:34
  164.1 1.0 copy-start.2
  169.1 2.6 copy-start.28
  171.7 0.8 copy-start.4
  171.7 1.0 copy-start.5
  178.9 0.8 copy-start.1
  183.1 11.6 %collective-permute-start.21 = (bf16[512,512]{1,0:T(8,128)(2,1)}, bf16[512,512]{1,0:T(8,128)(2,1)S(1)}, u32[]{:S(2)}, u32[]{:S(2)}) collective-permute-start(bf16[512,512]{1,0:T(8,128)(2,1)} %shard_map.77.inner), channel_id=1, source_target_pairs={{0,16},{16,0},{1,17},{17,1},{2,18},{18,2},{3,19},{19,3},{4,20},{20... | collective-permute-start | bytes 1572872 | tf_op jit(solution)/shard_map/ppermute | solution.py:34
  192.9 14.4 %collective-permute-start.22 = (bf16[512,512]{1,0:T(8,128)(2,1)}, bf16[512,512]{1,0:T(8,128)(2,1)S(1)}, u32[]{:S(2)}, u32[]{:S(2)}) collective-permute-start(bf16[512,512]{1,0:T(8,128)(2,1)} %shard_map.76.outer), channel_id=1, source_target_pairs={{16,4},{20,8},{24,12},{4,16},{8,20},{12,24},{17,5},{21,9},{25,13},... | collective-permute-start | bytes 1572872 | tf_op jit(solution)/shard_map/ppermute | solution.py:42
  194.8 0.8 copy-start.8
  202.0 5.9 %collective-permute-start.23 = (bf16[8,32,512]{2,1,0:T(8,128)(2,1)}, bf16[8,32,512]{2,1,0:T(8,128)(2,1)S(1)}, u32[]{:S(2)}, u32[]{:S(2)}) collective-permute-start(bf16[8,32,512]{2,1,0:T(8,128)(2,1)} %get-tuple-element.55), channel_id=1, source_target_pairs={{0,16},{16,0},{1,17},{17,1},{2,18},{18,2},{3,19},{19,3},{4,20},{20... | collective-permute-start | bytes 786440 | tf_op jit(solution)/shard_map/ppermute | solution.py:34
  207.2 0.8 copy-start.12
  207.9 0.7 copy-start.25
  213.0 5.0 %collective-permute-start.26 = (bf16[8,32,512]{2,1,0:T(8,128)(2,1)}, bf16[8,32,512]{2,1,0:T(8,128)(2,1)S(1)}, u32[]{:S(2)}, u32[]{:S(2)}) collective-permute-start(bf16[8,32,512]{2,1,0:T(8,128)(2,1)} %get-tuple-element.61), channel_id=1, source_target_pairs={{0,16},{16,0},{1,17},{17,1},{2,18},{18,2},{3,19},{19,3},{4,20},{20... | collective-permute-start | bytes 786440 | tf_op jit(solution)/shard_map/ppermute | solution.py:34
  252.2 28.0 %all-to-all-start.3 = ((bf16[16,2,32,512]{3,2,1,0:T(8,128)(2,1)}), bf16[16,2,32,512]{3,2,1,0:T(8,128)(2,1)S(1)}, u32[]{:S(2)}, u32[]{:S(2)}) async-start(bf16[16,2,32,512]{3,2,1,0:T(8,128)(2,1)} %bitcast.27), calls=%async_computation.3 | async-start | bytes 2097152 | tf_op jit(solution)/shard_map/all_to_all | solution.py:297
  258.1 17.8 %collective-permute-start.24 = (bf16[512,512]{1,0:T(8,128)(2,1)}, bf16[512,512]{1,0:T(8,128)(2,1)S(1)}, u32[]{:S(2)}, u32[]{:S(2)}) collective-permute-start(bf16[512,512]{1,0:T(8,128)(2,1)} %get-tuple-element.58), channel_id=1, source_target_pairs={{0,0},{1,1},{2,16},{3,17},{16,2},{17,3},{18,18},{19,19},{4,4},{5,5... | collective-permute-start | bytes 1572872 | tf_op jit(solution)/shard_map/ppermute | solution.py:47
  261.4 15.1 %collective-permute-start.25 = (bf16[512,512]{1,0:T(8,128)(2,1)}, bf16[512,512]{1,0:T(8,128)(2,1)S(1)}, u32[]{:S(2)}, u32[]{:S(2)}) collective-permute-start(bf16[512,512]{1,0:T(8,128)(2,1)} %get-tuple-element.59), channel_id=1, source_target_pairs={{0,1},{1,0},{2,17},{3,16},{16,3},{17,2},{18,19},{19,18},{4,5},{5,4... | collective-permute-start | bytes 1572872 | tf_op jit(solution)/shard_map/ppermute | solution.py:47
  275.9 0.8 copy-start.13
  276.7 0.8 copy-start.14

commit v5 on v4

--- a/solution.py
+++ b/solution.py
@@ -54,7 +54,7 @@
         in_specs=in_specs,
         out_specs=jax.tree.map(lambda _: VM, out_shape),
         scratch_shapes=list(scratch),
-        compiler_params=pltpu.CompilerParams(vmem_limit_bytes=56 * 1024 * 1024),
+        compiler_params=pltpu.CompilerParams(vmem_limit_bytes=16 * 1024 * 1024),
     )
 
 
@@ -78,6 +78,14 @@
 def own_body(keep_ref, at_ref, c_ref, ham_ref, own_ref, load_ref):
     own_ref[...] = dot_t(c_ref[...], c_ref[...]) * keep_ref[0]
     load_ref[...] = jnp.where(at_ref[0] == 0, ham_ref[...], c_ref[...])
+
+
+def returned(value, inner, slot):
+    pairs = []
+    for c in range(2):
+        block = (1 + c) if inner else 3 * c
+        pairs += [(c * WIDTH + i, (i // 2) * WIDTH + block) for i in range(slot, WIDTH, 2)]
+    return lax.ppermute(value, ("core", "x"), pairs)
 
 
 def place_halves(core, whole, mine, theirs):
@@ -97,11 +105,11 @@
     half_ref[...] = pair_ref[pl.ds(pl.multiple_of(core * half, half), half)].astype(jnp.bfloat16)
 
 
-def first_step(energy, inverse, ham, pair, eye, rotate):
-    base = energy * eye + BROAD * rotate - ham.astype(jnp.float32)
-    matrix = (base - inverse * pair.astype(jnp.float32)).astype(jnp.bfloat16).astype(jnp.float32)
-    residue = (2.0 * eye - inverse * matrix).astype(jnp.bfloat16).astype(jnp.float32)
-    return (inverse * residue).astype(jnp.bfloat16)
+def first_step(energy, inverse, ham, pair, eye):
+    square = inverse * inverse
+    return (
+        (square * inverse) * pair.astype(jnp.float32) + square * ham + (2.0 * inverse - square * energy) * eye
+    ).astype(jnp.bfloat16)
 
 
 def linked(green, link):
@@ -125,13 +133,17 @@
     for i in range(4):
         place_halves(at_ref[0], whole.at[i], mine_refs[i][...], theirs_refs[i][...])
     odd = lax.rem(at_ref[1], 2)
+    turn = BROAD * rotate
+    ham = ham_ref[...].astype(jnp.float32) - turn
+    ham_above = whole[0].astype(jnp.float32) - turn
+    ham_below = whole[1].astype(jnp.float32) - turn
     for e, same_ref in ((odd, first_ref), (1 - odd, second_ref)):
         energy, inverse = energy_ref[e], inverse_ref[e]
-        above = first_step(energy, inverse * edge_ref[0], whole[0], whole[2], eye, rotate)
-        below = first_step(energy, inverse * edge_ref[1], whole[1], whole[3], eye, rotate)
-        green = first_step(energy, inverse, ham_ref[...], pair_ref[...], eye, rotate)
-        base = energy * eye + BROAD * rotate - ham_ref[...].astype(jnp.float32)
-        matrix = (base - linked(above, c_ref[...]) - linked(below, lower_turned_ref[...])).astype(jnp.bfloat16)
+        above = first_step(energy, inverse * edge_ref[0], ham_above, whole[2], eye)
+        below = first_step(energy, inverse * edge_ref[1], ham_below, whole[3], eye)
+        green = first_step(energy, inverse, ham, pair_ref[...], eye)
+        terms = linked(above, c_ref[...]) + linked(below, lower_turned_ref[...])
+        matrix = (energy * eye - ham - terms).astype(jnp.bfloat16)
         result = finish(matrix, green, eye).astype(jnp.bfloat16)
         out_ref[:, e] = result.reshape(chunks, n // chunks, n)
         same_ref[...] = result
@@ -210,23 +222,25 @@
     give_ref[...] = scratch[:, 1 - core]
 
 
-def inner_body(
-    at_ref, energy_ref, energy_pair_ref, outer_ham, inner_ham, mid, mid_turned, near, mine_ref, theirs_ref, outer, inner, beside,
-    open_outer, whole_ref, keep_ref, give_ref, scratch,
+def part_body(
+    at_ref, energy_ref, energy_pair_ref, outer_ham, inner_ham, mid, mid_turned, mine_ref, theirs_ref, outer, inner,
+    open_outer, open_inner, scratch,
 ):
     core = at_ref[0]
     eye, rotate = tables(outer.shape[0])
     base = row_energy(at_ref, energy_ref, energy_pair_ref) * eye + BROAD * rotate
     self_part = joined_rows(core, 1 - core, mine_ref, theirs_ref, scratch)
-    matrix = (
-        base - inner_ham[...].astype(jnp.float32) - self_part - linked(outer[...], mid_turned[...])
-        - linked(beside[...], near[...])
-    ).astype(jnp.bfloat16)
+    open_inner[...] = base - inner_ham[...].astype(jnp.float32) - self_part - linked(outer[...], mid_turned[...])
+    self_part = joined_rows(core, core, mine_ref, theirs_ref, scratch)
+    open_outer[...] = base - outer_ham[...].astype(jnp.float32) - self_part - linked(inner[...], mid[...])
+
+
+def inner_body(at_ref, near, open_ref, inner, beside, whole_ref, keep_ref, give_ref, scratch):
+    eye, _ = tables(inner.shape[0])
+    matrix = (open_ref[...] - linked(beside[...], near[...])).astype(jnp.bfloat16)
     result = finish(matrix, inner[...], eye).astype(jnp.bfloat16)
     whole_ref[...] = result
-    split_rows(core, result, keep_ref, give_ref, scratch)
-    self_part = joined_rows(core, core, mine_ref, theirs_ref, scratch)
-    open_outer[...] = base - outer_ham[...].astype(jnp.float32) - self_part - linked(inner[...], mid[...])
+    split_rows(at_ref[0], result, keep_ref, give_ref, scratch)
 
 
 def outer_body(
@@ -245,39 +259,41 @@
     out_ref[3 - 3 * core] = got_inner[...]
 
 
-def spread_body(at_ref, first_ref, second_ref, out_ref):
-    odd = lax.rem(at_ref[1], 2)
-    out_ref[odd] = first_ref[...].astype(jnp.float32)
-    out_ref[1 - odd] = second_ref[...].astype(jnp.float32)
-
-
-def energy_body(place_in, place_out, offset_ref, green_ref, coulomb_ref, out_ref, padded, wide):
+def spread_body(at_ref, inner_0, inner_1, outer_0, outer_1, out_ref):
+    within = jnp.logical_and(at_ref[1] > 0, at_ref[1] < WIDTH - 1)
+    out_ref[0] = jnp.where(within, inner_0[...], outer_0[...]).astype(jnp.float32)
+    out_ref[1] = jnp.where(within, inner_1[...], outer_1[...]).astype(jnp.float32)
+
+
+def energy_body(place_in, place_out, offset_ref, green_ref, coulomb_ref, out_ref, padded):
     count, rows, columns = green_ref.shape
     offset_count = offset_ref.shape[0]
-    none = jnp.zeros((REACH, rows, columns), jnp.float32)
+    none = jnp.zeros((REACH, 8, 128), jnp.float32)
     padded[:REACH] = none
     padded[REACH + count :] = none
-    for e in range(count):
-        padded[REACH + e] = green_ref[place_in[e]].astype(jnp.float32)
-    wide[...] = coulomb_ref[...].astype(jnp.float32)
     column_tiles = columns // 128
 
     def tile(t, carry):
         row = pl.ds(pl.multiple_of(8 * (t // column_tiles), 8), 8)
         column = pl.ds(pl.multiple_of(128 * (t % column_tiles), 128), 128)
-        strength = wide[row, column]
-        own = padded[REACH : REACH + count, row, column]
-        total = jnp.zeros(own.shape, jnp.float32)
+        strength = coulomb_ref[row, column].astype(jnp.float32)
+        own = [green_ref[place_in[e], row, column].astype(jnp.float32) for e in range(count)]
+        for e in range(count):
+            padded[REACH + e] = own[e]
         screened = []
         for k in range(offset_count):
-            later = padded[pl.ds(REACH + offset_ref[k], count), row, column]
-            polarization = (4.0 / count) * jnp.sum(own * later, axis=0)
+            later = padded.at[pl.ds(REACH + offset_ref[k], count)]
+            sums = [own[e] * later[e] for e in range(4)]
+            for e in range(4, count):
+                sums[e % 4] = sums[e % 4] + own[e] * later[e]
+            polarization = (4.0 / count) * ((sums[0] + sums[1]) + (sums[2] + sums[3]))
             screened.append(strength * (1.0 + polarization * strength) * (1.0 / offset_count))
-        for k in range(offset_count):
-            total = total + screened[k][None] * padded[pl.ds(REACH - offset_ref[k], count), row, column]
-        total = total.astype(jnp.bfloat16)
+        earlier = [padded.at[pl.ds(REACH - offset_ref[k], count)] for k in range(offset_count)]
         for e in range(count):
-            out_ref[place_out[e], row, column] = total[e]
+            terms = [screened[k] * earlier[k][e] for k in range(offset_count)]
+            while len(terms) > 1:
+                terms = [a + b for a, b in zip(terms[::2], terms[1::2])] + terms[len(terms) // 2 * 2 :]
+            out_ref[place_out[e], row, column] = terms[0].astype(jnp.bfloat16)
         return carry
 
     lax.fori_loop(0, (rows // 8) * column_tiles, tile, 0)
@@ -289,7 +305,7 @@
         functools.partial(energy_body, place_in, place_out),
         jax.ShapeDtypeStruct((count, rows, columns), jnp.bfloat16),
         [SM, VM, VM],
-        [pltpu.VMEM((count + 2 * REACH, rows, columns), jnp.float32), pltpu.VMEM((rows, columns), jnp.float32)],
+        [pltpu.VMEM((count + 2 * REACH, 8, 128), jnp.float32)],
     )(offsets, received, coulomb)
 
 
@@ -368,11 +384,15 @@
     beyond = row_above(outer, True)
     inner = third(True, open_inner, inner)
     beside = swapped(inner)
-    open_outer, whole_inner, keep_inner, give_inner = run(
-        inner_body, (wide(n, n), thin(n, n), thin(pairs, rows, n), thin(pairs, rows, n)),
-        [SM] * 3 + [VM] * 10, at, energies, energy_pair, outer_ham, inner_ham, mid, mid_turned, near, self_mine,
-        self_theirs, outer, inner, beside, scratch=mix,
-    )
+    open_outer, open_inner = run(
+        part_body, (wide(n, n), wide(n, n)), [SM] * 3 + [VM] * 8, at, energies, energy_pair,
+        outer_ham, inner_ham, mid, mid_turned, self_mine, self_theirs, outer, inner, scratch=mix,
+    )
+    whole_inner, keep_inner, give_inner = run(
+        inner_body, (thin(n, n), thin(pairs, rows, n), thin(pairs, rows, n)), [SM] + [VM] * 4,
+        at, near, open_inner, inner, beside, scratch=mix,
+    )
+    back_inner = [returned(whole_inner, True, slot) for slot in range(2)]
     got_inner = swapped(give_inner)
     whole_outer, chunks, give_outer = run(
         outer_body, (thin(n, n), thin(WIDTH, pairs, rows, n), thin(pairs, rows, n)), [SM] + [VM] * 6,
@@ -381,11 +401,10 @@
     got_outer = swapped(give_outer)
     chunks = lax.dynamic_update_slice_in_dim(chunks, got_outer[None], 3 - 3 * core, 0)
     received = all_to_all(chunks.reshape(count, rows, n), ("x", "zlo", "y"))
-    first, second = run(role_body, (thin(n, n),) * 2, [SM, VM, VM], at, whole_outer, whole_inner)
-    first, second = flipped(first, 0), flipped(second, 1)
+    back_outer = [returned(whole_outer, False, slot) for slot in range(2)]
     result = convolved(received, strength, offsets, by_chip, natural)
     self_part = all_to_all(result.reshape(parts, 2, rows, n), ENERGY)
-    green = run(spread_body, wide(2, n, n), [SM, VM, VM], at, first, second)
+    green = run(spread_body, wide(2, n, n), [SM] + [VM] * 4, at, *back_inner, *back_outer)
     self_part = jnp.swapaxes(self_part, 0, 1).reshape(2, n, n)
     return (green[:, None], self_part[:, None])
 

time: 284 us -> 258 us (0.908)
  Pallas kernels: 70.3 us -> 39.7 us
  starting transfers between devices: 75.7 us -> 84.6 us
  local copies, waits for them, and re-layouts: 12.1 us -> 7.09 us
    pallas_call x13, Pallas kernels: 53.5 us -> 30 us  [run(): return call(body, out_shape, in_specs, scratch)(*operands)]
    ppermute x4 -> x2, waiting for transfers between devices: 17.6 us -> 4.75 us  [flipped(): return lax.ppermute(value, ('core', 'x'), pairs)]
    ppermute x0 -> x4, starting transfers between devices: none -> 11.3 us  [returned(): return lax.ppermute(value, ('core', 'x'), pairs)]
    ppermute x0 -> x4, waiting for transfers between devices: none -> 10.5 us  [returned(): return lax.ppermute(value, ('core', 'x'), pairs)]
    pallas_call x2, Pallas kernels: 16.8 us -> 9.72 us  [convolved(): call(functools.partial(energy_body, place_in, place_out), jax.ShapeDtypeS...]
    ppermute x4 -> x2, starting transfers between devices: 8.81 us -> 3.99 us  [flipped(): return lax.ppermute(value, ('core', 'x'), pairs)]
    ppermute x3, waiting for transfers between devices: 3.31 us -> 7.99 us  [row_above(): return lax.ppermute(value, ('core', 'row'), pairs)]
    unnamed x58 -> x20, local copies, waits for them, and re-layouts: 8.27 us -> 3.98 us
  transfers between devices with their start and end apart: 29 -> 31, of which waited for: 13 -> 12; matrix products, arithmetic and copies ran while one was open for 1% -> 0% of each run, Pallas kernels for 13% -> 8%
where the time goes in v5:
time: 258 us; the launch traced here: 254 us
  starting transfers between devices  84.6 us (33%)
  waiting for transfers between devices  75.3 us (29%)
  blocking collectives  45.9 us (18%)
  Pallas kernels  39.7 us (15%)
  local copies, waits for them, and re-layouts  7.09 us (3%)
    all_to_all x2, blocking collectives, all_to_all(): return lax.all_to_all(value, axes, split_axis=0, concat_axis=0, tiled=True)  45.9 us
    ppermute x3, waiting for transfers between devices, row_ring(): lax.ppermute(value, 'x', [(s, (s + steps) % WIDTH) for s in range(WIDTH)])  30.1 us
    pallas_call x13, Pallas kernels, run(): return call(body, out_shape, in_specs, scratch)(*operands)  30 us
    ppermute x5, starting transfers between devices, passed_along(): lax.ppermute(value, SLAB, [(source, source + steps) for source in range(l...  26.9 us
    ppermute x12, starting transfers between devices, swapped(): return lax.ppermute(value, 'core', [(0, 1), (1, 0)])  23.5 us
    ppermute x5, waiting for transfers between devices, passed_along(): lax.ppermute(value, SLAB, [(source, source + steps) for source in range(l...  19.4 us
    ppermute x4, starting transfers between devices, returned(): return lax.ppermute(value, ('core', 'x'), pairs)  11.3 us
    ppermute x4, waiting for transfers between devices, returned(): return lax.ppermute(value, ('core', 'x'), pairs)  10.5 us
  transfers between devices with their start and end apart: 31, of which 12 were waited for; matrix products, arithmetic and copies ran while one was open for 0% of the time, Pallas kernels for 8%

profile of v5, /device:TPU:70, one launch (start us, length us, event | category | flops | bytes accessed | tf_op | source)
XLA Modules:
  0.0 253.7 jit_solution(5132799400971196721)
XLA Ops:
  0.7 1.1 dynamic-slice_bitcast_fusion.1
  1.7 6.3 %collective-permute-start.6 = (bf16[256,512]{1,0:T(8,128)(2,1)S(1)}, bf16[256,512]{1,0:T(8,128)(2,1)S(1)}, u32[]{:S(2)}, u32[]{:S(2)}) collective-permute-start(bf16[256,512]{1,0:T(8,128)(2,1)S(1)} %dynamic-slice_bitcast_fusion.1), channel_id=1, source_target_pairs={{0,1},{1,2},{2,3},{3,4},{4,5},{5,6},{6,7},{7,8},{8,9},{9,10},{10,1... | collective-permute-start | bytes 786440 | tf_op jit(solution)/shard_map/ppermute | solution.py:26
  8.0 11.1 %collective-permute-done.6.mine_ref = bf16[256,512]{1,0:T(8,128)(2,1)S(1)} collective-permute-done((bf16[256,512]{1,0:T(8,128)(2,1)S(1)}, bf16[256,512]{1,0:T(8,128)(2,1)S(1)}, u32[]{:S(2)}, u32[]{:S(2)}) %collective-permute-start.6) | collective-permute-done | bytes 262176 | tf_op jit(solution)/shard_map/ppermute | solution.py:26
  19.1 1.0 dynamic-slice_bitcast_fusion
  20.1 1.9 collective-permute-start.8
  22.0 8.6 %collective-permute-start.9 = (bf16[256,512]{1,0:T(8,128)(2,1)S(1)}, bf16[256,512]{1,0:T(8,128)(2,1)S(1)}, u32[]{:S(2)}, u32[]{:S(2)}) collective-permute-start(bf16[256,512]{1,0:T(8,128)(2,1)S(1)} %dynamic-slice_bitcast_fusion), channel_id=1, source_target_pairs={{0,1},{1,2},{2,3},{3,4},{4,5},{5,6},{6,7},{7,8},{8,9},{9,10},{10,1... | collective-permute-start | bytes 786440 | tf_op jit(solution)/shard_map/ppermute | solution.py:26
  30.8 1.0 copy-done
  31.9 1.0 copy-done.2
  32.9 1.0 shard_map.68
  34.0 1.4 shard_map.71
  35.4 1.9 collective-permute-start.10
  37.3 8.1 %collective-permute-start.11 = (bf16[256,512]{1,0:T(8,128)(2,1)S(1)}, bf16[256,512]{1,0:T(8,128)(2,1)S(1)}, u32[]{:S(2)}, u32[]{:S(2)}) collective-permute-start(bf16[256,512]{1,0:T(8,128)(2,1)S(1)} %get-tuple-element.43), channel_id=1, source_target_pairs={{0,1},{1,2},{2,3},{3,4},{4,5},{5,6},{6,7},{7,8},{8,9},{9,10},{10,1... | collective-permute-start | bytes 786440 | tf_op jit(solution)/shard_map/ppermute | solution.py:26
  45.4 0.1 collective-permute-start.12
  45.6 0.5 collective-permute-start.13
  46.0 8.3 %collective-permute-done.10.refs_2_ = bf16[256,512]{1,0:T(8,128)(2,1)S(1)} collective-permute-done((bf16[256,512]{1,0:T(8,128)(2,1)S(1)}, bf16[256,512]{1,0:T(8,128)(2,1)S(1)}, u32[]{:S(2)}, u32[]{:S(2)}) %collective-permute-start.10) | collective-permute-done | bytes 262176 | tf_op jit(solution)/shard_map/ppermute | solution.py:26
  54.4 0.5 collective-permute-start.15
  54.9 1.0 collective-permute-done.14.refs_6_
  55.9 0.4 collective-permute-done.15.refs_7_
  56.2 5.6 %shard_map.72 = (bf16[16,2,32,512]{3,2,1,0:T(8,128)(2,1)S(1)}, bf16[512,512]{1,0:T(8,128)(2,1)}, bf16[512,512]{1,0:T(8,128)(2,1)}) custom-call(f32[2]{0:T(128)S(1)} %copy-done.7, f32[2]{0:T(128)S(1)} %convert_convert_fusion.inverse_ref, f32[2]{0:T(128)S(1)} %add_convert_fusion.edge_ref, s32[2]{0:T(128)S(1)} %pad_add_fusion.at_ref, ...), custom_call_target="tpu_custom_call" | custom-call | tf_op jit(solution)/shard_map/pallas_call | solution.py:333
  61.9 21.6 %all_to_all.20 = bf16[16,2,32,512]{3,2,1,0:T(8,128)(2,1)S(1)} all-to-all(bf16[16,2,32,512]{3,2,1,0:T(8,128)(2,1)S(1)} %get-tuple-element.44), channel_id=1, replica_groups=mesh['zlo'=2,'y'=4,'core'=2,'row'=4,'x'=4] {'zlo','y','core'}, dimensions={0} | all-to-all | bytes 2097152 | tf_op jit(solution)/shard_map/all_to_all | solution.py:313
  83.5 4.9 %shard_map.73 = bf16[32,32,512]{2,1,0:T(8,128)(2,1)} custom-call(s32[8]{0:T(128)S(1)} %copy-done.8, bf16[32,32,512]{2,1,0:T(8,128)(2,1)S(1)} %bitcast.27, bf16[32,512]{1,0:T(8,128)(2,1)S(1)} %bitcast.33), custom_call_target="tpu_custom_call" | custom-call | tf_op jit(solution)/shard_map/pallas_call | solution.py:304
  88.4 5.6 %all-to-all-start.1 = ((bf16[32,32,512]{2,1,0:T(8,128)(2,1)}), bf16[32,32,512]{2,1,0:T(8,128)(2,1)S(1)}, u32[]{:S(2)}, u32[]{:S(2)}) async-start(bf16[32,32,512]{2,1,0:T(8,128)(2,1)} %shard_map.73), calls=%async_computation.1 | async-start | bytes 2097152 | tf_op jit(solution)/shard_map/all_to_all | solution.py:313
  93.9 0.3 collective-permute-start
  94.2 1.8 collective-permute-start.2
  96.0 21.7 %collective-permute-done.one_ref = bf16[512,512]{1,0:T(8,128)(2,1)S(1)} collective-permute-done((bf16[512,512]{1,0:T(8,128)(2,1)S(1)}, bf16[512,512]{1,0:T(8,128)(2,1)S(1)}, u32[]{:S(2)}, u32[]{:S(2)}) %collective-permute-start) | collective-permute-done | bytes 524320 | tf_op jit(solution)/shard_map/ppermute | solution.py:30
  117.7 2.4 collective-permute-start.1
  120.1 1.9 collective-permute-start.17
  122.1 2.1 collective-permute-start.18
  124.1 8.4 %collective-permute-done.1.two_ref = bf16[512,512]{1,0:T(8,128)(2,1)S(1)} collective-permute-done((bf16[512,512]{1,0:T(8,128)(2,1)S(1)}, bf16[512,512]{1,0:T(8,128)(2,1)S(1)}, u32[]{:S(2)}, u32[]{:S(2)}) %collective-permute-start.1) | collective-permute-done | bytes 524320 | tf_op jit(solution)/shard_map/ppermute | solution.py:30
  132.5 1.0 copy-done.5
  133.6 1.8 shard_map.69
  135.3 0.8 copy-done.9
  136.1 1.3 collective-permute-start.4
  137.4 4.8 %collective-permute-done.18.second_ref = bf16[512,512]{1,0:T(8,128)(2,1)} collective-permute-done((bf16[512,512]{1,0:T(8,128)(2,1)}, bf16[512,512]{1,0:T(8,128)(2,1)}, u32[]{:S(2)}, u32[]{:S(2)}) %collective-permute-start.18) | collective-permute-done | bytes 524320 | tf_op jit(solution)/shard_map/ppermute | solution.py:47
  142.2 2.2 shard_map.74
  144.4 1.9 collective-permute-start.19
  146.4 4.9 %collective-permute-start.20 = (bf16[512,512]{1,0:T(8,128)(2,1)}, bf16[512,512]{1,0:T(8,128)(2,1)}, u32[]{:S(2)}, u32[]{:S(2)}) collective-permute-start(bf16[512,512]{1,0:T(8,128)(2,1)} %get-tuple-element.49.inner.green_ref), channel_id=1, source_target_pairs={{0,16},{16,0},{1,17},{17,1},{2,18},{18,2},{3,19},{19,3},{4,20},{20... | collective-permute-start | bytes 1572872 | tf_op jit(solution)/shard_map/ppermute | solution.py:34
  151.3 0.1 collective-permute-start.16
  151.4 0.8 collective-permute-start.5
  152.2 1.8 shard_map.70
  154.0 5.0 %collective-permute-done.19.beyond = bf16[512,512]{1,0:T(8,128)(2,1)} collective-permute-done((bf16[512,512]{1,0:T(8,128)(2,1)}, bf16[512,512]{1,0:T(8,128)(2,1)}, u32[]{:S(2)}, u32[]{:S(2)}) %collective-permute-start.19) | collective-permute-done | bytes 524320 | tf_op jit(solution)/shard_map/ppermute | solution.py:42
  159.0 4.3 %shard_map.75 = (f32[512,512]{1,0:T(8,128)S(1)}, f32[512,512]{1,0:T(8,128)S(1)}) custom-call(s32[2]{0:T(128)S(1)} %pad_add_fusion.at_ref, f32[2]{0:T(128)S(1)} %copy-done.7, f32[2]{0:T(128)S(1)} %collective-permute-done.5.energy_pair_ref, bf16[512,512]{1,0:T(8,128)(2,1)S(1)} %get-tuple-element.36.outer_ham, ...), custom_call_target="tpu_custom_call" | custom-call | tf_op jit(solution)/shard_map/pallas_call | solution.py:333
  163.3 1.9 shard_map.77.inner
  165.2 7.4 %collective-permute-start.21 = (bf16[512,512]{1,0:T(8,128)(2,1)S(1)}, bf16[512,512]{1,0:T(8,128)(2,1)S(1)}, u32[]{:S(2)}, u32[]{:S(2)}) collective-permute-start(bf16[512,512]{1,0:T(8,128)(2,1)S(1)} %shard_map.77.inner), channel_id=1, source_target_pairs={{0,16},{16,0},{1,17},{17,1},{2,18},{18,2},{3,19},{19,3},{4,20},{20... | collective-permute-start | bytes 1572872 | tf_op jit(solution)/shard_map/ppermute | solution.py:34
  172.5 1.9 shard_map.76.outer
  174.4 1.9 collective-permute-start.24
  176.3 2.1 shard_map.78
  178.4 2.0 shard_map.79
  180.4 4.7 %collective-permute-start.25 = (bf16[8,32,512]{2,1,0:T(8,128)(2,1)S(1)}, bf16[8,32,512]{2,1,0:T(8,128)(2,1)S(1)}, u32[]{:S(2)}, u32[]{:S(2)}) collective-permute-start(bf16[8,32,512]{2,1,0:T(8,128)(2,1)S(1)} %get-tuple-element.56), channel_id=1, source_target_pairs={{0,16},{16,0},{1,17},{17,1},{2,18},{18,2},{3,19},{19,3},{4,20},{20... | collective-permute-start | bytes 786440 | tf_op jit(solution)/shard_map/ppermute | solution.py:34
  185.1 3.0 %collective-permute-done.24.beyond = bf16[512,512]{1,0:T(8,128)(2,1)S(1)} collective-permute-done((bf16[512,512]{1,0:T(8,128)(2,1)S(1)}, bf16[512,512]{1,0:T(8,128)(2,1)S(1)}, u32[]{:S(2)}, u32[]{:S(2)}) %collective-permute-start.24) | collective-permute-done | bytes 524320 | tf_op jit(solution)/shard_map/ppermute | solution.py:42
  188.1 2.1 shard_map.80
  190.2 4.6 %collective-permute-start.28 = (bf16[8,32,512]{2,1,0:T(8,128)(2,1)S(1)}, bf16[8,32,512]{2,1,0:T(8,128)(2,1)S(1)}, u32[]{:S(2)}, u32[]{:S(2)}) collective-permute-start(bf16[8,32,512]{2,1,0:T(8,128)(2,1)S(1)} %get-tuple-element.59), channel_id=1, source_target_pairs={{0,16},{16,0},{1,17},{17,1},{2,18},{18,2},{3,19},{19,3},{4,20},{20... | collective-permute-start | bytes 786440 | tf_op jit(solution)/shard_map/ppermute | solution.py:34
  194.8 1.2 collective-permute-done.28
  196.0 24.3 %all_to_all.21.green_ref = bf16[32,32,512]{2,1,0:T(8,128)(2,1)S(1)} all-to-all(bf16[32,32,512]{2,1,0:T(8,128)(2,1)S(1)} %bitcast.32), channel_id=1, replica_groups=mesh['zlo'=2,'y'=4,'core'=2,'row'=4,'x'=4] {'x','zlo','y'}, dimensions={0} | all-to-all | bytes 2097152 | tf_op jit(solution)/shard_map/all_to_all | solution.py:313
  220.2 4.9 %shard_map.82 = bf16[32,32,512]{2,1,0:T(8,128)(2,1)} custom-call(s32[8]{0:T(128)S(1)} %copy-done.8, bf16[32,32,512]{2,1,0:T(8,128)(2,1)S(1)} %all_to_all.21.green_ref, bf16[32,512]{1,0:T(8,128)(2,1)S(1)} %bitcast.34), custom_call_target="tpu_custom_call" | custom-call | tf_op jit(solution)/shard_map/pallas_call | solution.py:304
  225.1 3.7 %all-to-all-start.3 = ((bf16[16,2,32,512]{3,2,1,0:T(8,128)(2,1)}), bf16[16,2,32,512]{3,2,1,0:T(8,128)(2,1)S(1)}, u32[]{:S(2)}, u32[]{:S(2)}) async-start(bf16[16,2,32,512]{3,2,1,0:T(8,128)(2,1)} %bitcast.15), calls=%async_computation.3 | async-start | bytes 2097152 | tf_op jit(solution)/shard_map/all_to_all | solution.py:313
  228.8 0.7 collective-permute-start.22
  229.5 3.9 %collective-permute-start.23 = (bf16[512,512]{1,0:T(8,128)(2,1)S(1)}, bf16[512,512]{1,0:T(8,128)(2,1)S(1)}, u32[]{:S(2)}, u32[]{:S(2)}) collective-permute-start(bf16[512,512]{1,0:T(8,128)(2,1)S(1)} %get-tuple-element.53), channel_id=1, source_target_pairs={{1,1},{3,17},{17,2},{19,18},{5,5},{7,21},{21,6},{23,22},{9,9},{11,... | collective-permute-start | bytes 1572872 | tf_op jit(solution)/shard_map/ppermute | solution.py:88
  233.3 1.3 collective-permute-start.26
  234.6 5.5 %collective-permute-start.27 = (bf16[512,512]{1,0:T(8,128)(2,1)S(1)}, bf16[512,512]{1,0:T(8,128)(2,1)S(1)}, u32[]{:S(2)}, u32[]{:S(2)}) collective-permute-start(bf16[512,512]{1,0:T(8,128)(2,1)S(1)} %get-tuple-element.57), channel_id=1, source_target_pairs={{1,0},{3,16},{17,3},{19,19},{5,4},{7,20},{21,7},{23,23},{9,8},{11,... | collective-permute-start | bytes 1572872 | tf_op jit(solution)/shard_map/ppermute | solution.py:88
  240.1 3.3 %collective-permute-done.23.inner_1 = bf16[512,512]{1,0:T(8,128)(2,1)S(1)} collective-permute-done((bf16[512,512]{1,0:T(8,128)(2,1)S(1)}, bf16[512,512]{1,0:T(8,128)(2,1)S(1)}, u32[]{:S(2)}, u32[]{:S(2)}) %collective-permute-start.23) | collective-permute-done | bytes 524320 | tf_op jit(solution)/shard_map/ppermute | solution.py:88
  243.4 7.2 %collective-permute-done.26.outer_0 = bf16[512,512]{1,0:T(8,128)(2,1)S(1)} collective-permute-done((bf16[512,512]{1,0:T(8,128)(2,1)S(1)}, bf16[512,512]{1,0:T(8,128)(2,1)S(1)}, u32[]{:S(2)}, u32[]{:S(2)}) %collective-permute-start.26) | collective-permute-done | bytes 524320 | tf_op jit(solution)/shard_map/ppermute | solution.py:88
  250.7 2.0 shard_map.81
  252.7 1.0 copy.7
  (43 shorter events, 0.3 us)
Async XLA Ops:
  0.6 55.6 %copy-start.1 = (bf16[1,512,512]{2,1,0:T(8,128)(2,1)S(1)}, bf16[1,512,512]{2,1,0:T(8,128)(2,1)}, u32[]{:S(2)}) copy-start(bf16[1,512,512]{2,1,0:T(8,128)(2,1)} %param.7) | copy-start | bytes 1572868
  0.6 55.6 %copy-start.3 = (bf16[1,512,512]{2,1,0:T(8,128)(2,1)S(1)}, bf16[1,512,512]{2,1,0:T(8,128)(2,1)}, u32[]{:S(2)}) copy-start(bf16[1,512,512]{2,1,0:T(8,128)(2,1)} %param.6) | copy-start | bytes 1572868
  0.7 54.2 %copy-start.7 = (f32[2]{0:T(128)S(1)}, f32[2]{0:T(128)}, u32[]{:S(2)}) copy-start(f32[2]{0:T(128)} %energy_ref.5) | copy-start | bytes 28
  1.7 17.4 %collective-permute-start.6 = (bf16[256,512]{1,0:T(8,128)(2,1)S(1)}, bf16[256,512]{1,0:T(8,128)(2,1)S(1)}, u32[]{:S(2)}, u32[]{:S(2)}) collective-permute-start(bf16[256,512]{1,0:T(8,128)(2,1)S(1)} %dynamic-slice_bitcast_fusion.1), channel_id=1, source_target_pairs={{0,1},{1,2},{2,3},{3,4},{4,5},{5,6},{6,7},{7,8},{8,9},{9,10},{10,1... | collective-permute-start | bytes 786440 | tf_op jit(solution)/shard_map/ppermute | solution.py:26
  19.1 14.8 %collective-permute-start.7 = (bf16[256,512]{1,0:T(8,128)(2,1)S(1)}, bf16[256,512]{1,0:T(8,128)(2,1)S(1)}, u32[]{:S(2)}, u32[]{:S(2)}) collective-permute-start(bf16[256,512]{1,0:T(8,128)(2,1)S(1)} %collective-permute-done.6.mine_ref), channel_id=1, source_target_pairs={{0,16},{16,0},{1,17},{17,1},{2,18},{18,2},{3,19},{19,3},{4,20},{20... | collective-permute-start | bytes 786440 | tf_op jit(solution)/shard_map/ppermute | solution.py:34
  20.1 25.3 %collective-permute-start.8 = (bf16[256,512]{1,0:T(8,128)(2,1)S(1)}, bf16[256,512]{1,0:T(8,128)(2,1)S(1)}, u32[]{:S(2)}, u32[]{:S(2)}) collective-permute-start(bf16[256,512]{1,0:T(8,128)(2,1)S(1)} %dynamic-slice_bitcast_fusion), channel_id=1, source_target_pairs={{1,0},{2,1},{3,2},{4,3},{5,4},{6,5},{7,6},{8,7},{9,8},{10,9},{11,1... | collective-permute-start | bytes 786440 | tf_op jit(solution)/shard_map/ppermute | solution.py:26
  22.0 23.5 %collective-permute-start.9 = (bf16[256,512]{1,0:T(8,128)(2,1)S(1)}, bf16[256,512]{1,0:T(8,128)(2,1)S(1)}, u32[]{:S(2)}, u32[]{:S(2)}) collective-permute-start(bf16[256,512]{1,0:T(8,128)(2,1)S(1)} %dynamic-slice_bitcast_fusion), channel_id=1, source_target_pairs={{0,1},{1,2},{2,3},{3,4},{4,5},{5,6},{6,7},{7,8},{8,9},{9,10},{10,1... | collective-permute-start | bytes 786440 | tf_op jit(solution)/shard_map/ppermute | solution.py:26
  30.8 1.0 copy-start
  31.9 1.0 copy-start.2
  34.0 60.2 %copy-start.4 = (bf16[512,512]{1,0:T(8,128)(2,1)}, bf16[512,512]{1,0:T(8,128)(2,1)S(1)}, u32[]{:S(2)}) copy-start(bf16[512,512]{1,0:T(8,128)(2,1)S(1)} %get-tuple-element.31.here_ref) | copy-start | bytes 1572868
  35.4 19.0 %collective-permute-start.10 = (bf16[256,512]{1,0:T(8,128)(2,1)S(1)}, bf16[256,512]{1,0:T(8,128)(2,1)S(1)}, u32[]{:S(2)}, u32[]{:S(2)}) collective-permute-start(bf16[256,512]{1,0:T(8,128)(2,1)S(1)} %get-tuple-element.43), channel_id=1, source_target_pairs={{1,0},{2,1},{3,2},{4,3},{5,4},{6,5},{7,6},{8,7},{9,8},{10,9},{11,1... | collective-permute-start | bytes 786440 | tf_op jit(solution)/shard_map/ppermute | solution.py:26
  37.3 17.1 %collective-permute-start.11 = (bf16[256,512]{1,0:T(8,128)(2,1)S(1)}, bf16[256,512]{1,0:T(8,128)(2,1)S(1)}, u32[]{:S(2)}, u32[]{:S(2)}) collective-permute-start(bf16[256,512]{1,0:T(8,128)(2,1)S(1)} %get-tuple-element.43), channel_id=1, source_target_pairs={{0,1},{1,2},{2,3},{3,4},{4,5},{5,6},{6,7},{7,8},{8,9},{9,10},{10,1... | collective-permute-start | bytes 786440 | tf_op jit(solution)/shard_map/ppermute | solution.py:26
  45.4 9.4 %collective-permute-start.12 = (bf16[256,512]{1,0:T(8,128)(2,1)S(1)}, bf16[256,512]{1,0:T(8,128)(2,1)S(1)}, u32[]{:S(2)}, u32[]{:S(2)}) collective-permute-start(bf16[256,512]{1,0:T(8,128)(2,1)S(1)} %collective-permute-done.8.refs_0_), channel_id=1, source_target_pairs={{0,16},{16,0},{1,17},{17,1},{2,18},{18,2},{3,19},{19,3},{4,20},{20... | collective-permute-start | bytes 786440 | tf_op jit(solution)/shard_map/ppermute | solution.py:34
  45.6 9.3 %collective-permute-start.13 = (bf16[256,512]{1,0:T(8,128)(2,1)S(1)}, bf16[256,512]{1,0:T(8,128)(2,1)S(1)}, u32[]{:S(2)}, u32[]{:S(2)}) collective-permute-start(bf16[256,512]{1,0:T(8,128)(2,1)S(1)} %collective-permute-done.9.refs_1_), channel_id=1, source_target_pairs={{0,16},{16,0},{1,17},{17,1},{2,18},{18,2},{3,19},{19,3},{4,20},{20... | collective-permute-start | bytes 786440 | tf_op jit(solution)/shard_map/ppermute | solution.py:34
  54.3 1.5 collective-permute-start.14
  54.4 1.9 collective-permute-start.15
  61.9 21.6 %copy-start.6 = (bf16[1,32,512]{2,1,0:T(8,128)(2,1)S(1)}, bf16[1,32,512]{2,1,0:T(8,128)(2,1)}, u32[]{:S(2)}) copy-start(bf16[1,32,512]{2,1,0:T(8,128)(2,1)} %param.8) | copy-start | bytes 98308
  61.9 21.6 %copy-start.8 = (s32[8]{0:T(128)S(1)}, s32[8]{0:T(128)}, u32[]{:S(2)}) copy-start(s32[8]{0:T(128)} %offset_ref.3) | copy-start | bytes 100
  88.4 62.9 %all-to-all-start.1 = ((bf16[32,32,512]{2,1,0:T(8,128)(2,1)}), bf16[32,32,512]{2,1,0:T(8,128)(2,1)S(1)}, u32[]{:S(2)}, u32[]{:S(2)}) async-start(bf16[32,32,512]{2,1,0:T(8,128)(2,1)} %shard_map.73), calls=%async_computation.1 | async-start | bytes 2097152 | tf_op jit(solution)/shard_map/all_to_all | solution.py:313
  93.9 23.8 %collective-permute-start = (bf16[512,512]{1,0:T(8,128)(2,1)S(1)}, bf16[512,512]{1,0:T(8,128)(2,1)S(1)}, u32[]{:S(2)}, u32[]{:S(2)}) collective-permute-start(bf16[512,512]{1,0:T(8,128)(2,1)S(1)} %get-tuple-element.31.here_ref), channel_id=1, source_target_pairs={{0,1},{1,2},{2,3},{3,0},{4,5},{5,6},{6,7},{7,4},{8,9},{9,10},{10,1... | collective-permute-start | bytes 1572872 | tf_op jit(solution)/shard_map/ppermute | solution.py:30
  94.2 29.9 %collective-permute-start.2 = (bf16[512,512]{1,0:T(8,128)(2,1)S(1)}, bf16[512,512]{1,0:T(8,128)(2,1)S(1)}, u32[]{:S(2)}, u32[]{:S(2)}) collective-permute-start(bf16[512,512]{1,0:T(8,128)(2,1)S(1)} %get-tuple-element.31.here_ref), channel_id=1, source_target_pairs={{0,3},{1,0},{2,1},{3,2},{4,7},{5,4},{6,5},{7,6},{8,11},{9,8},{10,9... | collective-permute-start | bytes 1572872 | tf_op jit(solution)/shard_map/ppermute | solution.py:30
  117.7 14.8 %collective-permute-start.1 = (bf16[512,512]{1,0:T(8,128)(2,1)S(1)}, bf16[512,512]{1,0:T(8,128)(2,1)S(1)}, u32[]{:S(2)}, u32[]{:S(2)}) collective-permute-start(bf16[512,512]{1,0:T(8,128)(2,1)S(1)} %collective-permute-done.one_ref), channel_id=1, source_target_pairs={{0,1},{1,2},{2,3},{3,0},{4,5},{5,6},{6,7},{7,4},{8,9},{9,10},{10,1... | collective-permute-start | bytes 1572872 | tf_op jit(solution)/shard_map/ppermute | solution.py:30
  120.1 17.3 %collective-permute-start.17 = (bf16[512,512]{1,0:T(8,128)(2,1)}, bf16[512,512]{1,0:T(8,128)(2,1)}, u32[]{:S(2)}, u32[]{:S(2)}) collective-permute-start(bf16[512,512]{1,0:T(8,128)(2,1)} %get-tuple-element.46), channel_id=1, source_target_pairs={{0,0},{1,1},{2,16},{3,17},{16,2},{17,3},{18,18},{19,19},{4,4},{5,5... | collective-permute-start | bytes 1572872 | tf_op jit(solution)/shard_map/ppermute | solution.py:47
  122.1 20.1 %collective-permute-start.18 = (bf16[512,512]{1,0:T(8,128)(2,1)}, bf16[512,512]{1,0:T(8,128)(2,1)}, u32[]{:S(2)}, u32[]{:S(2)}) collective-permute-start(bf16[512,512]{1,0:T(8,128)(2,1)} %get-tuple-element.47), channel_id=1, source_target_pairs={{0,1},{1,0},{2,17},{3,16},{16,3},{17,2},{18,19},{19,18},{4,5},{5,4... | collective-permute-start | bytes 1572872 | tf_op jit(solution)/shard_map/ppermute | solution.py:47
  132.5 1.0 copy-start.5
  135.3 0.8 copy-start.9
  136.1 16.0 %collective-permute-start.3 = (bf16[2,512,512]{2,1,0:T(8,128)(2,1)}, bf16[2,512,512]{2,1,0:T(8,128)(2,1)}, u32[]{:S(2)}, u32[]{:S(2)}) collective-permute-start(bf16[2,512,512]{2,1,0:T(8,128)(2,1)} %get-tuple-element.33), channel_id=1, source_target_pairs={{0,16},{16,0},{1,17},{17,1},{2,18},{18,2},{3,19},{19,3},{4,20},{20... | collective-permute-start | bytes 3145736 | tf_op jit(solution)/shard_map/ppermute | solution.py:34
  136.1 15.2 %collective-permute-start.4 = (bf16[512,512]{1,0:T(8,128)(2,1)}, bf16[512,512]{1,0:T(8,128)(2,1)}, u32[]{:S(2)}, u32[]{:S(2)}) collective-permute-start(bf16[512,512]{1,0:T(8,128)(2,1)} %copy-done.9), channel_id=1, source_target_pairs={{16,4},{20,8},{24,12},{17,5},{21,9},{25,13},{18,6},{22,10},{26,14}... | collective-permute-start | bytes 1572872 | tf_op jit(solution)/shard_map/ppermute | solution.py:42
  144.4 14.5 %collective-permute-start.19 = (bf16[512,512]{1,0:T(8,128)(2,1)}, bf16[512,512]{1,0:T(8,128)(2,1)}, u32[]{:S(2)}, u32[]{:S(2)}) collective-permute-start(bf16[512,512]{1,0:T(8,128)(2,1)} %get-tuple-element.48.outer.green_ref), channel_id=1, source_target_pairs={{16,4},{20,8},{24,12},{4,16},{8,20},{12,24},{17,5},{21,9},{25,13},... | collective-permute-start | bytes 1572872 | tf_op jit(solution)/shard_map/ppermute | solution.py:42
  146.4 12.6 %collective-permute-start.20 = (bf16[512,512]{1,0:T(8,128)(2,1)}, bf16[512,512]{1,0:T(8,128)(2,1)}, u32[]{:S(2)}, u32[]{:S(2)}) collective-permute-start(bf16[512,512]{1,0:T(8,128)(2,1)} %get-tuple-element.49.inner.green_ref), channel_id=1, source_target_pairs={{0,16},{16,0},{1,17},{17,1},{2,18},{18,2},{3,19},{19,3},{4,20},{20... | collective-permute-start | bytes 1572872 | tf_op jit(solution)/shard_map/ppermute | solution.py:34
  151.3 12.0 %collective-permute-start.16 = (bf16[2,8,32,512]{3,2,1,0:T(8,128)(2,1)S(1)}, bf16[2,8,32,512]{3,2,1,0:T(8,128)(2,1)S(1)}, u32[]{:S(2)}, u32[]{:S(2)}) collective-permute-start(bf16[2,8,32,512]{3,2,1,0:T(8,128)(2,1)S(1)} %constant_dynamic-slice_fusion), channel_id=1, source_target_pairs={{0,16},{16,0},{1,17},{17,1},{2,18},{18,2},{3,19},{19,3},{4,20},{20... | collective-permute-start | bytes 1572872 | tf_op jit(solution)/shard_map/ppermute | solution.py:34
  151.4 2.6 %collective-permute-start.5 = (f32[2]{0:T(128)S(1)}, f32[2]{0:T(128)S(1)}, u32[]{:S(2)}, u32[]{:S(2)}) collective-permute-start(f32[2]{0:T(128)S(1)} %copy-done.7), channel_id=1, source_target_pairs={{0,16},{16,0},{1,17},{17,1},{2,18},{18,2},{3,19},{19,3},{4,20},{20... | collective-permute-start | bytes 32 | tf_op jit(solution)/shard_map/ppermute | solution.py:34
  165.2 13.3 %collective-permute-start.21 = (bf16[512,512]{1,0:T(8,128)(2,1)S(1)}, bf16[512,512]{1,0:T(8,128)(2,1)S(1)}, u32[]{:S(2)}, u32[]{:S(2)}) collective-permute-start(bf16[512,512]{1,0:T(8,128)(2,1)S(1)} %shard_map.77.inner), channel_id=1, source_target_pairs={{0,16},{16,0},{1,17},{17,1},{2,18},{18,2},{3,19},{19,3},{4,20},{20... | collective-permute-start | bytes 1572872 | tf_op jit(solution)/shard_map/ppermute | solution.py:34
  174.4 13.7 %collective-permute-start.24 = (bf16[512,512]{1,0:T(8,128)(2,1)S(1)}, bf16[512,512]{1,0:T(8,128)(2,1)S(1)}, u32[]{:S(2)}, u32[]{:S(2)}) collective-permute-start(bf16[512,512]{1,0:T(8,128)(2,1)S(1)} %shard_map.76.outer), channel_id=1, source_target_pairs={{16,4},{20,8},{24,12},{4,16},{8,20},{12,24},{17,5},{21,9},{25,13},... | collective-permute-start | bytes 1572872 | tf_op jit(solution)/shard_map/ppermute | solution.py:42
  180.4 7.7 %collective-permute-start.25 = (bf16[8,32,512]{2,1,0:T(8,128)(2,1)S(1)}, bf16[8,32,512]{2,1,0:T(8,128)(2,1)S(1)}, u32[]{:S(2)}, u32[]{:S(2)}) collective-permute-start(bf16[8,32,512]{2,1,0:T(8,128)(2,1)S(1)} %get-tuple-element.56), channel_id=1, source_target_pairs={{0,16},{16,0},{1,17},{17,1},{2,18},{18,2},{3,19},{19,3},{4,20},{20... | collective-permute-start | bytes 786440 | tf_op jit(solution)/shard_map/ppermute | solution.py:34
  190.2 5.7 %collective-permute-start.28 = (bf16[8,32,512]{2,1,0:T(8,128)(2,1)S(1)}, bf16[8,32,512]{2,1,0:T(8,128)(2,1)S(1)}, u32[]{:S(2)}, u32[]{:S(2)}) collective-permute-start(bf16[8,32,512]{2,1,0:T(8,128)(2,1)S(1)} %get-tuple-element.59), channel_id=1, source_target_pairs={{0,16},{16,0},{1,17},{17,1},{2,18},{18,2},{3,19},{19,3},{4,20},{20... | collective-permute-start | bytes 786440 | tf_op jit(solution)/shard_map/ppermute | solution.py:34
  225.1 27.6 %all-to-all-start.3 = ((bf16[16,2,32,512]{3,2,1,0:T(8,128)(2,1)}), bf16[16,2,32,512]{3,2,1,0:T(8,128)(2,1)S(1)}, u32[]{:S(2)}, u32[]{:S(2)}) async-start(bf16[16,2,32,512]{3,2,1,0:T(8,128)(2,1)} %bitcast.15), calls=%async_computation.3 | async-start | bytes 2097152 | tf_op jit(solution)/shard_map/all_to_all | solution.py:313
  228.8 11.4 %collective-permute-start.22 = (bf16[512,512]{1,0:T(8,128)(2,1)S(1)}, bf16[512,512]{1,0:T(8,128)(2,1)S(1)}, u32[]{:S(2)}, u32[]{:S(2)}) collective-permute-start(bf16[512,512]{1,0:T(8,128)(2,1)S(1)} %get-tuple-element.53), channel_id=1, source_target_pairs={{0,1},{2,17},{16,2},{18,18},{4,5},{6,21},{20,6},{22,22},{8,9},{10,... | collective-permute-start | bytes 1572872 | tf_op jit(solution)/shard_map/ppermute | solution.py:88
  229.5 14.0 %collective-permute-start.23 = (bf16[512,512]{1,0:T(8,128)(2,1)S(1)}, bf16[512,512]{1,0:T(8,128)(2,1)S(1)}, u32[]{:S(2)}, u32[]{:S(2)}) collective-permute-start(bf16[512,512]{1,0:T(8,128)(2,1)S(1)} %get-tuple-element.53), channel_id=1, source_target_pairs={{1,1},{3,17},{17,2},{19,18},{5,5},{7,21},{21,6},{23,22},{9,9},{11,... | collective-permute-start | bytes 1572872 | tf_op jit(solution)/shard_map/ppermute | solution.py:88
  233.3 17.3 %collective-permute-start.26 = (bf16[512,512]{1,0:T(8,128)(2,1)S(1)}, bf16[512,512]{1,0:T(8,128)(2,1)S(1)}, u32[]{:S(2)}, u32[]{:S(2)}) collective-permute-start(bf16[512,512]{1,0:T(8,128)(2,1)S(1)} %get-tuple-element.57), channel_id=1, source_target_pairs={{0,0},{2,16},{16,3},{18,19},{4,4},{6,20},{20,7},{22,23},{8,8},{10,... | collective-permute-start | bytes 1572872 | tf_op jit(solution)/shard_map/ppermute | solution.py:88
  234.6 16.0 %collective-permute-start.27 = (bf16[512,512]{1,0:T(8,128)(2,1)S(1)}, bf16[512,512]{1,0:T(8,128)(2,1)S(1)}, u32[]{:S(2)}, u32[]{:S(2)}) collective-permute-start(bf16[512,512]{1,0:T(8,128)(2,1)S(1)} %get-tuple-element.57), channel_id=1, source_target_pairs={{1,0},{3,16},{17,3},{19,19},{5,4},{7,20},{21,7},{23,23},{9,8},{11,... | collective-permute-start | bytes 1572872 | tf_op jit(solution)/shard_map/ppermute | solution.py:88

commit v6 on v5

--- a/solution.py
+++ b/solution.py
@@ -34,12 +34,21 @@
     return lax.ppermute(value, "core", [(0, 1), (1, 0)])
 
 
-def row_above(value, both):
+def row_above(value):
     rows = lax.axis_size("row")
-    pairs = [(rows + r, r + 1) for r in range(rows - 1)]
-    if both:
-        pairs += [(r, rows + r - 1) for r in range(1, rows)]
+    pairs = [(rows + r, r + 1) for r in range(rows - 1)] + [(r, rows + r - 1) for r in range(1, rows)]
     return lax.ppermute(value, ("core", "row"), pairs)
+
+
+def climbed(value):
+    rows = lax.axis_size("row")
+    pairs = [(r * WIDTH, (r + 1) * WIDTH) for r in range(rows - 1)]
+    pairs += [(r * WIDTH + WIDTH - 1, r * WIDTH - 1) for r in range(1, rows)]
+    return lax.ppermute(value, ("core", "row", "x"), pairs)
+
+
+def sent(value, pairs):
+    return lax.ppermute(value, ("core", "x"), [(a * WIDTH + i, b * WIDTH + j) for (a, i), (b, j) in pairs])
 
 
 def flipped(value, side):
@@ -122,16 +131,24 @@
     return dot(green, residue)
 
 
+def near_body(at_ref, one_ref, three_ref, climbed_ref, previous_ref, next_ref):
+    first = at_ref[0] == 0
+    previous_ref[...] = jnp.where(jnp.logical_and(first, at_ref[1] == 0), climbed_ref[...], one_ref[...])
+    next_ref[...] = jnp.where(jnp.logical_and(first, at_ref[1] == WIDTH - 1), climbed_ref[...], three_ref[...])
+
+
 def second_body(
-    energy_ref, inverse_ref, edge_ref, at_ref, ham_ref, pair_ref, c_ref, lower_turned_ref, *refs
+    energy_ref, inverse_ref, edge_ref, at_ref, ham_ref, pair_ref, c_ref, lower_turned_ref, previous_ref, next_ref,
+    got_previous_ref, got_next_ref, up_ref, down_ref, got_up_ref, got_down_ref, out_ref, first_ref, second_ref, whole,
 ):
-    mine_refs, theirs_refs = refs[:4], refs[4:8]
-    out_ref, first_ref, second_ref, whole = refs[8:]
     n = c_ref.shape[0]
     eye, rotate = tables(n)
     chunks = out_ref.shape[0]
-    for i in range(4):
-        place_halves(at_ref[0], whole.at[i], mine_refs[i][...], theirs_refs[i][...])
+    first = at_ref[0] == 0
+    whole[0] = jnp.where(first, next_ref[...], got_next_ref[...])
+    whole[1] = jnp.where(first, previous_ref[...], got_previous_ref[...])
+    place_halves(at_ref[0], whole.at[2], up_ref[...], got_up_ref[...])
+    place_halves(at_ref[0], whole.at[3], down_ref[...], got_down_ref[...])
     odd = lax.rem(at_ref[1], 2)
     turn = BROAD * rotate
     ham = ham_ref[...].astype(jnp.float32) - turn
@@ -149,32 +166,39 @@
         same_ref[...] = result
 
 
-def gather_body(at_ref, here_ref, one_ref, two_ref, three_ref, all_ref, give_ref, last_ref):
-    core, x = at_ref[0], at_ref[1]
-    for k, ref in enumerate((here_ref, one_ref, two_ref, three_ref)):
-        all_ref[lax.rem(x + WIDTH - k, WIDTH)] = ref[...]
-    give_ref[...] = all_ref[pl.ds(2 * (1 - core), 2)]
-    last_ref[...] = all_ref[WIDTH - 1]
-
-
-def link_body(at_ref, all_ref, got_ref, below_ref, outer_ham, inner_ham, far, mid, mid_turned, near):
+def link_body(
+    at_ref, c_ref, ham_ref, below_ref, near_ref, middle_ref, mine_1, mine_2, mine_3, other_1, other_2, other_3, extra,
+    outer_ham, inner_ham, far, mid, mid_turned, near,
+):
+    x = at_ref[1]
+
+    def block(b, here, one, two, three):
+        k = lax.rem(x + WIDTH - b, WIDTH)
+        return jnp.where(k == 0, here, jnp.where(k == 1, one, jnp.where(k == 2, two, three)))
+
     @pl.when(at_ref[0] == 0)
     def _():
-        outer_ham[...] = all_ref[0]
-        inner_ham[...] = all_ref[1]
-        far[...] = below_ref[...].T
-        mid[...] = got_ref[0]
-        mid_turned[...] = got_ref[0].T
-        near[...] = got_ref[1]
+        hams = (ham_ref[...], mine_1[...], mine_2[...], mine_3[...])
+        links = (c_ref[...], other_1[...], other_2[...], other_3[...])
+        outer_ham[...] = block(0, *hams)
+        inner_ham[...] = block(1, *hams)
+        far[...] = jnp.where(x == 0, below_ref[...], jnp.where(x == 2, middle_ref[...], near_ref[...])).T
+        middle = block(0, *links)
+        mid[...] = middle
+        mid_turned[...] = middle.T
+        near[...] = block(1, *links)
 
     @pl.when(at_ref[0] == 1)
     def _():
-        outer_ham[...] = got_ref[1]
-        inner_ham[...] = got_ref[0]
-        far[...] = all_ref[3]
-        mid[...] = all_ref[2].T
-        mid_turned[...] = all_ref[2]
-        near[...] = all_ref[1].T
+        hams = (ham_ref[...], jnp.where(x == 0, extra[...], other_1[...]), other_2[...], other_3[...])
+        links = (c_ref[...], mine_1[...], mine_2[...], mine_3[...])
+        outer_ham[...] = block(3, *hams)
+        inner_ham[...] = block(2, *hams)
+        far[...] = block(3, *links)
+        middle = block(2, *links)
+        mid[...] = middle.T
+        mid_turned[...] = middle
+        near[...] = block(1, *links).T
 
 
 def row_energy(at_ref, energy_ref, pair_ref):
@@ -333,40 +357,38 @@
         return call(body, out_shape, in_specs, scratch)(*operands)
 
     lower_mine = passed_along(half(c), 1)
-    ham_half = half(ham)
-    ham_up = passed_along(ham_half, -1)
-    ham_down = passed_along(ham_half, 1)
     energy_pair = swapped(energies)
     own, load = run(own_body, (wide(n, n), thin(n, n)), [SM, SM, VM, VM], edge[:1], at, c, ham)
     lower_theirs = swapped(lower_mine)
     one, three = row_ring(load, 1), row_ring(load, -1)
-    pair, pair_half, _, lower_turned = run(
+    pair, pair_half, below_c, lower_turned = run(
         pair_body, (wide(n, n), thin(n // 2, n), thin(n, n), thin(n, n)), [SM, VM, VM, VM],
         at, own, lower_mine, lower_theirs,
     )
     pair_up, pair_down = passed_along(pair_half, -1), passed_along(pair_half, 1)
     two = row_ring(one, 1)
-    mine = [ham_up, ham_down, pair_up, pair_down]
-    theirs = [swapped(v) for v in mine[:2]] + [swapped(v) for v in mine[2:]]
+    climb = climbed(jnp.where(x == 0, one, three))
+    before, after = run(near_body, (thin(n, n),) * 2, [SM] + [VM] * 3, at, one, three, climb)
+    got_before, got_after = swapped(before), swapped(after)
+    got_up, got_down = swapped(pair_up), swapped(pair_down)
     chunks, first, second = run(
         second_body, (thin(parts, 2, rows, n), thin(n, n), thin(n, n)), [SM] * 4 + [VM] * 12,
-        energies, inverse, edge, at, ham, pair, c, lower_turned, *mine, *theirs,
-        scratch=[pltpu.VMEM((4, n, n), jnp.bfloat16)],
+        energies, inverse, edge, at, ham, pair, c, lower_turned, before, after, got_before, got_after,
+        pair_up, pair_down, got_up, got_down, scratch=[pltpu.VMEM((4, n, n), jnp.bfloat16)],
     )
     first, second = flipped(first, 0), flipped(second, 1)
     received = all_to_all(chunks, ENERGY)
 
-    everything, give, last = run(
-        gather_body, (thin(WIDTH, n, n), thin(2, n, n), thin(n, n)), [SM] + [VM] * 4,
-        at, load, one, two, three,
-    )
-    below_c = row_above(last, False)
-    got = swapped(give)
+    got_two = swapped(two)
+    extra = sent(one, [((0, 0), (1, 0))])
+    near_c = sent(below_c, [((0, 0), (0, 1)), ((1, 0), (0, 3))])
+    middle_c = sent(below_c, [((0, 0), (0, 2))])
     outer_ham, inner_ham, far, mid, mid_turned, near = run(
-        link_body, (thin(n, n),) * 6, [SM] + [VM] * 3, at, everything, got, below_c
+        link_body, (thin(n, n),) * 6, [SM] + [VM] * 12,
+        at, c, ham, below_c, near_c, middle_c, one, two, three, got_before, got_two, got_after, extra,
     )
     outer, inner = run(role_body, (thin(n, n),) * 2, [SM, VM, VM], at, first, second)
-    beyond = row_above(outer, True)
+    beyond = row_above(outer)
     beside = swapped(inner)
     open_outer, open_inner = run(
         open_body, (wide(n, n),) * 2, [SM] * 3 + [VM] * 10,
@@ -381,7 +403,7 @@
         at, opened, self_mine, self_theirs, green, scratch=mix,
     )
     outer = third(False, open_outer, outer)
-    beyond = row_above(outer, True)
+    beyond = row_above(outer)
     inner = third(True, open_inner, inner)
     beside = swapped(inner)
     open_outer, open_inner = run(

time: 258 us -> 236 us (0.915)
  the two profiles are of different devices: /device:TPU:70 before, /device:TPU:1 now
where the time goes in v6:
time: 236 us; the launch traced here: 234 us
  starting transfers between devices  77.4 us (33%)
  waiting for transfers between devices  67.3 us (29%)
  blocking collectives  40.1 us (17%)
  Pallas kernels  38.3 us (16%)
  local copies, waits for them, and re-layouts  9.82 us (4%)
    all_to_all x2, blocking collectives, all_to_all(): return lax.all_to_all(value, axes, split_axis=0, concat_axis=0, tiled=True)  40.1 us
    pallas_call x13, Pallas kernels, run(): return call(body, out_shape, in_specs, scratch)(*operands)  29.5 us
    ppermute x3, waiting for transfers between devices, row_ring(): lax.ppermute(value, 'x', [(s, (s + steps) % WIDTH) for s in range(WIDTH)])  19.1 us
    all_to_all x2, starting transfers between devices, all_to_all(): return lax.all_to_all(value, axes, split_axis=0, concat_axis=0, tiled=True)  16.5 us
    ppermute x2, waiting for transfers between devices, row_above(): return lax.ppermute(value, ('core', 'row'), pairs)  14.2 us
    ppermute x4, waiting for transfers between devices, returned(): return lax.ppermute(value, ('core', 'x'), pairs)  14.2 us
    ppermute x12, starting transfers between devices, swapped(): return lax.ppermute(value, 'core', [(0, 1), (1, 0)])  13.8 us
    ppermute x2, starting transfers between devices, row_above(): return lax.ppermute(value, ('core', 'row'), pairs)  11.4 us
  transfers between devices with their start and end apart: 32, of which 14 were waited for; matrix products, arithmetic and copies ran while one was open for 1% of the time, Pallas kernels for 8%

profile of v6, /device:TPU:1, one launch (start us, length us, event | category | flops | bytes accessed | tf_op | source)
XLA Modules:
  0.0 234.3 jit_solution(1171974749956416441)
XLA Ops:
  0.8 1.0 copy-done
  1.8 1.0 copy-done.2
  2.9 1.8 shard_map.68
  4.7 2.0 collective-permute-start.4
  6.7 1.3 collective-permute-start.6
  8.0 1.7 dynamic-slice_bitcast_fusion
  9.7 2.1 collective-permute-start
  11.8 5.8 %collective-permute-done.4.one_ref.mine_1 = bf16[512,512]{1,0:T(8,128)(2,1)S(1)} collective-permute-done((bf16[512,512]{1,0:T(8,128)(2,1)}, bf16[512,512]{1,0:T(8,128)(2,1)S(1)}, u32[]{:S(2)}, u32[]{:S(2)}) %collective-permute-start.4) | collective-permute-done | bytes 524320 | tf_op jit(solution)/shard_map/ppermute | solution.py:30
  17.7 1.6 collective-permute-done.6.three_ref.mine_3
  19.3 0.7 collective-permute-start.7
  20.0 3.0 %collective-permute-done.mine_ref = bf16[256,512]{1,0:T(8,128)(2,1)S(1)} collective-permute-done((bf16[256,512]{1,0:T(8,128)(2,1)}, bf16[256,512]{1,0:T(8,128)(2,1)S(1)}, u32[]{:S(2)}, u32[]{:S(2)}) %collective-permute-start) | collective-permute-done | bytes 262176 | tf_op jit(solution)/shard_map/ppermute | solution.py:26
  23.0 9.2 %collective-permute-start.1 = (bf16[256,512]{1,0:T(8,128)(2,1)S(1)}, bf16[256,512]{1,0:T(8,128)(2,1)S(1)}, u32[]{:S(2)}, u32[]{:S(2)}) collective-permute-start(bf16[256,512]{1,0:T(8,128)(2,1)S(1)} %collective-permute-done.mine_ref), channel_id=1, source_target_pairs={{0,16},{16,0},{1,17},{17,1},{2,18},{18,2},{3,19},{19,3},{4,20},{20... | collective-permute-start | bytes 786440 | tf_op jit(solution)/shard_map/ppermute | solution.py:34
  32.3 1.2 collective-permute-done.1.theirs_ref
  33.5 1.1 shard_map.69
  34.6 0.8 copy-done.9
  35.3 1.3 collective-permute-start.13
  36.6 4.0 %collective-permute-start.14 = (bf16[256,512]{1,0:T(8,128)(2,1)S(1)}, bf16[256,512]{1,0:T(8,128)(2,1)S(1)}, u32[]{:S(2)}, u32[]{:S(2)}) collective-permute-start(bf16[256,512]{1,0:T(8,128)(2,1)S(1)} %get-tuple-element.43), channel_id=1, source_target_pairs={{0,1},{1,2},{2,3},{3,4},{4,5},{5,6},{6,7},{7,8},{8,9},{9,10},{10,1... | collective-permute-start | bytes 786440 | tf_op jit(solution)/shard_map/ppermute | solution.py:26
  40.6 0.7 shard_map.70
  41.3 1.0 collective-permute-start.8
  42.4 2.3 collective-permute-done.13.up_ref
  44.7 1.2 collective-permute-start.15
  45.9 1.2 collective-permute-start.16
  47.1 1.2 collective-permute-done.16.got_down_ref
  48.3 4.9 %shard_map.72 = (bf16[16,2,32,512]{3,2,1,0:T(8,128)(2,1)S(1)}, bf16[512,512]{1,0:T(8,128)(2,1)S(1)}, bf16[512,512]{1,0:T(8,128)(2,1)S(1)}) custom-call(f32[2]{0:T(128)S(1)} %copy-done.12, f32[2]{0:T(128)S(1)} %convert_convert_fusion.inverse_ref, f32[2]{0:T(128)S(1)} %add_convert_fusion.edge_ref, s32[2]{0:T(128)S(1)} %pad_add_fusion.at_ref, ...), custom_call_target="tpu_custom_call" | custom-call | tf_op jit(solution)/shard_map/pallas_call | solution.py:357
  53.3 20.1 %all_to_all.20 = bf16[16,2,32,512]{3,2,1,0:T(8,128)(2,1)S(1)} all-to-all(bf16[16,2,32,512]{3,2,1,0:T(8,128)(2,1)S(1)} %get-tuple-element.44), channel_id=1, replica_groups=mesh['zlo'=2,'y'=4,'core'=2,'row'=4,'x'=4] {'zlo','y','core'}, dimensions={0} | all-to-all | bytes 2097152 | tf_op jit(solution)/shard_map/all_to_all | solution.py:337
  73.3 3.9 %shard_map.73 = bf16[32,32,512]{2,1,0:T(8,128)(2,1)S(1)} custom-call(s32[8]{0:T(128)S(1)} %copy-done.13, bf16[32,32,512]{2,1,0:T(8,128)(2,1)S(1)} %bitcast.31, bf16[32,512]{1,0:T(8,128)(2,1)S(1)} %bitcast.33), custom_call_target="tpu_custom_call" | custom-call | tf_op jit(solution)/shard_map/pallas_call | solution.py:328
  77.3 1.0 copy-done.4
  78.2 11.0 %all-to-all-start.1 = ((bf16[32,32,512]{2,1,0:T(8,128)(2,1)}), bf16[32,32,512]{2,1,0:T(8,128)(2,1)S(1)}, u32[]{:S(2)}, u32[]{:S(2)}) async-start(bf16[32,32,512]{2,1,0:T(8,128)(2,1)} %copy-done.4), calls=%async_computation.1 | async-start | bytes 2097152 | tf_op jit(solution)/shard_map/all_to_all | solution.py:337
  89.3 1.3 collective-permute-start.5
  90.6 5.5 %collective-permute-start.18 = (bf16[512,512]{1,0:T(8,128)(2,1)}, bf16[512,512]{1,0:T(8,128)(2,1)}, u32[]{:S(2)}, u32[]{:S(2)}) collective-permute-start(bf16[512,512]{1,0:T(8,128)(2,1)} %copy-done.15), channel_id=1, source_target_pairs={{0,0},{1,1},{2,16},{3,17},{16,2},{17,3},{18,18},{19,19},{4,4},{5,5... | collective-permute-start | bytes 1572872 | tf_op jit(solution)/shard_map/ppermute | solution.py:56
  96.4 5.4 %collective-permute-start.2 = (bf16[512,512]{1,0:T(8,128)(2,1)}, bf16[512,512]{1,0:T(8,128)(2,1)}, u32[]{:S(2)}, u32[]{:S(2)}) collective-permute-start(bf16[512,512]{1,0:T(8,128)(2,1)} %copy-done.9), channel_id=1, source_target_pairs={{0,1},{16,3},{4,5},{20,7},{8,9},{24,11},{12,13},{28,15},{32,33},{4... | collective-permute-start | bytes 1572872 | tf_op jit(solution)/shard_map/ppermute | solution.py:51
  101.8 1.4 collective-permute-start.3
  103.2 11.6 %collective-permute-done.5.mine_2 = bf16[512,512]{1,0:T(8,128)(2,1)} collective-permute-done((bf16[512,512]{1,0:T(8,128)(2,1)S(1)}, bf16[512,512]{1,0:T(8,128)(2,1)}, u32[]{:S(2)}, u32[]{:S(2)}) %collective-permute-start.5) | collective-permute-done | bytes 524320 | tf_op jit(solution)/shard_map/ppermute | solution.py:30
  114.9 1.3 collective-permute-start.11
  116.2 10.7 %collective-permute-done.18.first_ref = bf16[512,512]{1,0:T(8,128)(2,1)} collective-permute-done((bf16[512,512]{1,0:T(8,128)(2,1)}, bf16[512,512]{1,0:T(8,128)(2,1)}, u32[]{:S(2)}, u32[]{:S(2)}) %collective-permute-start.18) | collective-permute-done | bytes 524320 | tf_op jit(solution)/shard_map/ppermute | solution.py:56
  126.9 2.2 shard_map.74
  129.1 5.7 %collective-permute-start.20 = (bf16[512,512]{1,0:T(8,128)(2,1)}, bf16[512,512]{1,0:T(8,128)(2,1)}, u32[]{:S(2)}, u32[]{:S(2)}) collective-permute-start(bf16[512,512]{1,0:T(8,128)(2,1)} %get-tuple-element.48.outer.green_ref), channel_id=1, source_target_pairs={{16,4},{20,8},{24,12},{4,16},{8,20},{12,24},{17,5},{21,9},{25,13},... | collective-permute-start | bytes 1572872 | tf_op jit(solution)/shard_map/ppermute | solution.py:40
  135.0 0.6 collective-permute-start.17
  135.7 1.0 copy-done.6
  136.7 1.0 copy-done.8
  137.8 1.0 copy-done.10
  138.8 2.6 %shard_map.71 = (bf16[512,512]{1,0:T(8,128)(2,1)S(1)}, bf16[512,512]{1,0:T(8,128)(2,1)S(1)}, bf16[512,512]{1,0:T(8,128)(2,1)S(1)}, bf16[512,512]{1,0:T(8,128)(2,...) custom-call(s32[2]{0:T(128)S(1)} %pad_add_fusion.at_ref, bf16[512,512]{1,0:T(8,128)(2,1)S(1)} %bitcast.27, ...), custom_call_target="tpu_custom_call" | custom-call | tf_op jit(solution)/shard_map/pallas_call | solution.py:357
  141.4 6.2 %collective-permute-done.20.beyond = bf16[512,512]{1,0:T(8,128)(2,1)} collective-permute-done((bf16[512,512]{1,0:T(8,128)(2,1)}, bf16[512,512]{1,0:T(8,128)(2,1)}, u32[]{:S(2)}, u32[]{:S(2)}) %collective-permute-start.20) | collective-permute-done | bytes 524320 | tf_op jit(solution)/shard_map/ppermute | solution.py:40
  147.6 4.3 %shard_map.75 = (f32[512,512]{1,0:T(8,128)S(1)}, f32[512,512]{1,0:T(8,128)S(1)}) custom-call(s32[2]{0:T(128)S(1)} %pad_add_fusion.at_ref, f32[2]{0:T(128)S(1)} %copy-done.12, f32[2]{0:T(128)S(1)} %collective-permute-done.12.energy_pair_ref, bf16[512,512]{1,0:T(8,128)(2,1)S(1)} %get-tuple-element.37.outer_ham, ...), custom_call_target="tpu_custom_call" | custom-call | tf_op jit(solution)/shard_map/pallas_call | solution.py:357
  151.9 1.9 shard_map.77.inner
  153.9 1.9 shard_map.76.outer
  155.7 5.7 %collective-permute-start.25 = (bf16[512,512]{1,0:T(8,128)(2,1)S(1)}, bf16[512,512]{1,0:T(8,128)(2,1)S(1)}, u32[]{:S(2)}, u32[]{:S(2)}) collective-permute-start(bf16[512,512]{1,0:T(8,128)(2,1)S(1)} %shard_map.76.outer), channel_id=1, source_target_pairs={{16,4},{20,8},{24,12},{4,16},{8,20},{12,24},{17,5},{21,9},{25,13},... | collective-permute-start | bytes 1572872 | tf_op jit(solution)/shard_map/ppermute | solution.py:40
  161.5 2.1 shard_map.78
  163.6 2.0 shard_map.79
  165.7 8.0 %collective-permute-done.25.beyond = bf16[512,512]{1,0:T(8,128)(2,1)S(1)} collective-permute-done((bf16[512,512]{1,0:T(8,128)(2,1)S(1)}, bf16[512,512]{1,0:T(8,128)(2,1)S(1)}, u32[]{:S(2)}, u32[]{:S(2)}) %collective-permute-start.25) | collective-permute-done | bytes 524320 | tf_op jit(solution)/shard_map/ppermute | solution.py:40
  173.7 2.1 shard_map.80
  175.9 1.5 collective-permute-done.29
  177.5 20.0 %all_to_all.21.green_ref = bf16[32,32,512]{2,1,0:T(8,128)(2,1)S(1)} all-to-all(bf16[32,32,512]{2,1,0:T(8,128)(2,1)S(1)} %bitcast.32), channel_id=1, replica_groups=mesh['zlo'=2,'y'=4,'core'=2,'row'=4,'x'=4] {'x','zlo','y'}, dimensions={0} | all-to-all | bytes 2097152 | tf_op jit(solution)/shard_map/all_to_all | solution.py:337
  197.5 4.9 %shard_map.82 = bf16[32,32,512]{2,1,0:T(8,128)(2,1)} custom-call(s32[8]{0:T(128)S(1)} %copy-done.13, bf16[32,32,512]{2,1,0:T(8,128)(2,1)S(1)} %all_to_all.21.green_ref, bf16[32,512]{1,0:T(8,128)(2,1)S(1)} %bitcast.34), custom_call_target="tpu_custom_call" | custom-call | tf_op jit(solution)/shard_map/pallas_call | solution.py:328
  202.4 5.5 %all-to-all-start.3 = ((bf16[16,2,32,512]{3,2,1,0:T(8,128)(2,1)}), bf16[16,2,32,512]{3,2,1,0:T(8,128)(2,1)S(1)}, u32[]{:S(2)}, u32[]{:S(2)}) async-start(bf16[16,2,32,512]{3,2,1,0:T(8,128)(2,1)} %bitcast.14), calls=%async_computation.3 | async-start | bytes 2097152 | tf_op jit(solution)/shard_map/all_to_all | solution.py:337
  207.9 3.1 %collective-permute-start.23 = (bf16[512,512]{1,0:T(8,128)(2,1)S(1)}, bf16[512,512]{1,0:T(8,128)(2,1)S(1)}, u32[]{:S(2)}, u32[]{:S(2)}) collective-permute-start(bf16[512,512]{1,0:T(8,128)(2,1)S(1)} %get-tuple-element.53), channel_id=1, source_target_pairs={{0,1},{2,17},{16,2},{18,18},{4,5},{6,21},{20,6},{22,22},{8,9},{10,... | collective-permute-start | bytes 1572872 | tf_op jit(solution)/shard_map/ppermute | solution.py:97
  211.0 0.7 collective-permute-start.24
  211.7 4.0 %collective-permute-start.27 = (bf16[512,512]{1,0:T(8,128)(2,1)S(1)}, bf16[512,512]{1,0:T(8,128)(2,1)S(1)}, u32[]{:S(2)}, u32[]{:S(2)}) collective-permute-start(bf16[512,512]{1,0:T(8,128)(2,1)S(1)} %get-tuple-element.57), channel_id=1, source_target_pairs={{0,0},{2,16},{16,3},{18,19},{4,4},{6,20},{20,7},{22,23},{8,8},{10,... | collective-permute-start | bytes 1572872 | tf_op jit(solution)/shard_map/ppermute | solution.py:97
  215.7 1.3 collective-permute-start.28
  217.0 5.1 %collective-permute-done.23.inner_0 = bf16[512,512]{1,0:T(8,128)(2,1)S(1)} collective-permute-done((bf16[512,512]{1,0:T(8,128)(2,1)S(1)}, bf16[512,512]{1,0:T(8,128)(2,1)S(1)}, u32[]{:S(2)}, u32[]{:S(2)}) %collective-permute-start.23) | collective-permute-done | bytes 524320 | tf_op jit(solution)/shard_map/ppermute | solution.py:97
  222.1 5.3 %collective-permute-done.27.outer_0 = bf16[512,512]{1,0:T(8,128)(2,1)S(1)} collective-permute-done((bf16[512,512]{1,0:T(8,128)(2,1)S(1)}, bf16[512,512]{1,0:T(8,128)(2,1)S(1)}, u32[]{:S(2)}, u32[]{:S(2)}) %collective-permute-start.27) | collective-permute-done | bytes 524320 | tf_op jit(solution)/shard_map/ppermute | solution.py:97
  227.4 3.8 %collective-permute-done.28.outer_1 = bf16[512,512]{1,0:T(8,128)(2,1)S(1)} collective-permute-done((bf16[512,512]{1,0:T(8,128)(2,1)S(1)}, bf16[512,512]{1,0:T(8,128)(2,1)S(1)}, u32[]{:S(2)}, u32[]{:S(2)}) %collective-permute-start.28) | collective-permute-done | bytes 524320 | tf_op jit(solution)/shard_map/ppermute | solution.py:97
  231.2 2.0 shard_map.81
  233.2 1.1 copy.7
  (57 shorter events, 1.4 us)
Async XLA Ops:
  0.8 1.0 copy-start
  1.8 1.0 copy-start.2
  4.7 12.9 %collective-permute-start.4 = (bf16[512,512]{1,0:T(8,128)(2,1)}, bf16[512,512]{1,0:T(8,128)(2,1)S(1)}, u32[]{:S(2)}, u32[]{:S(2)}) collective-permute-start(bf16[512,512]{1,0:T(8,128)(2,1)} %get-tuple-element.33), channel_id=1, source_target_pairs={{0,1},{1,2},{2,3},{3,0},{4,5},{5,6},{6,7},{7,4},{8,9},{9,10},{10,1... | collective-permute-start | bytes 1572872 | tf_op jit(solution)/shard_map/ppermute | solution.py:30
  6.7 12.5 %collective-permute-start.6 = (bf16[512,512]{1,0:T(8,128)(2,1)}, bf16[512,512]{1,0:T(8,128)(2,1)S(1)}, u32[]{:S(2)}, u32[]{:S(2)}) collective-permute-start(bf16[512,512]{1,0:T(8,128)(2,1)} %get-tuple-element.33), channel_id=1, source_target_pairs={{0,3},{1,0},{2,1},{3,2},{4,7},{5,4},{6,5},{7,6},{8,11},{9,8},{10,9... | collective-permute-start | bytes 1572872 | tf_op jit(solution)/shard_map/ppermute | solution.py:30
  9.7 13.4 %collective-permute-start = (bf16[256,512]{1,0:T(8,128)(2,1)}, bf16[256,512]{1,0:T(8,128)(2,1)S(1)}, u32[]{:S(2)}, u32[]{:S(2)}) collective-permute-start(bf16[256,512]{1,0:T(8,128)(2,1)} %dynamic-slice_bitcast_fusion), channel_id=1, source_target_pairs={{0,1},{1,2},{2,3},{3,4},{4,5},{5,6},{6,7},{7,8},{8,9},{9,10},{10,1... | collective-permute-start | bytes 786440 | tf_op jit(solution)/shard_map/ppermute | solution.py:26
  11.8 35.3 %copy-start.12 = (f32[2]{0:T(128)S(1)}, f32[2]{0:T(128)}, u32[]{:S(2)}) copy-start(f32[2]{0:T(128)} %energy_ref.5) | copy-start | bytes 28
  11.8 36.5 %copy-start.1 = (bf16[1,512,512]{2,1,0:T(8,128)(2,1)S(1)}, bf16[1,512,512]{2,1,0:T(8,128)(2,1)}, u32[]{:S(2)}) copy-start(bf16[1,512,512]{2,1,0:T(8,128)(2,1)} %param.7) | copy-start | bytes 1572868
  11.8 36.5 %copy-start.3 = (bf16[1,512,512]{2,1,0:T(8,128)(2,1)S(1)}, bf16[1,512,512]{2,1,0:T(8,128)(2,1)}, u32[]{:S(2)}) copy-start(bf16[1,512,512]{2,1,0:T(8,128)(2,1)} %param.6) | copy-start | bytes 1572868
  19.3 21.3 %collective-permute-start.7 = (bf16[512,512]{1,0:T(8,128)(2,1)S(1)}, bf16[512,512]{1,0:T(8,128)(2,1)S(1)}, u32[]{:S(2)}, u32[]{:S(2)}) collective-permute-start(bf16[512,512]{1,0:T(8,128)(2,1)S(1)} %broadcast_select_fusion), channel_id=1, source_target_pairs={{0,4},{4,8},{8,12},{7,3},{11,7},{15,11},{32,36},{36,40},{40,44},{3... | collective-permute-start | bytes 1572872 | tf_op jit(solution)/shard_map/ppermute | solution.py:47
  23.0 10.4 %collective-permute-start.1 = (bf16[256,512]{1,0:T(8,128)(2,1)S(1)}, bf16[256,512]{1,0:T(8,128)(2,1)S(1)}, u32[]{:S(2)}, u32[]{:S(2)}) collective-permute-start(bf16[256,512]{1,0:T(8,128)(2,1)S(1)} %collective-permute-done.mine_ref), channel_id=1, source_target_pairs={{0,16},{16,0},{1,17},{17,1},{2,18},{18,2},{3,19},{19,3},{4,20},{20... | collective-permute-start | bytes 786440 | tf_op jit(solution)/shard_map/ppermute | solution.py:34
  34.5 0.8 copy-start.9
  35.3 9.4 %collective-permute-start.13 = (bf16[256,512]{1,0:T(8,128)(2,1)S(1)}, bf16[256,512]{1,0:T(8,128)(2,1)S(1)}, u32[]{:S(2)}, u32[]{:S(2)}) collective-permute-start(bf16[256,512]{1,0:T(8,128)(2,1)S(1)} %get-tuple-element.43), channel_id=1, source_target_pairs={{1,0},{2,1},{3,2},{4,3},{5,4},{6,5},{7,6},{8,7},{9,8},{10,9},{11,1... | collective-permute-start | bytes 786440 | tf_op jit(solution)/shard_map/ppermute | solution.py:26
  36.6 9.3 %collective-permute-start.14 = (bf16[256,512]{1,0:T(8,128)(2,1)S(1)}, bf16[256,512]{1,0:T(8,128)(2,1)S(1)}, u32[]{:S(2)}, u32[]{:S(2)}) collective-permute-start(bf16[256,512]{1,0:T(8,128)(2,1)S(1)} %get-tuple-element.43), channel_id=1, source_target_pairs={{0,1},{1,2},{2,3},{3,4},{4,5},{5,6},{6,7},{7,8},{8,9},{9,10},{10,1... | collective-permute-start | bytes 786440 | tf_op jit(solution)/shard_map/ppermute | solution.py:26
  41.3 7.0 %collective-permute-start.8 = (bf16[512,512]{1,0:T(8,128)(2,1)S(1)}, bf16[512,512]{1,0:T(8,128)(2,1)S(1)}, u32[]{:S(2)}, u32[]{:S(2)}) collective-permute-start(bf16[512,512]{1,0:T(8,128)(2,1)S(1)} %get-tuple-element.34.previous_ref), channel_id=1, source_target_pairs={{0,16},{16,0},{1,17},{17,1},{2,18},{18,2},{3,19},{19,3},{4,20},{20... | collective-permute-start | bytes 1572872 | tf_op jit(solution)/shard_map/ppermute | solution.py:34
  42.3 6.0 %collective-permute-start.10 = (bf16[512,512]{1,0:T(8,128)(2,1)S(1)}, bf16[512,512]{1,0:T(8,128)(2,1)S(1)}, u32[]{:S(2)}, u32[]{:S(2)}) collective-permute-start(bf16[512,512]{1,0:T(8,128)(2,1)S(1)} %get-tuple-element.35.next_ref), channel_id=1, source_target_pairs={{0,16},{16,0},{1,17},{17,1},{2,18},{18,2},{3,19},{19,3},{4,20},{20... | collective-permute-start | bytes 1572872 | tf_op jit(solution)/shard_map/ppermute | solution.py:34
  44.7 2.4 %collective-permute-start.15 = (bf16[256,512]{1,0:T(8,128)(2,1)S(1)}, bf16[256,512]{1,0:T(8,128)(2,1)S(1)}, u32[]{:S(2)}, u32[]{:S(2)}) collective-permute-start(bf16[256,512]{1,0:T(8,128)(2,1)S(1)} %collective-permute-done.13.up_ref), channel_id=1, source_target_pairs={{0,16},{16,0},{1,17},{17,1},{2,18},{18,2},{3,19},{19,3},{4,20},{20... | collective-permute-start | bytes 786440 | tf_op jit(solution)/shard_map/ppermute | solution.py:34
  45.9 2.3 collective-permute-start.16
  48.3 4.9 %copy-start.5 = (bf16[512,512]{1,0:T(8,128)(2,1)}, bf16[512,512]{1,0:T(8,128)(2,1)S(1)}, u32[]{:S(2)}) copy-start(bf16[512,512]{1,0:T(8,128)(2,1)S(1)} %collective-permute-done.8.other_1.got_previous_ref) | copy-start | bytes 1572868
  48.3 4.9 %copy-start.7 = (bf16[512,512]{1,0:T(8,128)(2,1)}, bf16[512,512]{1,0:T(8,128)(2,1)S(1)}, u32[]{:S(2)}) copy-start(bf16[512,512]{1,0:T(8,128)(2,1)S(1)} %collective-permute-done.10.other_3.got_next_ref) | copy-start | bytes 1572868
  53.2 20.1 %copy-start.14 = (bf16[512,512]{1,0:T(8,128)(2,1)}, bf16[512,512]{1,0:T(8,128)(2,1)S(1)}, u32[]{:S(2)}) copy-start(bf16[512,512]{1,0:T(8,128)(2,1)S(1)} %get-tuple-element.47) | copy-start | bytes 1572868
  53.2 20.1 %copy-start.15 = (bf16[512,512]{1,0:T(8,128)(2,1)}, bf16[512,512]{1,0:T(8,128)(2,1)S(1)}, u32[]{:S(2)}) copy-start(bf16[512,512]{1,0:T(8,128)(2,1)S(1)} %get-tuple-element.46) | copy-start | bytes 1572868
  53.2 20.1 %copy-start.11 = (bf16[1,32,512]{2,1,0:T(8,128)(2,1)S(1)}, bf16[1,32,512]{2,1,0:T(8,128)(2,1)}, u32[]{:S(2)}) copy-start(bf16[1,32,512]{2,1,0:T(8,128)(2,1)} %param.8) | copy-start | bytes 98308
  53.2 20.1 %copy-start.13 = (s32[8]{0:T(128)S(1)}, s32[8]{0:T(128)}, u32[]{:S(2)}) copy-start(s32[8]{0:T(128)} %offset_ref.3) | copy-start | bytes 100
  77.3 1.0 copy-start.4
  78.2 56.7 %all-to-all-start.1 = ((bf16[32,32,512]{2,1,0:T(8,128)(2,1)}), bf16[32,32,512]{2,1,0:T(8,128)(2,1)S(1)}, u32[]{:S(2)}, u32[]{:S(2)}) async-start(bf16[32,32,512]{2,1,0:T(8,128)(2,1)} %copy-done.4), calls=%async_computation.1 | async-start | bytes 2097152 | tf_op jit(solution)/shard_map/all_to_all | solution.py:337
  89.3 25.6 %collective-permute-start.5 = (bf16[512,512]{1,0:T(8,128)(2,1)S(1)}, bf16[512,512]{1,0:T(8,128)(2,1)}, u32[]{:S(2)}, u32[]{:S(2)}) collective-permute-start(bf16[512,512]{1,0:T(8,128)(2,1)S(1)} %collective-permute-done.4.one_ref.mine_1), channel_id=1, source_target_pairs={{0,1},{1,2},{2,3},{3,0},{4,5},{5,6},{6,7},{7,4},{8,9},{9,10},{10,1... | collective-permute-start | bytes 1572872 | tf_op jit(solution)/shard_map/ppermute | solution.py:30
  90.6 36.3 %collective-permute-start.18 = (bf16[512,512]{1,0:T(8,128)(2,1)}, bf16[512,512]{1,0:T(8,128)(2,1)}, u32[]{:S(2)}, u32[]{:S(2)}) collective-permute-start(bf16[512,512]{1,0:T(8,128)(2,1)} %copy-done.15), channel_id=1, source_target_pairs={{0,0},{1,1},{2,16},{3,17},{16,2},{17,3},{18,18},{19,19},{4,4},{5,5... | collective-permute-start | bytes 1572872 | tf_op jit(solution)/shard_map/ppermute | solution.py:56
  96.0 30.8 %collective-permute-start.19 = (bf16[512,512]{1,0:T(8,128)(2,1)}, bf16[512,512]{1,0:T(8,128)(2,1)}, u32[]{:S(2)}, u32[]{:S(2)}) collective-permute-start(bf16[512,512]{1,0:T(8,128)(2,1)} %copy-done.14), channel_id=1, source_target_pairs={{0,1},{1,0},{2,17},{3,16},{16,3},{17,2},{18,19},{19,18},{4,5},{5,4... | collective-permute-start | bytes 1572872 | tf_op jit(solution)/shard_map/ppermute | solution.py:56
  96.4 38.4 %collective-permute-start.2 = (bf16[512,512]{1,0:T(8,128)(2,1)}, bf16[512,512]{1,0:T(8,128)(2,1)}, u32[]{:S(2)}, u32[]{:S(2)}) collective-permute-start(bf16[512,512]{1,0:T(8,128)(2,1)} %copy-done.9), channel_id=1, source_target_pairs={{0,1},{16,3},{4,5},{20,7},{8,9},{24,11},{12,13},{28,15},{32,33},{4... | collective-permute-start | bytes 1572872 | tf_op jit(solution)/shard_map/ppermute | solution.py:51
  101.8 33.2 %collective-permute-start.3 = (bf16[512,512]{1,0:T(8,128)(2,1)}, bf16[512,512]{1,0:T(8,128)(2,1)}, u32[]{:S(2)}, u32[]{:S(2)}) collective-permute-start(bf16[512,512]{1,0:T(8,128)(2,1)} %copy-done.9), channel_id=1, source_target_pairs={{0,2},{4,6},{8,10},{12,14},{32,34},{36,38},{40,42},{44,46},{64,66}... | collective-permute-start | bytes 1572872 | tf_op jit(solution)/shard_map/ppermute | solution.py:51
  114.9 20.7 %collective-permute-start.11 = (bf16[512,512]{1,0:T(8,128)(2,1)S(1)}, bf16[512,512]{1,0:T(8,128)(2,1)}, u32[]{:S(2)}, u32[]{:S(2)}) collective-permute-start(bf16[512,512]{1,0:T(8,128)(2,1)S(1)} %collective-permute-done.4.one_ref.mine_1), channel_id=1, source_target_pairs={{0,16},{4,20},{8,24},{12,28},{32,48},{36,52},{40,56},{44,60},{64,8... | collective-permute-start | bytes 1572872 | tf_op jit(solution)/shard_map/ppermute | solution.py:51
  126.9 8.8 %collective-permute-start.9 = (bf16[512,512]{1,0:T(8,128)(2,1)}, bf16[512,512]{1,0:T(8,128)(2,1)}, u32[]{:S(2)}, u32[]{:S(2)}) collective-permute-start(bf16[512,512]{1,0:T(8,128)(2,1)} %collective-permute-done.5.mine_2), channel_id=1, source_target_pairs={{0,16},{16,0},{1,17},{17,1},{2,18},{18,2},{3,19},{19,3},{4,20},{20... | collective-permute-start | bytes 1572872 | tf_op jit(solution)/shard_map/ppermute | solution.py:34
  129.1 18.5 %collective-permute-start.20 = (bf16[512,512]{1,0:T(8,128)(2,1)}, bf16[512,512]{1,0:T(8,128)(2,1)}, u32[]{:S(2)}, u32[]{:S(2)}) collective-permute-start(bf16[512,512]{1,0:T(8,128)(2,1)} %get-tuple-element.48.outer.green_ref), channel_id=1, source_target_pairs={{16,4},{20,8},{24,12},{4,16},{8,20},{12,24},{17,5},{21,9},{25,13},... | collective-permute-start | bytes 1572872 | tf_op jit(solution)/shard_map/ppermute | solution.py:40
  134.8 12.8 %collective-permute-start.21 = (bf16[512,512]{1,0:T(8,128)(2,1)}, bf16[512,512]{1,0:T(8,128)(2,1)}, u32[]{:S(2)}, u32[]{:S(2)}) collective-permute-start(bf16[512,512]{1,0:T(8,128)(2,1)} %get-tuple-element.49.inner.green_ref), channel_id=1, source_target_pairs={{0,16},{16,0},{1,17},{17,1},{2,18},{18,2},{3,19},{19,3},{4,20},{20... | collective-permute-start | bytes 1572872 | tf_op jit(solution)/shard_map/ppermute | solution.py:34
  135.0 16.9 %collective-permute-start.17 = (bf16[2,8,32,512]{3,2,1,0:T(8,128)(2,1)S(1)}, bf16[2,8,32,512]{3,2,1,0:T(8,128)(2,1)S(1)}, u32[]{:S(2)}, u32[]{:S(2)}) collective-permute-start(bf16[2,8,32,512]{3,2,1,0:T(8,128)(2,1)S(1)} %constant_dynamic-slice_fusion), channel_id=1, source_target_pairs={{0,16},{16,0},{1,17},{17,1},{2,18},{18,2},{3,19},{19,3},{4,20},{20... | collective-permute-start | bytes 1572872 | tf_op jit(solution)/shard_map/ppermute | solution.py:34
  135.6 5.9 %collective-permute-start.12 = (f32[2]{0:T(128)S(1)}, f32[2]{0:T(128)S(1)}, u32[]{:S(2)}, u32[]{:S(2)}) collective-permute-start(f32[2]{0:T(128)S(1)} %copy-done.12), channel_id=1, source_target_pairs={{0,16},{16,0},{1,17},{17,1},{2,18},{18,2},{3,19},{19,3},{4,20},{20... | collective-permute-start | bytes 32 | tf_op jit(solution)/shard_map/ppermute | solution.py:34
  135.7 1.0 copy-start.6
  136.7 1.0 copy-start.8
  137.7 1.0 copy-start.10
  153.8 9.8 %collective-permute-start.22 = (bf16[512,512]{1,0:T(8,128)(2,1)S(1)}, bf16[512,512]{1,0:T(8,128)(2,1)S(1)}, u32[]{:S(2)}, u32[]{:S(2)}) collective-permute-start(bf16[512,512]{1,0:T(8,128)(2,1)S(1)} %shard_map.77.inner), channel_id=1, source_target_pairs={{0,16},{16,0},{1,17},{17,1},{2,18},{18,2},{3,19},{19,3},{4,20},{20... | collective-permute-start | bytes 1572872 | tf_op jit(solution)/shard_map/ppermute | solution.py:34
  155.7 18.0 %collective-permute-start.25 = (bf16[512,512]{1,0:T(8,128)(2,1)S(1)}, bf16[512,512]{1,0:T(8,128)(2,1)S(1)}, u32[]{:S(2)}, u32[]{:S(2)}) collective-permute-start(bf16[512,512]{1,0:T(8,128)(2,1)S(1)} %shard_map.76.outer), channel_id=1, source_target_pairs={{16,4},{20,8},{24,12},{4,16},{8,20},{12,24},{17,5},{21,9},{25,13},... | collective-permute-start | bytes 1572872 | tf_op jit(solution)/shard_map/ppermute | solution.py:40
  165.6 8.1 %collective-permute-start.26 = (bf16[8,32,512]{2,1,0:T(8,128)(2,1)S(1)}, bf16[8,32,512]{2,1,0:T(8,128)(2,1)S(1)}, u32[]{:S(2)}, u32[]{:S(2)}) collective-permute-start(bf16[8,32,512]{2,1,0:T(8,128)(2,1)S(1)} %get-tuple-element.56), channel_id=1, source_target_pairs={{0,16},{16,0},{1,17},{17,1},{2,18},{18,2},{3,19},{19,3},{4,20},{20... | collective-permute-start | bytes 786440 | tf_op jit(solution)/shard_map/ppermute | solution.py:34
  175.8 1.6 collective-permute-start.29
  202.4 30.8 %all-to-all-start.3 = ((bf16[16,2,32,512]{3,2,1,0:T(8,128)(2,1)}), bf16[16,2,32,512]{3,2,1,0:T(8,128)(2,1)S(1)}, u32[]{:S(2)}, u32[]{:S(2)}) async-start(bf16[16,2,32,512]{3,2,1,0:T(8,128)(2,1)} %bitcast.14), calls=%async_computation.3 | async-start | bytes 2097152 | tf_op jit(solution)/shard_map/all_to_all | solution.py:337
  207.9 14.1 %collective-permute-start.23 = (bf16[512,512]{1,0:T(8,128)(2,1)S(1)}, bf16[512,512]{1,0:T(8,128)(2,1)S(1)}, u32[]{:S(2)}, u32[]{:S(2)}) collective-permute-start(bf16[512,512]{1,0:T(8,128)(2,1)S(1)} %get-tuple-element.53), channel_id=1, source_target_pairs={{0,1},{2,17},{16,2},{18,18},{4,5},{6,21},{20,6},{22,22},{8,9},{10,... | collective-permute-start | bytes 1572872 | tf_op jit(solution)/shard_map/ppermute | solution.py:97
  211.0 11.1 %collective-permute-start.24 = (bf16[512,512]{1,0:T(8,128)(2,1)S(1)}, bf16[512,512]{1,0:T(8,128)(2,1)S(1)}, u32[]{:S(2)}, u32[]{:S(2)}) collective-permute-start(bf16[512,512]{1,0:T(8,128)(2,1)S(1)} %get-tuple-element.53), channel_id=1, source_target_pairs={{1,1},{3,17},{17,2},{19,18},{5,5},{7,21},{21,6},{23,22},{9,9},{11,... | collective-permute-start | bytes 1572872 | tf_op jit(solution)/shard_map/ppermute | solution.py:97
  211.7 15.7 %collective-permute-start.27 = (bf16[512,512]{1,0:T(8,128)(2,1)S(1)}, bf16[512,512]{1,0:T(8,128)(2,1)S(1)}, u32[]{:S(2)}, u32[]{:S(2)}) collective-permute-start(bf16[512,512]{1,0:T(8,128)(2,1)S(1)} %get-tuple-element.57), channel_id=1, source_target_pairs={{0,0},{2,16},{16,3},{18,19},{4,4},{6,20},{20,7},{22,23},{8,8},{10,... | collective-permute-start | bytes 1572872 | tf_op jit(solution)/shard_map/ppermute | solution.py:97
  215.7 15.5 %collective-permute-start.28 = (bf16[512,512]{1,0:T(8,128)(2,1)S(1)}, bf16[512,512]{1,0:T(8,128)(2,1)S(1)}, u32[]{:S(2)}, u32[]{:S(2)}) collective-permute-start(bf16[512,512]{1,0:T(8,128)(2,1)S(1)} %get-tuple-element.57), channel_id=1, source_target_pairs={{1,0},{3,16},{17,3},{19,19},{5,4},{7,20},{21,7},{23,23},{9,8},{11,... | collective-permute-start | bytes 1572872 | tf_op jit(solution)/shard_map/ppermute | solution.py:97

commit v7 on v6

--- a/solution.py
+++ b/solution.py
@@ -40,10 +40,10 @@
     return lax.ppermute(value, ("core", "row"), pairs)
 
 
-def climbed(value):
+def crossed(value):
     rows = lax.axis_size("row")
-    pairs = [(r * WIDTH, (r + 1) * WIDTH) for r in range(rows - 1)]
-    pairs += [(r * WIDTH + WIDTH - 1, r * WIDTH - 1) for r in range(1, rows)]
+    pairs = [(r * WIDTH - 1, r * WIDTH) for r in range(1, rows)]
+    pairs += [(r * WIDTH, r * WIDTH - 1) for r in range(1, rows)]
     return lax.ppermute(value, ("core", "row", "x"), pairs)
 
 
@@ -131,10 +131,10 @@
     return dot(green, residue)
 
 
-def near_body(at_ref, one_ref, three_ref, climbed_ref, previous_ref, next_ref):
+def near_body(at_ref, one_ref, three_ref, crossed_ref, previous_ref, next_ref):
     first = at_ref[0] == 0
-    previous_ref[...] = jnp.where(jnp.logical_and(first, at_ref[1] == 0), climbed_ref[...], one_ref[...])
-    next_ref[...] = jnp.where(jnp.logical_and(first, at_ref[1] == WIDTH - 1), climbed_ref[...], three_ref[...])
+    previous_ref[...] = jnp.where(jnp.logical_and(first, at_ref[1] == 0), crossed_ref[...], one_ref[...])
+    next_ref[...] = jnp.where(jnp.logical_and(first, at_ref[1] == WIDTH - 1), crossed_ref[...], three_ref[...])
 
 
 def second_body(
@@ -361,14 +361,14 @@
     own, load = run(own_body, (wide(n, n), thin(n, n)), [SM, SM, VM, VM], edge[:1], at, c, ham)
     lower_theirs = swapped(lower_mine)
     one, three = row_ring(load, 1), row_ring(load, -1)
+    crossing = crossed(ham)
     pair, pair_half, below_c, lower_turned = run(
         pair_body, (wide(n, n), thin(n // 2, n), thin(n, n), thin(n, n)), [SM, VM, VM, VM],
         at, own, lower_mine, lower_theirs,
     )
     pair_up, pair_down = passed_along(pair_half, -1), passed_along(pair_half, 1)
     two = row_ring(one, 1)
-    climb = climbed(jnp.where(x == 0, one, three))
-    before, after = run(near_body, (thin(n, n),) * 2, [SM] + [VM] * 3, at, one, three, climb)
+    before, after = run(near_body, (thin(n, n),) * 2, [SM] + [VM] * 3, at, one, three, crossing)
     got_before, got_after = swapped(before), swapped(after)
     got_up, got_down = swapped(pair_up), swapped(pair_down)
     chunks, first, second = run(

time: 236 us -> 247 us (1.047)
  the two profiles are of different devices: /device:TPU:1 before, /device:TPU:70 now
where the time goes in v7:
time: 247 us; the launch traced here: 242 us
  starting transfers between devices  78.2 us (32%)
  waiting for transfers between devices  67.7 us (27%)
  blocking collectives  48.3 us (20%)
  Pallas kernels  39.7 us (16%)
  local copies, waits for them, and re-layouts  7.07 us (3%)
    all_to_all x2, blocking collectives, all_to_all(): return lax.all_to_all(value, axes, split_axis=0, concat_axis=0, tiled=True)  48.3 us
    pallas_call x13, Pallas kernels, run(): return call(body, out_shape, in_specs, scratch)(*operands)  30 us
    ppermute x3, waiting for transfers between devices, passed_along(): lax.ppermute(value, SLAB, [(source, source + steps) for source in range(l...  28.7 us
    ppermute x12, starting transfers between devices, swapped(): return lax.ppermute(value, 'core', [(0, 1), (1, 0)])  20.6 us
    ppermute x3, waiting for transfers between devices, row_ring(): lax.ppermute(value, 'x', [(s, (s + steps) % WIDTH) for s in range(WIDTH)])  15.8 us
    ppermute x3, starting transfers between devices, passed_along(): lax.ppermute(value, SLAB, [(source, source + steps) for source in range(l...  13.1 us
    ppermute x4, starting transfers between devices, returned(): return lax.ppermute(value, ('core', 'x'), pairs)  11.3 us
    ppermute x4, waiting for transfers between devices, returned(): return lax.ppermute(value, ('core', 'x'), pairs)  10.5 us
  transfers between devices with their start and end apart: 32, of which 12 were waited for; matrix products, arithmetic and copies ran while one was open for 0% of the time, Pallas kernels for 8%

profile of v7, /device:TPU:70, one launch (start us, length us, event | category | flops | bytes accessed | tf_op | source)
XLA Modules:
  0.0 242.1 jit_solution(11496887988962584319)
XLA Ops:
  0.8 1.0 copy-done
  1.8 2.4 shard_map.68
  4.2 0.5 collective-permute-start.4
  4.7 1.5 collective-permute-start.6
  6.2 7.5 %collective-permute-start.7 = (bf16[512,512]{1,0:T(8,128)(2,1)}, bf16[512,512]{1,0:T(8,128)(2,1)S(1)}, u32[]{:S(2)}, u32[]{:S(2)}) collective-permute-start(bf16[512,512]{1,0:T(8,128)(2,1)} %bitcast.3.ham_ref), channel_id=1, source_target_pairs={{3,4},{7,8},{11,12},{4,3},{8,7},{12,11},{35,36},{39,40},{43,44},{3... | collective-permute-start | bytes 1572872 | tf_op jit(solution)/shard_map/ppermute | solution.py:47
  13.7 1.0 dynamic-slice_bitcast_fusion
  14.7 2.5 %collective-permute-start = (bf16[256,512]{1,0:T(8,128)(2,1)S(1)}, bf16[256,512]{1,0:T(8,128)(2,1)S(1)}, u32[]{:S(2)}, u32[]{:S(2)}) collective-permute-start(bf16[256,512]{1,0:T(8,128)(2,1)S(1)} %dynamic-slice_bitcast_fusion), channel_id=1, source_target_pairs={{0,1},{1,2},{2,3},{3,4},{4,5},{5,6},{6,7},{7,8},{8,9},{9,10},{10,1... | collective-permute-start | bytes 786440 | tf_op jit(solution)/shard_map/ppermute | solution.py:26
  17.3 19.9 %collective-permute-done.mine_ref = bf16[256,512]{1,0:T(8,128)(2,1)S(1)} collective-permute-done((bf16[256,512]{1,0:T(8,128)(2,1)S(1)}, bf16[256,512]{1,0:T(8,128)(2,1)S(1)}, u32[]{:S(2)}, u32[]{:S(2)}) %collective-permute-start) | collective-permute-done | bytes 262176 | tf_op jit(solution)/shard_map/ppermute | solution.py:26
  37.2 0.7 shard_map.70
  37.9 0.6 collective-permute-start.8
  38.5 0.3 collective-permute-done.1.theirs_ref
  38.7 1.4 shard_map.69
  40.1 1.9 collective-permute-start.13
  42.0 0.2 collective-permute-start.10
  42.2 8.6 %collective-permute-start.14 = (bf16[256,512]{1,0:T(8,128)(2,1)S(1)}, bf16[256,512]{1,0:T(8,128)(2,1)S(1)}, u32[]{:S(2)}, u32[]{:S(2)}) collective-permute-start(bf16[256,512]{1,0:T(8,128)(2,1)S(1)} %get-tuple-element.43), channel_id=1, source_target_pairs={{0,1},{1,2},{2,3},{3,4},{4,5},{5,6},{6,7},{7,8},{8,9},{9,10},{10,1... | collective-permute-start | bytes 786440 | tf_op jit(solution)/shard_map/ppermute | solution.py:26
  50.8 8.8 %collective-permute-done.13.up_ref = bf16[256,512]{1,0:T(8,128)(2,1)S(1)} collective-permute-done((bf16[256,512]{1,0:T(8,128)(2,1)S(1)}, bf16[256,512]{1,0:T(8,128)(2,1)S(1)}, u32[]{:S(2)}, u32[]{:S(2)}) %collective-permute-start.13) | collective-permute-done | bytes 262176 | tf_op jit(solution)/shard_map/ppermute | solution.py:26
  59.6 0.5 collective-permute-start.16
  60.2 1.0 collective-permute-done.15.got_up_ref
  61.2 0.4 collective-permute-done.16.got_down_ref
  61.5 5.4 %shard_map.72 = (bf16[16,2,32,512]{3,2,1,0:T(8,128)(2,1)S(1)}, bf16[512,512]{1,0:T(8,128)(2,1)S(1)}, bf16[512,512]{1,0:T(8,128)(2,1)S(1)}) custom-call(f32[2]{0:T(128)S(1)} %copy-done.9, f32[2]{0:T(128)S(1)} %convert_convert_fusion.inverse_ref, f32[2]{0:T(128)S(1)} %add_convert_fusion.edge_ref, s32[2]{0:T(128)S(1)} %pad_add_fusion.at_ref, ...), custom_call_target="tpu_custom_call" | custom-call | tf_op jit(solution)/shard_map/pallas_call | solution.py:357
  67.0 22.2 %all_to_all.20 = bf16[16,2,32,512]{3,2,1,0:T(8,128)(2,1)S(1)} all-to-all(bf16[16,2,32,512]{3,2,1,0:T(8,128)(2,1)S(1)} %get-tuple-element.44), channel_id=1, replica_groups=mesh['zlo'=2,'y'=4,'core'=2,'row'=4,'x'=4] {'zlo','y','core'}, dimensions={0} | all-to-all | bytes 2097152 | tf_op jit(solution)/shard_map/all_to_all | solution.py:337
  89.2 4.9 %shard_map.73 = bf16[32,32,512]{2,1,0:T(8,128)(2,1)} custom-call(s32[8]{0:T(128)S(1)} %copy-done.10, bf16[32,32,512]{2,1,0:T(8,128)(2,1)S(1)} %bitcast.28, bf16[32,512]{1,0:T(8,128)(2,1)S(1)} %bitcast.30), custom_call_target="tpu_custom_call" | custom-call | tf_op jit(solution)/shard_map/pallas_call | solution.py:328
  94.1 5.6 %all-to-all-start.1 = ((bf16[32,32,512]{2,1,0:T(8,128)(2,1)}), bf16[32,32,512]{2,1,0:T(8,128)(2,1)S(1)}, u32[]{:S(2)}, u32[]{:S(2)}) async-start(bf16[32,32,512]{2,1,0:T(8,128)(2,1)} %shard_map.73), calls=%async_computation.1 | async-start | bytes 2097152 | tf_op jit(solution)/shard_map/all_to_all | solution.py:337
  99.6 0.3 collective-permute-start.5
  99.9 3.5 %collective-permute-start.18 = (bf16[512,512]{1,0:T(8,128)(2,1)}, bf16[512,512]{1,0:T(8,128)(2,1)S(1)}, u32[]{:S(2)}, u32[]{:S(2)}) collective-permute-start(bf16[512,512]{1,0:T(8,128)(2,1)} %copy-done.12), channel_id=1, source_target_pairs={{0,0},{1,1},{2,16},{3,17},{16,2},{17,3},{18,18},{19,19},{4,4},{5,5... | collective-permute-start | bytes 1572872 | tf_op jit(solution)/shard_map/ppermute | solution.py:56
  103.4 2.7 %collective-permute-start.19 = (bf16[512,512]{1,0:T(8,128)(2,1)}, bf16[512,512]{1,0:T(8,128)(2,1)}, u32[]{:S(2)}, u32[]{:S(2)}) collective-permute-start(bf16[512,512]{1,0:T(8,128)(2,1)} %copy-done.11), channel_id=1, source_target_pairs={{0,1},{1,0},{2,17},{3,16},{16,3},{17,2},{18,19},{19,18},{4,5},{5,4... | collective-permute-start | bytes 1572872 | tf_op jit(solution)/shard_map/ppermute | solution.py:56
  106.1 1.3 collective-permute-start.2
  107.4 1.5 collective-permute-start.3
  108.9 15.8 %collective-permute-done.5.mine_2 = bf16[512,512]{1,0:T(8,128)(2,1)} collective-permute-done((bf16[512,512]{1,0:T(8,128)(2,1)S(1)}, bf16[512,512]{1,0:T(8,128)(2,1)}, u32[]{:S(2)}, u32[]{:S(2)}) %collective-permute-start.5) | collective-permute-done | bytes 524320 | tf_op jit(solution)/shard_map/ppermute | solution.py:30
  124.6 1.5 collective-permute-start.11
  126.1 0.8 copy-done.6
  126.9 5.0 %collective-permute-done.19.second_ref = bf16[512,512]{1,0:T(8,128)(2,1)} collective-permute-done((bf16[512,512]{1,0:T(8,128)(2,1)}, bf16[512,512]{1,0:T(8,128)(2,1)}, u32[]{:S(2)}, u32[]{:S(2)}) %collective-permute-start.19) | collective-permute-done | bytes 524320 | tf_op jit(solution)/shard_map/ppermute | solution.py:56
  131.9 1.0 copy-done.7
  133.0 1.9 shard_map.74
  134.9 1.9 collective-permute-start.20
  136.8 4.8 %collective-permute-start.21 = (bf16[512,512]{1,0:T(8,128)(2,1)}, bf16[512,512]{1,0:T(8,128)(2,1)}, u32[]{:S(2)}, u32[]{:S(2)}) collective-permute-start(bf16[512,512]{1,0:T(8,128)(2,1)} %get-tuple-element.49.inner.green_ref), channel_id=1, source_target_pairs={{0,16},{16,0},{1,17},{17,1},{2,18},{18,2},{3,19},{19,3},{4,20},{20... | collective-permute-start | bytes 1572872 | tf_op jit(solution)/shard_map/ppermute | solution.py:34
  141.8 0.5 collective-permute-start.12
  142.3 1.0 copy-done.3
  143.3 1.0 copy-done.5
  144.4 2.8 %shard_map.71 = (bf16[512,512]{1,0:T(8,128)(2,1)S(1)}, bf16[512,512]{1,0:T(8,128)(2,1)S(1)}, bf16[512,512]{1,0:T(8,128)(2,1)S(1)}, bf16[512,512]{1,0:T(8,128)(2,...) custom-call(s32[2]{0:T(128)S(1)} %pad_add_fusion.at_ref, bf16[512,512]{1,0:T(8,128)(2,1)S(1)} %bitcast.27, ...), custom_call_target="tpu_custom_call" | custom-call | tf_op jit(solution)/shard_map/pallas_call | solution.py:357
  147.2 1.9 collective-permute-done.20.beyond
  149.1 4.1 %shard_map.75 = (f32[512,512]{1,0:T(8,128)S(1)}, f32[512,512]{1,0:T(8,128)S(1)}) custom-call(s32[2]{0:T(128)S(1)} %pad_add_fusion.at_ref, f32[2]{0:T(128)S(1)} %copy-done.9, f32[2]{0:T(128)S(1)} %collective-permute-done.12.energy_pair_ref, bf16[512,512]{1,0:T(8,128)(2,1)S(1)} %get-tuple-element.37.outer_ham, ...), custom_call_target="tpu_custom_call" | custom-call | tf_op jit(solution)/shard_map/pallas_call | solution.py:357
  153.3 1.9 shard_map.77.inner
  155.2 5.7 %collective-permute-start.22 = (bf16[512,512]{1,0:T(8,128)(2,1)S(1)}, bf16[512,512]{1,0:T(8,128)(2,1)S(1)}, u32[]{:S(2)}, u32[]{:S(2)}) collective-permute-start(bf16[512,512]{1,0:T(8,128)(2,1)S(1)} %shard_map.77.inner), channel_id=1, source_target_pairs={{0,16},{16,0},{1,17},{17,1},{2,18},{18,2},{3,19},{19,3},{4,20},{20... | collective-permute-start | bytes 1572872 | tf_op jit(solution)/shard_map/ppermute | solution.py:34
  160.9 1.3 shard_map.76.outer
  162.2 1.9 collective-permute-start.25
  164.1 2.1 shard_map.78
  166.2 2.0 shard_map.79
  168.2 3.6 %collective-permute-start.26 = (bf16[8,32,512]{2,1,0:T(8,128)(2,1)S(1)}, bf16[8,32,512]{2,1,0:T(8,128)(2,1)S(1)}, u32[]{:S(2)}, u32[]{:S(2)}) collective-permute-start(bf16[8,32,512]{2,1,0:T(8,128)(2,1)S(1)} %get-tuple-element.56), channel_id=1, source_target_pairs={{0,16},{16,0},{1,17},{17,1},{2,18},{18,2},{3,19},{19,3},{4,20},{20... | collective-permute-start | bytes 786440 | tf_op jit(solution)/shard_map/ppermute | solution.py:34
  171.8 2.9 %collective-permute-done.25.beyond = bf16[512,512]{1,0:T(8,128)(2,1)S(1)} collective-permute-done((bf16[512,512]{1,0:T(8,128)(2,1)S(1)}, bf16[512,512]{1,0:T(8,128)(2,1)S(1)}, u32[]{:S(2)}, u32[]{:S(2)}) %collective-permute-start.25) | collective-permute-done | bytes 524320 | tf_op jit(solution)/shard_map/ppermute | solution.py:40
  174.7 2.1 shard_map.80
  176.8 4.6 %collective-permute-start.29 = (bf16[8,32,512]{2,1,0:T(8,128)(2,1)S(1)}, bf16[8,32,512]{2,1,0:T(8,128)(2,1)S(1)}, u32[]{:S(2)}, u32[]{:S(2)}) collective-permute-start(bf16[8,32,512]{2,1,0:T(8,128)(2,1)S(1)} %get-tuple-element.59), channel_id=1, source_target_pairs={{0,16},{16,0},{1,17},{17,1},{2,18},{18,2},{3,19},{19,3},{4,20},{20... | collective-permute-start | bytes 786440 | tf_op jit(solution)/shard_map/ppermute | solution.py:34
  181.4 1.2 collective-permute-done.29
  182.6 26.0 %all_to_all.21.green_ref = bf16[32,32,512]{2,1,0:T(8,128)(2,1)S(1)} all-to-all(bf16[32,32,512]{2,1,0:T(8,128)(2,1)S(1)} %bitcast.29), channel_id=1, replica_groups=mesh['zlo'=2,'y'=4,'core'=2,'row'=4,'x'=4] {'x','zlo','y'}, dimensions={0} | all-to-all | bytes 2097152 | tf_op jit(solution)/shard_map/all_to_all | solution.py:337
  208.6 4.9 %shard_map.82 = bf16[32,32,512]{2,1,0:T(8,128)(2,1)} custom-call(s32[8]{0:T(128)S(1)} %copy-done.10, bf16[32,32,512]{2,1,0:T(8,128)(2,1)S(1)} %all_to_all.21.green_ref, bf16[32,512]{1,0:T(8,128)(2,1)S(1)} %bitcast.31), custom_call_target="tpu_custom_call" | custom-call | tf_op jit(solution)/shard_map/pallas_call | solution.py:328
  213.5 3.7 %all-to-all-start.3 = ((bf16[16,2,32,512]{3,2,1,0:T(8,128)(2,1)}), bf16[16,2,32,512]{3,2,1,0:T(8,128)(2,1)S(1)}, u32[]{:S(2)}, u32[]{:S(2)}) async-start(bf16[16,2,32,512]{3,2,1,0:T(8,128)(2,1)} %bitcast.14), calls=%async_computation.3 | async-start | bytes 2097152 | tf_op jit(solution)/shard_map/all_to_all | solution.py:337
  217.2 0.7 collective-permute-start.23
  217.9 3.9 %collective-permute-start.24 = (bf16[512,512]{1,0:T(8,128)(2,1)S(1)}, bf16[512,512]{1,0:T(8,128)(2,1)S(1)}, u32[]{:S(2)}, u32[]{:S(2)}) collective-permute-start(bf16[512,512]{1,0:T(8,128)(2,1)S(1)} %get-tuple-element.53), channel_id=1, source_target_pairs={{1,1},{3,17},{17,2},{19,18},{5,5},{7,21},{21,6},{23,22},{9,9},{11,... | collective-permute-start | bytes 1572872 | tf_op jit(solution)/shard_map/ppermute | solution.py:97
  221.8 1.3 collective-permute-start.27
  223.1 5.5 %collective-permute-start.28 = (bf16[512,512]{1,0:T(8,128)(2,1)S(1)}, bf16[512,512]{1,0:T(8,128)(2,1)S(1)}, u32[]{:S(2)}, u32[]{:S(2)}) collective-permute-start(bf16[512,512]{1,0:T(8,128)(2,1)S(1)} %get-tuple-element.57), channel_id=1, source_target_pairs={{1,0},{3,16},{17,3},{19,19},{5,4},{7,20},{21,7},{23,23},{9,8},{11,... | collective-permute-start | bytes 1572872 | tf_op jit(solution)/shard_map/ppermute | solution.py:97
  228.6 3.3 %collective-permute-done.24.inner_1 = bf16[512,512]{1,0:T(8,128)(2,1)S(1)} collective-permute-done((bf16[512,512]{1,0:T(8,128)(2,1)S(1)}, bf16[512,512]{1,0:T(8,128)(2,1)S(1)}, u32[]{:S(2)}, u32[]{:S(2)}) %collective-permute-start.24) | collective-permute-done | bytes 524320 | tf_op jit(solution)/shard_map/ppermute | solution.py:97
  231.8 7.2 %collective-permute-done.27.outer_0 = bf16[512,512]{1,0:T(8,128)(2,1)S(1)} collective-permute-done((bf16[512,512]{1,0:T(8,128)(2,1)S(1)}, bf16[512,512]{1,0:T(8,128)(2,1)S(1)}, u32[]{:S(2)}, u32[]{:S(2)}) %collective-permute-start.27) | collective-permute-done | bytes 524320 | tf_op jit(solution)/shard_map/ppermute | solution.py:97
  239.1 2.0 shard_map.81
  241.1 1.0 copy.7
  (50 shorter events, 0.4 us)
Async XLA Ops:
  0.8 1.0 copy-start
  4.2 55.9 %copy-start.9 = (f32[2]{0:T(128)S(1)}, f32[2]{0:T(128)}, u32[]{:S(2)}) copy-start(f32[2]{0:T(128)} %energy_ref.5) | copy-start | bytes 28
  4.2 57.3 %copy-start.1 = (bf16[1,512,512]{2,1,0:T(8,128)(2,1)S(1)}, bf16[1,512,512]{2,1,0:T(8,128)(2,1)}, u32[]{:S(2)}) copy-start(bf16[1,512,512]{2,1,0:T(8,128)(2,1)} %param.7) | copy-start | bytes 1572868
  4.2 33.0 %collective-permute-start.4 = (bf16[512,512]{1,0:T(8,128)(2,1)}, bf16[512,512]{1,0:T(8,128)(2,1)S(1)}, u32[]{:S(2)}, u32[]{:S(2)}) collective-permute-start(bf16[512,512]{1,0:T(8,128)(2,1)} %get-tuple-element.33), channel_id=1, source_target_pairs={{0,1},{1,2},{2,3},{3,0},{4,5},{5,6},{6,7},{7,4},{8,9},{9,10},{10,1... | collective-permute-start | bytes 1572872 | tf_op jit(solution)/shard_map/ppermute | solution.py:30
  4.7 32.5 %collective-permute-start.6 = (bf16[512,512]{1,0:T(8,128)(2,1)}, bf16[512,512]{1,0:T(8,128)(2,1)S(1)}, u32[]{:S(2)}, u32[]{:S(2)}) collective-permute-start(bf16[512,512]{1,0:T(8,128)(2,1)} %get-tuple-element.33), channel_id=1, source_target_pairs={{0,3},{1,0},{2,1},{3,2},{4,7},{5,4},{6,5},{7,6},{8,11},{9,8},{10,9... | collective-permute-start | bytes 1572872 | tf_op jit(solution)/shard_map/ppermute | solution.py:30
  6.2 31.0 %collective-permute-start.7 = (bf16[512,512]{1,0:T(8,128)(2,1)}, bf16[512,512]{1,0:T(8,128)(2,1)S(1)}, u32[]{:S(2)}, u32[]{:S(2)}) collective-permute-start(bf16[512,512]{1,0:T(8,128)(2,1)} %bitcast.3.ham_ref), channel_id=1, source_target_pairs={{3,4},{7,8},{11,12},{4,3},{8,7},{12,11},{35,36},{39,40},{43,44},{3... | collective-permute-start | bytes 1572872 | tf_op jit(solution)/shard_map/ppermute | solution.py:47
  14.7 22.5 %collective-permute-start = (bf16[256,512]{1,0:T(8,128)(2,1)S(1)}, bf16[256,512]{1,0:T(8,128)(2,1)S(1)}, u32[]{:S(2)}, u32[]{:S(2)}) collective-permute-start(bf16[256,512]{1,0:T(8,128)(2,1)S(1)} %dynamic-slice_bitcast_fusion), channel_id=1, source_target_pairs={{0,1},{1,2},{2,3},{3,4},{4,5},{5,6},{6,7},{7,8},{8,9},{9,10},{10,1... | collective-permute-start | bytes 786440 | tf_op jit(solution)/shard_map/ppermute | solution.py:26
  37.2 1.5 collective-permute-start.1
  37.9 22.3 %collective-permute-start.8 = (bf16[512,512]{1,0:T(8,128)(2,1)S(1)}, bf16[512,512]{1,0:T(8,128)(2,1)S(1)}, u32[]{:S(2)}, u32[]{:S(2)}) collective-permute-start(bf16[512,512]{1,0:T(8,128)(2,1)S(1)} %get-tuple-element.34.previous_ref), channel_id=1, source_target_pairs={{0,16},{16,0},{1,17},{17,1},{2,18},{18,2},{3,19},{19,3},{4,20},{20... | collective-permute-start | bytes 1572872 | tf_op jit(solution)/shard_map/ppermute | solution.py:34
  40.1 19.5 %collective-permute-start.13 = (bf16[256,512]{1,0:T(8,128)(2,1)S(1)}, bf16[256,512]{1,0:T(8,128)(2,1)S(1)}, u32[]{:S(2)}, u32[]{:S(2)}) collective-permute-start(bf16[256,512]{1,0:T(8,128)(2,1)S(1)} %get-tuple-element.43), channel_id=1, source_target_pairs={{1,0},{2,1},{3,2},{4,3},{5,4},{6,5},{7,6},{8,7},{9,8},{10,9},{11,1... | collective-permute-start | bytes 786440 | tf_op jit(solution)/shard_map/ppermute | solution.py:26
  42.0 18.1 %collective-permute-start.10 = (bf16[512,512]{1,0:T(8,128)(2,1)S(1)}, bf16[512,512]{1,0:T(8,128)(2,1)S(1)}, u32[]{:S(2)}, u32[]{:S(2)}) collective-permute-start(bf16[512,512]{1,0:T(8,128)(2,1)S(1)} %get-tuple-element.35.next_ref), channel_id=1, source_target_pairs={{0,16},{16,0},{1,17},{17,1},{2,18},{18,2},{3,19},{19,3},{4,20},{20... | collective-permute-start | bytes 1572872 | tf_op jit(solution)/shard_map/ppermute | solution.py:34
  42.2 17.4 %collective-permute-start.14 = (bf16[256,512]{1,0:T(8,128)(2,1)S(1)}, bf16[256,512]{1,0:T(8,128)(2,1)S(1)}, u32[]{:S(2)}, u32[]{:S(2)}) collective-permute-start(bf16[256,512]{1,0:T(8,128)(2,1)S(1)} %get-tuple-element.43), channel_id=1, source_target_pairs={{0,1},{1,2},{2,3},{3,4},{4,5},{5,6},{6,7},{7,8},{8,9},{9,10},{10,1... | collective-permute-start | bytes 786440 | tf_op jit(solution)/shard_map/ppermute | solution.py:26
  59.6 1.5 collective-permute-start.15
  59.6 1.9 collective-permute-start.16
  60.2 6.8 %copy-start.2 = (bf16[512,512]{1,0:T(8,128)(2,1)}, bf16[512,512]{1,0:T(8,128)(2,1)S(1)}, u32[]{:S(2)}) copy-start(bf16[512,512]{1,0:T(8,128)(2,1)S(1)} %collective-permute-done.8.other_1.got_previous_ref) | copy-start | bytes 1572868
  60.2 6.7 %copy-start.4 = (bf16[512,512]{1,0:T(8,128)(2,1)}, bf16[512,512]{1,0:T(8,128)(2,1)S(1)}, u32[]{:S(2)}) copy-start(bf16[512,512]{1,0:T(8,128)(2,1)S(1)} %collective-permute-done.10.other_3.got_next_ref) | copy-start | bytes 1572868
  66.9 22.3 %copy-start.11 = (bf16[512,512]{1,0:T(8,128)(2,1)}, bf16[512,512]{1,0:T(8,128)(2,1)S(1)}, u32[]{:S(2)}) copy-start(bf16[512,512]{1,0:T(8,128)(2,1)S(1)} %get-tuple-element.47) | copy-start | bytes 1572868
  66.9 22.3 %copy-start.12 = (bf16[512,512]{1,0:T(8,128)(2,1)}, bf16[512,512]{1,0:T(8,128)(2,1)S(1)}, u32[]{:S(2)}) copy-start(bf16[512,512]{1,0:T(8,128)(2,1)S(1)} %get-tuple-element.46) | copy-start | bytes 1572868
  66.9 22.2 %copy-start.8 = (bf16[1,32,512]{2,1,0:T(8,128)(2,1)S(1)}, bf16[1,32,512]{2,1,0:T(8,128)(2,1)}, u32[]{:S(2)}) copy-start(bf16[1,32,512]{2,1,0:T(8,128)(2,1)} %param.8) | copy-start | bytes 98308
  67.0 22.2 %copy-start.10 = (s32[8]{0:T(128)S(1)}, s32[8]{0:T(128)}, u32[]{:S(2)}) copy-start(s32[8]{0:T(128)} %offset_ref.3) | copy-start | bytes 100
  94.1 47.6 %all-to-all-start.1 = ((bf16[32,32,512]{2,1,0:T(8,128)(2,1)}), bf16[32,32,512]{2,1,0:T(8,128)(2,1)S(1)}, u32[]{:S(2)}, u32[]{:S(2)}) async-start(bf16[32,32,512]{2,1,0:T(8,128)(2,1)} %shard_map.73), calls=%async_computation.1 | async-start | bytes 2097152 | tf_op jit(solution)/shard_map/all_to_all | solution.py:337
  99.6 25.0 %collective-permute-start.5 = (bf16[512,512]{1,0:T(8,128)(2,1)S(1)}, bf16[512,512]{1,0:T(8,128)(2,1)}, u32[]{:S(2)}, u32[]{:S(2)}) collective-permute-start(bf16[512,512]{1,0:T(8,128)(2,1)S(1)} %collective-permute-done.4.one_ref.mine_1), channel_id=1, source_target_pairs={{0,1},{1,2},{2,3},{3,0},{4,5},{5,6},{6,7},{7,4},{8,9},{9,10},{10,1... | collective-permute-start | bytes 1572872 | tf_op jit(solution)/shard_map/ppermute | solution.py:30
  99.9 26.2 %collective-permute-start.18 = (bf16[512,512]{1,0:T(8,128)(2,1)}, bf16[512,512]{1,0:T(8,128)(2,1)S(1)}, u32[]{:S(2)}, u32[]{:S(2)}) collective-permute-start(bf16[512,512]{1,0:T(8,128)(2,1)} %copy-done.12), channel_id=1, source_target_pairs={{0,0},{1,1},{2,16},{3,17},{16,2},{17,3},{18,18},{19,19},{4,4},{5,5... | collective-permute-start | bytes 1572872 | tf_op jit(solution)/shard_map/ppermute | solution.py:56
  103.4 28.6 %collective-permute-start.19 = (bf16[512,512]{1,0:T(8,128)(2,1)}, bf16[512,512]{1,0:T(8,128)(2,1)}, u32[]{:S(2)}, u32[]{:S(2)}) collective-permute-start(bf16[512,512]{1,0:T(8,128)(2,1)} %copy-done.11), channel_id=1, source_target_pairs={{0,1},{1,0},{2,17},{3,16},{16,3},{17,2},{18,19},{19,18},{4,5},{5,4... | collective-permute-start | bytes 1572872 | tf_op jit(solution)/shard_map/ppermute | solution.py:56
  106.1 30.7 %collective-permute-start.2 = (bf16[512,512]{1,0:T(8,128)(2,1)}, bf16[512,512]{1,0:T(8,128)(2,1)}, u32[]{:S(2)}, u32[]{:S(2)}) collective-permute-start(bf16[512,512]{1,0:T(8,128)(2,1)} %get-tuple-element.32.below_ref), channel_id=1, source_target_pairs={{0,1},{16,3},{4,5},{20,7},{8,9},{24,11},{12,13},{28,15},{32,33},{4... | collective-permute-start | bytes 1572872 | tf_op jit(solution)/shard_map/ppermute | solution.py:51
  107.4 34.3 %collective-permute-start.3 = (bf16[512,512]{1,0:T(8,128)(2,1)}, bf16[512,512]{1,0:T(8,128)(2,1)}, u32[]{:S(2)}, u32[]{:S(2)}) collective-permute-start(bf16[512,512]{1,0:T(8,128)(2,1)} %get-tuple-element.32.below_ref), channel_id=1, source_target_pairs={{0,2},{4,6},{8,10},{12,14},{32,34},{36,38},{40,42},{44,46},{64,66}... | collective-permute-start | bytes 1572872 | tf_op jit(solution)/shard_map/ppermute | solution.py:51
  124.6 17.2 %collective-permute-start.11 = (bf16[512,512]{1,0:T(8,128)(2,1)S(1)}, bf16[512,512]{1,0:T(8,128)(2,1)}, u32[]{:S(2)}, u32[]{:S(2)}) collective-permute-start(bf16[512,512]{1,0:T(8,128)(2,1)S(1)} %collective-permute-done.4.one_ref.mine_1), channel_id=1, source_target_pairs={{0,16},{4,20},{8,24},{12,28},{32,48},{36,52},{40,56},{44,60},{64,8... | collective-permute-start | bytes 1572872 | tf_op jit(solution)/shard_map/ppermute | solution.py:51
  126.1 0.8 copy-start.6
  126.9 15.4 %collective-permute-start.9 = (bf16[512,512]{1,0:T(8,128)(2,1)}, bf16[512,512]{1,0:T(8,128)(2,1)}, u32[]{:S(2)}, u32[]{:S(2)}) collective-permute-start(bf16[512,512]{1,0:T(8,128)(2,1)} %collective-permute-done.5.mine_2), channel_id=1, source_target_pairs={{0,16},{16,0},{1,17},{17,1},{2,18},{18,2},{3,19},{19,3},{4,20},{20... | collective-permute-start | bytes 1572872 | tf_op jit(solution)/shard_map/ppermute | solution.py:34
  131.9 1.0 copy-start.7
  134.9 14.2 %collective-permute-start.20 = (bf16[512,512]{1,0:T(8,128)(2,1)S(1)}, bf16[512,512]{1,0:T(8,128)(2,1)}, u32[]{:S(2)}, u32[]{:S(2)}) collective-permute-start(bf16[512,512]{1,0:T(8,128)(2,1)S(1)} %get-tuple-element.48.outer.green_ref), channel_id=1, source_target_pairs={{16,4},{20,8},{24,12},{4,16},{8,20},{12,24},{17,5},{21,9},{25,13},... | collective-permute-start | bytes 1572872 | tf_op jit(solution)/shard_map/ppermute | solution.py:40
  136.8 12.3 %collective-permute-start.21 = (bf16[512,512]{1,0:T(8,128)(2,1)}, bf16[512,512]{1,0:T(8,128)(2,1)}, u32[]{:S(2)}, u32[]{:S(2)}) collective-permute-start(bf16[512,512]{1,0:T(8,128)(2,1)} %get-tuple-element.49.inner.green_ref), channel_id=1, source_target_pairs={{0,16},{16,0},{1,17},{17,1},{2,18},{18,2},{3,19},{19,3},{4,20},{20... | collective-permute-start | bytes 1572872 | tf_op jit(solution)/shard_map/ppermute | solution.py:34
  141.7 11.6 %collective-permute-start.17 = (bf16[2,8,32,512]{3,2,1,0:T(8,128)(2,1)S(1)}, bf16[2,8,32,512]{3,2,1,0:T(8,128)(2,1)S(1)}, u32[]{:S(2)}, u32[]{:S(2)}) collective-permute-start(bf16[2,8,32,512]{3,2,1,0:T(8,128)(2,1)S(1)} %constant_dynamic-slice_fusion), channel_id=1, source_target_pairs={{0,16},{16,0},{1,17},{17,1},{2,18},{18,2},{3,19},{19,3},{4,20},{20... | collective-permute-start | bytes 1572872 | tf_op jit(solution)/shard_map/ppermute | solution.py:34
  141.8 5.4 %collective-permute-start.12 = (f32[2]{0:T(128)S(1)}, f32[2]{0:T(128)S(1)}, u32[]{:S(2)}, u32[]{:S(2)}) collective-permute-start(f32[2]{0:T(128)S(1)} %copy-done.9), channel_id=1, source_target_pairs={{0,16},{16,0},{1,17},{17,1},{2,18},{18,2},{3,19},{19,3},{4,20},{20... | collective-permute-start | bytes 32 | tf_op jit(solution)/shard_map/ppermute | solution.py:34
  142.3 1.0 copy-start.3
  143.3 1.0 copy-start.5
  155.2 11.1 %collective-permute-start.22 = (bf16[512,512]{1,0:T(8,128)(2,1)S(1)}, bf16[512,512]{1,0:T(8,128)(2,1)S(1)}, u32[]{:S(2)}, u32[]{:S(2)}) collective-permute-start(bf16[512,512]{1,0:T(8,128)(2,1)S(1)} %shard_map.77.inner), channel_id=1, source_target_pairs={{0,16},{16,0},{1,17},{17,1},{2,18},{18,2},{3,19},{19,3},{4,20},{20... | collective-permute-start | bytes 1572872 | tf_op jit(solution)/shard_map/ppermute | solution.py:34
  162.2 12.5 %collective-permute-start.25 = (bf16[512,512]{1,0:T(8,128)(2,1)S(1)}, bf16[512,512]{1,0:T(8,128)(2,1)S(1)}, u32[]{:S(2)}, u32[]{:S(2)}) collective-permute-start(bf16[512,512]{1,0:T(8,128)(2,1)S(1)} %shard_map.76.outer), channel_id=1, source_target_pairs={{16,4},{20,8},{24,12},{4,16},{8,20},{12,24},{17,5},{21,9},{25,13},... | collective-permute-start | bytes 1572872 | tf_op jit(solution)/shard_map/ppermute | solution.py:40
  168.2 6.5 %collective-permute-start.26 = (bf16[8,32,512]{2,1,0:T(8,128)(2,1)S(1)}, bf16[8,32,512]{2,1,0:T(8,128)(2,1)S(1)}, u32[]{:S(2)}, u32[]{:S(2)}) collective-permute-start(bf16[8,32,512]{2,1,0:T(8,128)(2,1)S(1)} %get-tuple-element.56), channel_id=1, source_target_pairs={{0,16},{16,0},{1,17},{17,1},{2,18},{18,2},{3,19},{19,3},{4,20},{20... | collective-permute-start | bytes 786440 | tf_op jit(solution)/shard_map/ppermute | solution.py:34
  176.8 5.7 %collective-permute-start.29 = (bf16[8,32,512]{2,1,0:T(8,128)(2,1)S(1)}, bf16[8,32,512]{2,1,0:T(8,128)(2,1)S(1)}, u32[]{:S(2)}, u32[]{:S(2)}) collective-permute-start(bf16[8,32,512]{2,1,0:T(8,128)(2,1)S(1)} %get-tuple-element.59), channel_id=1, source_target_pairs={{0,16},{16,0},{1,17},{17,1},{2,18},{18,2},{3,19},{19,3},{4,20},{20... | collective-permute-start | bytes 786440 | tf_op jit(solution)/shard_map/ppermute | solution.py:34
  213.5 27.6 %all-to-all-start.3 = ((bf16[16,2,32,512]{3,2,1,0:T(8,128)(2,1)}), bf16[16,2,32,512]{3,2,1,0:T(8,128)(2,1)S(1)}, u32[]{:S(2)}, u32[]{:S(2)}) async-start(bf16[16,2,32,512]{3,2,1,0:T(8,128)(2,1)} %bitcast.14), calls=%async_computation.3 | async-start | bytes 2097152 | tf_op jit(solution)/shard_map/all_to_all | solution.py:337
  217.2 11.4 %collective-permute-start.23 = (bf16[512,512]{1,0:T(8,128)(2,1)S(1)}, bf16[512,512]{1,0:T(8,128)(2,1)S(1)}, u32[]{:S(2)}, u32[]{:S(2)}) collective-permute-start(bf16[512,512]{1,0:T(8,128)(2,1)S(1)} %get-tuple-element.53), channel_id=1, source_target_pairs={{0,1},{2,17},{16,2},{18,18},{4,5},{6,21},{20,6},{22,22},{8,9},{10,... | collective-permute-start | bytes 1572872 | tf_op jit(solution)/shard_map/ppermute | solution.py:97
  217.9 14.0 %collective-permute-start.24 = (bf16[512,512]{1,0:T(8,128)(2,1)S(1)}, bf16[512,512]{1,0:T(8,128)(2,1)S(1)}, u32[]{:S(2)}, u32[]{:S(2)}) collective-permute-start(bf16[512,512]{1,0:T(8,128)(2,1)S(1)} %get-tuple-element.53), channel_id=1, source_target_pairs={{1,1},{3,17},{17,2},{19,18},{5,5},{7,21},{21,6},{23,22},{9,9},{11,... | collective-permute-start | bytes 1572872 | tf_op jit(solution)/shard_map/ppermute | solution.py:97
  221.8 17.3 %collective-permute-start.27 = (bf16[512,512]{1,0:T(8,128)(2,1)S(1)}, bf16[512,512]{1,0:T(8,128)(2,1)S(1)}, u32[]{:S(2)}, u32[]{:S(2)}) collective-permute-start(bf16[512,512]{1,0:T(8,128)(2,1)S(1)} %get-tuple-element.57), channel_id=1, source_target_pairs={{0,0},{2,16},{16,3},{18,19},{4,4},{6,20},{20,7},{22,23},{8,8},{10,... | collective-permute-start | bytes 1572872 | tf_op jit(solution)/shard_map/ppermute | solution.py:97
  223.1 16.0 %collective-permute-start.28 = (bf16[512,512]{1,0:T(8,128)(2,1)S(1)}, bf16[512,512]{1,0:T(8,128)(2,1)S(1)}, u32[]{:S(2)}, u32[]{:S(2)}) collective-permute-start(bf16[512,512]{1,0:T(8,128)(2,1)S(1)} %get-tuple-element.57), channel_id=1, source_target_pairs={{1,0},{3,16},{17,3},{19,19},{5,4},{7,20},{21,7},{23,23},{9,8},{11,... | collective-permute-start | bytes 1572872 | tf_op jit(solution)/shard_map/ppermute | solution.py:97

commit v8 on v7

--- a/solution.py
+++ b/solution.py
@@ -114,6 +114,11 @@
     half_ref[...] = pair_ref[pl.ds(pl.multiple_of(core * half, half), half)].astype(jnp.bfloat16)
 
 
+def above_body(keep_ref, at_ref, c_ref, mine_ref, theirs_ref, out_ref, whole):
+    place_halves(at_ref[0], whole, mine_ref[...], theirs_ref[...])
+    out_ref[...] = dot_t(whole[...], whole[...]) * keep_ref[0] + dot(c_ref[...].T, c_ref[...])
+
+
 def first_step(energy, inverse, ham, pair, eye):
     square = inverse * inverse
     return (
@@ -139,7 +144,7 @@
 
 def second_body(
     energy_ref, inverse_ref, edge_ref, at_ref, ham_ref, pair_ref, c_ref, lower_turned_ref, previous_ref, next_ref,
-    got_previous_ref, got_next_ref, up_ref, down_ref, got_up_ref, got_down_ref, out_ref, first_ref, second_ref, whole,
+    got_previous_ref, got_next_ref, above_ref, down_ref, got_down_ref, out_ref, first_ref, second_ref, whole,
 ):
     n = c_ref.shape[0]
     eye, rotate = tables(n)
@@ -147,8 +152,7 @@
     first = at_ref[0] == 0
     whole[0] = jnp.where(first, next_ref[...], got_next_ref[...])
     whole[1] = jnp.where(first, previous_ref[...], got_previous_ref[...])
-    place_halves(at_ref[0], whole.at[2], up_ref[...], got_up_ref[...])
-    place_halves(at_ref[0], whole.at[3], down_ref[...], got_down_ref[...])
+    place_halves(at_ref[0], whole.at[2], down_ref[...], got_down_ref[...])
     odd = lax.rem(at_ref[1], 2)
     turn = BROAD * rotate
     ham = ham_ref[...].astype(jnp.float32) - turn
@@ -156,8 +160,8 @@
     ham_below = whole[1].astype(jnp.float32) - turn
     for e, same_ref in ((odd, first_ref), (1 - odd, second_ref)):
         energy, inverse = energy_ref[e], inverse_ref[e]
-        above = first_step(energy, inverse * edge_ref[0], ham_above, whole[2], eye)
-        below = first_step(energy, inverse * edge_ref[1], ham_below, whole[3], eye)
+        above = first_step(energy, inverse * edge_ref[0], ham_above, above_ref[...], eye)
+        below = first_step(energy, inverse * edge_ref[1], ham_below, whole[2], eye)
         green = first_step(energy, inverse, ham, pair_ref[...], eye)
         terms = linked(above, c_ref[...]) + linked(below, lower_turned_ref[...])
         matrix = (energy * eye - ham - terms).astype(jnp.bfloat16)
@@ -344,7 +348,7 @@
     rows, pairs = n // parts, parts // 2
     count = 2 * parts
     place, x, core = lax.axis_index(SLAB), lax.axis_index("x"), lax.axis_index("core")
-    edge = jnp.stack([place < lax.axis_size(SLAB) - 1, place > 0]).astype(jnp.float32)
+    edge = jnp.stack([place < lax.axis_size(SLAB) - 1, place > 0, place < lax.axis_size(SLAB) - 2]).astype(jnp.float32)
     at = jnp.stack([core, x]).astype(jnp.int32)
     inverse = (1.0 / energies).astype(jnp.bfloat16).astype(jnp.float32)
     half = lambda value: lax.dynamic_slice_in_dim(value, core * (n // 2), n // 2, 0)
@@ -356,7 +360,9 @@
     def run(body, out_shape, in_specs, *operands, scratch=()):
         return call(body, out_shape, in_specs, scratch)(*operands)
 
-    lower_mine = passed_along(half(c), 1)
+    c_half = half(c)
+    lower_mine = passed_along(c_half, 1)
+    upper_mine = passed_along(c_half, -1)
     energy_pair = swapped(energies)
     own, load = run(own_body, (wide(n, n), thin(n, n)), [SM, SM, VM, VM], edge[:1], at, c, ham)
     lower_theirs = swapped(lower_mine)
@@ -366,15 +372,20 @@
         pair_body, (wide(n, n), thin(n // 2, n), thin(n, n), thin(n, n)), [SM, VM, VM, VM],
         at, own, lower_mine, lower_theirs,
     )
-    pair_up, pair_down = passed_along(pair_half, -1), passed_along(pair_half, 1)
+    pair_down = passed_along(pair_half, 1)
+    upper_theirs = swapped(upper_mine)
+    above = run(
+        above_body, wide(n, n), [SM, SM, VM, VM, VM], edge[2:], at, c, upper_mine, upper_theirs,
+        scratch=[pltpu.VMEM((n, n), jnp.bfloat16)],
+    )
     two = row_ring(one, 1)
     before, after = run(near_body, (thin(n, n),) * 2, [SM] + [VM] * 3, at, one, three, crossing)
     got_before, got_after = swapped(before), swapped(after)
-    got_up, got_down = swapped(pair_up), swapped(pair_down)
+    got_down = swapped(pair_down)
     chunks, first, second = run(
-        second_body, (thin(parts, 2, rows, n), thin(n, n), thin(n, n)), [SM] * 4 + [VM] * 12,
+        second_body, (thin(parts, 2, rows, n), thin(n, n), thin(n, n)), [SM] * 4 + [VM] * 11,
         energies, inverse, edge, at, ham, pair, c, lower_turned, before, after, got_before, got_after,
-        pair_up, pair_down, got_up, got_down, scratch=[pltpu.VMEM((4, n, n), jnp.bfloat16)],
+        above, pair_down, got_down, scratch=[pltpu.VMEM((3, n, n), jnp.bfloat16)],
     )
     first, second = flipped(first, 0), flipped(second, 1)
     received = all_to_all(chunks, ENERGY)

time: 247 us -> 249 us (level)
  Pallas kernels: 39.7 us -> 42.2 us
    pallas_call x13 -> x14, Pallas kernels: 30 us -> 32.4 us  [run(): return call(body, out_shape, in_specs, scratch)(*operands)]
  transfers between devices with their start and end apart: 32 -> 32, of which waited for: 12 -> 10; matrix products, arithmetic and copies ran while one was open for 0% -> 0% of each run, Pallas kernels for 8% -> 9%
where the time goes in v8:
time: 249 us; the launch traced here: 244 us
  starting transfers between devices  77.7 us (31%)
  waiting for transfers between devices  67 us (27%)
  blocking collectives  48.4 us (19%)
  Pallas kernels  42.2 us (17%)
  local copies, waits for them, and re-layouts  7.72 us (3%)
    all_to_all x2, blocking collectives, all_to_all(): return lax.all_to_all(value, axes, split_axis=0, concat_axis=0, tiled=True)  48.4 us
    pallas_call x14, Pallas kernels, run(): return call(body, out_shape, in_specs, scratch)(*operands)  32.4 us
    ppermute x3, waiting for transfers between devices, passed_along(): lax.ppermute(value, SLAB, [(source, source + steps) for source in range(l...  28.6 us
    ppermute x12, starting transfers between devices, swapped(): return lax.ppermute(value, 'core', [(0, 1), (1, 0)])  19.9 us
    ppermute x3, waiting for transfers between devices, row_ring(): lax.ppermute(value, 'x', [(s, (s + steps) % WIDTH) for s in range(WIDTH)])  15.6 us
    ppermute x3, starting transfers between devices, passed_along(): lax.ppermute(value, SLAB, [(source, source + steps) for source in range(l...  13.1 us
    ppermute x4, starting transfers between devices, returned(): return lax.ppermute(value, ('core', 'x'), pairs)  11.3 us
    ppermute x4, waiting for transfers between devices, returned(): return lax.ppermute(value, ('core', 'x'), pairs)  10.5 us
  transfers between devices with their start and end apart: 32, of which 10 were waited for; matrix products, arithmetic and copies ran while one was open for 0% of the time, Pallas kernels for 9%

profile of v8, /device:TPU:70, one launch (start us, length us, event | category | flops | bytes accessed | tf_op | source)
XLA Modules:
  0.0 244.2 jit_solution(7244712860260668243)
XLA Ops:
  0.7 0.6 fusion
  1.4 1.0 copy-done
  2.4 2.2 shard_map.68
  4.6 1.0 copy-done.4
  5.6 0.5 collective-permute-start.4
  6.1 1.6 collective-permute-start.6
  7.6 7.5 %collective-permute-start.7 = (bf16[512,512]{1,0:T(8,128)(2,1)}, bf16[512,512]{1,0:T(8,128)(2,1)S(1)}, u32[]{:S(2)}, u32[]{:S(2)}) collective-permute-start(bf16[512,512]{1,0:T(8,128)(2,1)} %bitcast.3.ham_ref), channel_id=1, source_target_pairs={{3,4},{7,8},{11,12},{4,3},{8,7},{12,11},{35,36},{39,40},{43,44},{3... | collective-permute-start | bytes 1572872 | tf_op jit(solution)/shard_map/ppermute | solution.py:47
  15.2 1.1 dynamic-slice_bitcast_fusion
  16.2 2.5 %collective-permute-start = (bf16[256,512]{1,0:T(8,128)(2,1)S(1)}, bf16[256,512]{1,0:T(8,128)(2,1)S(1)}, u32[]{:S(2)}, u32[]{:S(2)}) collective-permute-start(bf16[256,512]{1,0:T(8,128)(2,1)S(1)} %dynamic-slice_bitcast_fusion), channel_id=1, source_target_pairs={{0,1},{1,2},{2,3},{3,4},{4,5},{5,6},{6,7},{7,8},{8,9},{9,10},{10,1... | collective-permute-start | bytes 786440 | tf_op jit(solution)/shard_map/ppermute | solution.py:26
  18.8 19.9 %collective-permute-done.mine_ref = bf16[256,512]{1,0:T(8,128)(2,1)S(1)} collective-permute-done((bf16[256,512]{1,0:T(8,128)(2,1)S(1)}, bf16[256,512]{1,0:T(8,128)(2,1)S(1)}, u32[]{:S(2)}, u32[]{:S(2)}) %collective-permute-start) | collective-permute-done | bytes 262176 | tf_op jit(solution)/shard_map/ppermute | solution.py:26
  38.7 1.9 collective-permute-start.13
  40.7 0.7 shard_map.70
  41.3 0.6 collective-permute-start.10
  41.9 0.1 collective-permute-start.8
  42.0 1.1 shard_map.69
  43.1 0.8 copy-done.6
  43.9 8.6 %collective-permute-start.15 = (bf16[256,512]{1,0:T(8,128)(2,1)S(1)}, bf16[256,512]{1,0:T(8,128)(2,1)S(1)}, u32[]{:S(2)}, u32[]{:S(2)}) collective-permute-start(bf16[256,512]{1,0:T(8,128)(2,1)S(1)} %get-tuple-element.43), channel_id=1, source_target_pairs={{0,1},{1,2},{2,3},{3,4},{4,5},{5,6},{6,7},{7,8},{8,9},{9,10},{10,1... | collective-permute-start | bytes 786440 | tf_op jit(solution)/shard_map/ppermute | solution.py:26
  52.5 6.1 %collective-permute-done.13.mine_ref = bf16[256,512]{1,0:T(8,128)(2,1)S(1)} collective-permute-done((bf16[256,512]{1,0:T(8,128)(2,1)S(1)}, bf16[256,512]{1,0:T(8,128)(2,1)S(1)}, u32[]{:S(2)}, u32[]{:S(2)}) %collective-permute-start.13) | collective-permute-done | bytes 262176 | tf_op jit(solution)/shard_map/ppermute | solution.py:26
  58.6 2.6 %collective-permute-done.15.down_ref = bf16[256,512]{1,0:T(8,128)(2,1)S(1)} collective-permute-done((bf16[256,512]{1,0:T(8,128)(2,1)S(1)}, bf16[256,512]{1,0:T(8,128)(2,1)S(1)}, u32[]{:S(2)}, u32[]{:S(2)}) %collective-permute-start.15) | collective-permute-done | bytes 262176 | tf_op jit(solution)/shard_map/ppermute | solution.py:26
  61.2 1.9 shard_map.72.above_ref
  63.2 5.4 %shard_map.73 = (bf16[16,2,32,512]{3,2,1,0:T(8,128)(2,1)S(1)}, bf16[512,512]{1,0:T(8,128)(2,1)S(1)}, bf16[512,512]{1,0:T(8,128)(2,1)S(1)}) custom-call(f32[2]{0:T(128)S(1)} %copy-done.9, f32[2]{0:T(128)S(1)} %convert_convert_fusion.inverse_ref, f32[3]{0:T(128)S(1)} %add_convert_fusion.edge_ref, s32[2]{0:T(128)S(1)} %pad_add_fusion.at_ref, ...), custom_call_target="tpu_custom_call" | custom-call | tf_op jit(solution)/shard_map/pallas_call | solution.py:361
  68.6 22.9 %all_to_all.20 = bf16[16,2,32,512]{3,2,1,0:T(8,128)(2,1)S(1)} all-to-all(bf16[16,2,32,512]{3,2,1,0:T(8,128)(2,1)S(1)} %get-tuple-element.44), channel_id=1, replica_groups=mesh['zlo'=2,'y'=4,'core'=2,'row'=4,'x'=4] {'zlo','y','core'}, dimensions={0} | all-to-all | bytes 2097152 | tf_op jit(solution)/shard_map/all_to_all | solution.py:341
  91.5 4.9 %shard_map.74 = bf16[32,32,512]{2,1,0:T(8,128)(2,1)} custom-call(s32[8]{0:T(128)S(1)} %copy-done.10, bf16[32,32,512]{2,1,0:T(8,128)(2,1)S(1)} %bitcast.29, bf16[32,512]{1,0:T(8,128)(2,1)S(1)} %bitcast.31), custom_call_target="tpu_custom_call" | custom-call | tf_op jit(solution)/shard_map/pallas_call | solution.py:332
  96.4 5.6 %all-to-all-start.1 = ((bf16[32,32,512]{2,1,0:T(8,128)(2,1)}), bf16[32,32,512]{2,1,0:T(8,128)(2,1)S(1)}, u32[]{:S(2)}, u32[]{:S(2)}) async-start(bf16[32,32,512]{2,1,0:T(8,128)(2,1)} %shard_map.74), calls=%async_computation.1 | async-start | bytes 2097152 | tf_op jit(solution)/shard_map/all_to_all | solution.py:341
  102.0 0.3 collective-permute-start.5
  102.3 3.5 %collective-permute-start.18 = (bf16[512,512]{1,0:T(8,128)(2,1)}, bf16[512,512]{1,0:T(8,128)(2,1)}, u32[]{:S(2)}, u32[]{:S(2)}) collective-permute-start(bf16[512,512]{1,0:T(8,128)(2,1)} %copy-done.12), channel_id=1, source_target_pairs={{0,0},{1,1},{2,16},{3,17},{16,2},{17,3},{18,18},{19,19},{4,4},{5,5... | collective-permute-start | bytes 1572872 | tf_op jit(solution)/shard_map/ppermute | solution.py:56
  105.7 2.9 %collective-permute-start.19 = (bf16[512,512]{1,0:T(8,128)(2,1)}, bf16[512,512]{1,0:T(8,128)(2,1)}, u32[]{:S(2)}, u32[]{:S(2)}) collective-permute-start(bf16[512,512]{1,0:T(8,128)(2,1)} %copy-done.11), channel_id=1, source_target_pairs={{0,1},{1,0},{2,17},{3,16},{16,3},{17,2},{18,19},{19,18},{4,5},{5,4... | collective-permute-start | bytes 1572872 | tf_op jit(solution)/shard_map/ppermute | solution.py:56
  108.7 1.3 collective-permute-start.2
  110.0 1.5 collective-permute-start.3
  111.4 15.6 %collective-permute-done.5.mine_2 = bf16[512,512]{1,0:T(8,128)(2,1)} collective-permute-done((bf16[512,512]{1,0:T(8,128)(2,1)S(1)}, bf16[512,512]{1,0:T(8,128)(2,1)}, u32[]{:S(2)}, u32[]{:S(2)}) %collective-permute-start.5) | collective-permute-done | bytes 524320 | tf_op jit(solution)/shard_map/ppermute | solution.py:30
  127.0 1.5 collective-permute-start.11
  128.5 5.8 %collective-permute-done.19.second_ref = bf16[512,512]{1,0:T(8,128)(2,1)} collective-permute-done((bf16[512,512]{1,0:T(8,128)(2,1)}, bf16[512,512]{1,0:T(8,128)(2,1)}, u32[]{:S(2)}, u32[]{:S(2)}) %collective-permute-start.19) | collective-permute-done | bytes 524320 | tf_op jit(solution)/shard_map/ppermute | solution.py:56
  134.3 2.2 shard_map.75
  136.5 1.9 collective-permute-start.20
  138.5 4.8 %collective-permute-start.21 = (bf16[512,512]{1,0:T(8,128)(2,1)}, bf16[512,512]{1,0:T(8,128)(2,1)}, u32[]{:S(2)}, u32[]{:S(2)}) collective-permute-start(bf16[512,512]{1,0:T(8,128)(2,1)} %get-tuple-element.49.inner.green_ref), channel_id=1, source_target_pairs={{0,16},{16,0},{1,17},{17,1},{2,18},{18,2},{3,19},{19,3},{4,20},{20... | collective-permute-start | bytes 1572872 | tf_op jit(solution)/shard_map/ppermute | solution.py:34
  143.3 0.1 collective-permute-start.17
  143.4 0.5 collective-permute-start.12
  143.9 1.0 copy-done.3
  145.0 1.0 copy-done.7
  146.0 2.7 %shard_map.71 = (bf16[512,512]{1,0:T(8,128)(2,1)S(1)}, bf16[512,512]{1,0:T(8,128)(2,1)S(1)}, bf16[512,512]{1,0:T(8,128)(2,1)S(1)}, bf16[512,512]{1,0:T(8,128)(2,...) custom-call(s32[2]{0:T(128)S(1)} %pad_add_fusion.at_ref, bf16[512,512]{1,0:T(8,128)(2,1)S(1)} %bitcast.28, ...), custom_call_target="tpu_custom_call" | custom-call | tf_op jit(solution)/shard_map/pallas_call | solution.py:361
  148.7 2.4 collective-permute-done.20.beyond
  151.1 4.3 %shard_map.76 = (f32[512,512]{1,0:T(8,128)S(1)}, f32[512,512]{1,0:T(8,128)S(1)}) custom-call(s32[2]{0:T(128)S(1)} %pad_add_fusion.at_ref, f32[2]{0:T(128)S(1)} %copy-done.9, f32[2]{0:T(128)S(1)} %collective-permute-done.12.energy_pair_ref, bf16[512,512]{1,0:T(8,128)(2,1)S(1)} %get-tuple-element.37.outer_ham, ...), custom_call_target="tpu_custom_call" | custom-call | tf_op jit(solution)/shard_map/pallas_call | solution.py:361
  155.4 1.9 shard_map.78.inner
  157.3 5.6 %collective-permute-start.22 = (bf16[512,512]{1,0:T(8,128)(2,1)S(1)}, bf16[512,512]{1,0:T(8,128)(2,1)S(1)}, u32[]{:S(2)}, u32[]{:S(2)}) collective-permute-start(bf16[512,512]{1,0:T(8,128)(2,1)S(1)} %shard_map.78.inner), channel_id=1, source_target_pairs={{0,16},{16,0},{1,17},{17,1},{2,18},{18,2},{3,19},{19,3},{4,20},{20... | collective-permute-start | bytes 1572872 | tf_op jit(solution)/shard_map/ppermute | solution.py:34
  162.8 1.9 shard_map.77.outer
  164.7 1.9 collective-permute-start.25
  166.6 2.1 shard_map.79
  168.7 2.0 shard_map.80
  170.8 3.6 %collective-permute-start.26 = (bf16[8,32,512]{2,1,0:T(8,128)(2,1)S(1)}, bf16[8,32,512]{2,1,0:T(8,128)(2,1)S(1)}, u32[]{:S(2)}, u32[]{:S(2)}) collective-permute-start(bf16[8,32,512]{2,1,0:T(8,128)(2,1)S(1)} %get-tuple-element.56), channel_id=1, source_target_pairs={{0,16},{16,0},{1,17},{17,1},{2,18},{18,2},{3,19},{19,3},{4,20},{20... | collective-permute-start | bytes 786440 | tf_op jit(solution)/shard_map/ppermute | solution.py:34
  174.3 2.9 %collective-permute-done.25.beyond = bf16[512,512]{1,0:T(8,128)(2,1)S(1)} collective-permute-done((bf16[512,512]{1,0:T(8,128)(2,1)S(1)}, bf16[512,512]{1,0:T(8,128)(2,1)S(1)}, u32[]{:S(2)}, u32[]{:S(2)}) %collective-permute-start.25) | collective-permute-done | bytes 524320 | tf_op jit(solution)/shard_map/ppermute | solution.py:40
  177.2 2.1 shard_map.81
  179.3 4.6 %collective-permute-start.29 = (bf16[8,32,512]{2,1,0:T(8,128)(2,1)S(1)}, bf16[8,32,512]{2,1,0:T(8,128)(2,1)S(1)}, u32[]{:S(2)}, u32[]{:S(2)}) collective-permute-start(bf16[8,32,512]{2,1,0:T(8,128)(2,1)S(1)} %get-tuple-element.59), channel_id=1, source_target_pairs={{0,16},{16,0},{1,17},{17,1},{2,18},{18,2},{3,19},{19,3},{4,20},{20... | collective-permute-start | bytes 786440 | tf_op jit(solution)/shard_map/ppermute | solution.py:34
  183.9 1.2 collective-permute-done.29
  185.1 25.5 %all_to_all.21.green_ref = bf16[32,32,512]{2,1,0:T(8,128)(2,1)S(1)} all-to-all(bf16[32,32,512]{2,1,0:T(8,128)(2,1)S(1)} %bitcast.30), channel_id=1, replica_groups=mesh['zlo'=2,'y'=4,'core'=2,'row'=4,'x'=4] {'x','zlo','y'}, dimensions={0} | all-to-all | bytes 2097152 | tf_op jit(solution)/shard_map/all_to_all | solution.py:341
  210.6 4.9 %shard_map.83 = bf16[32,32,512]{2,1,0:T(8,128)(2,1)} custom-call(s32[8]{0:T(128)S(1)} %copy-done.10, bf16[32,32,512]{2,1,0:T(8,128)(2,1)S(1)} %all_to_all.21.green_ref, bf16[32,512]{1,0:T(8,128)(2,1)S(1)} %bitcast.32), custom_call_target="tpu_custom_call" | custom-call | tf_op jit(solution)/shard_map/pallas_call | solution.py:332
  215.5 3.7 %all-to-all-start.3 = ((bf16[16,2,32,512]{3,2,1,0:T(8,128)(2,1)}), bf16[16,2,32,512]{3,2,1,0:T(8,128)(2,1)S(1)}, u32[]{:S(2)}, u32[]{:S(2)}) async-start(bf16[16,2,32,512]{3,2,1,0:T(8,128)(2,1)} %bitcast.15), calls=%async_computation.3 | async-start | bytes 2097152 | tf_op jit(solution)/shard_map/all_to_all | solution.py:341
  219.2 0.7 collective-permute-start.23
  219.9 3.9 %collective-permute-start.24 = (bf16[512,512]{1,0:T(8,128)(2,1)S(1)}, bf16[512,512]{1,0:T(8,128)(2,1)S(1)}, u32[]{:S(2)}, u32[]{:S(2)}) collective-permute-start(bf16[512,512]{1,0:T(8,128)(2,1)S(1)} %get-tuple-element.53), channel_id=1, source_target_pairs={{1,1},{3,17},{17,2},{19,18},{5,5},{7,21},{21,6},{23,22},{9,9},{11,... | collective-permute-start | bytes 1572872 | tf_op jit(solution)/shard_map/ppermute | solution.py:97
  223.8 1.3 collective-permute-start.27
  225.1 5.5 %collective-permute-start.28 = (bf16[512,512]{1,0:T(8,128)(2,1)S(1)}, bf16[512,512]{1,0:T(8,128)(2,1)S(1)}, u32[]{:S(2)}, u32[]{:S(2)}) collective-permute-start(bf16[512,512]{1,0:T(8,128)(2,1)S(1)} %get-tuple-element.57), channel_id=1, source_target_pairs={{1,0},{3,16},{17,3},{19,19},{5,4},{7,20},{21,7},{23,23},{9,8},{11,... | collective-permute-start | bytes 1572872 | tf_op jit(solution)/shard_map/ppermute | solution.py:97
  230.6 3.3 %collective-permute-done.24.inner_1 = bf16[512,512]{1,0:T(8,128)(2,1)S(1)} collective-permute-done((bf16[512,512]{1,0:T(8,128)(2,1)S(1)}, bf16[512,512]{1,0:T(8,128)(2,1)S(1)}, u32[]{:S(2)}, u32[]{:S(2)}) %collective-permute-start.24) | collective-permute-done | bytes 524320 | tf_op jit(solution)/shard_map/ppermute | solution.py:97
  233.8 7.2 %collective-permute-done.27.outer_0 = bf16[512,512]{1,0:T(8,128)(2,1)S(1)} collective-permute-done((bf16[512,512]{1,0:T(8,128)(2,1)S(1)}, bf16[512,512]{1,0:T(8,128)(2,1)S(1)}, u32[]{:S(2)}, u32[]{:S(2)}) %collective-permute-start.27) | collective-permute-done | bytes 524320 | tf_op jit(solution)/shard_map/ppermute | solution.py:97
  241.1 2.0 shard_map.82
  243.1 1.1 copy.7
  (52 shorter events, 0.4 us)
Async XLA Ops:
  1.4 1.0 copy-start
  4.6 1.0 copy-start.4
  5.6 55.6 %copy-start.9 = (f32[2]{0:T(128)S(1)}, f32[2]{0:T(128)}, u32[]{:S(2)}) copy-start(f32[2]{0:T(128)} %energy_ref.5) | copy-start | bytes 28
  5.6 55.6 %copy-start.1 = (bf16[1,512,512]{2,1,0:T(8,128)(2,1)S(1)}, bf16[1,512,512]{2,1,0:T(8,128)(2,1)}, u32[]{:S(2)}) copy-start(bf16[1,512,512]{2,1,0:T(8,128)(2,1)} %param.7) | copy-start | bytes 1572868
  5.6 35.0 %collective-permute-start.4 = (bf16[512,512]{1,0:T(8,128)(2,1)S(1)}, bf16[512,512]{1,0:T(8,128)(2,1)S(1)}, u32[]{:S(2)}, u32[]{:S(2)}) collective-permute-start(bf16[512,512]{1,0:T(8,128)(2,1)S(1)} %get-tuple-element.33), channel_id=1, source_target_pairs={{0,1},{1,2},{2,3},{3,0},{4,5},{5,6},{6,7},{7,4},{8,9},{9,10},{10,1... | collective-permute-start | bytes 1572872 | tf_op jit(solution)/shard_map/ppermute | solution.py:30
  6.1 34.6 %collective-permute-start.6 = (bf16[512,512]{1,0:T(8,128)(2,1)S(1)}, bf16[512,512]{1,0:T(8,128)(2,1)S(1)}, u32[]{:S(2)}, u32[]{:S(2)}) collective-permute-start(bf16[512,512]{1,0:T(8,128)(2,1)S(1)} %get-tuple-element.33), channel_id=1, source_target_pairs={{0,3},{1,0},{2,1},{3,2},{4,7},{5,4},{6,5},{7,6},{8,11},{9,8},{10,9... | collective-permute-start | bytes 1572872 | tf_op jit(solution)/shard_map/ppermute | solution.py:30
  7.6 33.0 %collective-permute-start.7 = (bf16[512,512]{1,0:T(8,128)(2,1)}, bf16[512,512]{1,0:T(8,128)(2,1)S(1)}, u32[]{:S(2)}, u32[]{:S(2)}) collective-permute-start(bf16[512,512]{1,0:T(8,128)(2,1)} %bitcast.3.ham_ref), channel_id=1, source_target_pairs={{3,4},{7,8},{11,12},{4,3},{8,7},{12,11},{35,36},{39,40},{43,44},{3... | collective-permute-start | bytes 1572872 | tf_op jit(solution)/shard_map/ppermute | solution.py:47
  15.2 26.9 %copy-start.5 = (f32[512,512]{1,0:T(8,128)S(1)}, f32[512,512]{1,0:T(8,128)}, u32[]{:S(2)}) copy-start(f32[512,512]{1,0:T(8,128)} %copy-done.4) | copy-start | bytes 3145732
  16.2 22.5 %collective-permute-start = (bf16[256,512]{1,0:T(8,128)(2,1)S(1)}, bf16[256,512]{1,0:T(8,128)(2,1)S(1)}, u32[]{:S(2)}, u32[]{:S(2)}) collective-permute-start(bf16[256,512]{1,0:T(8,128)(2,1)S(1)} %dynamic-slice_bitcast_fusion), channel_id=1, source_target_pairs={{0,1},{1,2},{2,3},{3,4},{4,5},{5,6},{6,7},{7,8},{8,9},{9,10},{10,1... | collective-permute-start | bytes 786440 | tf_op jit(solution)/shard_map/ppermute | solution.py:26
  38.7 3.3 %collective-permute-start.1 = (bf16[256,512]{1,0:T(8,128)(2,1)S(1)}, bf16[256,512]{1,0:T(8,128)(2,1)S(1)}, u32[]{:S(2)}, u32[]{:S(2)}) collective-permute-start(bf16[256,512]{1,0:T(8,128)(2,1)S(1)} %collective-permute-done.mine_ref), channel_id=1, source_target_pairs={{0,16},{16,0},{1,17},{17,1},{2,18},{18,2},{3,19},{19,3},{4,20},{20... | collective-permute-start | bytes 786440 | tf_op jit(solution)/shard_map/ppermute | solution.py:34
  38.7 19.9 %collective-permute-start.13 = (bf16[256,512]{1,0:T(8,128)(2,1)S(1)}, bf16[256,512]{1,0:T(8,128)(2,1)S(1)}, u32[]{:S(2)}, u32[]{:S(2)}) collective-permute-start(bf16[256,512]{1,0:T(8,128)(2,1)S(1)} %dynamic-slice_bitcast_fusion), channel_id=1, source_target_pairs={{1,0},{2,1},{3,2},{4,3},{5,4},{6,5},{7,6},{8,7},{9,8},{10,9},{11,1... | collective-permute-start | bytes 786440 | tf_op jit(solution)/shard_map/ppermute | solution.py:26
  40.7 22.5 %copy-start.2 = (bf16[512,512]{1,0:T(8,128)(2,1)}, bf16[512,512]{1,0:T(8,128)(2,1)S(1)}, u32[]{:S(2)}) copy-start(bf16[512,512]{1,0:T(8,128)(2,1)S(1)} %collective-permute-done.6.three_ref.mine_3) | copy-start | bytes 1572868
  41.3 21.8 %collective-permute-start.10 = (bf16[512,512]{1,0:T(8,128)(2,1)S(1)}, bf16[512,512]{1,0:T(8,128)(2,1)S(1)}, u32[]{:S(2)}, u32[]{:S(2)}) collective-permute-start(bf16[512,512]{1,0:T(8,128)(2,1)S(1)} %get-tuple-element.35.next_ref), channel_id=1, source_target_pairs={{0,16},{16,0},{1,17},{17,1},{2,18},{18,2},{3,19},{19,3},{4,20},{20... | collective-permute-start | bytes 1572872 | tf_op jit(solution)/shard_map/ppermute | solution.py:34
  41.9 21.2 %collective-permute-start.8 = (bf16[512,512]{1,0:T(8,128)(2,1)S(1)}, bf16[512,512]{1,0:T(8,128)(2,1)S(1)}, u32[]{:S(2)}, u32[]{:S(2)}) collective-permute-start(bf16[512,512]{1,0:T(8,128)(2,1)S(1)} %get-tuple-element.34.previous_ref), channel_id=1, source_target_pairs={{0,16},{16,0},{1,17},{17,1},{2,18},{18,2},{3,19},{19,3},{4,20},{20... | collective-permute-start | bytes 1572872 | tf_op jit(solution)/shard_map/ppermute | solution.py:34
  43.1 0.8 copy-start.6
  43.9 17.2 %collective-permute-start.15 = (bf16[256,512]{1,0:T(8,128)(2,1)S(1)}, bf16[256,512]{1,0:T(8,128)(2,1)S(1)}, u32[]{:S(2)}, u32[]{:S(2)}) collective-permute-start(bf16[256,512]{1,0:T(8,128)(2,1)S(1)} %get-tuple-element.43), channel_id=1, source_target_pairs={{0,1},{1,2},{2,3},{3,4},{4,5},{5,6},{6,7},{7,8},{8,9},{9,10},{10,1... | collective-permute-start | bytes 786440 | tf_op jit(solution)/shard_map/ppermute | solution.py:26
  58.6 2.6 %collective-permute-start.14 = (bf16[256,512]{1,0:T(8,128)(2,1)S(1)}, bf16[256,512]{1,0:T(8,128)(2,1)S(1)}, u32[]{:S(2)}, u32[]{:S(2)}) collective-permute-start(bf16[256,512]{1,0:T(8,128)(2,1)S(1)} %collective-permute-done.13.mine_ref), channel_id=1, source_target_pairs={{0,16},{16,0},{1,17},{17,1},{2,18},{18,2},{3,19},{19,3},{4,20},{20... | collective-permute-start | bytes 786440 | tf_op jit(solution)/shard_map/ppermute | solution.py:34
  61.1 2.0 collective-permute-start.16
  68.6 22.9 %copy-start.11 = (bf16[512,512]{1,0:T(8,128)(2,1)}, bf16[512,512]{1,0:T(8,128)(2,1)S(1)}, u32[]{:S(2)}) copy-start(bf16[512,512]{1,0:T(8,128)(2,1)S(1)} %get-tuple-element.47) | copy-start | bytes 1572868
  68.6 22.9 %copy-start.12 = (bf16[512,512]{1,0:T(8,128)(2,1)}, bf16[512,512]{1,0:T(8,128)(2,1)S(1)}, u32[]{:S(2)}) copy-start(bf16[512,512]{1,0:T(8,128)(2,1)S(1)} %get-tuple-element.46) | copy-start | bytes 1572868
  68.6 22.9 %copy-start.8 = (bf16[1,32,512]{2,1,0:T(8,128)(2,1)S(1)}, bf16[1,32,512]{2,1,0:T(8,128)(2,1)}, u32[]{:S(2)}) copy-start(bf16[1,32,512]{2,1,0:T(8,128)(2,1)} %param.8) | copy-start | bytes 98308
  68.6 22.9 %copy-start.10 = (s32[8]{0:T(128)S(1)}, s32[8]{0:T(128)}, u32[]{:S(2)}) copy-start(s32[8]{0:T(128)} %offset_ref.3) | copy-start | bytes 100
  96.4 46.8 %all-to-all-start.1 = ((bf16[32,32,512]{2,1,0:T(8,128)(2,1)}), bf16[32,32,512]{2,1,0:T(8,128)(2,1)S(1)}, u32[]{:S(2)}, u32[]{:S(2)}) async-start(bf16[32,32,512]{2,1,0:T(8,128)(2,1)} %shard_map.74), calls=%async_computation.1 | async-start | bytes 2097152 | tf_op jit(solution)/shard_map/all_to_all | solution.py:341
  102.0 25.0 %collective-permute-start.5 = (bf16[512,512]{1,0:T(8,128)(2,1)S(1)}, bf16[512,512]{1,0:T(8,128)(2,1)}, u32[]{:S(2)}, u32[]{:S(2)}) collective-permute-start(bf16[512,512]{1,0:T(8,128)(2,1)S(1)} %collective-permute-done.4.one_ref.mine_1), channel_id=1, source_target_pairs={{0,1},{1,2},{2,3},{3,0},{4,5},{5,6},{6,7},{7,4},{8,9},{9,10},{10,1... | collective-permute-start | bytes 1572872 | tf_op jit(solution)/shard_map/ppermute | solution.py:30
  102.3 26.2 %collective-permute-start.18 = (bf16[512,512]{1,0:T(8,128)(2,1)}, bf16[512,512]{1,0:T(8,128)(2,1)}, u32[]{:S(2)}, u32[]{:S(2)}) collective-permute-start(bf16[512,512]{1,0:T(8,128)(2,1)} %copy-done.12), channel_id=1, source_target_pairs={{0,0},{1,1},{2,16},{3,17},{16,2},{17,3},{18,18},{19,19},{4,4},{5,5... | collective-permute-start | bytes 1572872 | tf_op jit(solution)/shard_map/ppermute | solution.py:56
  105.7 28.6 %collective-permute-start.19 = (bf16[512,512]{1,0:T(8,128)(2,1)}, bf16[512,512]{1,0:T(8,128)(2,1)}, u32[]{:S(2)}, u32[]{:S(2)}) collective-permute-start(bf16[512,512]{1,0:T(8,128)(2,1)} %copy-done.11), channel_id=1, source_target_pairs={{0,1},{1,0},{2,17},{3,16},{16,3},{17,2},{18,19},{19,18},{4,5},{5,4... | collective-permute-start | bytes 1572872 | tf_op jit(solution)/shard_map/ppermute | solution.py:56
  108.7 29.8 %collective-permute-start.2 = (bf16[512,512]{1,0:T(8,128)(2,1)}, bf16[512,512]{1,0:T(8,128)(2,1)}, u32[]{:S(2)}, u32[]{:S(2)}) collective-permute-start(bf16[512,512]{1,0:T(8,128)(2,1)} %copy-done.6), channel_id=1, source_target_pairs={{0,1},{16,3},{4,5},{20,7},{8,9},{24,11},{12,13},{28,15},{32,33},{4... | collective-permute-start | bytes 1572872 | tf_op jit(solution)/shard_map/ppermute | solution.py:51
  110.0 33.4 %collective-permute-start.3 = (bf16[512,512]{1,0:T(8,128)(2,1)}, bf16[512,512]{1,0:T(8,128)(2,1)}, u32[]{:S(2)}, u32[]{:S(2)}) collective-permute-start(bf16[512,512]{1,0:T(8,128)(2,1)} %copy-done.6), channel_id=1, source_target_pairs={{0,2},{4,6},{8,10},{12,14},{32,34},{36,38},{40,42},{44,46},{64,66}... | collective-permute-start | bytes 1572872 | tf_op jit(solution)/shard_map/ppermute | solution.py:51
  127.0 16.4 %collective-permute-start.11 = (bf16[512,512]{1,0:T(8,128)(2,1)S(1)}, bf16[512,512]{1,0:T(8,128)(2,1)}, u32[]{:S(2)}, u32[]{:S(2)}) collective-permute-start(bf16[512,512]{1,0:T(8,128)(2,1)S(1)} %collective-permute-done.4.one_ref.mine_1), channel_id=1, source_target_pairs={{0,16},{4,20},{8,24},{12,28},{32,48},{36,52},{40,56},{44,60},{64,8... | collective-permute-start | bytes 1572872 | tf_op jit(solution)/shard_map/ppermute | solution.py:51
  128.5 15.4 %collective-permute-start.9 = (bf16[512,512]{1,0:T(8,128)(2,1)}, bf16[512,512]{1,0:T(8,128)(2,1)}, u32[]{:S(2)}, u32[]{:S(2)}) collective-permute-start(bf16[512,512]{1,0:T(8,128)(2,1)} %collective-permute-done.5.mine_2), channel_id=1, source_target_pairs={{0,16},{16,0},{1,17},{17,1},{2,18},{18,2},{3,19},{19,3},{4,20},{20... | collective-permute-start | bytes 1572872 | tf_op jit(solution)/shard_map/ppermute | solution.py:34
  136.5 14.5 %collective-permute-start.20 = (bf16[512,512]{1,0:T(8,128)(2,1)}, bf16[512,512]{1,0:T(8,128)(2,1)}, u32[]{:S(2)}, u32[]{:S(2)}) collective-permute-start(bf16[512,512]{1,0:T(8,128)(2,1)} %get-tuple-element.48.outer.green_ref), channel_id=1, source_target_pairs={{16,4},{20,8},{24,12},{4,16},{8,20},{12,24},{17,5},{21,9},{25,13},... | collective-permute-start | bytes 1572872 | tf_op jit(solution)/shard_map/ppermute | solution.py:40
  138.5 12.6 %collective-permute-start.21 = (bf16[512,512]{1,0:T(8,128)(2,1)}, bf16[512,512]{1,0:T(8,128)(2,1)}, u32[]{:S(2)}, u32[]{:S(2)}) collective-permute-start(bf16[512,512]{1,0:T(8,128)(2,1)} %get-tuple-element.49.inner.green_ref), channel_id=1, source_target_pairs={{0,16},{16,0},{1,17},{17,1},{2,18},{18,2},{3,19},{19,3},{4,20},{20... | collective-permute-start | bytes 1572872 | tf_op jit(solution)/shard_map/ppermute | solution.py:34
  143.3 12.1 %collective-permute-start.17 = (bf16[2,8,32,512]{3,2,1,0:T(8,128)(2,1)S(1)}, bf16[2,8,32,512]{3,2,1,0:T(8,128)(2,1)S(1)}, u32[]{:S(2)}, u32[]{:S(2)}) collective-permute-start(bf16[2,8,32,512]{3,2,1,0:T(8,128)(2,1)S(1)} %constant_dynamic-slice_fusion), channel_id=1, source_target_pairs={{0,16},{16,0},{1,17},{17,1},{2,18},{18,2},{3,19},{19,3},{4,20},{20... | collective-permute-start | bytes 1572872 | tf_op jit(solution)/shard_map/ppermute | solution.py:34
  143.4 5.3 %collective-permute-start.12 = (f32[2]{0:T(128)S(1)}, f32[2]{0:T(128)S(1)}, u32[]{:S(2)}, u32[]{:S(2)}) collective-permute-start(f32[2]{0:T(128)S(1)} %copy-done.9), channel_id=1, source_target_pairs={{0,16},{16,0},{1,17},{17,1},{2,18},{18,2},{3,19},{19,3},{4,20},{20... | collective-permute-start | bytes 32 | tf_op jit(solution)/shard_map/ppermute | solution.py:34
  143.9 1.0 copy-start.3
  145.0 1.0 copy-start.7
  157.3 11.5 %collective-permute-start.22 = (bf16[512,512]{1,0:T(8,128)(2,1)S(1)}, bf16[512,512]{1,0:T(8,128)(2,1)S(1)}, u32[]{:S(2)}, u32[]{:S(2)}) collective-permute-start(bf16[512,512]{1,0:T(8,128)(2,1)S(1)} %shard_map.78.inner), channel_id=1, source_target_pairs={{0,16},{16,0},{1,17},{17,1},{2,18},{18,2},{3,19},{19,3},{4,20},{20... | collective-permute-start | bytes 1572872 | tf_op jit(solution)/shard_map/ppermute | solution.py:34
  164.7 12.5 %collective-permute-start.25 = (bf16[512,512]{1,0:T(8,128)(2,1)S(1)}, bf16[512,512]{1,0:T(8,128)(2,1)S(1)}, u32[]{:S(2)}, u32[]{:S(2)}) collective-permute-start(bf16[512,512]{1,0:T(8,128)(2,1)S(1)} %shard_map.77.outer), channel_id=1, source_target_pairs={{16,4},{20,8},{24,12},{4,16},{8,20},{12,24},{17,5},{21,9},{25,13},... | collective-permute-start | bytes 1572872 | tf_op jit(solution)/shard_map/ppermute | solution.py:40
  170.8 6.5 %collective-permute-start.26 = (bf16[8,32,512]{2,1,0:T(8,128)(2,1)S(1)}, bf16[8,32,512]{2,1,0:T(8,128)(2,1)S(1)}, u32[]{:S(2)}, u32[]{:S(2)}) collective-permute-start(bf16[8,32,512]{2,1,0:T(8,128)(2,1)S(1)} %get-tuple-element.56), channel_id=1, source_target_pairs={{0,16},{16,0},{1,17},{17,1},{2,18},{18,2},{3,19},{19,3},{4,20},{20... | collective-permute-start | bytes 786440 | tf_op jit(solution)/shard_map/ppermute | solution.py:34
  179.3 5.7 %collective-permute-start.29 = (bf16[8,32,512]{2,1,0:T(8,128)(2,1)S(1)}, bf16[8,32,512]{2,1,0:T(8,128)(2,1)S(1)}, u32[]{:S(2)}, u32[]{:S(2)}) collective-permute-start(bf16[8,32,512]{2,1,0:T(8,128)(2,1)S(1)} %get-tuple-element.59), channel_id=1, source_target_pairs={{0,16},{16,0},{1,17},{17,1},{2,18},{18,2},{3,19},{19,3},{4,20},{20... | collective-permute-start | bytes 786440 | tf_op jit(solution)/shard_map/ppermute | solution.py:34
  215.5 27.6 %all-to-all-start.3 = ((bf16[16,2,32,512]{3,2,1,0:T(8,128)(2,1)}), bf16[16,2,32,512]{3,2,1,0:T(8,128)(2,1)S(1)}, u32[]{:S(2)}, u32[]{:S(2)}) async-start(bf16[16,2,32,512]{3,2,1,0:T(8,128)(2,1)} %bitcast.15), calls=%async_computation.3 | async-start | bytes 2097152 | tf_op jit(solution)/shard_map/all_to_all | solution.py:341
  219.2 11.4 %collective-permute-start.23 = (bf16[512,512]{1,0:T(8,128)(2,1)S(1)}, bf16[512,512]{1,0:T(8,128)(2,1)S(1)}, u32[]{:S(2)}, u32[]{:S(2)}) collective-permute-start(bf16[512,512]{1,0:T(8,128)(2,1)S(1)} %get-tuple-element.53), channel_id=1, source_target_pairs={{0,1},{2,17},{16,2},{18,18},{4,5},{6,21},{20,6},{22,22},{8,9},{10,... | collective-permute-start | bytes 1572872 | tf_op jit(solution)/shard_map/ppermute | solution.py:97
  219.9 14.0 %collective-permute-start.24 = (bf16[512,512]{1,0:T(8,128)(2,1)S(1)}, bf16[512,512]{1,0:T(8,128)(2,1)S(1)}, u32[]{:S(2)}, u32[]{:S(2)}) collective-permute-start(bf16[512,512]{1,0:T(8,128)(2,1)S(1)} %get-tuple-element.53), channel_id=1, source_target_pairs={{1,1},{3,17},{17,2},{19,18},{5,5},{7,21},{21,6},{23,22},{9,9},{11,... | collective-permute-start | bytes 1572872 | tf_op jit(solution)/shard_map/ppermute | solution.py:97
  223.8 17.3 %collective-permute-start.27 = (bf16[512,512]{1,0:T(8,128)(2,1)S(1)}, bf16[512,512]{1,0:T(8,128)(2,1)S(1)}, u32[]{:S(2)}, u32[]{:S(2)}) collective-permute-start(bf16[512,512]{1,0:T(8,128)(2,1)S(1)} %get-tuple-element.57), channel_id=1, source_target_pairs={{0,0},{2,16},{16,3},{18,19},{4,4},{6,20},{20,7},{22,23},{8,8},{10,... | collective-permute-start | bytes 1572872 | tf_op jit(solution)/shard_map/ppermute | solution.py:97
  225.1 16.0 %collective-permute-start.28 = (bf16[512,512]{1,0:T(8,128)(2,1)S(1)}, bf16[512,512]{1,0:T(8,128)(2,1)S(1)}, u32[]{:S(2)}, u32[]{:S(2)}) collective-permute-start(bf16[512,512]{1,0:T(8,128)(2,1)S(1)} %get-tuple-element.57), channel_id=1, source_target_pairs={{1,0},{3,16},{17,3},{19,19},{5,4},{7,20},{21,7},{23,23},{9,8},{11,... | collective-permute-start | bytes 1572872 | tf_op jit(solution)/shard_map/ppermute | solution.py:97

commit v9 on v8

--- a/solution.py
+++ b/solution.py
@@ -28,6 +28,10 @@
 
 def row_ring(value, steps):
     return lax.ppermute(value, "x", [(s, (s + steps) % WIDTH) for s in range(WIDTH)])
+
+
+def row_step(value, steps):
+    return lax.ppermute(value, "x", [(s, s + steps) for s in range(WIDTH) if 0 <= s + steps < WIDTH])
 
 
 def swapped(value):
@@ -171,7 +175,7 @@
 
 
 def link_body(
-    at_ref, c_ref, ham_ref, below_ref, near_ref, middle_ref, mine_1, mine_2, mine_3, other_1, other_2, other_3, extra,
+    at_ref, c_ref, ham_ref, below_ref, spread_0, spread_1, spread_2, mine_1, mine_2, mine_3, other_1, other_2, other_3,
     outer_ham, inner_ham, far, mid, mid_turned, near,
 ):
     x = at_ref[1]
@@ -182,11 +186,12 @@
 
     @pl.when(at_ref[0] == 0)
     def _():
-        hams = (ham_ref[...], mine_1[...], mine_2[...], mine_3[...])
-        links = (c_ref[...], other_1[...], other_2[...], other_3[...])
+        end = x == WIDTH - 1
+        hams = (ham_ref[...], mine_1[...], mine_2[...], jnp.where(end, spread_2[...], mine_3[...]))
+        links = (c_ref[...], other_1[...], other_2[...], jnp.where(end, spread_1[...], other_3[...]))
         outer_ham[...] = block(0, *hams)
         inner_ham[...] = block(1, *hams)
-        far[...] = jnp.where(x == 0, below_ref[...], jnp.where(x == 2, middle_ref[...], near_ref[...])).T
+        far[...] = jnp.where(x == 0, below_ref[...], jnp.where(x == 2, spread_1[...], spread_0[...])).T
         middle = block(0, *links)
         mid[...] = middle
         mid_turned[...] = middle.T
@@ -194,8 +199,8 @@
 
     @pl.when(at_ref[0] == 1)
     def _():
-        hams = (ham_ref[...], jnp.where(x == 0, extra[...], other_1[...]), other_2[...], other_3[...])
-        links = (c_ref[...], mine_1[...], mine_2[...], mine_3[...])
+        hams = (ham_ref[...], jnp.where(x == 0, spread_0[...], other_1[...]), other_2[...], other_3[...])
+        links = (c_ref[...], jnp.where(x == 0, spread_1[...], mine_1[...]), mine_2[...], mine_3[...])
         outer_ham[...] = block(3, *hams)
         inner_ham[...] = block(2, *hams)
         far[...] = block(3, *links)
@@ -366,7 +371,7 @@
     energy_pair = swapped(energies)
     own, load = run(own_body, (wide(n, n), thin(n, n)), [SM, SM, VM, VM], edge[:1], at, c, ham)
     lower_theirs = swapped(lower_mine)
-    one, three = row_ring(load, 1), row_ring(load, -1)
+    one, three = row_step(load, 1), row_step(load, -1)
     crossing = crossed(ham)
     pair, pair_half, below_c, lower_turned = run(
         pair_body, (wide(n, n), thin(n // 2, n), thin(n, n), thin(n, n)), [SM, VM, VM, VM],
@@ -378,7 +383,7 @@
         above_body, wide(n, n), [SM, SM, VM, VM, VM], edge[2:], at, c, upper_mine, upper_theirs,
         scratch=[pltpu.VMEM((n, n), jnp.bfloat16)],
     )
-    two = row_ring(one, 1)
+    two = row_ring(load, 2)
     before, after = run(near_body, (thin(n, n),) * 2, [SM] + [VM] * 3, at, one, three, crossing)
     got_before, got_after = swapped(before), swapped(after)
     got_down = swapped(pair_down)
@@ -391,12 +396,16 @@
     received = all_to_all(chunks, ENERGY)
 
     got_two = swapped(two)
-    extra = sent(one, [((0, 0), (1, 0))])
-    near_c = sent(below_c, [((0, 0), (0, 1)), ((1, 0), (0, 3))])
-    middle_c = sent(below_c, [((0, 0), (0, 2))])
+    starts = jnp.where(x == 0, below_c, load), jnp.where(jnp.logical_and(x == 0, core == 0), below_c, load), load
+    routes = (
+        [((0, 0), (0, 1)), ((1, 0), (0, 3)), ((0, 3), (1, 0))],
+        [((0, 0), (0, 2)), ((1, 0), (0, 3)), ((1, 3), (1, 0))],
+        [((0, 0), (0, 3))],
+    )
+    spread = [sent(value, route) for value, route in zip(starts, routes)]
     outer_ham, inner_ham, far, mid, mid_turned, near = run(
         link_body, (thin(n, n),) * 6, [SM] + [VM] * 12,
-        at, c, ham, below_c, near_c, middle_c, one, two, three, got_before, got_two, got_after, extra,
+        at, c, ham, below_c, *spread, one, two, three, got_before, got_two, got_after,
     )
     outer, inner = run(role_body, (thin(n, n),) * 2, [SM, VM, VM], at, first, second)
     beyond = row_above(outer)

time: 249 us -> 245 us (0.984); the launches traced: 244 us -> 244 us
  blocking collectives: 48.4 us -> 44.4 us
    ppermute x3, waiting for transfers between devices: 28.6 us -> 20.8 us  [passed_along(): lax.ppermute(value, SLAB, [(source, source + steps) for source in range(l...]
    ppermute x0 -> x2, starting transfers between devices: none -> 5.99 us  [row_step(): lax.ppermute(value, 'x', [(s, s + steps) for s in range(WIDTH) if 0 <= s...]
    all_to_all x2, blocking collectives: 48.4 us -> 44.4 us  [all_to_all(): return lax.all_to_all(value, axes, split_axis=0, concat_axis=0, tiled=True)]
    ppermute x4, waiting for transfers between devices: 10.5 us -> 14.2 us  [returned(): return lax.ppermute(value, ('core', 'x'), pairs)]
    ppermute x3 -> x1, waiting for transfers between devices: 15.6 us -> 18.8 us  [row_ring(): lax.ppermute(value, 'x', [(s, (s + steps) % WIDTH) for s in range(WIDTH)])]
    ppermute x3, starting transfers between devices: 4.19 us -> 7.09 us  [sent(): lax.ppermute(value, ('core', 'x'), [(a * WIDTH + i, b * WIDTH + j) for (a...]
    unnamed x26 -> x36, local copies, waits for them, and re-layouts: 4.92 us -> 6.23 us
  transfers between devices with their start and end apart: 32 -> 32, of which waited for: 10 -> 12; matrix products, arithmetic and copies ran while one was open for 0% -> 2% of each run, Pallas kernels for 9% -> 9%
where the time goes in v9:
time: 245 us; the launch traced here: 244 us
  starting transfers between devices  78.6 us (32%)
  waiting for transfers between devices  67.1 us (27%)
  blocking collectives  44.4 us (18%)
  Pallas kernels  41 us (17%)
  local copies, waits for them, and re-layouts  8.98 us (4%)
    all_to_all x2, blocking collectives, all_to_all(): return lax.all_to_all(value, axes, split_axis=0, concat_axis=0, tiled=True)  44.4 us
    pallas_call x14, Pallas kernels, run(): return call(body, out_shape, in_specs, scratch)(*operands)  31.3 us
    ppermute x3, waiting for transfers between devices, passed_along(): lax.ppermute(value, SLAB, [(source, source + steps) for source in range(l...  20.8 us
    ppermute x12, starting transfers between devices, swapped(): return lax.ppermute(value, 'core', [(0, 1), (1, 0)])  19 us
    ppermute x1, waiting for transfers between devices, row_ring(): lax.ppermute(value, 'x', [(s, (s + steps) % WIDTH) for s in range(WIDTH)])  18.8 us
    ppermute x4, waiting for transfers between devices, returned(): return lax.ppermute(value, ('core', 'x'), pairs)  14.2 us
    ppermute x3, starting transfers between devices, passed_along(): lax.ppermute(value, SLAB, [(source, source + steps) for source in range(l...  12.4 us
    pallas_call x2, Pallas kernels, convolved(): call(functools.partial(energy_body, place_in, place_out), jax.ShapeDtypeS...  9.72 us
  transfers between devices with their start and end apart: 32, of which 12 were waited for; matrix products, arithmetic and copies ran while one was open for 2% of the time, Pallas kernels for 9%

profile of v9, /device:TPU:70, one launch (start us, length us, event | category | flops | bytes accessed | tf_op | source)
XLA Modules:
  0.0 243.7 jit_solution(16181227013475880220)
XLA Ops:
  0.6 6.3 %collective-permute-start.8 = (bf16[512,512]{1,0:T(8,128)(2,1)}, bf16[512,512]{1,0:T(8,128)(2,1)S(1)}, u32[]{:S(2)}, u32[]{:S(2)}) collective-permute-start(bf16[512,512]{1,0:T(8,128)(2,1)} %bitcast.29), channel_id=1, source_target_pairs={{3,4},{7,8},{11,12},{4,3},{8,7},{12,11},{35,36},{39,40},{43,44},{3... | collective-permute-start | bytes 1572872 | tf_op jit(solution)/shard_map/ppermute | solution.py:51
  7.0 0.6 fusion
  7.7 1.0 copy-done
  8.7 1.0 copy-done.2
  9.8 1.7 shard_map.68
  11.5 1.0 copy-done.10
  12.4 1.4 collective-permute-start.5
  13.9 4.6 %collective-permute-start.7 = (bf16[512,512]{1,0:T(8,128)(2,1)S(1)}, bf16[512,512]{1,0:T(8,128)(2,1)S(1)}, u32[]{:S(2)}, u32[]{:S(2)}) collective-permute-start(bf16[512,512]{1,0:T(8,128)(2,1)S(1)} %get-tuple-element.33), channel_id=1, source_target_pairs={{1,0},{2,1},{3,2},{5,4},{6,5},{7,6},{9,8},{10,9},{11,10},{13,12},{... | collective-permute-start | bytes 1572872 | tf_op jit(solution)/shard_map/ppermute | solution.py:34
  18.5 1.1 dynamic-slice_bitcast_fusion
  19.5 1.9 collective-permute-start
  21.5 9.2 %collective-permute-done.mine_ref = bf16[256,512]{1,0:T(8,128)(2,1)S(1)} collective-permute-done((bf16[256,512]{1,0:T(8,128)(2,1)S(1)}, bf16[256,512]{1,0:T(8,128)(2,1)S(1)}, u32[]{:S(2)}, u32[]{:S(2)}) %collective-permute-start) | collective-permute-done | bytes 262176 | tf_op jit(solution)/shard_map/ppermute | solution.py:26
  30.7 1.9 collective-permute-start.13
  32.7 0.7 shard_map.70
  34.0 1.1 shard_map.69
  35.1 8.6 %collective-permute-start.15 = (bf16[256,512]{1,0:T(8,128)(2,1)S(1)}, bf16[256,512]{1,0:T(8,128)(2,1)S(1)}, u32[]{:S(2)}, u32[]{:S(2)}) collective-permute-start(bf16[256,512]{1,0:T(8,128)(2,1)S(1)} %get-tuple-element.43), channel_id=1, source_target_pairs={{0,1},{1,2},{2,3},{3,4},{4,5},{5,6},{6,7},{7,8},{8,9},{9,10},{10,1... | collective-permute-start | bytes 786440 | tf_op jit(solution)/shard_map/ppermute | solution.py:26
  43.7 6.7 %collective-permute-done.13.mine_ref = bf16[256,512]{1,0:T(8,128)(2,1)S(1)} collective-permute-done((bf16[256,512]{1,0:T(8,128)(2,1)S(1)}, bf16[256,512]{1,0:T(8,128)(2,1)S(1)}, u32[]{:S(2)}, u32[]{:S(2)}) %collective-permute-start.13) | collective-permute-done | bytes 262176 | tf_op jit(solution)/shard_map/ppermute | solution.py:26
  50.4 4.9 %collective-permute-done.15.down_ref = bf16[256,512]{1,0:T(8,128)(2,1)S(1)} collective-permute-done((bf16[256,512]{1,0:T(8,128)(2,1)S(1)}, bf16[256,512]{1,0:T(8,128)(2,1)S(1)}, u32[]{:S(2)}, u32[]{:S(2)}) %collective-permute-start.15) | collective-permute-done | bytes 262176 | tf_op jit(solution)/shard_map/ppermute | solution.py:26
  55.4 1.9 shard_map.72.above_ref
  57.4 4.9 %shard_map.73 = (bf16[16,2,32,512]{3,2,1,0:T(8,128)(2,1)S(1)}, bf16[512,512]{1,0:T(8,128)(2,1)S(1)}, bf16[512,512]{1,0:T(8,128)(2,1)S(1)}) custom-call(f32[2]{0:T(128)S(1)} %copy-done.14, f32[2]{0:T(128)S(1)} %convert_convert_fusion.inverse_ref, f32[3]{0:T(128)S(1)} %add_convert_fusion.edge_ref, s32[2]{0:T(128)S(1)} %pad_add_fusion.at_ref, ...), custom_call_target="tpu_custom_call" | custom-call | tf_op jit(solution)/shard_map/pallas_call | solution.py:366
  62.4 21.0 %all_to_all.20 = bf16[16,2,32,512]{3,2,1,0:T(8,128)(2,1)S(1)} all-to-all(bf16[16,2,32,512]{3,2,1,0:T(8,128)(2,1)S(1)} %get-tuple-element.44), channel_id=1, replica_groups=mesh['zlo'=2,'y'=4,'core'=2,'row'=4,'x'=4] {'zlo','y','core'}, dimensions={0} | all-to-all | bytes 2097152 | tf_op jit(solution)/shard_map/all_to_all | solution.py:346
  83.5 4.9 %shard_map.74 = bf16[32,32,512]{2,1,0:T(8,128)(2,1)} custom-call(s32[8]{0:T(128)S(1)} %copy-done.15, bf16[32,32,512]{2,1,0:T(8,128)(2,1)S(1)} %bitcast.33, bf16[32,512]{1,0:T(8,128)(2,1)S(1)} %bitcast.35), custom_call_target="tpu_custom_call" | custom-call | tf_op jit(solution)/shard_map/pallas_call | solution.py:337
  88.3 5.6 %all-to-all-start.1 = ((bf16[32,32,512]{2,1,0:T(8,128)(2,1)}), bf16[32,32,512]{2,1,0:T(8,128)(2,1)S(1)}, u32[]{:S(2)}, u32[]{:S(2)}) async-start(bf16[32,32,512]{2,1,0:T(8,128)(2,1)} %shard_map.74), calls=%async_computation.1 | async-start | bytes 2097152 | tf_op jit(solution)/shard_map/all_to_all | solution.py:346
  93.9 1.5 collective-permute-start.6
  95.4 2.9 %collective-permute-start.18 = (bf16[512,512]{1,0:T(8,128)(2,1)}, bf16[512,512]{1,0:T(8,128)(2,1)}, u32[]{:S(2)}, u32[]{:S(2)}) collective-permute-start(bf16[512,512]{1,0:T(8,128)(2,1)} %copy-done.17), channel_id=1, source_target_pairs={{0,0},{1,1},{2,16},{3,17},{16,2},{17,3},{18,18},{19,19},{4,4},{5,5... | collective-permute-start | bytes 1572872 | tf_op jit(solution)/shard_map/ppermute | solution.py:60
  98.3 1.1 collective-permute-start.19
  99.4 1.3 collective-permute-start.4
  100.7 18.8 %collective-permute-done.6.mine_2 = bf16[512,512]{1,0:T(8,128)(2,1)} collective-permute-done((bf16[512,512]{1,0:T(8,128)(2,1)}, bf16[512,512]{1,0:T(8,128)(2,1)}, u32[]{:S(2)}, u32[]{:S(2)}) %collective-permute-start.6) | collective-permute-done | bytes 524320 | tf_op jit(solution)/shard_map/ppermute | solution.py:30
  119.5 2.3 broadcast_select_fusion
  121.8 1.3 collective-permute-start.3
  123.1 5.4 %collective-permute-done.18.first_ref = bf16[512,512]{1,0:T(8,128)(2,1)} collective-permute-done((bf16[512,512]{1,0:T(8,128)(2,1)}, bf16[512,512]{1,0:T(8,128)(2,1)}, u32[]{:S(2)}, u32[]{:S(2)}) %collective-permute-start.18) | collective-permute-done | bytes 524320 | tf_op jit(solution)/shard_map/ppermute | solution.py:60
  128.5 4.5 %collective-permute-start.2 = (bf16[512,512]{1,0:T(8,128)(2,1)}, bf16[512,512]{1,0:T(8,128)(2,1)}, u32[]{:S(2)}, u32[]{:S(2)}) collective-permute-start(bf16[512,512]{1,0:T(8,128)(2,1)} %get-tuple-element.63), channel_id=1, source_target_pairs={{0,1},{16,3},{3,16},{4,5},{20,7},{7,20},{8,9},{24,11},{11,24},{12,... | collective-permute-start | bytes 1572872 | tf_op jit(solution)/shard_map/ppermute | solution.py:55
  133.0 1.3 collective-permute-done.19.second_ref
  134.4 2.3 shard_map.75
  136.6 1.9 collective-permute-start.20
  138.6 4.8 %collective-permute-start.21 = (bf16[512,512]{1,0:T(8,128)(2,1)}, bf16[512,512]{1,0:T(8,128)(2,1)}, u32[]{:S(2)}, u32[]{:S(2)}) collective-permute-start(bf16[512,512]{1,0:T(8,128)(2,1)} %get-tuple-element.49.inner.green_ref), channel_id=1, source_target_pairs={{0,16},{16,0},{1,17},{17,1},{2,18},{18,2},{3,19},{19,3},{4,20},{20... | collective-permute-start | bytes 1572872 | tf_op jit(solution)/shard_map/ppermute | solution.py:38
  144.1 1.8 collective-permute-done.2.spread_0
  145.9 1.0 copy-done.5
  146.9 1.0 copy-done.7
  148.0 1.0 copy-done.9
  149.0 2.5 %shard_map.71 = (bf16[512,512]{1,0:T(8,128)(2,1)S(1)}, bf16[512,512]{1,0:T(8,128)(2,1)S(1)}, bf16[512,512]{1,0:T(8,128)(2,1)S(1)}, bf16[512,512]{1,0:T(8,128)(2,...) custom-call(s32[2]{0:T(128)S(1)} %pad_add_fusion.at_ref, bf16[512,512]{1,0:T(8,128)(2,1)S(1)} %bitcast.28, ...), custom_call_target="tpu_custom_call" | custom-call | tf_op jit(solution)/shard_map/pallas_call | solution.py:366
  151.6 4.3 %shard_map.76 = (f32[512,512]{1,0:T(8,128)S(1)}, f32[512,512]{1,0:T(8,128)S(1)}) custom-call(s32[2]{0:T(128)S(1)} %pad_add_fusion.at_ref, f32[2]{0:T(128)S(1)} %copy-done.14, f32[2]{0:T(128)S(1)} %collective-permute-done.12.energy_pair_ref, bf16[512,512]{1,0:T(8,128)(2,1)S(1)} %get-tuple-element.37.outer_ham, ...), custom_call_target="tpu_custom_call" | custom-call | tf_op jit(solution)/shard_map/pallas_call | solution.py:366
  155.9 1.9 shard_map.78.inner
  157.8 3.3 %collective-permute-start.22 = (bf16[512,512]{1,0:T(8,128)(2,1)S(1)}, bf16[512,512]{1,0:T(8,128)(2,1)S(1)}, u32[]{:S(2)}, u32[]{:S(2)}) collective-permute-start(bf16[512,512]{1,0:T(8,128)(2,1)S(1)} %shard_map.78.inner), channel_id=1, source_target_pairs={{0,16},{16,0},{1,17},{17,1},{2,18},{18,2},{3,19},{19,3},{4,20},{20... | collective-permute-start | bytes 1572872 | tf_op jit(solution)/shard_map/ppermute | solution.py:38
  161.1 1.9 shard_map.77.outer
  163.0 1.9 collective-permute-start.25
  164.9 2.1 shard_map.79
  167.0 2.0 shard_map.80
  169.0 4.7 %collective-permute-start.26 = (bf16[8,32,512]{2,1,0:T(8,128)(2,1)S(1)}, bf16[8,32,512]{2,1,0:T(8,128)(2,1)S(1)}, u32[]{:S(2)}, u32[]{:S(2)}) collective-permute-start(bf16[8,32,512]{2,1,0:T(8,128)(2,1)S(1)} %get-tuple-element.56), channel_id=1, source_target_pairs={{0,16},{16,0},{1,17},{17,1},{2,18},{18,2},{3,19},{19,3},{4,20},{20... | collective-permute-start | bytes 786440 | tf_op jit(solution)/shard_map/ppermute | solution.py:38
  173.7 3.5 %collective-permute-done.25.beyond = bf16[512,512]{1,0:T(8,128)(2,1)S(1)} collective-permute-done((bf16[512,512]{1,0:T(8,128)(2,1)S(1)}, bf16[512,512]{1,0:T(8,128)(2,1)S(1)}, u32[]{:S(2)}, u32[]{:S(2)}) %collective-permute-start.25) | collective-permute-done | bytes 524320 | tf_op jit(solution)/shard_map/ppermute | solution.py:44
  177.2 2.1 shard_map.81
  179.3 4.8 %collective-permute-start.29 = (bf16[8,32,512]{2,1,0:T(8,128)(2,1)S(1)}, bf16[8,32,512]{2,1,0:T(8,128)(2,1)S(1)}, u32[]{:S(2)}, u32[]{:S(2)}) collective-permute-start(bf16[8,32,512]{2,1,0:T(8,128)(2,1)S(1)} %get-tuple-element.59), channel_id=1, source_target_pairs={{0,16},{16,0},{1,17},{17,1},{2,18},{18,2},{3,19},{19,3},{4,20},{20... | collective-permute-start | bytes 786440 | tf_op jit(solution)/shard_map/ppermute | solution.py:38
  184.1 1.2 collective-permute-done.29
  185.3 23.3 %all_to_all.21.green_ref = bf16[32,32,512]{2,1,0:T(8,128)(2,1)S(1)} all-to-all(bf16[32,32,512]{2,1,0:T(8,128)(2,1)S(1)} %bitcast.34), channel_id=1, replica_groups=mesh['zlo'=2,'y'=4,'core'=2,'row'=4,'x'=4] {'x','zlo','y'}, dimensions={0} | all-to-all | bytes 2097152 | tf_op jit(solution)/shard_map/all_to_all | solution.py:346
  208.7 4.9 %shard_map.83 = bf16[32,32,512]{2,1,0:T(8,128)(2,1)} custom-call(s32[8]{0:T(128)S(1)} %copy-done.15, bf16[32,32,512]{2,1,0:T(8,128)(2,1)S(1)} %all_to_all.21.green_ref, bf16[32,512]{1,0:T(8,128)(2,1)S(1)} %bitcast.36), custom_call_target="tpu_custom_call" | custom-call | tf_op jit(solution)/shard_map/pallas_call | solution.py:337
  213.5 3.7 %all-to-all-start.3 = ((bf16[16,2,32,512]{3,2,1,0:T(8,128)(2,1)}), bf16[16,2,32,512]{3,2,1,0:T(8,128)(2,1)S(1)}, u32[]{:S(2)}, u32[]{:S(2)}) async-start(bf16[16,2,32,512]{3,2,1,0:T(8,128)(2,1)} %bitcast.15), calls=%async_computation.3 | async-start | bytes 2097152 | tf_op jit(solution)/shard_map/all_to_all | solution.py:346
  217.2 3.3 %collective-permute-start.24 = (bf16[512,512]{1,0:T(8,128)(2,1)S(1)}, bf16[512,512]{1,0:T(8,128)(2,1)S(1)}, u32[]{:S(2)}, u32[]{:S(2)}) collective-permute-start(bf16[512,512]{1,0:T(8,128)(2,1)S(1)} %get-tuple-element.53), channel_id=1, source_target_pairs={{1,1},{3,17},{17,2},{19,18},{5,5},{7,21},{21,6},{23,22},{9,9},{11,... | collective-permute-start | bytes 1572872 | tf_op jit(solution)/shard_map/ppermute | solution.py:101
  220.5 0.7 collective-permute-start.23
  221.2 4.0 %collective-permute-start.28 = (bf16[512,512]{1,0:T(8,128)(2,1)S(1)}, bf16[512,512]{1,0:T(8,128)(2,1)S(1)}, u32[]{:S(2)}, u32[]{:S(2)}) collective-permute-start(bf16[512,512]{1,0:T(8,128)(2,1)S(1)} %get-tuple-element.57), channel_id=1, source_target_pairs={{1,0},{3,16},{17,3},{19,19},{5,4},{7,20},{21,7},{23,23},{9,8},{11,... | collective-permute-start | bytes 1572872 | tf_op jit(solution)/shard_map/ppermute | solution.py:101
  225.2 1.3 collective-permute-start.27
  226.5 4.7 %collective-permute-done.24.inner_1 = bf16[512,512]{1,0:T(8,128)(2,1)S(1)} collective-permute-done((bf16[512,512]{1,0:T(8,128)(2,1)S(1)}, bf16[512,512]{1,0:T(8,128)(2,1)S(1)}, u32[]{:S(2)}, u32[]{:S(2)}) %collective-permute-start.24) | collective-permute-done | bytes 524320 | tf_op jit(solution)/shard_map/ppermute | solution.py:101
  231.2 6.8 %collective-permute-done.28.outer_1 = bf16[512,512]{1,0:T(8,128)(2,1)S(1)} collective-permute-done((bf16[512,512]{1,0:T(8,128)(2,1)S(1)}, bf16[512,512]{1,0:T(8,128)(2,1)S(1)}, u32[]{:S(2)}, u32[]{:S(2)}) %collective-permute-start.28) | collective-permute-done | bytes 524320 | tf_op jit(solution)/shard_map/ppermute | solution.py:101
  238.0 2.7 %collective-permute-done.27.outer_0 = bf16[512,512]{1,0:T(8,128)(2,1)S(1)} collective-permute-done((bf16[512,512]{1,0:T(8,128)(2,1)S(1)}, bf16[512,512]{1,0:T(8,128)(2,1)S(1)}, u32[]{:S(2)}, u32[]{:S(2)}) %collective-permute-start.27) | collective-permute-done | bytes 524320 | tf_op jit(solution)/shard_map/ppermute | solution.py:101
  240.6 2.0 shard_map.82
  242.7 1.0 copy.7
  (63 shorter events, 1.6 us)
Async XLA Ops:
  0.6 32.0 %collective-permute-start.8 = (bf16[512,512]{1,0:T(8,128)(2,1)}, bf16[512,512]{1,0:T(8,128)(2,1)S(1)}, u32[]{:S(2)}, u32[]{:S(2)}) collective-permute-start(bf16[512,512]{1,0:T(8,128)(2,1)} %bitcast.29), channel_id=1, source_target_pairs={{3,4},{7,8},{11,12},{4,3},{8,7},{12,11},{35,36},{39,40},{43,44},{3... | collective-permute-start | bytes 1572872 | tf_op jit(solution)/shard_map/ppermute | solution.py:51
  7.7 1.0 copy-start
  8.7 1.0 copy-start.2
  11.5 1.0 copy-start.10
  12.4 20.2 %copy-start.12 = (bf16[512,512]{1,0:T(8,128)(2,1)}, bf16[512,512]{1,0:T(8,128)(2,1)S(1)}, u32[]{:S(2)}) copy-start(bf16[512,512]{1,0:T(8,128)(2,1)S(1)} %get-tuple-element.33) | copy-start | bytes 1572868
  12.4 42.9 %copy-start.14 = (f32[2]{0:T(128)S(1)}, f32[2]{0:T(128)}, u32[]{:S(2)}) copy-start(f32[2]{0:T(128)} %energy_ref.5) | copy-start | bytes 28
  12.4 43.0 %copy-start.1 = (bf16[1,512,512]{2,1,0:T(8,128)(2,1)S(1)}, bf16[1,512,512]{2,1,0:T(8,128)(2,1)}, u32[]{:S(2)}) copy-start(bf16[1,512,512]{2,1,0:T(8,128)(2,1)} %param.7) | copy-start | bytes 1572868
  12.4 20.2 %collective-permute-start.5 = (bf16[512,512]{1,0:T(8,128)(2,1)S(1)}, bf16[512,512]{1,0:T(8,128)(2,1)S(1)}, u32[]{:S(2)}, u32[]{:S(2)}) collective-permute-start(bf16[512,512]{1,0:T(8,128)(2,1)S(1)} %get-tuple-element.33), channel_id=1, source_target_pairs={{0,1},{1,2},{2,3},{4,5},{5,6},{6,7},{8,9},{9,10},{10,11},{12,13},{... | collective-permute-start | bytes 1572872 | tf_op jit(solution)/shard_map/ppermute | solution.py:34
  13.9 18.8 %collective-permute-start.7 = (bf16[512,512]{1,0:T(8,128)(2,1)S(1)}, bf16[512,512]{1,0:T(8,128)(2,1)S(1)}, u32[]{:S(2)}, u32[]{:S(2)}) collective-permute-start(bf16[512,512]{1,0:T(8,128)(2,1)S(1)} %get-tuple-element.33), channel_id=1, source_target_pairs={{1,0},{2,1},{3,2},{5,4},{6,5},{7,6},{9,8},{10,9},{11,10},{13,12},{... | collective-permute-start | bytes 1572872 | tf_op jit(solution)/shard_map/ppermute | solution.py:34
  18.4 15.6 %copy-start.11 = (f32[512,512]{1,0:T(8,128)S(1)}, f32[512,512]{1,0:T(8,128)}, u32[]{:S(2)}) copy-start(f32[512,512]{1,0:T(8,128)} %copy-done.10) | copy-start | bytes 3145732
  19.5 11.2 %collective-permute-start = (bf16[256,512]{1,0:T(8,128)(2,1)S(1)}, bf16[256,512]{1,0:T(8,128)(2,1)S(1)}, u32[]{:S(2)}, u32[]{:S(2)}) collective-permute-start(bf16[256,512]{1,0:T(8,128)(2,1)S(1)} %dynamic-slice_bitcast_fusion), channel_id=1, source_target_pairs={{0,1},{1,2},{2,3},{3,4},{4,5},{5,6},{6,7},{7,8},{8,9},{9,10},{10,1... | collective-permute-start | bytes 786440 | tf_op jit(solution)/shard_map/ppermute | solution.py:26
  30.7 3.4 %collective-permute-start.1 = (bf16[256,512]{1,0:T(8,128)(2,1)S(1)}, bf16[256,512]{1,0:T(8,128)(2,1)S(1)}, u32[]{:S(2)}, u32[]{:S(2)}) collective-permute-start(bf16[256,512]{1,0:T(8,128)(2,1)S(1)} %collective-permute-done.mine_ref), channel_id=1, source_target_pairs={{0,16},{16,0},{1,17},{17,1},{2,18},{18,2},{3,19},{19,3},{4,20},{20... | collective-permute-start | bytes 786440 | tf_op jit(solution)/shard_map/ppermute | solution.py:38
  30.7 19.7 %collective-permute-start.13 = (bf16[256,512]{1,0:T(8,128)(2,1)S(1)}, bf16[256,512]{1,0:T(8,128)(2,1)S(1)}, u32[]{:S(2)}, u32[]{:S(2)}) collective-permute-start(bf16[256,512]{1,0:T(8,128)(2,1)S(1)} %dynamic-slice_bitcast_fusion), channel_id=1, source_target_pairs={{1,0},{2,1},{3,2},{4,3},{5,4},{6,5},{7,6},{8,7},{9,8},{10,9},{11,1... | collective-permute-start | bytes 786440 | tf_op jit(solution)/shard_map/ppermute | solution.py:26
  32.6 24.7 %copy-start.4 = (bf16[512,512]{1,0:T(8,128)(2,1)}, bf16[512,512]{1,0:T(8,128)(2,1)S(1)}, u32[]{:S(2)}) copy-start(bf16[512,512]{1,0:T(8,128)(2,1)S(1)} %collective-permute-done.5.one_ref.mine_1) | copy-start | bytes 1572868
  32.6 24.7 %copy-start.6 = (bf16[512,512]{1,0:T(8,128)(2,1)}, bf16[512,512]{1,0:T(8,128)(2,1)S(1)}, u32[]{:S(2)}) copy-start(bf16[512,512]{1,0:T(8,128)(2,1)S(1)} %collective-permute-done.7.three_ref.mine_3) | copy-start | bytes 1572868
  33.3 24.1 %copy-start.3 = (bf16[1,512,512]{2,1,0:T(8,128)(2,1)S(1)}, bf16[1,512,512]{2,1,0:T(8,128)(2,1)}, u32[]{:S(2)}) copy-start(bf16[1,512,512]{2,1,0:T(8,128)(2,1)} %param.6) | copy-start | bytes 1572868
  33.3 24.0 %collective-permute-start.9 = (bf16[512,512]{1,0:T(8,128)(2,1)S(1)}, bf16[512,512]{1,0:T(8,128)(2,1)S(1)}, u32[]{:S(2)}, u32[]{:S(2)}) collective-permute-start(bf16[512,512]{1,0:T(8,128)(2,1)S(1)} %get-tuple-element.34.previous_ref), channel_id=1, source_target_pairs={{0,16},{16,0},{1,17},{17,1},{2,18},{18,2},{3,19},{19,3},{4,20},{20... | collective-permute-start | bytes 1572872 | tf_op jit(solution)/shard_map/ppermute | solution.py:38
  33.9 23.5 %collective-permute-start.11 = (bf16[512,512]{1,0:T(8,128)(2,1)S(1)}, bf16[512,512]{1,0:T(8,128)(2,1)S(1)}, u32[]{:S(2)}, u32[]{:S(2)}) collective-permute-start(bf16[512,512]{1,0:T(8,128)(2,1)S(1)} %get-tuple-element.35.next_ref), channel_id=1, source_target_pairs={{0,16},{16,0},{1,17},{17,1},{2,18},{18,2},{3,19},{19,3},{4,20},{20... | collective-permute-start | bytes 1572872 | tf_op jit(solution)/shard_map/ppermute | solution.py:38
  35.1 22.3 %copy-start.8 = (bf16[512,512]{1,0:T(8,128)(2,1)}, bf16[512,512]{1,0:T(8,128)(2,1)S(1)}, u32[]{:S(2)}) copy-start(bf16[512,512]{1,0:T(8,128)(2,1)S(1)} %get-tuple-element.32.below_ref) | copy-start | bytes 1572868
  35.1 20.3 %collective-permute-start.15 = (bf16[256,512]{1,0:T(8,128)(2,1)S(1)}, bf16[256,512]{1,0:T(8,128)(2,1)S(1)}, u32[]{:S(2)}, u32[]{:S(2)}) collective-permute-start(bf16[256,512]{1,0:T(8,128)(2,1)S(1)} %get-tuple-element.43), channel_id=1, source_target_pairs={{0,1},{1,2},{2,3},{3,4},{4,5},{5,6},{6,7},{7,8},{8,9},{9,10},{10,1... | collective-permute-start | bytes 786440 | tf_op jit(solution)/shard_map/ppermute | solution.py:26
  50.4 5.0 %collective-permute-start.14 = (bf16[256,512]{1,0:T(8,128)(2,1)S(1)}, bf16[256,512]{1,0:T(8,128)(2,1)S(1)}, u32[]{:S(2)}, u32[]{:S(2)}) collective-permute-start(bf16[256,512]{1,0:T(8,128)(2,1)S(1)} %collective-permute-done.13.mine_ref), channel_id=1, source_target_pairs={{0,16},{16,0},{1,17},{17,1},{2,18},{18,2},{3,19},{19,3},{4,20},{20... | collective-permute-start | bytes 786440 | tf_op jit(solution)/shard_map/ppermute | solution.py:38
  55.4 2.0 collective-permute-start.16
  62.4 21.1 %copy-start.16 = (bf16[512,512]{1,0:T(8,128)(2,1)}, bf16[512,512]{1,0:T(8,128)(2,1)S(1)}, u32[]{:S(2)}) copy-start(bf16[512,512]{1,0:T(8,128)(2,1)S(1)} %get-tuple-element.47) | copy-start | bytes 1572868
  62.4 21.1 %copy-start.17 = (bf16[512,512]{1,0:T(8,128)(2,1)}, bf16[512,512]{1,0:T(8,128)(2,1)S(1)}, u32[]{:S(2)}) copy-start(bf16[512,512]{1,0:T(8,128)(2,1)S(1)} %get-tuple-element.46) | copy-start | bytes 1572868
  62.4 21.1 %copy-start.13 = (bf16[1,32,512]{2,1,0:T(8,128)(2,1)S(1)}, bf16[1,32,512]{2,1,0:T(8,128)(2,1)}, u32[]{:S(2)}) copy-start(bf16[1,32,512]{2,1,0:T(8,128)(2,1)} %param.8) | copy-start | bytes 98308
  62.4 21.1 %copy-start.15 = (s32[8]{0:T(128)S(1)}, s32[8]{0:T(128)}, u32[]{:S(2)}) copy-start(s32[8]{0:T(128)} %offset_ref.3) | copy-start | bytes 100
  88.3 55.1 %all-to-all-start.1 = ((bf16[32,32,512]{2,1,0:T(8,128)(2,1)}), bf16[32,32,512]{2,1,0:T(8,128)(2,1)S(1)}, u32[]{:S(2)}, u32[]{:S(2)}) async-start(bf16[32,32,512]{2,1,0:T(8,128)(2,1)} %shard_map.74), calls=%async_computation.1 | async-start | bytes 2097152 | tf_op jit(solution)/shard_map/all_to_all | solution.py:346
  93.9 25.6 %collective-permute-start.6 = (bf16[512,512]{1,0:T(8,128)(2,1)}, bf16[512,512]{1,0:T(8,128)(2,1)}, u32[]{:S(2)}, u32[]{:S(2)}) collective-permute-start(bf16[512,512]{1,0:T(8,128)(2,1)} %copy-done.12), channel_id=1, source_target_pairs={{0,2},{1,3},{2,0},{3,1},{4,6},{5,7},{6,4},{7,5},{8,10},{9,11},{10,... | collective-permute-start | bytes 1572872 | tf_op jit(solution)/shard_map/ppermute | solution.py:30
  95.4 33.1 %collective-permute-start.18 = (bf16[512,512]{1,0:T(8,128)(2,1)}, bf16[512,512]{1,0:T(8,128)(2,1)}, u32[]{:S(2)}, u32[]{:S(2)}) collective-permute-start(bf16[512,512]{1,0:T(8,128)(2,1)} %copy-done.17), channel_id=1, source_target_pairs={{0,0},{1,1},{2,16},{3,17},{16,2},{17,3},{18,18},{19,19},{4,4},{5,5... | collective-permute-start | bytes 1572872 | tf_op jit(solution)/shard_map/ppermute | solution.py:60
  98.3 36.0 %collective-permute-start.19 = (bf16[512,512]{1,0:T(8,128)(2,1)}, bf16[512,512]{1,0:T(8,128)(2,1)}, u32[]{:S(2)}, u32[]{:S(2)}) collective-permute-start(bf16[512,512]{1,0:T(8,128)(2,1)} %copy-done.16), channel_id=1, source_target_pairs={{0,1},{1,0},{2,17},{3,16},{16,3},{17,2},{18,19},{19,18},{4,5},{5,4... | collective-permute-start | bytes 1572872 | tf_op jit(solution)/shard_map/ppermute | solution.py:60
  99.4 39.1 %collective-permute-start.4 = (bf16[512,512]{1,0:T(8,128)(2,1)}, bf16[512,512]{1,0:T(8,128)(2,1)}, u32[]{:S(2)}, u32[]{:S(2)}) collective-permute-start(bf16[512,512]{1,0:T(8,128)(2,1)} %copy-done.12), channel_id=1, source_target_pairs={{0,3},{4,7},{8,11},{12,15},{32,35},{36,39},{40,43},{44,47},{64,67}... | collective-permute-start | bytes 1572872 | tf_op jit(solution)/shard_map/ppermute | solution.py:55
  119.5 23.9 %collective-permute-start.10 = (bf16[512,512]{1,0:T(8,128)(2,1)}, bf16[512,512]{1,0:T(8,128)(2,1)}, u32[]{:S(2)}, u32[]{:S(2)}) collective-permute-start(bf16[512,512]{1,0:T(8,128)(2,1)} %collective-permute-done.6.mine_2), channel_id=1, source_target_pairs={{0,16},{16,0},{1,17},{17,1},{2,18},{18,2},{3,19},{19,3},{4,20},{20... | collective-permute-start | bytes 1572872 | tf_op jit(solution)/shard_map/ppermute | solution.py:38
  121.8 21.8 %collective-permute-start.3 = (bf16[512,512]{1,0:T(8,128)(2,1)}, bf16[512,512]{1,0:T(8,128)(2,1)}, u32[]{:S(2)}, u32[]{:S(2)}) collective-permute-start(bf16[512,512]{1,0:T(8,128)(2,1)} %get-tuple-element.62), channel_id=1, source_target_pairs={{0,2},{16,3},{19,16},{4,6},{20,7},{23,20},{8,10},{24,11},{27,24},{... | collective-permute-start | bytes 1572872 | tf_op jit(solution)/shard_map/ppermute | solution.py:55
  128.5 17.4 %collective-permute-start.2 = (bf16[512,512]{1,0:T(8,128)(2,1)}, bf16[512,512]{1,0:T(8,128)(2,1)}, u32[]{:S(2)}, u32[]{:S(2)}) collective-permute-start(bf16[512,512]{1,0:T(8,128)(2,1)} %get-tuple-element.63), channel_id=1, source_target_pairs={{0,1},{16,3},{3,16},{4,5},{20,7},{7,20},{8,9},{24,11},{11,24},{12,... | collective-permute-start | bytes 1572872 | tf_op jit(solution)/shard_map/ppermute | solution.py:55
  136.6 14.9 %collective-permute-start.20 = (bf16[512,512]{1,0:T(8,128)(2,1)}, bf16[512,512]{1,0:T(8,128)(2,1)}, u32[]{:S(2)}, u32[]{:S(2)}) collective-permute-start(bf16[512,512]{1,0:T(8,128)(2,1)} %get-tuple-element.48.outer.green_ref), channel_id=1, source_target_pairs={{16,4},{20,8},{24,12},{4,16},{8,20},{12,24},{17,5},{21,9},{25,13},... | collective-permute-start | bytes 1572872 | tf_op jit(solution)/shard_map/ppermute | solution.py:44
  138.6 13.0 %collective-permute-start.21 = (bf16[512,512]{1,0:T(8,128)(2,1)}, bf16[512,512]{1,0:T(8,128)(2,1)}, u32[]{:S(2)}, u32[]{:S(2)}) collective-permute-start(bf16[512,512]{1,0:T(8,128)(2,1)} %get-tuple-element.49.inner.green_ref), channel_id=1, source_target_pairs={{0,16},{16,0},{1,17},{17,1},{2,18},{18,2},{3,19},{19,3},{4,20},{20... | collective-permute-start | bytes 1572872 | tf_op jit(solution)/shard_map/ppermute | solution.py:38
  143.5 12.4 %collective-permute-start.17 = (bf16[2,8,32,512]{3,2,1,0:T(8,128)(2,1)S(1)}, bf16[2,8,32,512]{3,2,1,0:T(8,128)(2,1)S(1)}, u32[]{:S(2)}, u32[]{:S(2)}) collective-permute-start(bf16[2,8,32,512]{3,2,1,0:T(8,128)(2,1)S(1)} %constant_dynamic-slice_fusion), channel_id=1, source_target_pairs={{0,16},{16,0},{1,17},{17,1},{2,18},{18,2},{3,19},{19,3},{4,20},{20... | collective-permute-start | bytes 1572872 | tf_op jit(solution)/shard_map/ppermute | solution.py:38
  143.6 8.0 %collective-permute-start.12 = (f32[2]{0:T(128)S(1)}, f32[2]{0:T(128)S(1)}, u32[]{:S(2)}, u32[]{:S(2)}) collective-permute-start(f32[2]{0:T(128)S(1)} %copy-done.14), channel_id=1, source_target_pairs={{0,16},{16,0},{1,17},{17,1},{2,18},{18,2},{3,19},{19,3},{4,20},{20... | collective-permute-start | bytes 32 | tf_op jit(solution)/shard_map/ppermute | solution.py:38
  145.9 1.0 copy-start.5
  146.9 1.0 copy-start.7
  148.0 1.0 copy-start.9
  157.8 9.2 %collective-permute-start.22 = (bf16[512,512]{1,0:T(8,128)(2,1)S(1)}, bf16[512,512]{1,0:T(8,128)(2,1)S(1)}, u32[]{:S(2)}, u32[]{:S(2)}) collective-permute-start(bf16[512,512]{1,0:T(8,128)(2,1)S(1)} %shard_map.78.inner), channel_id=1, source_target_pairs={{0,16},{16,0},{1,17},{17,1},{2,18},{18,2},{3,19},{19,3},{4,20},{20... | collective-permute-start | bytes 1572872 | tf_op jit(solution)/shard_map/ppermute | solution.py:38
  163.0 14.2 %collective-permute-start.25 = (bf16[512,512]{1,0:T(8,128)(2,1)S(1)}, bf16[512,512]{1,0:T(8,128)(2,1)S(1)}, u32[]{:S(2)}, u32[]{:S(2)}) collective-permute-start(bf16[512,512]{1,0:T(8,128)(2,1)S(1)} %shard_map.77.outer), channel_id=1, source_target_pairs={{16,4},{20,8},{24,12},{4,16},{8,20},{12,24},{17,5},{21,9},{25,13},... | collective-permute-start | bytes 1572872 | tf_op jit(solution)/shard_map/ppermute | solution.py:44
  169.0 8.2 %collective-permute-start.26 = (bf16[8,32,512]{2,1,0:T(8,128)(2,1)S(1)}, bf16[8,32,512]{2,1,0:T(8,128)(2,1)S(1)}, u32[]{:S(2)}, u32[]{:S(2)}) collective-permute-start(bf16[8,32,512]{2,1,0:T(8,128)(2,1)S(1)} %get-tuple-element.56), channel_id=1, source_target_pairs={{0,16},{16,0},{1,17},{17,1},{2,18},{18,2},{3,19},{19,3},{4,20},{20... | collective-permute-start | bytes 786440 | tf_op jit(solution)/shard_map/ppermute | solution.py:38
  179.3 6.0 %collective-permute-start.29 = (bf16[8,32,512]{2,1,0:T(8,128)(2,1)S(1)}, bf16[8,32,512]{2,1,0:T(8,128)(2,1)S(1)}, u32[]{:S(2)}, u32[]{:S(2)}) collective-permute-start(bf16[8,32,512]{2,1,0:T(8,128)(2,1)S(1)} %get-tuple-element.59), channel_id=1, source_target_pairs={{0,16},{16,0},{1,17},{17,1},{2,18},{18,2},{3,19},{19,3},{4,20},{20... | collective-permute-start | bytes 786440 | tf_op jit(solution)/shard_map/ppermute | solution.py:38
  213.5 29.1 %all-to-all-start.3 = ((bf16[16,2,32,512]{3,2,1,0:T(8,128)(2,1)}), bf16[16,2,32,512]{3,2,1,0:T(8,128)(2,1)S(1)}, u32[]{:S(2)}, u32[]{:S(2)}) async-start(bf16[16,2,32,512]{3,2,1,0:T(8,128)(2,1)} %bitcast.15), calls=%async_computation.3 | async-start | bytes 2097152 | tf_op jit(solution)/shard_map/all_to_all | solution.py:346
  217.2 14.0 %collective-permute-start.24 = (bf16[512,512]{1,0:T(8,128)(2,1)S(1)}, bf16[512,512]{1,0:T(8,128)(2,1)S(1)}, u32[]{:S(2)}, u32[]{:S(2)}) collective-permute-start(bf16[512,512]{1,0:T(8,128)(2,1)S(1)} %get-tuple-element.53), channel_id=1, source_target_pairs={{1,1},{3,17},{17,2},{19,18},{5,5},{7,21},{21,6},{23,22},{9,9},{11,... | collective-permute-start | bytes 1572872 | tf_op jit(solution)/shard_map/ppermute | solution.py:101
  220.5 10.7 %collective-permute-start.23 = (bf16[512,512]{1,0:T(8,128)(2,1)S(1)}, bf16[512,512]{1,0:T(8,128)(2,1)S(1)}, u32[]{:S(2)}, u32[]{:S(2)}) collective-permute-start(bf16[512,512]{1,0:T(8,128)(2,1)S(1)} %get-tuple-element.53), channel_id=1, source_target_pairs={{0,1},{2,17},{16,2},{18,18},{4,5},{6,21},{20,6},{22,22},{8,9},{10,... | collective-permute-start | bytes 1572872 | tf_op jit(solution)/shard_map/ppermute | solution.py:101
  221.2 16.8 %collective-permute-start.28 = (bf16[512,512]{1,0:T(8,128)(2,1)S(1)}, bf16[512,512]{1,0:T(8,128)(2,1)S(1)}, u32[]{:S(2)}, u32[]{:S(2)}) collective-permute-start(bf16[512,512]{1,0:T(8,128)(2,1)S(1)} %get-tuple-element.57), channel_id=1, source_target_pairs={{1,0},{3,16},{17,3},{19,19},{5,4},{7,20},{21,7},{23,23},{9,8},{11,... | collective-permute-start | bytes 1572872 | tf_op jit(solution)/shard_map/ppermute | solution.py:101
  225.2 15.5 %collective-permute-start.27 = (bf16[512,512]{1,0:T(8,128)(2,1)S(1)}, bf16[512,512]{1,0:T(8,128)(2,1)S(1)}, u32[]{:S(2)}, u32[]{:S(2)}) collective-permute-start(bf16[512,512]{1,0:T(8,128)(2,1)S(1)} %get-tuple-element.57), channel_id=1, source_target_pairs={{0,0},{2,16},{16,3},{18,19},{4,4},{6,20},{20,7},{22,23},{8,8},{10,... | collective-permute-start | bytes 1572872 | tf_op jit(solution)/shard_map/ppermute | solution.py:101
